TPU v7x, 32 devices: a whole 2x2x4 slice. The times are simulated.
32 devices in a mesh: expert: 16 (over z, y, core), dp: 2 (over x).
Axes of the slice: x: 2, y: 2, z: 4, core: 2. Of those that a mesh axis runs over, the one named last changes fastest.
Arguments:
- tokens: bfloat16 [2, 512, 2048], P('dp', 'expert'), may hold values from -6 to 6
- cotangent: bfloat16 [2, 512, 2048], P('dp', 'expert'), may hold values from -6 to 6
- expert_ids: int32 [2, 512, 8], P('dp', 'expert'), may hold values from 0 to 15, all different within a row; in each aligned block of 32 rows (0 to 31, 32 to 63, ..., all dimensions but the last counted through in order) at most 24 rows name the same one
- gate_probs: bfloat16 [2, 512, 8], P('dp', 'expert'), may hold values from 0.029907227 to 0.59765625
- alpha: float32 [1], replicated, may hold values from 0.4 to 1.2
- gamma: float32 [2048], replicated, may hold values from 0.5 to 1.5
- beta: float32 [2048], replicated, may hold values from -1.5 to 1.5
- w_in: bfloat16 [16, 2, 768, 2048], P('expert', None, 'dp'), may hold values from -0.125 to 0.125
- w_down: bfloat16 [16, 768, 2048], P('expert', 'dp'), may hold values from -0.21875 to 0.21875
Outputs:
- grad_tokens: bfloat16 [2, 512, 2048], P('dp', 'expert')
- grad_probs: bfloat16 [2, 512, 8], P('dp', 'expert')
- grad_down: bfloat16 [16, 768, 2048], P('expert', 'dp')
- grad_gamma: float32 [2048], replicated
- grad_beta: float32 [2048], replicated
- grad_alpha: float32 [1], replicated
Inputs may be any that keep to these rules, and one draw needn't show every extreme that they name: `expert_ids`: each token names 8 different experts; among the 32 tokens of one block no expert is named by more than 24 tokens, and in some block some expert is named by exactly 24.
All inputs are finite; a program needn't handle non-finite values.
Results may differ from a plain program's by a relative error of at most 0.008.
Values may be sent and summed in bfloat16 or wider, within the bound.
No kernel may reach another device: no remote copies, remote signals or barrier semaphores. Data moves between devices by JAX's collectives and lax.ppermute only.
A program may use at most 64 MiB of HBM per device.

v0:
```python
import jax
import jax.numpy as jnp
from jax import lax
from jax.sharding import PartitionSpec as P

residual_scale = 0.7071


def contract_width(left, right):
    return lax.dot_general(
        left, right, (((1,), (1,)), ((), ())), preferred_element_type=jnp.float32
    )


def slot_layout(ids_local, expert_count, capacity):
    token_count, top_count = ids_local.shape
    labels = jnp.arange(expert_count, dtype=jnp.int32)
    onehot = (ids_local[:, :, None] == labels[None, None, :]).astype(jnp.int32)
    picks = jnp.sum(onehot, axis=1)
    before = jnp.cumsum(picks, axis=0) - picks
    slots = jnp.sum(onehot * before[:, None, :], axis=2)
    position = ids_local * capacity + slots
    pairs = jnp.arange(token_count * top_count, dtype=jnp.int32)
    table = jnp.full((expert_count * capacity,), token_count * top_count, jnp.int32)
    table = table.at[position.reshape(-1)].set(pairs)
    return (position, table)


def shards(tokens, cotangent, expert_ids, gate_probs, alpha, gamma, beta, w_in, w_down):
    expert_count = lax.axis_size("expert")
    token_count = tokens.shape[1]
    top_count = expert_ids.shape[2]
    width = tokens.shape[2]
    capacity = 3 * token_count * top_count // (2 * expert_count)
    rows_total = expert_count * capacity
    inputs = tokens[0].astype(jnp.float32)
    squashed = jnp.tanh(alpha[0] * inputs)
    normed = (gamma * squashed + beta).astype(jnp.bfloat16)
    position, table = slot_layout(expert_ids[0], expert_count, capacity)
    source_token = table // top_count
    zero_row = jnp.zeros((1, width), jnp.bfloat16)
    normed_pad = jnp.concatenate([normed, zero_row], axis=0)
    cot_pad = jnp.concatenate([cotangent[0], zero_row], axis=0)
    prob_pad = jnp.concatenate([gate_probs[0].reshape(-1), jnp.zeros((1,), jnp.bfloat16)], axis=0)
    send_rows = normed_pad[source_token].reshape(expert_count, capacity, width)
    send_cot = cot_pad[source_token].reshape(expert_count, capacity, width)
    send_prob = prob_pad[table].reshape(expert_count, capacity)
    recv_rows, recv_cot, recv_prob = (
        lax.all_to_all(send_rows, "expert", split_axis=0, concat_axis=0, tiled=True),
        lax.all_to_all(send_cot, "expert", split_axis=0, concat_axis=0, tiled=True),
        lax.all_to_all(send_prob, "expert", split_axis=0, concat_axis=0, tiled=True),
    )
    in_rows = recv_rows.reshape(rows_total, width)
    cot_rows = recv_cot.reshape(rows_total, width)
    prob_rows = recv_prob.reshape(rows_total).astype(jnp.float32)
    gate_up, lower_full = (
        lax.all_gather(w_in, "dp", axis=2, tiled=True),
        lax.all_gather(w_down, "dp", axis=1, tiled=True),
    )
    gate_pre = contract_width(in_rows, gate_up[0, 0])
    up_value = contract_width(in_rows, gate_up[0, 1])
    w_gate = gate_up[0, 0]
    w_upper = gate_up[0, 1]
    w_lower = lower_full[0]
    sigma = jax.nn.sigmoid(gate_pre)
    activation = (gate_pre * sigma * up_value).astype(jnp.bfloat16)
    back = contract_width(cot_rows, w_lower)
    weight_row = residual_scale * prob_rows
    scaled_cot = (weight_row[:, None] * cot_rows.astype(jnp.float32)).astype(jnp.bfloat16)
    row_grad = residual_scale * jnp.sum(activation.astype(jnp.float32) * back, axis=1)
    d_act = weight_row[:, None] * back
    d_gate = (d_act * up_value * sigma * (1.0 + gate_pre * (1.0 - sigma))).astype(jnp.bfloat16)
    d_up = (d_act * gate_pre * sigma).astype(jnp.bfloat16)
    d_rows = (
        jnp.dot(d_gate, w_gate, preferred_element_type=jnp.float32)
        + jnp.dot(d_up, w_upper, preferred_element_type=jnp.float32)
    ).astype(jnp.bfloat16)
    back_rows, back_probs = (
        lax.all_to_all(
            d_rows.reshape(expert_count, capacity, width),
            "expert",
            split_axis=0,
            concat_axis=0,
            tiled=True,
        ),
        lax.all_to_all(
            row_grad.astype(jnp.bfloat16).reshape(expert_count, capacity),
            "expert",
            split_axis=0,
            concat_axis=0,
            tiled=True,
        ),
    )
    partial_grad = lax.dot_general(
        activation, scaled_cot, (((0,), (0,)), ((), ())), preferred_element_type=jnp.float32
    )
    grad_down = lax.psum_scatter(
        partial_grad[None].astype(jnp.bfloat16), "dp", scatter_dimension=1, tiled=True
    )
    picked = back_rows.reshape(rows_total, width)[position]
    grad_normed = jnp.sum(picked.astype(jnp.float32), axis=1)
    grad_probs = back_probs.reshape(rows_total)[position]
    gamma_part = jnp.sum(grad_normed * squashed, axis=0)
    beta_part = jnp.sum(grad_normed, axis=0)
    pre_grad = grad_normed * gamma * (1.0 - squashed * squashed)
    alpha_part = jnp.sum(pre_grad * inputs).reshape(1)
    grad_gamma, grad_beta, grad_alpha = lax.psum(
        (gamma_part, beta_part, alpha_part), ("expert", "dp")
    )
    grad_tokens = (cotangent[0].astype(jnp.float32) + alpha[0] * pre_grad).astype(jnp.bfloat16)
    return (grad_tokens[None], grad_probs[None], grad_down, grad_gamma, grad_beta, grad_alpha)


def solution(mesh):
    placed = (
        P("dp", "expert", None),
        P("dp", "expert", None),
        P("dp", "expert", None),
        P("dp", "expert", None),
        P(),
        P(),
        P(),
        P("expert", None, "dp", None),
        P("expert", "dp", None),
    )
    return jax.shard_map(
        shards,
        mesh=mesh,
        in_specs=placed,
        out_specs=(
            P("dp", "expert", None),
            P("dp", "expert", None),
            P("expert", "dp", None),
            P(),
            P(),
            P(),
        ),
        check_vma=False,
    )
```

profile of v0, /device:TPU:0, one launch (start us, length us, event | category | flops | bytes accessed | tf_op | source)
XLA Modules:
  0.0 256.3 jit_solution(2240395038127851113)
XLA Ops:
  8.8 1.4 scatter_custom_fusion
  10.2 2.8 %gather_fusion = bf16[384]{0:T(512)(128)(2,1)S(1)} fusion(bf16[257]{0:T(512)(128)(2,1)S(1)} %pad_maximum_fusion, s32[1024]{0:T(1024)S(1)} %get-tuple-element.35), kind=kCustom, calls=%fused_computation | custom fusion | bytes 3072 | tf_op jit(solution)/shard_map/gather | solution.py:47
  13.8 7.4 %all-to-all-start = ((bf16[16,1,24]{2,1,0:T(2,128)(2,1)}), bf16[16,1,24]{2,1,0:T(2,128)(2,1)S(1)}, u32[]{:S(2)}, u32[]{:S(2)}) async-start(bf16[16,1,24]{2,1,0:T(2,128)(2,1)} %all_to_all.25), calls=%async_computation | async-start | bytes 16384 | tf_op jit(solution)/shard_map/all_to_all | solution.py:51
  21.9 3.1 %gather_fusion.2 = bf16[384,2048]{1,0:T(8,128)(2,1)} fusion(bf16[33,2048]{1,0:T(8,128)(2,1)S(1)} %concatenate.11, s32[1024]{0:T(1024)S(1)} %get-tuple-element.34), kind=kCustom, calls=%fused_computation.2 | custom fusion | bytes 3147264 | tf_op jit(solution)/shard_map/gather | solution.py:45
  25.0 2.4 all-to-all-done
  27.5 3.7 %all-to-all-start.2 = ((bf16[16,24,2048]{2,1,0:T(8,128)(2,1)}), bf16[16,24,2048]{2,1,0:T(8,128)(2,1)S(1)}, u32[]{:S(2)}, u32[]{:S(2)}) async-start(bf16[16,24,2048]{2,1,0:T(8,128)(2,1)} %bitcast.8), calls=%async_computation.2 | async-start | bytes 3145728 | tf_op jit(solution)/shard_map/all_to_all | solution.py:49
  32.1 3.1 %gather_fusion.1 = bf16[384,2048]{1,0:T(8,128)(2,1)} fusion(bf16[33,2048]{1,0:T(8,128)(2,1)S(1)} %concatenate.10, s32[1024]{0:T(1024)S(1)} %get-tuple-element.34), kind=kCustom, calls=%fused_computation.1 | custom fusion | bytes 3147264 | tf_op jit(solution)/shard_map/gather | solution.py:46
  35.3 27.8 %all-to-all-done.2 = bf16[16,24,2048]{2,1,0:T(8,128)(2,1)S(1)} async-done(((bf16[16,24,2048]{2,1,0:T(8,128)(2,1)}), bf16[16,24,2048]{2,1,0:T(8,128)(2,1)S(1)}, u32[]{:S(2)}, u32[]{:S(2)}) %all-to-all-start.2) | async-done | bytes 1572896 | tf_op jit(solution)/shard_map/all_to_all | solution.py:49
  63.1 9.1 %all-to-all-start.1 = ((bf16[16,24,2048]{2,1,0:T(8,128)(2,1)}), bf16[16,24,2048]{2,1,0:T(8,128)(2,1)S(1)}, u32[]{:S(2)}, u32[]{:S(2)}) async-start(bf16[16,24,2048]{2,1,0:T(8,128)(2,1)} %bitcast.4), calls=%async_computation.1 | async-start | bytes 3145728 | tf_op jit(solution)/shard_map/all_to_all | solution.py:50
  72.4 20.3 %all-gather.5.cloned.1.call-done = bf16[1,2,768,2048]{3,2,1,0:T(8,128)(2,1)} async-done(((bf16[1,2,384,2048]{3,2,1,0:T(8,128)(2,1)}), bf16[1,2,768,2048]{3,2,1,0:T(8,128)(2,1)}) %all-gather.5.cloned.1.call-update) | async-done | bytes 6291472 | tf_op jit(solution)/shard_map/all_gather | solution.py:57
  92.7 4.6 %fusion.5 = f32[384,768]{1,0:T(8,128)} fusion(bf16[384,2048]{1,0:T(8,128)(2,1)S(1)} %bitcast.79, bf16[1,2,768,2048]{3,2,1,0:T(8,128)(2,1)} %all-gather.5.cloned.1.call-done), kind=kOutput, calls=%fused_computation.16 | convolution fusion | flops 1207959552 | bytes 5898240 | tf_op jit(solution)/shard_map/dot_general | solution.py:10
  97.3 2.5 fusion.3
  99.8 4.4 %all-to-all-done.1 = bf16[16,24,2048]{2,1,0:T(8,128)(2,1)S(1)} async-done(((bf16[16,24,2048]{2,1,0:T(8,128)(2,1)}), bf16[16,24,2048]{2,1,0:T(8,128)(2,1)S(1)}, u32[]{:S(2)}, u32[]{:S(2)}) %all-to-all-start.1) | async-done | bytes 1572896 | tf_op jit(solution)/shard_map/all_to_all | solution.py:50
  104.2 35.0 %all-gather.3.cloned.1.call-done = bf16[1,768,2048]{2,1,0:T(8,128)(2,1)} async-done(((bf16[1,384,2048]{2,1,0:T(8,128)(2,1)}), bf16[1,768,2048]{2,1,0:T(8,128)(2,1)}) %all-gather.3.cloned.1.call-update) | async-done | bytes 3145744 | tf_op jit(solution)/shard_map/all_gather | solution.py:58
  139.2 5.0 %multiply_reduce_fusion = (f32[384]{0:T(512)S(1)}, bf16[384,768]{1,0:T(8,128)(2,1)S(1)}, f32[384,768]{1,0:T(8,128)}) fusion(f32[384,768]{1,0:T(8,128)} %fusion.3, f32[384,768]{1,0:T(8,128)} %fusion.5, bf16[384,2048]{1,0:T(8,128)(2,1)S(1)} %bitcast.81, bf16[1,768,2048]{2,1,0:T(8,128)(2,1)} %all-gather.3.cloned.1.call-done), kind=kOutput, calls=%fused_computation.21 | convolution fusion | flops 1210613376 | bytes 8848896 | tf_op jit(solution)/shard_map/dot_general | solution.py:10
  144.2 3.6 %fusion.2 = bf16[1,768,2048]{2,1,0:T(8,128)(2,1)} fusion(bf16[384,768]{1,0:T(8,128)(2,1)S(1)} %get-tuple-element.30, bf16[384,2048]{1,0:T(8,128)(2,1)S(1)} %bitcast.82, f32[384]{0:T(512)S(1)} %mul.166), kind=kOutput, calls=%fused_computation.13 | convolution fusion | flops 1211891712 | bytes 5309952 | tf_op jit(solution)/shard_map/dot_general | solution.py:94
  148.6 5.6 %all-to-all-start.4 = ((bf16[16,1,24]{2,1,0:T(2,128)(2,1)}), bf16[16,1,24]{2,1,0:T(2,128)(2,1)S(1)}, u32[]{:S(2)}, u32[]{:S(2)}) async-start(bf16[16,1,24]{2,1,0:T(2,128)(2,1)} %convert_element_type.97), calls=%async_computation.4 | async-start | bytes 16384 | tf_op jit(solution)/shard_map/all_to_all | solution.py:86
  154.3 4.4 %fusion.4 = f32[384,2048]{1,0:T(8,128)S(1)} fusion(bf16[1,2,768,2048]{3,2,1,0:T(8,128)(2,1)} %all-gather.5.cloned.1.call-done, f32[384,768]{1,0:T(8,128)S(1)} %copy-done.8, f32[384,768]{1,0:T(8,128)S(1)} %copy-done.9, f32[384,768]{1,0:T(8,128)} %get-tuple-element.33, f32[384]{0:T(512)S(1)} %mul.166), kind=kOutput, calls=%fused_computation.15 | convolution fusion | flops 1211203584 | bytes 9831936 | tf_op jit(solution)/shard_map/dot_general | solution.py:75
  158.7 4.7 %add_convert_fusion = bf16[384,2048]{1,0:T(8,128)(2,1)} fusion(f32[384,2048]{1,0:T(8,128)S(1)} %fusion.4, bf16[1,2,768,2048]{3,2,1,0:T(8,128)(2,1)} %all-gather.5.cloned.1.call-done, f32[384,768]{1,0:T(8,128)S(1)} %copy-done.8, f32[384,768]{1,0:T(8,128)S(1)} %copy-done.10, f32[384]{0:T(512)S(1)} %mul.166), kind=kOutput, calls=%fused_computation.12 | convolution fusion | flops 1211596800 | bytes 10225152 | tf_op jit(solution)/shard_map/dot_general | solution.py:76
  163.4 6.0 %all-to-all-start.3 = ((bf16[16,24,2048]{2,1,0:T(8,128)(2,1)}), bf16[16,24,2048]{2,1,0:T(8,128)(2,1)S(1)}, u32[]{:S(2)}, u32[]{:S(2)}) async-start(bf16[16,24,2048]{2,1,0:T(8,128)(2,1)} %bitcast.12), calls=%async_computation.3 | async-start | bytes 3145728 | tf_op jit(solution)/shard_map/all_to_all | solution.py:79
  169.7 1.9 gather_fusion.4
  172.4 28.9 %all-to-all-done.3 = bf16[16,24,2048]{2,1,0:T(8,128)(2,1)S(1)} async-done(((bf16[16,24,2048]{2,1,0:T(8,128)(2,1)}), bf16[16,24,2048]{2,1,0:T(8,128)(2,1)S(1)}, u32[]{:S(2)}, u32[]{:S(2)}) %all-to-all-start.3) | async-done | bytes 1572896 | tf_op jit(solution)/shard_map/all_to_all | solution.py:79
  201.4 1.4 gather_fusion.3
  204.3 44.7 %all-reduce.2 = (f32[2048]{0:T(1024)}, f32[2048]{0:T(1024)}, f32[1]{0:T(128)}) all-reduce(f32[2048]{0:T(1024)S(1)} %get-tuple-element.25, f32[2048]{0:T(1024)S(1)} %convert_reduce_fusion, f32[1]{0:T(128)} %bitcast.19), channel_id=1, replica_groups=mesh['expert'=16,'dp'=2] {'expert','dp'}, use_global_device_ids=true, to_apply=%region_8.9 | all-reduce | flops 4097 | bytes 32776 | tf_op jit(solution)/shard_map/psum | solution.py:107
  (68 shorter events, 7.5 us)
Async XLA Ops:
  7.2 0.8 copy-start.6
  7.2 1.0 copy-start.4
  7.2 14.6 %copy-start = (bf16[1,32,2048]{2,1,0:T(8,128)(2,1)S(1)}, bf16[1,32,2048]{2,1,0:T(8,128)(2,1)}, u32[]{:S(2)}) copy-start(bf16[1,32,2048]{2,1,0:T(8,128)(2,1)} %param.9) | copy-start | bytes 393220
  7.2 14.6 %copy-start.3 = (f32[2048]{0:T(1024)S(1)}, f32[2048]{0:T(1024)}, u32[]{:S(2)}) copy-start(f32[2048]{0:T(1024)} %param.14) | copy-start | bytes 24580
  7.2 14.6 %copy-start.5 = (f32[2048]{0:T(1024)S(1)}, f32[2048]{0:T(1024)}, u32[]{:S(2)}) copy-start(f32[2048]{0:T(1024)} %param.15) | copy-start | bytes 24580
  7.2 85.5 %all-gather.5.cloned.1.call-start = ((), (), s32[]{:S(2)}) async-start(), calls=%async_computation.7 | async-start | bytes 9437184 | tf_op jit(solution)/shard_map/all_gather | solution.py:57
  13.8 13.7 %all-to-all-start = ((bf16[16,1,24]{2,1,0:T(2,128)(2,1)}), bf16[16,1,24]{2,1,0:T(2,128)(2,1)S(1)}, u32[]{:S(2)}, u32[]{:S(2)}) async-start(bf16[16,1,24]{2,1,0:T(2,128)(2,1)} %all_to_all.25), calls=%async_computation | async-start | bytes 16384 | tf_op jit(solution)/shard_map/all_to_all | solution.py:51
  27.5 35.6 %all-to-all-start.2 = ((bf16[16,24,2048]{2,1,0:T(8,128)(2,1)}), bf16[16,24,2048]{2,1,0:T(8,128)(2,1)S(1)}, u32[]{:S(2)}, u32[]{:S(2)}) async-start(bf16[16,24,2048]{2,1,0:T(8,128)(2,1)} %bitcast.8), calls=%async_computation.2 | async-start | bytes 3145728 | tf_op jit(solution)/shard_map/all_to_all | solution.py:49
  31.2 0.9 copy-start.1
  31.2 108.0 %all-gather.3.cloned.1.call-start = ((), (), s32[]{:S(2)}) async-start(), calls=%async_computation.6 | async-start | bytes 4718592 | tf_op jit(solution)/shard_map/all_gather | solution.py:58
  63.1 41.1 %all-to-all-start.1 = ((bf16[16,24,2048]{2,1,0:T(8,128)(2,1)}), bf16[16,24,2048]{2,1,0:T(8,128)(2,1)S(1)}, u32[]{:S(2)}, u32[]{:S(2)}) async-start(bf16[16,24,2048]{2,1,0:T(8,128)(2,1)} %bitcast.4), calls=%async_computation.1 | async-start | bytes 3145728 | tf_op jit(solution)/shard_map/all_to_all | solution.py:50
  72.2 177.6 %reduce-scatter.2.cloned.1.call-start = ((), (), s32[]{:S(2)}) async-start(), calls=%async_computation.8 | async-start | bytes 4718592 | tf_op jit(solution)/shard_map/reduce_scatter | solution.py:97
  92.7 4.6 %copy-start.7 = (bf16[1,2,768,2048]{3,2,1,0:T(8,128)(2,1)S(1)}, bf16[1,2,768,2048]{3,2,1,0:T(8,128)(2,1)}, u32[]{:S(2)}) copy-start(bf16[1,2,768,2048]{3,2,1,0:T(8,128)(2,1)} %all-gather.5.cloned.1.call-done) | copy-start | bytes 18874372
  147.9 6.4 %copy-start.8 = (f32[384,768]{1,0:T(8,128)S(1)}, f32[384,768]{1,0:T(8,128)}, u32[]{:S(2)}) copy-start(f32[384,768]{1,0:T(8,128)} %fusion.5) | copy-start | bytes 3538948
  147.9 6.4 %copy-start.9 = (f32[384,768]{1,0:T(8,128)S(1)}, f32[384,768]{1,0:T(8,128)}, u32[]{:S(2)}) copy-start(f32[384,768]{1,0:T(8,128)} %fusion.3) | copy-start | bytes 3538948
  148.6 14.8 %all-to-all-start.4 = ((bf16[16,1,24]{2,1,0:T(2,128)(2,1)}), bf16[16,1,24]{2,1,0:T(2,128)(2,1)S(1)}, u32[]{:S(2)}, u32[]{:S(2)}) async-start(bf16[16,1,24]{2,1,0:T(2,128)(2,1)} %convert_element_type.97), calls=%async_computation.4 | async-start | bytes 16384 | tf_op jit(solution)/shard_map/all_to_all | solution.py:86
  154.2 4.4 %copy-start.10 = (f32[384,768]{1,0:T(8,128)S(1)}, f32[384,768]{1,0:T(8,128)}, u32[]{:S(2)}) copy-start(f32[384,768]{1,0:T(8,128)} %get-tuple-element.33) | copy-start | bytes 3538948
  163.4 38.0 %all-to-all-start.3 = ((bf16[16,24,2048]{2,1,0:T(8,128)(2,1)}), bf16[16,24,2048]{2,1,0:T(8,128)(2,1)S(1)}, u32[]{:S(2)}, u32[]{:S(2)}) async-start(bf16[16,24,2048]{2,1,0:T(8,128)(2,1)} %bitcast.12), calls=%async_computation.3 | async-start | bytes 3145728 | tf_op jit(solution)/shard_map/all_to_all | solution.py:79
  202.7 46.3 %copy-start.2 = (bf16[1,32,2048]{2,1,0:T(8,128)(2,1)S(1)}, bf16[1,32,2048]{2,1,0:T(8,128)(2,1)}, u32[]{:S(2)}) copy-start(bf16[1,32,2048]{2,1,0:T(8,128)(2,1)} %param.10) | copy-start | bytes 393220
Sparse Core Ops, SparseCore 0:
  9.6 83.0 all-gather.4
  94.2 44.9 all-gather.2
  148.0 43.3 reduce-scatter.1
where the time goes:
time: 257 us; the launch traced here: 256 us
  waiting for transfers between devices  120 us (47%)
  blocking collectives  44.7 us (17%)
  starting transfers between devices  31.9 us (12%)
  matrix products  24.8 us (10%)
  local copies, waits for them, and re-layouts  17.1 us (7%)
  between operations  14.7 us (6%)
  other arithmetic  2.6 us (1%)
    psum x1, blocking collectives, shards(): lax.psum((gamma_part, beta_part, alpha_part), ('expert', 'dp'))  44.7 us
    all_gather x1, waiting for transfers between devices, shards(): lax.all_gather(w_down, 'dp', axis=1, tiled=True)  35 us
    all_to_all x1, waiting for transfers between devices, shards(): lax.all_to_all(d_rows.reshape(expert_count, capacity, width), 'expert', s...  28.9 us
    all_to_all x1, waiting for transfers between devices, shards(): lax.all_to_all(send_rows, 'expert', split_axis=0, concat_axis=0, tiled=True)  27.8 us
    all_gather x1, waiting for transfers between devices, shards(): lax.all_gather(w_in, 'dp', axis=2, tiled=True)  20.3 us
    dot_general x3, matrix products, contract_width(): lax.dot_general(left, right, (((1,), (1,)), ((), ())), preferred_element_...  12.1 us
    all_to_all x1, starting transfers between devices, shards(): lax.all_to_all(send_cot, 'expert', split_axis=0, concat_axis=0, tiled=True)  9.08 us
    all_to_all x1, starting transfers between devices, shards(): lax.all_to_all(send_prob, 'expert', split_axis=0, concat_axis=0, tiled=True)  7.39 us
  transfers between devices with their start and end apart: 8, of which 6 were waited for; matrix products, arithmetic and copies ran while one was open for 14% of the time, Pallas kernels for 0%

commit v1 on v0

--- a/solution.py
+++ b/solution.py
@@ -1,14 +1,294 @@
+import functools
 import jax
 import jax.numpy as jnp
 from jax import lax
+from jax.experimental import pallas as pl
+from jax.experimental.pallas import tpu as pltpu
 from jax.sharding import PartitionSpec as P
 
 residual_scale = 0.7071
+LANES = 128
+f32 = jnp.float32
+bf16 = jnp.bfloat16
 
 
 def contract_width(left, right):
     return lax.dot_general(
-        left, right, (((1,), (1,)), ((), ())), preferred_element_type=jnp.float32
+        left, right, (((1,), (1,)), ((), ())), preferred_element_type=f32
+    )
+
+
+def add16(left, right):
+    return (left.astype(f32) + right.astype(f32)).astype(bf16)
+
+
+def rows_kernel(segments, width, hidden, *refs):
+    count = len(segments)
+    blocks = refs[:count]
+    (w_in, w_down, gamma, beta, alpha, expert) = refs[count : count + 6]
+    (grads_out, act_out, scaled_out, tail_out) = refs[count + 6 : count + 10]
+    (normed, cot, weight) = refs[count + 10 :]
+    rows = normed.shape[0]
+    gain = alpha[0]
+    mine = expert[0]
+    gamma_row = gamma[...]
+    beta_row = beta[...]
+    for source, places in zip(blocks, segments):
+        size = source.shape[0] // len(places)
+        for part, to in enumerate(places):
+            here, there = slice(part * size, (part + 1) * size), slice(to, to + size)
+            squashed = jnp.tanh(gain * source[here, 0:width].astype(f32))
+            normed[there, :] = (gamma_row * squashed + beta_row).astype(bf16)
+            rows_cot = source[here, width : 2 * width]
+            cot[there, :] = rows_cot
+            gates = source[here, 2 * width :].astype(f32)
+            lane = lax.broadcasted_iota(jnp.int32, gates.shape, 1)
+            own = jnp.sum(jnp.where(lane == mine, gates, 0.0), axis=1, keepdims=True)
+            own = residual_scale * own
+            weight[there, :] = jnp.broadcast_to(own, (size, LANES))
+            scaled_out[there, :] = (own * rows_cot.astype(f32)).astype(bf16)
+    pre = contract_width(normed[...], w_in[...])
+    back = contract_width(cot[...], w_down[...])
+    gate_pre = pre[:, :hidden]
+    up_value = pre[:, hidden:]
+    sigma = jax.nn.sigmoid(gate_pre)
+    silu = gate_pre * sigma
+    activation = (silu * up_value).astype(bf16)
+    act_out[...] = activation
+    row_grad = residual_scale * jnp.sum(activation.astype(f32) * back, axis=1, keepdims=True)
+    d_act = weight[:, 0:1] * back
+    d_gate = d_act * up_value * sigma * (1.0 + gate_pre * (1.0 - sigma))
+    grads_out[:, :hidden] = d_gate.astype(bf16)
+    grads_out[:, hidden:] = (d_act * gate_pre * sigma).astype(bf16)
+    lane = lax.broadcasted_iota(jnp.int32, (rows, LANES), 1)
+    tail_out[...] = jnp.where(lane == mine, row_grad, 0.0).astype(bf16)
+
+
+def grad_kernel(segments, half, *refs):
+    count = len(segments)
+    blocks = refs[:count]
+    (near, far, w_near, w_far, tail, alpha, side) = refs[count : count + 7]
+    (d_own, d_other, sums) = refs[count + 7 : count + 10]
+    (squash, slope) = refs[count + 10 :]
+    rows = near.shape[0]
+    block = rows // 8
+    gain = alpha[0]
+    start = pl.multiple_of(side[0] * half, half)
+    for source, places in zip(blocks, segments):
+        size = source.shape[0] // len(places)
+        for part, to in enumerate(places):
+            inputs = source[part * size : (part + 1) * size, pl.ds(start, half)].astype(f32)
+            squashed = jnp.tanh(gain * inputs)
+            squash[to : to + size, :] = squashed
+            slope[to : to + size, :] = (1.0 - squashed * squashed) * inputs
+    mirrored = jnp.concatenate([far[rows // 2 :, :], far[: rows // 2, :]], axis=0)
+
+    def place(cols, value):
+        for x in range(2):
+            for y in range(2):
+                row = (x * 4 + y) * block
+                d_own[x, y, :, cols] = value[row : row + block]
+                row = (x * 4 + 2 + y) * block
+                d_other[x, y, :, cols] = value[row : row + block]
+
+    place(slice(half, half + LANES), tail[...])
+    step = 512
+    for at in range(0, half, step):
+        cols = slice(at, at + step)
+        part = jnp.dot(near[...], w_near[:, cols], preferred_element_type=f32)
+        part = part + jnp.dot(mirrored, w_far[:, cols], preferred_element_type=f32)
+        short = part.astype(bf16)
+        place(cols, short)
+        part = short.astype(f32)
+        sums[0:1, cols] = jnp.sum(part, axis=0, keepdims=True)
+        sums[1:2, cols] = jnp.sum(part * squash[:, cols], axis=0, keepdims=True)
+        sums[2:3, cols] = jnp.sum(part * slope[:, cols], axis=0, keepdims=True)
+        sums[3:8, cols] = jnp.zeros((5, step), f32)
+
+
+def down_kernel(count, *refs):
+    acts = refs[:count]
+    scaled = refs[count : 2 * count]
+    out = refs[2 * count]
+    left, right = refs[2 * count + 1 :]
+    half = acts[0].shape[0] // 2
+    total = None
+    for batch in range(2):
+        for k in range(count):
+            left[k * half : (k + 1) * half, :] = acts[k][batch * half : (batch + 1) * half, :]
+            right[k * half : (k + 1) * half, :] = scaled[k][batch * half : (batch + 1) * half, :]
+        term = lax.dot_general(
+            left[...], right[...], (((0,), (0,)), ((), ())), preferred_element_type=f32
+        )
+        term = term.astype(bf16).astype(f32)
+        total = term if total is None else total + term
+    out[...] = total.astype(bf16)
+
+
+def whole():
+    return pl.BlockSpec(memory_space=pltpu.VMEM)
+
+
+def scalar():
+    return pl.BlockSpec(memory_space=pltpu.SMEM)
+
+
+def dense_shards(tokens, cotangent, expert_ids, gate_probs, alpha, gamma, beta, w_in, w_down):
+    experts = lax.axis_size("expert")
+    planes = experts // 4
+    block = tokens.shape[1]
+    width = tokens.shape[2]
+    hidden = w_down.shape[1]
+    rows = 8 * block
+    me = lax.axis_index("expert")
+
+    def go_x(v):
+        return lax.ppermute(v, "dp", [(0, 1), (1, 0)])
+
+    def go_y(v):
+        return lax.ppermute(v, "expert", [(e, e ^ 2) for e in range(experts)])
+
+    def go_core(v):
+        return lax.ppermute(v, "expert", [(e, e ^ 1) for e in range(experts)])
+
+    def go_z(v):
+        return lax.ppermute(v, "expert", [(e, (e + 4) % experts) for e in range(experts)])
+
+    lanes = jnp.arange(LANES, dtype=jnp.int32)
+    picks = expert_ids[0][:, :, None] == lanes[None, None, :]
+    gates = jnp.sum(jnp.where(picks, gate_probs[0].astype(f32)[:, :, None], 0.0), axis=1)
+    own = jnp.concatenate([tokens[0], cotangent[0], gates.astype(bf16)], axis=1)
+
+    flat_in = w_in[0].reshape(2 * hidden, width)
+    flat_down = w_down[0]
+    gamma_row = gamma.reshape(1, width)
+    beta_row = beta.reshape(1, width)
+    mine = me.reshape(1).astype(jnp.int32)
+    half = width // 2
+    side = lax.axis_index("dp").astype(jnp.int32)
+    w_near = lax.dynamic_slice_in_dim(flat_in, side * half, half, axis=1)
+    w_send = lax.dynamic_slice_in_dim(flat_in, (1 - side) * half, half, axis=1)
+
+    segments = tuple(
+        tuple((x * 4 + core * 2 + y) * block for x in range(2))
+        for core in range(2)
+        for y in range(2)
+    )
+    params = pltpu.CompilerParams(vmem_limit_bytes=40 << 20)
+
+    def first_half(arrays):
+        return pl.pallas_call(
+            functools.partial(rows_kernel, segments, width, hidden),
+            out_shape=(
+                jax.ShapeDtypeStruct((rows, 2 * hidden), bf16),
+                jax.ShapeDtypeStruct((rows, hidden), bf16),
+                jax.ShapeDtypeStruct((rows, width), bf16),
+                jax.ShapeDtypeStruct((rows, LANES), bf16),
+            ),
+            in_specs=[whole()] * 8 + [scalar(), scalar()],
+            out_specs=(whole(),) * 4,
+            scratch_shapes=[
+                pltpu.VMEM((rows, width), bf16),
+                pltpu.VMEM((rows, width), bf16),
+                pltpu.VMEM((rows, LANES), f32),
+            ],
+            compiler_params=params,
+            name="rows",
+        )(*arrays, flat_in, flat_down, gamma_row, beta_row, alpha, mine)
+
+    def second_half(arrays, near, far, w_far, tail):
+        return pl.pallas_call(
+            functools.partial(grad_kernel, segments, half),
+            out_shape=(
+                jax.ShapeDtypeStruct((2, 2, block, half + LANES), bf16),
+                jax.ShapeDtypeStruct((2, 2, block, half + LANES), bf16),
+                jax.ShapeDtypeStruct((8, half), f32),
+            ),
+            in_specs=[whole()] * 9 + [scalar(), scalar()],
+            out_specs=(whole(),) * 3,
+            scratch_shapes=[
+                pltpu.VMEM((rows, half), f32),
+                pltpu.VMEM((rows, half), f32),
+            ],
+            compiler_params=params,
+            name="grads",
+        )(*arrays, near, far, w_near, w_far, tail, alpha, side.reshape(1))
+
+    def settle(d_own, d_other):
+        got = go_core(d_other)
+        send = add16(d_own[:, 1], got[:, 1])
+        keep = d_own[:, 0].astype(f32) + got[:, 0].astype(f32)
+        return keep + go_y(send).astype(f32)
+
+    own = jnp.concatenate([own, go_x(own)], axis=0)
+    own, w_send = lax.optimization_barrier((own, w_send))
+    w_far = go_x(w_send)
+    planed = [own]
+    for _ in range(planes - 1):
+        planed.append(go_z(planed[-1]))
+    order = list(range(planes))
+    arrays, acts, scaled, totals, ready = {}, {}, {}, [], {}
+    for k in order:
+        far = go_y(planed[k])
+        arrays[k] = (planed[k], far, go_core(planed[k]), go_core(far))
+        grads, acts[k], scaled[k], tail = first_half(arrays[k])
+        ready[k] = (grads, go_x(grads), w_far, tail)
+    carry = None
+    for k in order[1:] + order[:1]:
+        d_own, d_other, sums = second_half(arrays[k], *ready[k])
+        totals.append(sums)
+        value = settle(d_own, d_other)
+        if carry is not None:
+            value = value + go_z(carry).astype(f32)
+        carry = value.astype(bf16)
+    acts = [acts[k] for k in order]
+    scaled = [scaled[k] for k in order]
+    other = go_x(carry[1]).astype(f32)
+    first = jnp.where(side == 0, value[0, :, :half], other[:, :half])
+    last = jnp.where(side == 0, other[:, :half], value[0, :, :half])
+    grad_normed = jnp.concatenate([first, last], axis=1)
+    row_grads = value[0, :, half:] + other[:, half:]
+
+    sums = sum(totals[1:], totals[0])
+    for go in (go_core, go_y):
+        sums = sums + go(sums)
+    hop = 4
+    while hop < experts:
+        sums = sums + lax.ppermute(sums, "expert", [(e, e ^ hop) for e in range(experts)])
+        hop *= 2
+    crossed = go_x(sums)
+    sums = jnp.concatenate(
+        [jnp.where(side == 0, sums, crossed), jnp.where(side == 0, crossed, sums)], axis=1
+    )
+
+    grad_down = pl.pallas_call(
+        functools.partial(down_kernel, planes),
+        out_shape=jax.ShapeDtypeStruct((hidden, width), bf16),
+        in_specs=[whole()] * (2 * planes),
+        out_specs=whole(),
+        scratch_shapes=[
+            pltpu.VMEM((planes * rows // 2, hidden), bf16),
+            pltpu.VMEM((planes * rows // 2, width), bf16),
+        ],
+        compiler_params=pltpu.CompilerParams(vmem_limit_bytes=40 << 20),
+        name="down",
+    )(*acts, *scaled)
+
+    inputs = tokens[0].astype(f32)
+    squashed = jnp.tanh(alpha[0] * inputs)
+    pre_grad = grad_normed * gamma * (1.0 - squashed * squashed)
+    grad_tokens = (cotangent[0].astype(f32) + alpha[0] * pre_grad).astype(bf16)
+    grad_probs = jnp.sum(jnp.where(picks, row_grads[:, None, :], 0.0), axis=2).astype(bf16)
+    grad_beta = sums[0]
+    grad_gamma = sums[1]
+    grad_alpha = jnp.sum(sums[2] * gamma).reshape(1)
+    return (
+        grad_tokens[None],
+        grad_probs[None],
+        grad_down[None],
+        grad_gamma,
+        grad_beta,
+        grad_alpha,
     )
 
 
@@ -17,8 +297,10 @@
     labels = jnp.arange(expert_count, dtype=jnp.int32)
     onehot = (ids_local[:, :, None] == labels[None, None, :]).astype(jnp.int32)
     picks = jnp.sum(onehot, axis=1)
-    before = jnp.cumsum(picks, axis=0) - picks
-    slots = jnp.sum(onehot * before[:, None, :], axis=2)
+    order = jnp.arange(token_count, dtype=jnp.int32)
+    earlier = (order[None, :] < order[:, None]).astype(f32)
+    before = jnp.dot(earlier, picks.astype(f32), precision=lax.Precision.HIGHEST)
+    slots = jnp.sum(onehot * before.astype(jnp.int32)[:, None, :], axis=2)
     position = ids_local * capacity + slots
     pairs = jnp.arange(token_count * top_count, dtype=jnp.int32)
     table = jnp.full((expert_count * capacity,), token_count * top_count, jnp.int32)
@@ -26,7 +308,7 @@
     return (position, table)
 
 
-def shards(tokens, cotangent, expert_ids, gate_probs, alpha, gamma, beta, w_in, w_down):
+def routed_shards(tokens, cotangent, expert_ids, gate_probs, alpha, gamma, beta, w_in, w_down):
     expert_count = lax.axis_size("expert")
     token_count = tokens.shape[1]
     top_count = expert_ids.shape[2]
@@ -45,23 +327,19 @@
     send_rows = normed_pad[source_token].reshape(expert_count, capacity, width)
     send_cot = cot_pad[source_token].reshape(expert_count, capacity, width)
     send_prob = prob_pad[table].reshape(expert_count, capacity)
-    recv_rows, recv_cot, recv_prob = (
-        lax.all_to_all(send_rows, "expert", split_axis=0, concat_axis=0, tiled=True),
-        lax.all_to_all(send_cot, "expert", split_axis=0, concat_axis=0, tiled=True),
-        lax.all_to_all(send_prob, "expert", split_axis=0, concat_axis=0, tiled=True),
-    )
-    in_rows = recv_rows.reshape(rows_total, width)
-    cot_rows = recv_cot.reshape(rows_total, width)
-    prob_rows = recv_prob.reshape(rows_total).astype(jnp.float32)
-    gate_up, lower_full = (
-        lax.all_gather(w_in, "dp", axis=2, tiled=True),
-        lax.all_gather(w_down, "dp", axis=1, tiled=True),
-    )
-    gate_pre = contract_width(in_rows, gate_up[0, 0])
-    up_value = contract_width(in_rows, gate_up[0, 1])
+
+    def swap(value):
+        return lax.all_to_all(value, "expert", split_axis=0, concat_axis=0, tiled=True)
+
+    in_rows = swap(send_rows).reshape(rows_total, width)
+    cot_rows = swap(send_cot).reshape(rows_total, width)
+    prob_rows = swap(send_prob).reshape(rows_total).astype(jnp.float32)
+    gate_up = lax.all_gather(w_in, "dp", axis=2, tiled=True)
+    w_lower = lax.all_gather(w_down, "dp", axis=1, tiled=True)[0]
     w_gate = gate_up[0, 0]
     w_upper = gate_up[0, 1]
-    w_lower = lower_full[0]
+    gate_pre = contract_width(in_rows, w_gate)
+    up_value = contract_width(in_rows, w_upper)
     sigma = jax.nn.sigmoid(gate_pre)
     activation = (gate_pre * sigma * up_value).astype(jnp.bfloat16)
     back = contract_width(cot_rows, w_lower)
@@ -75,22 +353,8 @@
         jnp.dot(d_gate, w_gate, preferred_element_type=jnp.float32)
         + jnp.dot(d_up, w_upper, preferred_element_type=jnp.float32)
     ).astype(jnp.bfloat16)
-    back_rows, back_probs = (
-        lax.all_to_all(
-            d_rows.reshape(expert_count, capacity, width),
-            "expert",
-            split_axis=0,
-            concat_axis=0,
-            tiled=True,
-        ),
-        lax.all_to_all(
-            row_grad.astype(jnp.bfloat16).reshape(expert_count, capacity),
-            "expert",
-            split_axis=0,
-            concat_axis=0,
-            tiled=True,
-        ),
-    )
+    back_rows = swap(d_rows.reshape(expert_count, capacity, width))
+    back_probs = swap(row_grad.astype(jnp.bfloat16).reshape(expert_count, capacity))
     partial_grad = lax.dot_general(
         activation, scaled_cot, (((0,), (0,)), ((), ())), preferred_element_type=jnp.float32
     )
@@ -109,6 +373,19 @@
     )
     grad_tokens = (cotangent[0].astype(jnp.float32) + alpha[0] * pre_grad).astype(jnp.bfloat16)
     return (grad_tokens[None], grad_probs[None], grad_down, grad_gamma, grad_beta, grad_alpha)
+
+
+def shards(*arrays):
+    experts = lax.axis_size("expert")
+    top_count = arrays[2].shape[2]
+    dense = (
+        lax.axis_size("dp") == 2
+        and experts % 4 == 0
+        and (experts & (experts - 1)) == 0
+        and experts <= LANES
+        and 2 * top_count >= experts
+    )
+    return (dense_shards if dense else routed_shards)(*arrays)
 
 
 def solution(mesh):

time: 257 us -> 166 us (0.65)
  waiting for transfers between devices: 120 us -> 75.2 us
  blocking collectives: 44.7 us -> 0 us
  Pallas kernels: 0 us -> 29 us
  matrix products: 24.8 us -> 0 us
  between operations: 14.7 us -> 1.71 us
  other arithmetic: 2.6 us -> 8.9 us
  local copies, waits for them, and re-layouts: 17.1 us -> 21.6 us
  starting transfers between devices: 31.9 us -> 28.8 us
    ppermute x0 -> x38, waiting for transfers between devices: none -> 75.2 us  [the longest x6 26.6 us: go_z(): lax.ppermute(v, 'expert', [(e, (e + 4) % experts) for e in range(experts)])]
    all_to_all x5 -> x0, waiting for transfers between devices: 63.6 us -> none  [the longest x1 28.9 us: shards(): lax.all_to_all(d_rows.reshape(expert_count, capacity, width), 'expert', s...]
    all_gather x2 -> x0, waiting for transfers between devices: 55.4 us -> none  [the longest x1 35 us: shards(): lax.all_gather(w_down, 'dp', axis=1, tiled=True)]
    psum x1 -> x0, blocking collectives: 44.7 us -> none  [shards(): lax.psum((gamma_part, beta_part, alpha_part), ('expert', 'dp'))]
    all_to_all x5 -> x0, starting transfers between devices: 31.8 us -> none  [the longest x1 9.08 us: shards(): lax.all_to_all(send_cot, 'expert', split_axis=0, concat_axis=0, tiled=True)]
    pallas_call x0 -> x9, Pallas kernels: none -> 29 us  [the longest x4 13.6 us: second_half(): pl.pallas_call(functools.partial(grad_kernel, segments, half), out_shape=...]
    ppermute x0 -> x38, starting transfers between devices: none -> 28.8 us  [the longest x8 10.8 us: go_x(): return lax.ppermute(v, 'dp', [(0, 1), (1, 0)])]
    dot_general x6 -> x0, matrix products: 24.8 us -> none  [the longest x3 12.1 us: contract_width(): lax.dot_general(left, right, (((1,), (1,)), ((), ())), preferred_element_...]
  transfers between devices with their start and end apart: 8 -> 38, of which waited for: 6 -> 18; matrix products, arithmetic and copies ran while one was open for 14% -> 5% of each run, Pallas kernels for 0% -> 18%
where the time goes in v1:
time: 166 us; the launch traced here: 165 us
  waiting for transfers between devices  75.2 us (45%)
  Pallas kernels  29 us (17%)
  starting transfers between devices  28.8 us (17%)
  local copies, waits for them, and re-layouts  21.6 us (13%)
  other arithmetic  8.9 us (5%)
  between operations  1.71 us (1%)
    ppermute x6, waiting for transfers between devices, go_z(): lax.ppermute(v, 'expert', [(e, (e + 4) % experts) for e in range(experts)])  26.6 us
    ppermute x9, waiting for transfers between devices, go_y(): return lax.ppermute(v, 'expert', [(e, e ^ 2) for e in range(experts)])  22.9 us
    ppermute x8, waiting for transfers between devices, go_x(): return lax.ppermute(v, 'dp', [(0, 1), (1, 0)])  22.7 us
    unnamed x75, local copies, waits for them, and re-layouts  16.5 us
    pallas_call x4, Pallas kernels, second_half(): pl.pallas_call(functools.partial(grad_kernel, segments, half), out_shape=...  13.6 us
    pallas_call x4, Pallas kernels, first_half(): pl.pallas_call(functools.partial(rows_kernel, segments, width, hidden), o...  12.4 us
    ppermute x8, starting transfers between devices, go_x(): return lax.ppermute(v, 'dp', [(0, 1), (1, 0)])  10.8 us
    ppermute x9, starting transfers between devices, go_y(): return lax.ppermute(v, 'expert', [(e, e ^ 2) for e in range(experts)])  9.73 us
  transfers between devices with their start and end apart: 38, of which 18 were waited for; matrix products, arithmetic and copies ran while one was open for 5% of the time, Pallas kernels for 18%

profile of v1, /device:TPU:0, one launch (start us, length us, event | category | flops | bytes accessed | tf_op | source)
XLA Modules:
  0.0 165.2 jit_solution(13807173587664586898)
XLA Ops:
  4.0 2.9 %collective-permute-start = (bf16[32,4224]{1,0:T(8,128)(2,1)}, bf16[32,4224]{1,0:T(8,128)(2,1)}, u32[]{:S(2)}, u32[]{:S(2)}) collective-permute-start(bf16[32,4224]{1,0:T(8,128)(2,1)} %pad_maximum_fusion.1), channel_id=1, source_target_pairs={{0,1},{1,0},{2,3},{3,2},{4,5},{5,4},{6,7},{7,6},{8,9},{9,8},{10,11... | collective-permute-start | bytes 811016 | tf_op jit(solution)/shard_map/ppermute | solution.py:146
  7.0 4.0 %constant_dynamic-slice_fusion = (bf16[768,1024]{1,0:T(8,128)(2,1)}, bf16[768,1024]{1,0:T(8,128)(2,1)}) fusion(bf16[768,2048]{1,0:T(8,128)(2,1)} %bitcast.70, s32[]{:T(128)S(6)} %select_n.41, s32[]{:T(128)S(6)} %select_n.40), kind=kLoop, calls=%fused_computation.45 | loop fusion | bytes 6291464 | tf_op jit(solution)/shard_map/dynamic_slice | solution.py:169
  11.0 2.7 %collective-permute-done = bf16[32,4224]{1,0:T(8,128)(2,1)} collective-permute-done((bf16[32,4224]{1,0:T(8,128)(2,1)}, bf16[32,4224]{1,0:T(8,128)(2,1)}, u32[]{:S(2)}, u32[]{:S(2)}) %collective-permute-start) | collective-permute-done | bytes 270368 | tf_op jit(solution)/shard_map/ppermute | solution.py:146
  17.4 13.6 %collective-permute-done.8.refs_0_ = bf16[64,4224]{1,0:T(8,128)(2,1)S(1)} collective-permute-done((bf16[64,4224]{1,0:T(8,128)(2,1)}, bf16[64,4224]{1,0:T(8,128)(2,1)S(1)}, u32[]{:S(2)}, u32[]{:S(2)}) %collective-permute-start.8) | collective-permute-done | bytes 540704 | tf_op jit(solution)/shard_map/ppermute | solution.py:155
  35.3 10.9 %collective-permute-done.23.refs_1_ = bf16[64,4224]{1,0:T(8,128)(2,1)S(1)} collective-permute-done((bf16[64,4224]{1,0:T(8,128)(2,1)S(1)}, bf16[64,4224]{1,0:T(8,128)(2,1)S(1)}, u32[]{:S(2)}, u32[]{:S(2)}) %collective-permute-start.23) | collective-permute-done | bytes 540704 | tf_op jit(solution)/shard_map/ppermute | solution.py:149
  47.0 8.2 %collective-permute-done.1.refs_1_ = bf16[64,4224]{1,0:T(8,128)(2,1)} collective-permute-done((bf16[64,4224]{1,0:T(8,128)(2,1)}, bf16[64,4224]{1,0:T(8,128)(2,1)}, u32[]{:S(2)}, u32[]{:S(2)}) %collective-permute-start.1) | collective-permute-done | bytes 540704 | tf_op jit(solution)/shard_map/ppermute | solution.py:149
  58.6 5.2 %collective-permute-done.10.refs_0_ = bf16[64,4224]{1,0:T(8,128)(2,1)} collective-permute-done((bf16[64,4224]{1,0:T(8,128)(2,1)}, bf16[64,4224]{1,0:T(8,128)(2,1)}, u32[]{:S(2)}, u32[]{:S(2)}) %collective-permute-start.10) | collective-permute-done | bytes 540704 | tf_op jit(solution)/shard_map/ppermute | solution.py:155
  71.6 1.9 %rows.7 = (bf16[256,768]{1,0:T(8,128)(2,1)S(1)}, bf16[256,384]{1,0:T(8,128)(2,1)S(1)}, bf16[256,2048]{1,0:T(8,128)(2,1)S(1)}, bf16[256,128]{1,0:T(8,128)(2,1)S(1)}) custom-call(bf16[64,4224]{1,0:T(8,128)(2,1)S(1)} %copy-done.6, bf16[64,4224]{1,0:T(8,128)(2,1)S(1)} %copy-done.8, bf16[64,4224]{1,0:T(8,128)(2,1)S(1)} %copy-done.10, ...), custom_call_target="tpu_custom_call" | custom-call | tf_op jit(solution)/shard_map/rows/pallas_call | solution.py:180
  76.7 3.5 %rows.4 = (bf16[256,768]{1,0:T(8,128)(2,1)S(1)}, bf16[256,384]{1,0:T(8,128)(2,1)S(1)}, bf16[256,2048]{1,0:T(8,128)(2,1)S(1)}, bf16[256,128]{1,0:T(8,128)(2,1)S(1)}) custom-call(bf16[64,4224]{1,0:T(8,128)(2,1)} %pad_maximum_fusion.refs_0_, bf16[64,4224]{1,0:T(8,128)(2,1)} %collective-permute-done.1.refs_1_, bf16[64,4224]{1,0:T(8,128)(2,1)} %collective-permute-done.2.refs_2_, ...), custom_call_target="tpu_custom_call" | custom-call | tf_op jit(solution)/shard_map/rows/pallas_call | solution.py:180
  81.4 5.9 %collective-permute-done.26.refs_5_ = bf16[256,768]{1,0:T(8,128)(2,1)S(1)} collective-permute-done((bf16[256,768]{1,0:T(8,128)(2,1)S(1)}, bf16[256,768]{1,0:T(8,128)(2,1)S(1)}, u32[]{:S(2)}, u32[]{:S(2)}) %collective-permute-start.26) | collective-permute-done | bytes 393248 | tf_op jit(solution)/shard_map/ppermute | solution.py:146
  87.8 3.4 %grads.7 = (bf16[2,2,32,1152]{3,2,1,0:T(8,128)(2,1)S(1)}, bf16[2,2,32,1152]{3,2,1,0:T(8,128)(2,1)}, f32[8,1024]{1,0:T(8,128)S(1)}) custom-call(bf16[64,4224]{1,0:T(8,128)(2,1)S(1)} %copy-done.6, bf16[64,4224]{1,0:T(8,128)(2,1)S(1)} %copy-done.8, bf16[64,4224]{1,0:T(8,128)(2,1)S(1)} %copy-done.10, bf16[64,4224]{1,0:T(8,128)(2,1)S(1)} %copy-done.12, ...), custom_call_target="tpu_custom_call" | custom-call | tf_op jit(solution)/shard_map/grads/pallas_call | solution.py:200
  98.1 3.4 %grads.4 = (bf16[2,2,32,1152]{3,2,1,0:T(8,128)(2,1)S(1)}, bf16[2,2,32,1152]{3,2,1,0:T(8,128)(2,1)S(1)}, f32[8,1024]{1,0:T(8,128)S(1)}) custom-call(bf16[64,4224]{1,0:T(8,128)(2,1)} %pad_maximum_fusion.refs_0_, bf16[64,4224]{1,0:T(8,128)(2,1)} %collective-permute-done.1.refs_1_, bf16[64,4224]{1,0:T(8,128)(2,1)} %collective-permute-done.2.refs_2_, ...), custom_call_target="tpu_custom_call" | custom-call | tf_op jit(solution)/shard_map/grads/pallas_call | solution.py:200
  102.2 3.5 %rows.6 = (bf16[256,768]{1,0:T(8,128)(2,1)S(1)}, bf16[256,384]{1,0:T(8,128)(2,1)S(1)}, bf16[256,2048]{1,0:T(8,128)(2,1)S(1)}, bf16[256,128]{1,0:T(8,128)(2,1)S(1)}) custom-call(bf16[64,4224]{1,0:T(8,128)(2,1)} %collective-permute-done.9.refs_0_, bf16[64,4224]{1,0:T(8,128)(2,1)} %collective-permute-done.17.refs_1_, ...), custom_call_target="tpu_custom_call" | custom-call | tf_op jit(solution)/shard_map/rows/pallas_call | solution.py:180
  107.3 3.5 %rows.5 = (bf16[256,768]{1,0:T(8,128)(2,1)S(1)}, bf16[256,384]{1,0:T(8,128)(2,1)S(1)}, bf16[256,2048]{1,0:T(8,128)(2,1)S(1)}, bf16[256,128]{1,0:T(8,128)(2,1)S(1)}) custom-call(bf16[64,4224]{1,0:T(8,128)(2,1)} %collective-permute-done.10.refs_0_, bf16[64,4224]{1,0:T(8,128)(2,1)} %collective-permute-done.11.refs_1_, ...), custom_call_target="tpu_custom_call" | custom-call | tf_op jit(solution)/shard_map/rows/pallas_call | solution.py:180
  112.9 4.8 %collective-permute-done.20.refs_5_ = bf16[256,768]{1,0:T(8,128)(2,1)S(1)} collective-permute-done((bf16[256,768]{1,0:T(8,128)(2,1)S(1)}, bf16[256,768]{1,0:T(8,128)(2,1)S(1)}, u32[]{:S(2)}, u32[]{:S(2)}) %collective-permute-start.20) | collective-permute-done | bytes 393248 | tf_op jit(solution)/shard_map/ppermute | solution.py:146
  117.8 3.4 %grads.6 = (bf16[2,2,32,1152]{3,2,1,0:T(8,128)(2,1)S(1)}, bf16[2,2,32,1152]{3,2,1,0:T(8,128)(2,1)S(1)}, f32[8,1024]{1,0:T(8,128)S(1)}) custom-call(bf16[64,4224]{1,0:T(8,128)(2,1)} %collective-permute-done.9.refs_0_, bf16[64,4224]{1,0:T(8,128)(2,1)} %collective-permute-done.17.refs_1_, bf16[64,4224]{1,0:T(8,128)(2,1)} %collective-permute-done.18.refs_2_, ...), custom_call_target="tpu_custom_call" | custom-call | tf_op jit(solution)/shard_map/grads/pallas_call | solution.py:200
  121.4 3.9 %collective-permute-done.14.refs_5_ = bf16[256,768]{1,0:T(8,128)(2,1)S(1)} collective-permute-done((bf16[256,768]{1,0:T(8,128)(2,1)S(1)}, bf16[256,768]{1,0:T(8,128)(2,1)S(1)}, u32[]{:S(2)}, u32[]{:S(2)}) %collective-permute-start.14) | collective-permute-done | bytes 393248 | tf_op jit(solution)/shard_map/ppermute | solution.py:146
  125.3 3.4 %grads.5 = (bf16[2,2,32,1152]{3,2,1,0:T(8,128)(2,1)S(1)}, bf16[2,2,32,1152]{3,2,1,0:T(8,128)(2,1)S(1)}, f32[8,1024]{1,0:T(8,128)S(1)}) custom-call(bf16[64,4224]{1,0:T(8,128)(2,1)} %collective-permute-done.10.refs_0_, bf16[64,4224]{1,0:T(8,128)(2,1)} %collective-permute-done.11.refs_1_, bf16[64,4224]{1,0:T(8,128)(2,1)} %collective-permute-done.12.refs_2_, ...), custom_call_target="tpu_custom_call" | custom-call | tf_op jit(solution)/shard_map/grads/pallas_call | solution.py:200
  132.2 2.1 %collective-permute-done.34 = f32[8,1024]{1,0:T(8,128)S(1)} collective-permute-done((f32[8,1024]{1,0:T(8,128)S(1)}, f32[8,1024]{1,0:T(8,128)S(1)}, u32[]{:S(2)}, u32[]{:S(2)}) %collective-permute-start.34) | collective-permute-done | bytes 32800 | tf_op jit(solution)/shard_map/ppermute | solution.py:149
  134.7 3.0 %down.1 = bf16[384,2048]{1,0:T(8,128)(2,1)} custom-call(bf16[256,384]{1,0:T(8,128)(2,1)S(1)} %copy-done.25, bf16[256,384]{1,0:T(8,128)(2,1)S(1)} %copy-done.23, bf16[256,384]{1,0:T(8,128)(2,1)S(1)} %get-tuple-element.56.refs_2_, bf16[256,384]{1,0:T(8,128)(2,1)S(1)} %get-tuple-element.57.refs_3_, bf16[256,2048]{1,0:T(8,128)(2,1)S(1)} %copy-done.16, ...), custom_call_target="tpu_custom_call" | custom-call | tf_op jit(solution)/shard_map/down/pallas_call | solution.py:264
  138.7 3.6 %collective-permute-start.36 = (f32[8,1024]{1,0:T(8,128)S(1)}, f32[8,1024]{1,0:T(8,128)S(1)}, u32[]{:S(2)}, u32[]{:S(2)}) collective-permute-start(f32[8,1024]{1,0:T(8,128)S(1)} %add.123), channel_id=1, source_target_pairs={{0,16},{2,18},{4,20},{6,22},{8,24},{10,26},{12,28},{14,30},{16,0},... | collective-permute-start | bytes 98312 | tf_op jit(solution)/shard_map/ppermute | solution.py:257
  142.7 2.0 %collective-permute-done.36 = f32[8,1024]{1,0:T(8,128)S(1)} collective-permute-done((f32[8,1024]{1,0:T(8,128)S(1)}, f32[8,1024]{1,0:T(8,128)S(1)}, u32[]{:S(2)}, u32[]{:S(2)}) %collective-permute-start.36) | collective-permute-done | bytes 32800 | tf_op jit(solution)/shard_map/ppermute | solution.py:257
  152.7 6.3 %collective-permute-done.31 = bf16[2,32,1152]{2,1,0:T(8,128)(2,1)S(1)} collective-permute-done((bf16[2,32,1152]{2,1,0:T(8,128)(2,1)S(1)}, bf16[2,32,1152]{2,1,0:T(8,128)(2,1)S(1)}, u32[]{:S(2)}, u32[]{:S(2)}) %collective-permute-start.31) | collective-permute-done | bytes 147488 | tf_op jit(solution)/shard_map/ppermute | solution.py:155
  160.3 3.2 %collective-permute-done.32 = bf16[32,1152]{1,0:T(8,128)(2,1)S(1)} collective-permute-done((bf16[32,1152]{1,0:T(8,128)(2,1)S(1)}, bf16[32,1152]{1,0:T(8,128)(2,1)S(1)}, u32[]{:S(2)}, u32[]{:S(2)}) %collective-permute-start.32) | collective-permute-done | bytes 73760 | tf_op jit(solution)/shard_map/ppermute | solution.py:146
  (168 shorter events, 55.0 us)
Async XLA Ops:
  15.5 15.5 %collective-permute-start.8 = (bf16[64,4224]{1,0:T(8,128)(2,1)}, bf16[64,4224]{1,0:T(8,128)(2,1)S(1)}, u32[]{:S(2)}, u32[]{:S(2)}) collective-permute-start(bf16[64,4224]{1,0:T(8,128)(2,1)} %pad_maximum_fusion.refs_0_), channel_id=1, source_target_pairs={{0,8},{2,10},{4,12},{6,14},{8,16},{10,18},{12,20},{14,22},{16,24},... | collective-permute-start | bytes 1622024 | tf_op jit(solution)/shard_map/ppermute | solution.py:155
  31.0 15.2 %collective-permute-start.23 = (bf16[64,4224]{1,0:T(8,128)(2,1)S(1)}, bf16[64,4224]{1,0:T(8,128)(2,1)S(1)}, u32[]{:S(2)}, u32[]{:S(2)}) collective-permute-start(bf16[64,4224]{1,0:T(8,128)(2,1)S(1)} %collective-permute-done.8.refs_0_), channel_id=1, source_target_pairs={{0,4},{2,6},{4,0},{6,2},{8,12},{10,14},{12,8},{14,10},{16,20},{18,... | collective-permute-start | bytes 1622024 | tf_op jit(solution)/shard_map/ppermute | solution.py:149
  32.5 14.5 %collective-permute-start.9 = (bf16[64,4224]{1,0:T(8,128)(2,1)S(1)}, bf16[64,4224]{1,0:T(8,128)(2,1)}, u32[]{:S(2)}, u32[]{:S(2)}) collective-permute-start(bf16[64,4224]{1,0:T(8,128)(2,1)S(1)} %collective-permute-done.8.refs_0_), channel_id=1, source_target_pairs={{0,8},{2,10},{4,12},{6,14},{8,16},{10,18},{12,20},{14,22},{16,24},... | collective-permute-start | bytes 1622024 | tf_op jit(solution)/shard_map/ppermute | solution.py:155
  32.5 48.3 %collective-permute-start.5 = (bf16[768,1024]{1,0:T(8,128)(2,1)}, bf16[768,1024]{1,0:T(8,128)(2,1)}, u32[]{:S(2)}, u32[]{:S(2)}) collective-permute-start(bf16[768,1024]{1,0:T(8,128)(2,1)} %get-tuple-element.38), channel_id=1, source_target_pairs={{0,1},{1,0},{2,3},{3,2},{4,5},{5,4},{6,7},{7,6},{8,9},{9,8},{10,11... | collective-permute-start | bytes 4718600 | tf_op jit(solution)/shard_map/ppermute | solution.py:146
  34.0 21.2 %collective-permute-start.1 = (bf16[64,4224]{1,0:T(8,128)(2,1)}, bf16[64,4224]{1,0:T(8,128)(2,1)}, u32[]{:S(2)}, u32[]{:S(2)}) collective-permute-start(bf16[64,4224]{1,0:T(8,128)(2,1)} %pad_maximum_fusion.refs_0_), channel_id=1, source_target_pairs={{0,4},{2,6},{4,0},{6,2},{8,12},{10,14},{12,8},{14,10},{16,20},{18,... | collective-permute-start | bytes 1622024 | tf_op jit(solution)/shard_map/ppermute | solution.py:149
  34.5 20.7 %collective-permute-start.24 = (bf16[64,4224]{1,0:T(8,128)(2,1)S(1)}, bf16[64,4224]{1,0:T(8,128)(2,1)S(1)}, u32[]{:S(2)}, u32[]{:S(2)}) collective-permute-start(bf16[64,4224]{1,0:T(8,128)(2,1)S(1)} %collective-permute-done.8.refs_0_), channel_id=1, source_target_pairs={{0,2},{2,0},{4,6},{6,4},{8,10},{10,8},{12,14},{14,12},{16,18},{18,... | collective-permute-start | bytes 1622024 | tf_op jit(solution)/shard_map/ppermute | solution.py:152
  47.0 16.8 %collective-permute-start.10 = (bf16[64,4224]{1,0:T(8,128)(2,1)}, bf16[64,4224]{1,0:T(8,128)(2,1)}, u32[]{:S(2)}, u32[]{:S(2)}) collective-permute-start(bf16[64,4224]{1,0:T(8,128)(2,1)} %collective-permute-done.9.refs_0_), channel_id=1, source_target_pairs={{0,8},{2,10},{4,12},{6,14},{8,16},{10,18},{12,20},{14,22},{16,24},... | collective-permute-start | bytes 1622024 | tf_op jit(solution)/shard_map/ppermute | solution.py:155
  55.2 20.0 %collective-permute-start.2 = (bf16[64,4224]{1,0:T(8,128)(2,1)}, bf16[64,4224]{1,0:T(8,128)(2,1)}, u32[]{:S(2)}, u32[]{:S(2)}) collective-permute-start(bf16[64,4224]{1,0:T(8,128)(2,1)} %pad_maximum_fusion.refs_0_), channel_id=1, source_target_pairs={{0,2},{2,0},{4,6},{6,4},{8,10},{10,8},{12,14},{14,12},{16,18},{18,... | collective-permute-start | bytes 1622024 | tf_op jit(solution)/shard_map/ppermute | solution.py:152
  56.0 20.7 %collective-permute-start.3 = (bf16[64,4224]{1,0:T(8,128)(2,1)}, bf16[64,4224]{1,0:T(8,128)(2,1)}, u32[]{:S(2)}, u32[]{:S(2)}) collective-permute-start(bf16[64,4224]{1,0:T(8,128)(2,1)} %collective-permute-done.1.refs_1_), channel_id=1, source_target_pairs={{0,2},{2,0},{4,6},{6,4},{8,10},{10,8},{12,14},{14,12},{16,18},{18,... | collective-permute-start | bytes 1622024 | tf_op jit(solution)/shard_map/ppermute | solution.py:152
  57.3 23.5 %collective-permute-start.17 = (bf16[64,4224]{1,0:T(8,128)(2,1)}, bf16[64,4224]{1,0:T(8,128)(2,1)}, u32[]{:S(2)}, u32[]{:S(2)}) collective-permute-start(bf16[64,4224]{1,0:T(8,128)(2,1)} %collective-permute-done.9.refs_0_), channel_id=1, source_target_pairs={{0,4},{2,6},{4,0},{6,2},{8,12},{10,14},{12,8},{14,10},{16,20},{18,... | collective-permute-start | bytes 1622024 | tf_op jit(solution)/shard_map/ppermute | solution.py:149
  63.8 23.5 %collective-permute-start.11 = (bf16[64,4224]{1,0:T(8,128)(2,1)}, bf16[64,4224]{1,0:T(8,128)(2,1)}, u32[]{:S(2)}, u32[]{:S(2)}) collective-permute-start(bf16[64,4224]{1,0:T(8,128)(2,1)} %collective-permute-done.10.refs_0_), channel_id=1, source_target_pairs={{0,4},{2,6},{4,0},{6,2},{8,12},{10,14},{12,8},{14,10},{16,20},{18,... | collective-permute-start | bytes 1622024 | tf_op jit(solution)/shard_map/ppermute | solution.py:149
  75.2 12.1 %collective-permute-start.26 = (bf16[256,768]{1,0:T(8,128)(2,1)S(1)}, bf16[256,768]{1,0:T(8,128)(2,1)S(1)}, u32[]{:S(2)}, u32[]{:S(2)}) collective-permute-start(bf16[256,768]{1,0:T(8,128)(2,1)S(1)} %get-tuple-element.50.refs_4_), channel_id=1, source_target_pairs={{0,1},{1,0},{2,3},{3,2},{4,5},{5,4},{6,7},{7,6},{8,9},{9,8},{10,11... | collective-permute-start | bytes 1179656 | tf_op jit(solution)/shard_map/ppermute | solution.py:146
  80.2 13.9 %collective-permute-start.4 = (bf16[256,768]{1,0:T(8,128)(2,1)S(1)}, bf16[256,768]{1,0:T(8,128)(2,1)S(1)}, u32[]{:S(2)}, u32[]{:S(2)}) collective-permute-start(bf16[256,768]{1,0:T(8,128)(2,1)S(1)} %get-tuple-element.37.refs_4_), channel_id=1, source_target_pairs={{0,1},{1,0},{2,3},{3,2},{4,5},{5,4},{6,7},{7,6},{8,9},{9,8},{10,11... | collective-permute-start | bytes 1179656 | tf_op jit(solution)/shard_map/ppermute | solution.py:146
  80.8 20.8 %collective-permute-start.18 = (bf16[64,4224]{1,0:T(8,128)(2,1)}, bf16[64,4224]{1,0:T(8,128)(2,1)}, u32[]{:S(2)}, u32[]{:S(2)}) collective-permute-start(bf16[64,4224]{1,0:T(8,128)(2,1)} %collective-permute-done.9.refs_0_), channel_id=1, source_target_pairs={{0,2},{2,0},{4,6},{6,4},{8,10},{10,8},{12,14},{14,12},{16,18},{18,... | collective-permute-start | bytes 1622024 | tf_op jit(solution)/shard_map/ppermute | solution.py:152
  80.9 21.4 %collective-permute-start.19 = (bf16[64,4224]{1,0:T(8,128)(2,1)}, bf16[64,4224]{1,0:T(8,128)(2,1)}, u32[]{:S(2)}, u32[]{:S(2)}) collective-permute-start(bf16[64,4224]{1,0:T(8,128)(2,1)} %collective-permute-done.17.refs_1_), channel_id=1, source_target_pairs={{0,2},{2,0},{4,6},{6,4},{8,10},{10,8},{12,14},{14,12},{16,18},{18,... | collective-permute-start | bytes 1622024 | tf_op jit(solution)/shard_map/ppermute | solution.py:152
  87.3 20.0 %collective-permute-start.12 = (bf16[64,4224]{1,0:T(8,128)(2,1)}, bf16[64,4224]{1,0:T(8,128)(2,1)}, u32[]{:S(2)}, u32[]{:S(2)}) collective-permute-start(bf16[64,4224]{1,0:T(8,128)(2,1)} %collective-permute-done.10.refs_0_), channel_id=1, source_target_pairs={{0,2},{2,0},{4,6},{6,4},{8,10},{10,8},{12,14},{14,12},{16,18},{18,... | collective-permute-start | bytes 1622024 | tf_op jit(solution)/shard_map/ppermute | solution.py:152
  87.3 20.0 %collective-permute-start.13 = (bf16[64,4224]{1,0:T(8,128)(2,1)}, bf16[64,4224]{1,0:T(8,128)(2,1)}, u32[]{:S(2)}, u32[]{:S(2)}) collective-permute-start(bf16[64,4224]{1,0:T(8,128)(2,1)} %collective-permute-done.11.refs_1_), channel_id=1, source_target_pairs={{0,2},{2,0},{4,6},{6,4},{8,10},{10,8},{12,14},{14,12},{16,18},{18,... | collective-permute-start | bytes 1622024 | tf_op jit(solution)/shard_map/ppermute | solution.py:152
  94.9 16.5 %collective-permute-start.27 = (bf16[2,2,32,1152]{3,2,1,0:T(8,128)(2,1)}, bf16[2,2,32,1152]{3,2,1,0:T(8,128)(2,1)}, u32[]{:S(2)}, u32[]{:S(2)}) collective-permute-start(bf16[2,2,32,1152]{3,2,1,0:T(8,128)(2,1)} %get-tuple-element.53), channel_id=1, source_target_pairs={{0,2},{2,0},{4,6},{6,4},{8,10},{10,8},{12,14},{14,12},{16,18},{18,... | collective-permute-start | bytes 884744 | tf_op jit(solution)/shard_map/ppermute | solution.py:152
  101.6 32.7 %collective-permute-start.6 = (bf16[2,2,32,1152]{3,2,0,1:T(8,128)(2,1)S(1)}, bf16[2,2,32,1152]{3,2,0,1:T(8,128)(2,1)S(1)}, u32[]{:S(2)}, u32[]{:S(2)}) collective-permute-start(bf16[2,2,32,1152]{3,2,0,1:T(8,128)(2,1)S(1)} %copy.31), channel_id=1, source_target_pairs={{0,2},{2,0},{4,6},{6,4},{8,10},{10,8},{12,14},{14,12},{16,18},{18,... | collective-permute-start | bytes 884744 | tf_op jit(solution)/shard_map/ppermute | solution.py:152
  105.7 12.0 %collective-permute-start.20 = (bf16[256,768]{1,0:T(8,128)(2,1)S(1)}, bf16[256,768]{1,0:T(8,128)(2,1)S(1)}, u32[]{:S(2)}, u32[]{:S(2)}) collective-permute-start(bf16[256,768]{1,0:T(8,128)(2,1)S(1)} %get-tuple-element.46.refs_4_), channel_id=1, source_target_pairs={{0,1},{1,0},{2,3},{3,2},{4,5},{5,4},{6,7},{7,6},{8,9},{9,8},{10,11... | collective-permute-start | bytes 1179656 | tf_op jit(solution)/shard_map/ppermute | solution.py:146
  110.8 14.5 %collective-permute-start.14 = (bf16[256,768]{1,0:T(8,128)(2,1)S(1)}, bf16[256,768]{1,0:T(8,128)(2,1)S(1)}, u32[]{:S(2)}, u32[]{:S(2)}) collective-permute-start(bf16[256,768]{1,0:T(8,128)(2,1)S(1)} %get-tuple-element.42.refs_4_), channel_id=1, source_target_pairs={{0,1},{1,0},{2,3},{3,2},{4,5},{5,4},{6,7},{7,6},{8,9},{9,8},{10,11... | collective-permute-start | bytes 1179656 | tf_op jit(solution)/shard_map/ppermute | solution.py:146
  112.3 16.5 %collective-permute-start.28 = (bf16[2,32,1152]{2,1,0:T(8,128)(2,1)S(1)}, bf16[2,32,1152]{2,1,0:T(8,128)(2,1)S(1)}, u32[]{:S(2)}, u32[]{:S(2)}) collective-permute-start(bf16[2,32,1152]{2,1,0:T(8,128)(2,1)S(1)} %fusion.13), channel_id=1, source_target_pairs={{0,4},{2,6},{4,0},{6,2},{8,12},{10,14},{12,8},{14,10},{16,20},{18,... | collective-permute-start | bytes 442376 | tf_op jit(solution)/shard_map/ppermute | solution.py:149
  129.9 12.3 %collective-permute-start.29 = (bf16[2,32,1152]{2,1,0:T(8,128)(2,1)S(1)}, bf16[2,32,1152]{2,1,0:T(8,128)(2,1)S(1)}, u32[]{:S(2)}, u32[]{:S(2)}) collective-permute-start(bf16[2,32,1152]{2,1,0:T(8,128)(2,1)S(1)} %fusion), channel_id=1, source_target_pairs={{0,8},{2,10},{4,12},{6,14},{8,16},{10,18},{12,20},{14,22},{16,24},... | collective-permute-start | bytes 442376 | tf_op jit(solution)/shard_map/ppermute | solution.py:155
  134.4 18.3 %collective-permute-start.7 = (bf16[2,32,1152]{2,1,0:T(8,128)(2,1)S(1)}, bf16[2,32,1152]{2,1,0:T(8,128)(2,1)S(1)}, u32[]{:S(2)}, u32[]{:S(2)}) collective-permute-start(bf16[2,32,1152]{2,1,0:T(8,128)(2,1)S(1)} %fusion.10), channel_id=1, source_target_pairs={{0,4},{2,6},{4,0},{6,2},{8,12},{10,14},{12,8},{14,10},{16,20},{18,... | collective-permute-start | bytes 442376 | tf_op jit(solution)/shard_map/ppermute | solution.py:149
  (51 other events, 445.0 us)

commit v2 on v1

--- a/solution.py
+++ b/solution.py
@@ -64,12 +64,11 @@
     tail_out[...] = jnp.where(lane == mine, row_grad, 0.0).astype(bf16)
 
 
-def grad_kernel(segments, half, *refs):
+def grad_kernel(segments, half, parts, *refs):
     count = len(segments)
     blocks = refs[:count]
-    (near, far, w_near, w_far, tail, alpha, side) = refs[count : count + 7]
-    (d_own, d_other, sums) = refs[count + 7 : count + 10]
-    (squash, slope) = refs[count + 10 :]
+    (near, far, w_in, *w_far) = refs[count : count + 3 + parts]
+    (tail, alpha, side, d_own, d_other, sums, squash, slope) = refs[count + 3 + parts :]
     rows = near.shape[0]
     block = rows // 8
     gain = alpha[0]
@@ -95,8 +94,18 @@
     step = 512
     for at in range(0, half, step):
         cols = slice(at, at + step)
-        part = jnp.dot(near[...], w_near[:, cols], preferred_element_type=f32)
-        part = part + jnp.dot(mirrored, w_far[:, cols], preferred_element_type=f32)
+        part = jnp.dot(
+            near[...],
+            w_in[:, pl.ds(pl.multiple_of(start + at, step), step)],
+            preferred_element_type=f32,
+        )
+        for index, held in enumerate(w_far):
+            deep = held.shape[0]
+            part = part + jnp.dot(
+                mirrored[:, index * deep : (index + 1) * deep],
+                held[:, cols],
+                preferred_element_type=f32,
+            )
         short = part.astype(bf16)
         place(cols, short)
         part = short.astype(f32)
@@ -166,7 +175,6 @@
     mine = me.reshape(1).astype(jnp.int32)
     half = width // 2
     side = lax.axis_index("dp").astype(jnp.int32)
-    w_near = lax.dynamic_slice_in_dim(flat_in, side * half, half, axis=1)
     w_send = lax.dynamic_slice_in_dim(flat_in, (1 - side) * half, half, axis=1)
 
     segments = tuple(
@@ -198,13 +206,13 @@
 
     def second_half(arrays, near, far, w_far, tail):
         return pl.pallas_call(
-            functools.partial(grad_kernel, segments, half),
+            functools.partial(grad_kernel, segments, half, len(w_far)),
             out_shape=(
                 jax.ShapeDtypeStruct((2, 2, block, half + LANES), bf16),
                 jax.ShapeDtypeStruct((2, 2, block, half + LANES), bf16),
                 jax.ShapeDtypeStruct((8, half), f32),
             ),
-            in_specs=[whole()] * 9 + [scalar(), scalar()],
+            in_specs=[whole()] * (8 + len(w_far)) + [scalar(), scalar()],
             out_specs=(whole(),) * 3,
             scratch_shapes=[
                 pltpu.VMEM((rows, half), f32),
@@ -212,7 +220,7 @@
             ],
             compiler_params=params,
             name="grads",
-        )(*arrays, near, far, w_near, w_far, tail, alpha, side.reshape(1))
+        )(*arrays, near, far, flat_in, *w_far, tail, alpha, side.reshape(1))
 
     def settle(d_own, d_other):
         got = go_core(d_other)
@@ -220,22 +228,48 @@
         keep = d_own[:, 0].astype(f32) + got[:, 0].astype(f32)
         return keep + go_y(send).astype(f32)
 
+    fence = lax.optimization_barrier
     own = jnp.concatenate([own, go_x(own)], axis=0)
-    own, w_send = lax.optimization_barrier((own, w_send))
-    w_far = go_x(w_send)
-    planed = [own]
-    for _ in range(planes - 1):
-        planed.append(go_z(planed[-1]))
+    parts = planes - 1
+    deep = 2 * hidden // parts
+    w_parts = [w_send[k * deep : (k + 1) * deep] for k in range(parts)]
+    near, far, near_c, far_c, w_far = {0: own}, {}, {}, {}, []
+    near[0], w_parts = fence((near[0], w_parts))
+    first, other, acts, scaled, totals = {}, {}, {}, {}, []
+
+    def rows_of(k):
+        arrays = (near[k], far[k], near_c[k], far_c[k])
+        grads, acts[k], scaled[k], tail = first_half(arrays)
+        first[k] = (arrays, grads, tail)
+
+    for k in range(planes):
+        if k < parts:
+            near[k + 1] = go_z(near[k])
+        far[k] = go_y(near[k])
+        if k < parts:
+            w_far.append(go_x(w_parts[k]))
+        near_c[k] = go_core(near[k])
+        if k:
+            far_c[k - 1] = go_core(far[k - 1])
+            rows_of(k - 1)
+        if k == parts:
+            for j in range(k - 1):
+                other[j] = go_x(first[j][1])
+        near, far, near_c, far_c, w_far, first, other = fence(
+            (near, far, near_c, far_c, w_far, first, other)
+        )
+    last = planes - 1
+    far_c[last] = go_core(far[last])
+    other[last - 1] = go_x(first[last - 1][1])
+    rows_of(last)
+    first, other = fence((first, other))
+    other[last] = go_x(first[last][1])
+
+    carry = None
     order = list(range(planes))
-    arrays, acts, scaled, totals, ready = {}, {}, {}, [], {}
-    for k in order:
-        far = go_y(planed[k])
-        arrays[k] = (planed[k], far, go_core(planed[k]), go_core(far))
-        grads, acts[k], scaled[k], tail = first_half(arrays[k])
-        ready[k] = (grads, go_x(grads), w_far, tail)
-    carry = None
     for k in order[1:] + order[:1]:
-        d_own, d_other, sums = second_half(arrays[k], *ready[k])
+        arrays, grads, tail = first[k]
+        d_own, d_other, sums = second_half(arrays, grads, other[k], w_far, tail)
         totals.append(sums)
         value = settle(d_own, d_other)
         if carry is not None:
@@ -243,11 +277,11 @@
         carry = value.astype(bf16)
     acts = [acts[k] for k in order]
     scaled = [scaled[k] for k in order]
-    other = go_x(carry[1]).astype(f32)
-    first = jnp.where(side == 0, value[0, :, :half], other[:, :half])
-    last = jnp.where(side == 0, other[:, :half], value[0, :, :half])
-    grad_normed = jnp.concatenate([first, last], axis=1)
-    row_grads = value[0, :, half:] + other[:, half:]
+    crossed = go_x(carry[1]).astype(f32)
+    left = jnp.where(side == 0, value[0, :, :half], crossed[:, :half])
+    right = jnp.where(side == 0, crossed[:, :half], value[0, :, :half])
+    grad_normed = jnp.concatenate([left, right], axis=1)
+    row_grads = value[0, :, half:] + crossed[:, half:]
 
     sums = sum(totals[1:], totals[0])
     for go in (go_core, go_y):
@@ -384,6 +418,7 @@
         and (experts & (experts - 1)) == 0
         and experts <= LANES
         and 2 * top_count >= experts
+        and 2 * arrays[8].shape[1] % (16 * (experts // 4 - 1)) == 0
     )
     return (dense_shards if dense else routed_shards)(*arrays)
 

time: 166 us -> 167 us (level)
  waiting for transfers between devices: 75.2 us -> 66 us
  starting transfers between devices: 28.8 us -> 35.9 us
  local copies, waits for them, and re-layouts: 21.6 us -> 26.9 us
    ppermute x8 -> x10, waiting for transfers between devices: 22.7 us -> 48.5 us  [go_x(): return lax.ppermute(v, 'dp', [(0, 1), (1, 0)])]
    ppermute x9, waiting for transfers between devices: 22.9 us -> 3.67 us  [go_y(): return lax.ppermute(v, 'expert', [(e, e ^ 2) for e in range(experts)])]
    ppermute x6, waiting for transfers between devices: 26.6 us -> 10.1 us  [go_z(): lax.ppermute(v, 'expert', [(e, (e + 4) % experts) for e in range(experts)])]
    unnamed x75 -> x143, local copies, waits for them, and re-layouts: 16.5 us -> 23.3 us
    ppermute x6, starting transfers between devices: 2.37 us -> 7.38 us  [go_z(): lax.ppermute(v, 'expert', [(e, (e + 4) % experts) for e in range(experts)])]
    dynamic_slice x1 -> x0, local copies, waits for them, and re-layouts: 4.01 us -> none  [dense_shards(): w_near = lax.dynamic_slice_in_dim(flat_in, side * half, half, axis=1)]
    ppermute x8 -> x10, starting transfers between devices: 10.8 us -> 14.6 us  [go_x(): return lax.ppermute(v, 'dp', [(0, 1), (1, 0)])]
    slice x0 -> x1, local copies, waits for them, and re-layouts: none -> 2.7 us  [dense_shards(): w_parts = [w_send[k * deep:(k + 1) * deep] for k in range(parts)]]
  transfers between devices with their start and end apart: 38 -> 40, of which waited for: 18 -> 16; matrix products, arithmetic and copies ran while one was open for 5% -> 4% of each run, Pallas kernels for 18% -> 17%
where the time goes in v2:
time: 167 us; the launch traced here: 166 us
  waiting for transfers between devices  66 us (40%)
  starting transfers between devices  35.9 us (21%)
  Pallas kernels  27.5 us (16%)
  local copies, waits for them, and re-layouts  26.9 us (16%)
  other arithmetic  8.06 us (5%)
  between operations  1.99 us (1%)
    ppermute x10, waiting for transfers between devices, go_x(): return lax.ppermute(v, 'dp', [(0, 1), (1, 0)])  48.5 us
    unnamed x143, local copies, waits for them, and re-layouts  23.3 us
    ppermute x10, starting transfers between devices, go_x(): return lax.ppermute(v, 'dp', [(0, 1), (1, 0)])  14.6 us
    pallas_call x4, Pallas kernels, first_half(): pl.pallas_call(functools.partial(rows_kernel, segments, width, hidden), o...  12.7 us
    pallas_call x4, Pallas kernels, second_half(): pl.pallas_call(functools.partial(grad_kernel, segments, half, len(w_far))...  11.8 us
    ppermute x9, starting transfers between devices, go_y(): return lax.ppermute(v, 'expert', [(e, e ^ 2) for e in range(experts)])  11 us
    ppermute x6, waiting for transfers between devices, go_z(): lax.ppermute(v, 'expert', [(e, (e + 4) % experts) for e in range(experts)])  10.1 us
    ppermute x6, starting transfers between devices, go_z(): lax.ppermute(v, 'expert', [(e, (e + 4) % experts) for e in range(experts)])  7.38 us
  transfers between devices with their start and end apart: 40, of which 16 were waited for; matrix products, arithmetic and copies ran while one was open for 4% of the time, Pallas kernels for 17%

profile of v2, /device:TPU:0, one launch (start us, length us, event | category | flops | bytes accessed | tf_op | source)
XLA Modules:
  0.0 166.3 jit_solution(13368243803432013368)
XLA Ops:
  4.1 2.9 %collective-permute-start = (bf16[32,4224]{1,0:T(8,128)(2,1)}, bf16[32,4224]{1,0:T(8,128)(2,1)}, u32[]{:S(2)}, u32[]{:S(2)}) collective-permute-start(bf16[32,4224]{1,0:T(8,128)(2,1)} %pad_maximum_fusion.1), channel_id=1, source_target_pairs={{0,1},{1,0},{2,3},{3,2},{4,5},{5,4},{6,7},{7,6},{8,9},{9,8},{10,11... | collective-permute-start | bytes 811016 | tf_op jit(solution)/shard_map/ppermute | solution.py:155
  7.0 2.7 %fusion.15 = (bf16[256,1024]{1,0:T(8,128)(2,1)}, bf16[256,1024]{1,0:T(8,128)(2,1)}, bf16[256,1024]{1,0:T(8,128)(2,1)S(1)}) fusion(bf16[768,2048]{1,0:T(8,128)(2,1)} %bitcast.70, s32[]{:T(128)S(6)} %add.122, s32[]{:T(128)S(6)} %select_n.37, s32[]{:T(128)S(6)} %add.121), kind=kLoop, calls=%fused_computation.46 | loop fusion | bytes 3145740 | tf_op jit(solution)/shard_map/slice | solution.py:235
  9.7 4.1 %collective-permute-done = bf16[32,4224]{1,0:T(8,128)(2,1)} collective-permute-done((bf16[32,4224]{1,0:T(8,128)(2,1)}, bf16[32,4224]{1,0:T(8,128)(2,1)}, u32[]{:S(2)}, u32[]{:S(2)}) %collective-permute-start) | collective-permute-done | bytes 270368 | tf_op jit(solution)/shard_map/ppermute | solution.py:155
  14.8 1.9 %collective-permute-start.1 = (bf16[64,4224]{1,0:T(8,128)(2,1)S(1)}, bf16[64,4224]{1,0:T(8,128)(2,1)}, u32[]{:S(2)}, u32[]{:S(2)}) collective-permute-start(bf16[64,4224]{1,0:T(8,128)(2,1)S(1)} %pad_maximum_fusion.refs_0_), channel_id=1, source_target_pairs={{0,8},{2,10},{4,12},{6,14},{8,16},{10,18},{12,20},{14,22},{16,24},... | collective-permute-start | bytes 1622024 | tf_op jit(solution)/shard_map/ppermute | solution.py:164
  20.5 12.8 %collective-permute-done.4.refs_7_ = bf16[256,1024]{1,0:T(8,128)(2,1)S(1)} collective-permute-done((bf16[256,1024]{1,0:T(8,128)(2,1)S(1)}, bf16[256,1024]{1,0:T(8,128)(2,1)S(1)}, u32[]{:S(2)}, u32[]{:S(2)}) %collective-permute-start.4) | collective-permute-done | bytes 524320 | tf_op jit(solution)/shard_map/ppermute | solution.py:155
  42.7 3.4 %rows.4 = (bf16[256,768]{1,0:T(8,128)(2,1)S(1)}, bf16[256,384]{1,0:T(8,128)(2,1)S(1)}, bf16[256,2048]{1,0:T(8,128)(2,1)S(1)}, bf16[256,128]{1,0:T(8,128)(2,1)S(1)}) custom-call(bf16[64,4224]{1,0:T(8,128)(2,1)S(1)} %copy-done.11, bf16[64,4224]{1,0:T(8,128)(2,1)} %collective-permute-done.2.refs_1_, bf16[64,4224]{1,0:T(8,128)(2,1)S(1)} %copy-done.14, ...), custom_call_target="tpu_custom_call" | custom-call | tf_op jit(solution)/shard_map/rows/pallas_call | solution.py:188
  47.7 4.0 %collective-permute-done.9.refs_8_ = bf16[256,1024]{1,0:T(8,128)(2,1)} collective-permute-done((bf16[256,1024]{1,0:T(8,128)(2,1)}, bf16[256,1024]{1,0:T(8,128)(2,1)}, u32[]{:S(2)}, u32[]{:S(2)}) %collective-permute-start.9) | collective-permute-done | bytes 524320 | tf_op jit(solution)/shard_map/ppermute | solution.py:155
  56.6 3.3 %rows.5 = (bf16[256,768]{1,0:T(8,128)(2,1)S(1)}, bf16[256,384]{1,0:T(8,128)(2,1)S(1)}, bf16[256,2048]{1,0:T(8,128)(2,1)S(1)}, bf16[256,128]{1,0:T(8,128)(2,1)S(1)}) custom-call(bf16[64,4224]{1,0:T(8,128)(2,1)} %collective-permute-done.1.refs_0_, bf16[64,4224]{1,0:T(8,128)(2,1)} %collective-permute-done.6.refs_1_, ...), custom_call_target="tpu_custom_call" | custom-call | tf_op jit(solution)/shard_map/rows/pallas_call | solution.py:188
  61.6 7.8 %collective-permute-done.14.refs_9_ = bf16[256,1024]{1,0:T(8,128)(2,1)S(1)} collective-permute-done((bf16[256,1024]{1,0:T(8,128)(2,1)S(1)}, bf16[256,1024]{1,0:T(8,128)(2,1)S(1)}, u32[]{:S(2)}, u32[]{:S(2)}) %collective-permute-start.14) | collective-permute-done | bytes 524320 | tf_op jit(solution)/shard_map/ppermute | solution.py:155
  72.3 3.2 %rows.6 = (bf16[256,768]{1,0:T(8,128)(2,1)S(1)}, bf16[256,384]{1,0:T(8,128)(2,1)S(1)}, bf16[256,2048]{1,0:T(8,128)(2,1)S(1)}, bf16[256,128]{1,0:T(8,128)(2,1)S(1)}) custom-call(bf16[64,4224]{1,0:T(8,128)(2,1)} %collective-permute-done.5.refs_0_, bf16[64,4224]{1,0:T(8,128)(2,1)S(1)} %collective-permute-done.11.refs_1_, ...), custom_call_target="tpu_custom_call" | custom-call | tf_op jit(solution)/shard_map/rows/pallas_call | solution.py:188
  77.9 4.4 %collective-permute-done.18.refs_5_ = bf16[256,768]{1,0:T(8,128)(2,1)S(1)} collective-permute-done((bf16[256,768]{1,0:T(8,128)(2,1)S(1)}, bf16[256,768]{1,0:T(8,128)(2,1)S(1)}, u32[]{:S(2)}, u32[]{:S(2)}) %collective-permute-start.18) | collective-permute-done | bytes 393248 | tf_op jit(solution)/shard_map/ppermute | solution.py:155
  83.0 7.1 %collective-permute-done.19.refs_5_ = bf16[256,768]{1,0:T(8,128)(2,1)S(1)} collective-permute-done((bf16[256,768]{1,0:T(8,128)(2,1)S(1)}, bf16[256,768]{1,0:T(8,128)(2,1)S(1)}, u32[]{:S(2)}, u32[]{:S(2)}) %collective-permute-start.19) | collective-permute-done | bytes 393248 | tf_op jit(solution)/shard_map/ppermute | solution.py:155
  92.1 2.7 %rows.7 = (bf16[256,768]{1,0:T(8,128)(2,1)}, bf16[256,384]{1,0:T(8,128)(2,1)S(1)}, bf16[256,2048]{1,0:T(8,128)(2,1)S(1)}, bf16[256,128]{1,0:T(8,128)(2,1)S(1)}) custom-call(bf16[64,4224]{1,0:T(8,128)(2,1)S(1)} %collective-permute-done.10.refs_0_, bf16[64,4224]{1,0:T(8,128)(2,1)S(1)} %collective-permute-done.15.refs_1_, ...), custom_call_target="tpu_custom_call" | custom-call | tf_op jit(solution)/shard_map/rows/pallas_call | solution.py:188
  97.2 4.6 %collective-permute-done.21.refs_5_ = bf16[256,768]{1,0:T(8,128)(2,1)S(1)} collective-permute-done((bf16[256,768]{1,0:T(8,128)(2,1)S(1)}, bf16[256,768]{1,0:T(8,128)(2,1)S(1)}, u32[]{:S(2)}, u32[]{:S(2)}) %collective-permute-start.21) | collective-permute-done | bytes 393248 | tf_op jit(solution)/shard_map/ppermute | solution.py:155
  104.0 3.5 %grads.7 = (bf16[2,2,32,1152]{3,2,1,0:T(8,128)(2,1)S(1)}, bf16[2,2,32,1152]{3,2,1,0:T(8,128)(2,1)}, f32[8,1024]{1,0:T(8,128)S(1)}) custom-call(bf16[64,4224]{1,0:T(8,128)(2,1)} %collective-permute-done.1.refs_0_, bf16[64,4224]{1,0:T(8,128)(2,1)} %collective-permute-done.6.refs_1_, bf16[64,4224]{1,0:T(8,128)(2,1)} %collective-permute-done.7.refs_2_, ...), custom_call_target="tpu_custom_call" | custom-call | tf_op jit(solution)/shard_map/grads/pallas_call | solution.py:208
  114.8 2.8 %grads.4 = (bf16[2,2,32,1152]{3,2,1,0:T(8,128)(2,1)S(1)}, bf16[2,2,32,1152]{3,2,1,0:T(8,128)(2,1)S(1)}, f32[8,1024]{1,0:T(8,128)S(1)}) custom-call(bf16[64,4224]{1,0:T(8,128)(2,1)S(1)} %copy-done.12, bf16[64,4224]{1,0:T(8,128)(2,1)} %collective-permute-done.2.refs_1_, bf16[64,4224]{1,0:T(8,128)(2,1)S(1)} %copy-done.15, ...), custom_call_target="tpu_custom_call" | custom-call | tf_op jit(solution)/shard_map/grads/pallas_call | solution.py:208
  118.4 2.6 %grads.6 = (bf16[2,2,32,1152]{3,2,1,0:T(8,128)(2,1)S(1)}, bf16[2,2,32,1152]{3,2,1,0:T(8,128)(2,1)S(1)}, f32[8,1024]{1,0:T(8,128)S(1)}) custom-call(bf16[64,4224]{1,0:T(8,128)(2,1)} %collective-permute-done.5.refs_0_, bf16[64,4224]{1,0:T(8,128)(2,1)S(1)} %copy-done.19, bf16[64,4224]{1,0:T(8,128)(2,1)S(1)} %copy-done.23, bf16[64,4224]{1,0:T(8,128)(2,1)S(1)} %copy-done.27, ...), custom_call_target="tpu_custom_call" | custom-call | tf_op jit(solution)/shard_map/grads/pallas_call | solution.py:208
  121.3 3.1 %down.1 = bf16[384,2048]{1,0:T(8,128)(2,1)} custom-call(bf16[256,384]{1,0:T(8,128)(2,1)S(1)} %copy-done.48, bf16[256,384]{1,0:T(8,128)(2,1)S(1)} %copy-done.50, bf16[256,384]{1,0:T(8,128)(2,1)S(1)} %copy-done.52, bf16[256,384]{1,0:T(8,128)(2,1)S(1)} %copy-done.54, bf16[256,2048]{1,0:T(8,128)(2,1)S(1)} %copy-done.31, bf16[256,2048]{1,0:T(8,128)(2,1)S(1)} %copy-done.33, ...), custom_call_target="tpu_custom_call" | custom-call | tf_op jit(solution)/shard_map/down/pallas_call | solution.py:298
  124.4 2.8 %grads.5 = (bf16[2,2,32,1152]{3,2,1,0:T(8,128)(2,1)S(1)}, bf16[2,2,32,1152]{3,2,1,0:T(8,128)(2,1)S(1)}, f32[8,1024]{1,0:T(8,128)S(1)}) custom-call(bf16[64,4224]{1,0:T(8,128)(2,1)S(1)} %copy-done.17, bf16[64,4224]{1,0:T(8,128)(2,1)S(1)} %copy-done.21, bf16[64,4224]{1,0:T(8,128)(2,1)S(1)} %copy-done.25, bf16[64,4224]{1,0:T(8,128)(2,1)S(1)} %copy-done.29, ...), custom_call_target="tpu_custom_call" | custom-call | tf_op jit(solution)/shard_map/grads/pallas_call | solution.py:208
  132.6 3.7 %collective-permute-done.36 = f32[8,1024]{1,0:T(8,128)S(1)} collective-permute-done((f32[8,1024]{1,0:T(8,128)S(1)}, f32[8,1024]{1,0:T(8,128)S(1)}, u32[]{:S(2)}, u32[]{:S(2)}) %collective-permute-start.36) | collective-permute-done | bytes 32800 | tf_op jit(solution)/shard_map/ppermute | solution.py:158
  143.4 2.0 %collective-permute-done.38 = f32[8,1024]{1,0:T(8,128)S(1)} collective-permute-done((f32[8,1024]{1,0:T(8,128)S(1)}, f32[8,1024]{1,0:T(8,128)S(1)}, u32[]{:S(2)}, u32[]{:S(2)}) %collective-permute-start.38) | collective-permute-done | bytes 32800 | tf_op jit(solution)/shard_map/ppermute | solution.py:291
  149.3 3.7 %collective-permute-done.32 = bf16[2,32,1152]{2,1,0:T(8,128)(2,1)S(1)} collective-permute-done((bf16[2,32,1152]{2,1,0:T(8,128)(2,1)S(1)}, bf16[2,32,1152]{2,1,0:T(8,128)(2,1)S(1)}, u32[]{:S(2)}, u32[]{:S(2)}) %collective-permute-start.32) | collective-permute-done | bytes 147488 | tf_op jit(solution)/shard_map/ppermute | solution.py:164
  153.8 6.3 %collective-permute-done.33 = bf16[2,32,1152]{2,1,0:T(8,128)(2,1)S(1)} collective-permute-done((bf16[2,32,1152]{2,1,0:T(8,128)(2,1)S(1)}, bf16[2,32,1152]{2,1,0:T(8,128)(2,1)S(1)}, u32[]{:S(2)}, u32[]{:S(2)}) %collective-permute-start.33) | collective-permute-done | bytes 147488 | tf_op jit(solution)/shard_map/ppermute | solution.py:164
  162.4 2.3 %collective-permute-done.34 = bf16[32,1152]{1,0:T(8,128)(2,1)S(1)} collective-permute-done((bf16[32,1152]{1,0:T(8,128)(2,1)S(1)}, bf16[32,1152]{1,0:T(8,128)(2,1)S(1)}, u32[]{:S(2)}, u32[]{:S(2)}) %collective-permute-start.34) | collective-permute-done | bytes 73760 | tf_op jit(solution)/shard_map/ppermute | solution.py:155
  (240 shorter events, 66.6 us)
Async XLA Ops:
  4.1 9.7 %collective-permute-start = (bf16[32,4224]{1,0:T(8,128)(2,1)}, bf16[32,4224]{1,0:T(8,128)(2,1)}, u32[]{:S(2)}, u32[]{:S(2)}) collective-permute-start(bf16[32,4224]{1,0:T(8,128)(2,1)} %pad_maximum_fusion.1), channel_id=1, source_target_pairs={{0,1},{1,0},{2,3},{3,2},{4,5},{5,4},{6,7},{7,6},{8,9},{9,8},{10,11... | collective-permute-start | bytes 811016 | tf_op jit(solution)/shard_map/ppermute | solution.py:155
  14.8 19.3 %collective-permute-start.1 = (bf16[64,4224]{1,0:T(8,128)(2,1)S(1)}, bf16[64,4224]{1,0:T(8,128)(2,1)}, u32[]{:S(2)}, u32[]{:S(2)}) collective-permute-start(bf16[64,4224]{1,0:T(8,128)(2,1)S(1)} %pad_maximum_fusion.refs_0_), channel_id=1, source_target_pairs={{0,8},{2,10},{4,12},{6,14},{8,16},{10,18},{12,20},{14,22},{16,24},... | collective-permute-start | bytes 1622024 | tf_op jit(solution)/shard_map/ppermute | solution.py:164
  16.7 17.4 %collective-permute-start.2 = (bf16[64,4224]{1,0:T(8,128)(2,1)S(1)}, bf16[64,4224]{1,0:T(8,128)(2,1)}, u32[]{:S(2)}, u32[]{:S(2)}) collective-permute-start(bf16[64,4224]{1,0:T(8,128)(2,1)S(1)} %pad_maximum_fusion.refs_0_), channel_id=1, source_target_pairs={{0,4},{2,6},{4,0},{6,2},{8,12},{10,14},{12,8},{14,10},{16,20},{18,... | collective-permute-start | bytes 1622024 | tf_op jit(solution)/shard_map/ppermute | solution.py:158
  18.2 15.9 %collective-permute-start.3 = (bf16[64,4224]{1,0:T(8,128)(2,1)S(1)}, bf16[64,4224]{1,0:T(8,128)(2,1)S(1)}, u32[]{:S(2)}, u32[]{:S(2)}) collective-permute-start(bf16[64,4224]{1,0:T(8,128)(2,1)S(1)} %pad_maximum_fusion.refs_0_), channel_id=1, source_target_pairs={{0,2},{2,0},{4,6},{6,4},{8,10},{10,8},{12,14},{14,12},{16,18},{18,... | collective-permute-start | bytes 1622024 | tf_op jit(solution)/shard_map/ppermute | solution.py:161
  19.0 14.3 %collective-permute-start.4 = (bf16[256,1024]{1,0:T(8,128)(2,1)S(1)}, bf16[256,1024]{1,0:T(8,128)(2,1)S(1)}, u32[]{:S(2)}, u32[]{:S(2)}) collective-permute-start(bf16[256,1024]{1,0:T(8,128)(2,1)S(1)} %get-tuple-element.128), channel_id=1, source_target_pairs={{0,1},{1,0},{2,3},{3,2},{4,5},{5,4},{6,7},{7,6},{8,9},{9,8},{10,11... | collective-permute-start | bytes 1572872 | tf_op jit(solution)/shard_map/ppermute | solution.py:155
  34.9 16.8 %collective-permute-start.5 = (bf16[64,4224]{1,0:T(8,128)(2,1)}, bf16[64,4224]{1,0:T(8,128)(2,1)}, u32[]{:S(2)}, u32[]{:S(2)}) collective-permute-start(bf16[64,4224]{1,0:T(8,128)(2,1)} %collective-permute-done.1.refs_0_), channel_id=1, source_target_pairs={{0,8},{2,10},{4,12},{6,14},{8,16},{10,18},{12,20},{14,22},{16,24},... | collective-permute-start | bytes 1622024 | tf_op jit(solution)/shard_map/ppermute | solution.py:164
  36.5 15.2 %collective-permute-start.6 = (bf16[64,4224]{1,0:T(8,128)(2,1)}, bf16[64,4224]{1,0:T(8,128)(2,1)}, u32[]{:S(2)}, u32[]{:S(2)}) collective-permute-start(bf16[64,4224]{1,0:T(8,128)(2,1)} %collective-permute-done.1.refs_0_), channel_id=1, source_target_pairs={{0,4},{2,6},{4,0},{6,2},{8,12},{10,14},{12,8},{14,10},{16,20},{18,... | collective-permute-start | bytes 1622024 | tf_op jit(solution)/shard_map/ppermute | solution.py:158
  37.0 14.7 %collective-permute-start.7 = (bf16[64,4224]{1,0:T(8,128)(2,1)}, bf16[64,4224]{1,0:T(8,128)(2,1)}, u32[]{:S(2)}, u32[]{:S(2)}) collective-permute-start(bf16[64,4224]{1,0:T(8,128)(2,1)} %collective-permute-done.1.refs_0_), channel_id=1, source_target_pairs={{0,2},{2,0},{4,6},{6,4},{8,10},{10,8},{12,14},{14,12},{16,18},{18,... | collective-permute-start | bytes 1622024 | tf_op jit(solution)/shard_map/ppermute | solution.py:161
  37.0 14.7 %collective-permute-start.9 = (bf16[256,1024]{1,0:T(8,128)(2,1)}, bf16[256,1024]{1,0:T(8,128)(2,1)}, u32[]{:S(2)}, u32[]{:S(2)}) collective-permute-start(bf16[256,1024]{1,0:T(8,128)(2,1)} %get-tuple-element.134), channel_id=1, source_target_pairs={{0,1},{1,0},{2,3},{3,2},{4,5},{5,4},{6,7},{7,6},{8,9},{9,8},{10,11... | collective-permute-start | bytes 1572872 | tf_op jit(solution)/shard_map/ppermute | solution.py:155
  51.8 17.7 %collective-permute-start.10 = (bf16[64,4224]{1,0:T(8,128)(2,1)}, bf16[64,4224]{1,0:T(8,128)(2,1)S(1)}, u32[]{:S(2)}, u32[]{:S(2)}) collective-permute-start(bf16[64,4224]{1,0:T(8,128)(2,1)} %collective-permute-done.5.refs_0_), channel_id=1, source_target_pairs={{0,8},{2,10},{4,12},{6,14},{8,16},{10,18},{12,20},{14,22},{16,24},... | collective-permute-start | bytes 1622024 | tf_op jit(solution)/shard_map/ppermute | solution.py:164
  53.6 15.9 %collective-permute-start.11 = (bf16[64,4224]{1,0:T(8,128)(2,1)}, bf16[64,4224]{1,0:T(8,128)(2,1)S(1)}, u32[]{:S(2)}, u32[]{:S(2)}) collective-permute-start(bf16[64,4224]{1,0:T(8,128)(2,1)} %collective-permute-done.5.refs_0_), channel_id=1, source_target_pairs={{0,4},{2,6},{4,0},{6,2},{8,12},{10,14},{12,8},{14,10},{16,20},{18,... | collective-permute-start | bytes 1622024 | tf_op jit(solution)/shard_map/ppermute | solution.py:158
  55.1 14.4 %collective-permute-start.12 = (bf16[64,4224]{1,0:T(8,128)(2,1)}, bf16[64,4224]{1,0:T(8,128)(2,1)S(1)}, u32[]{:S(2)}, u32[]{:S(2)}) collective-permute-start(bf16[64,4224]{1,0:T(8,128)(2,1)} %collective-permute-done.5.refs_0_), channel_id=1, source_target_pairs={{0,2},{2,0},{4,6},{6,4},{8,10},{10,8},{12,14},{14,12},{16,18},{18,... | collective-permute-start | bytes 1622024 | tf_op jit(solution)/shard_map/ppermute | solution.py:161
  55.1 14.3 %collective-permute-start.14 = (bf16[256,1024]{1,0:T(8,128)(2,1)S(1)}, bf16[256,1024]{1,0:T(8,128)(2,1)S(1)}, u32[]{:S(2)}, u32[]{:S(2)}) collective-permute-start(bf16[256,1024]{1,0:T(8,128)(2,1)S(1)} %copy-done.68), channel_id=1, source_target_pairs={{0,1},{1,0},{2,3},{3,2},{4,5},{5,4},{6,7},{7,6},{8,9},{9,8},{10,11... | collective-permute-start | bytes 1572872 | tf_op jit(solution)/shard_map/ppermute | solution.py:155
  69.6 20.5 %collective-permute-start.15 = (bf16[64,4224]{1,0:T(8,128)(2,1)S(1)}, bf16[64,4224]{1,0:T(8,128)(2,1)S(1)}, u32[]{:S(2)}, u32[]{:S(2)}) collective-permute-start(bf16[64,4224]{1,0:T(8,128)(2,1)S(1)} %collective-permute-done.10.refs_0_), channel_id=1, source_target_pairs={{0,4},{2,6},{4,0},{6,2},{8,12},{10,14},{12,8},{14,10},{16,20},{18,... | collective-permute-start | bytes 1622024 | tf_op jit(solution)/shard_map/ppermute | solution.py:158
  70.1 20.0 %collective-permute-start.16 = (bf16[64,4224]{1,0:T(8,128)(2,1)S(1)}, bf16[64,4224]{1,0:T(8,128)(2,1)S(1)}, u32[]{:S(2)}, u32[]{:S(2)}) collective-permute-start(bf16[64,4224]{1,0:T(8,128)(2,1)S(1)} %collective-permute-done.10.refs_0_), channel_id=1, source_target_pairs={{0,2},{2,0},{4,6},{6,4},{8,10},{10,8},{12,14},{14,12},{16,18},{18,... | collective-permute-start | bytes 1622024 | tf_op jit(solution)/shard_map/ppermute | solution.py:161
  70.3 11.9 %collective-permute-start.18 = (bf16[256,768]{1,0:T(8,128)(2,1)S(1)}, bf16[256,768]{1,0:T(8,128)(2,1)S(1)}, u32[]{:S(2)}, u32[]{:S(2)}) collective-permute-start(bf16[256,768]{1,0:T(8,128)(2,1)S(1)} %get-tuple-element.202.refs_4_), channel_id=1, source_target_pairs={{0,1},{1,0},{2,3},{3,2},{4,5},{5,4},{6,7},{7,6},{8,9},{9,8},{10,11... | collective-permute-start | bytes 1179656 | tf_op jit(solution)/shard_map/ppermute | solution.py:155
  71.8 18.3 %collective-permute-start.19 = (bf16[256,768]{1,0:T(8,128)(2,1)S(1)}, bf16[256,768]{1,0:T(8,128)(2,1)S(1)}, u32[]{:S(2)}, u32[]{:S(2)}) collective-permute-start(bf16[256,768]{1,0:T(8,128)(2,1)S(1)} %get-tuple-element.231.refs_4_), channel_id=1, source_target_pairs={{0,1},{1,0},{2,3},{3,2},{4,5},{5,4},{6,7},{7,6},{8,9},{9,8},{10,11... | collective-permute-start | bytes 1179656 | tf_op jit(solution)/shard_map/ppermute | solution.py:155
  90.2 11.5 %collective-permute-start.21 = (bf16[256,768]{1,0:T(8,128)(2,1)S(1)}, bf16[256,768]{1,0:T(8,128)(2,1)S(1)}, u32[]{:S(2)}, u32[]{:S(2)}) collective-permute-start(bf16[256,768]{1,0:T(8,128)(2,1)S(1)} %get-tuple-element.222.refs_4_), channel_id=1, source_target_pairs={{0,1},{1,0},{2,3},{3,2},{4,5},{5,4},{6,7},{7,6},{8,9},{9,8},{10,11... | collective-permute-start | bytes 1179656 | tf_op jit(solution)/shard_map/ppermute | solution.py:155
  102.5 21.9 %collective-permute-start.24 = (bf16[256,768]{1,0:T(8,128)(2,1)}, bf16[256,768]{1,0:T(8,128)(2,1)}, u32[]{:S(2)}, u32[]{:S(2)}) collective-permute-start(bf16[256,768]{1,0:T(8,128)(2,1)} %get-tuple-element.214.refs_4_), channel_id=1, source_target_pairs={{0,1},{1,0},{2,3},{3,2},{4,5},{5,4},{6,7},{7,6},{8,9},{9,8},{10,11... | collective-permute-start | bytes 1179656 | tf_op jit(solution)/shard_map/ppermute | solution.py:155
  108.8 19.0 %collective-permute-start.29 = (bf16[2,2,32,1152]{3,2,1,0:T(8,128)(2,1)}, bf16[2,2,32,1152]{3,2,1,0:T(8,128)(2,1)}, u32[]{:S(2)}, u32[]{:S(2)}) collective-permute-start(bf16[2,2,32,1152]{3,2,1,0:T(8,128)(2,1)} %get-tuple-element.235), channel_id=1, source_target_pairs={{0,2},{2,0},{4,6},{6,4},{8,10},{10,8},{12,14},{14,12},{16,18},{18,... | collective-permute-start | bytes 884744 | tf_op jit(solution)/shard_map/ppermute | solution.py:161
  117.7 23.9 %collective-permute-start.22 = (bf16[2,2,32,1152]{3,2,0,1:T(8,128)(2,1)S(1)}, bf16[2,2,32,1152]{3,2,0,1:T(8,128)(2,1)S(1)}, u32[]{:S(2)}, u32[]{:S(2)}) collective-permute-start(bf16[2,2,32,1152]{3,2,0,1:T(8,128)(2,1)S(1)} %copy.31), channel_id=1, source_target_pairs={{0,2},{2,0},{4,6},{6,4},{8,10},{10,8},{12,14},{14,12},{16,18},{18,... | collective-permute-start | bytes 884744 | tf_op jit(solution)/shard_map/ppermute | solution.py:161
  121.0 9.9 %collective-permute-start.27 = (bf16[2,2,32,1152]{3,2,0,1:T(8,128)(2,1)S(1)}, bf16[2,2,32,1152]{3,2,0,1:T(8,128)(2,1)S(1)}, u32[]{:S(2)}, u32[]{:S(2)}) collective-permute-start(bf16[2,2,32,1152]{3,2,0,1:T(8,128)(2,1)S(1)} %copy.37), channel_id=1, source_target_pairs={{0,2},{2,0},{4,6},{6,4},{8,10},{10,8},{12,14},{14,12},{16,18},{18,... | collective-permute-start | bytes 884744 | tf_op jit(solution)/shard_map/ppermute | solution.py:161
  131.0 15.0 %collective-permute-start.28 = (bf16[2,32,1152]{2,1,0:T(8,128)(2,1)S(1)}, bf16[2,32,1152]{2,1,0:T(8,128)(2,1)S(1)}, u32[]{:S(2)}, u32[]{:S(2)}) collective-permute-start(bf16[2,32,1152]{2,1,0:T(8,128)(2,1)S(1)} %fusion.12), channel_id=1, source_target_pairs={{0,4},{2,6},{4,0},{6,2},{8,12},{10,14},{12,8},{14,10},{16,20},{18,... | collective-permute-start | bytes 442376 | tf_op jit(solution)/shard_map/ppermute | solution.py:158
  141.7 12.2 %collective-permute-start.23 = (bf16[2,32,1152]{2,1,0:T(8,128)(2,1)S(1)}, bf16[2,32,1152]{2,1,0:T(8,128)(2,1)S(1)}, u32[]{:S(2)}, u32[]{:S(2)}) collective-permute-start(bf16[2,32,1152]{2,1,0:T(8,128)(2,1)S(1)} %fusion.10), channel_id=1, source_target_pairs={{0,4},{2,6},{4,0},{6,2},{8,12},{10,14},{12,8},{14,10},{16,20},{18,... | collective-permute-start | bytes 442376 | tf_op jit(solution)/shard_map/ppermute | solution.py:158
  (87 other events, 488.0 us)

commit v3 on v2

--- a/solution.py
+++ b/solution.py
@@ -26,8 +26,8 @@
     count = len(segments)
     blocks = refs[:count]
     (w_in, w_down, gamma, beta, alpha, expert) = refs[count : count + 6]
-    (grads_out, act_out, scaled_out, tail_out) = refs[count + 6 : count + 10]
-    (normed, cot, weight) = refs[count + 10 :]
+    (grads_out, kept_out, tail_out) = refs[count + 6 : count + 9]
+    (normed, cot, weight, kept, sems) = refs[count + 9 :]
     rows = normed.shape[0]
     gain = alpha[0]
     mine = expert[0]
@@ -46,7 +46,10 @@
             own = jnp.sum(jnp.where(lane == mine, gates, 0.0), axis=1, keepdims=True)
             own = residual_scale * own
             weight[there, :] = jnp.broadcast_to(own, (size, LANES))
-            scaled_out[there, :] = (own * rows_cot.astype(f32)).astype(bf16)
+            kept[there, hidden:] = (own * rows_cot.astype(f32)).astype(bf16)
+    wide = slice(hidden, hidden + width)
+    save_cot = pltpu.make_async_copy(kept.at[:, wide], kept_out.at[:, wide], sems.at[0])
+    save_cot.start()
     pre = contract_width(normed[...], w_in[...])
     back = contract_width(cot[...], w_down[...])
     gate_pre = pre[:, :hidden]
@@ -54,7 +57,11 @@
     sigma = jax.nn.sigmoid(gate_pre)
     silu = gate_pre * sigma
     activation = (silu * up_value).astype(bf16)
-    act_out[...] = activation
+    kept[:, :hidden] = activation
+    save_act = pltpu.make_async_copy(
+        kept.at[:, :hidden], kept_out.at[:, :hidden], sems.at[1]
+    )
+    save_act.start()
     row_grad = residual_scale * jnp.sum(activation.astype(f32) * back, axis=1, keepdims=True)
     d_act = weight[:, 0:1] * back
     d_gate = d_act * up_value * sigma * (1.0 + gate_pre * (1.0 - sigma))
@@ -62,6 +69,8 @@
     grads_out[:, hidden:] = (d_act * gate_pre * sigma).astype(bf16)
     lane = lax.broadcasted_iota(jnp.int32, (rows, LANES), 1)
     tail_out[...] = jnp.where(lane == mine, row_grad, 0.0).astype(bf16)
+    save_cot.wait()
+    save_act.wait()
 
 
 def grad_kernel(segments, half, parts, *refs):
@@ -91,21 +100,16 @@
                 d_other[x, y, :, cols] = value[row : row + block]
 
     place(slice(half, half + LANES), tail[...])
-    step = 512
-    for at in range(0, half, step):
+    at = 0
+    for held in w_far:
+        step = held.shape[1]
         cols = slice(at, at + step)
         part = jnp.dot(
             near[...],
-            w_in[:, pl.ds(pl.multiple_of(start + at, step), step)],
+            w_in[:, pl.ds(pl.multiple_of(start + at, LANES), step)],
             preferred_element_type=f32,
         )
-        for index, held in enumerate(w_far):
-            deep = held.shape[0]
-            part = part + jnp.dot(
-                mirrored[:, index * deep : (index + 1) * deep],
-                held[:, cols],
-                preferred_element_type=f32,
-            )
+        part = part + jnp.dot(mirrored, held[...], preferred_element_type=f32)
         short = part.astype(bf16)
         place(cols, short)
         part = short.astype(f32)
@@ -113,21 +117,49 @@
         sums[1:2, cols] = jnp.sum(part * squash[:, cols], axis=0, keepdims=True)
         sums[2:3, cols] = jnp.sum(part * slope[:, cols], axis=0, keepdims=True)
         sums[3:8, cols] = jnp.zeros((5, step), f32)
-
-
-def down_kernel(count, *refs):
-    acts = refs[:count]
-    scaled = refs[count : 2 * count]
-    out = refs[2 * count]
-    left, right = refs[2 * count + 1 :]
-    half = acts[0].shape[0] // 2
+        at += step
+
+
+def pack_kernel(tokens, cotangent, ids, probs, out):
+    width = tokens.shape[1]
+    top, block = ids.shape
+    names = ids[...]
+    shares = probs[...].astype(f32)
+    label = lax.broadcasted_iota(jnp.int32, (LANES, block), 0)
+    table = jnp.zeros((LANES, block), f32)
+    for k in range(top):
+        table = table + jnp.where(label == names[k : k + 1, :], shares[k : k + 1, :], 0.0)
+    row = lax.broadcasted_iota(jnp.int32, (block, block), 0)
+    column = lax.broadcasted_iota(jnp.int32, (block, block), 1)
+    unit = jnp.where(row == column, 1.0, 0.0).astype(bf16)
+    out[:, 2 * width :] = contract_width(unit, table.astype(bf16)).astype(bf16)
+    out[:, :width] = tokens[...]
+    out[:, width : 2 * width] = cotangent[...]
+
+
+def down_kernel(count, hidden, *refs):
+    kept = refs[:count]
+    out, held, sems = refs[count:]
+    half = kept[0].shape[0] // 2
+    copies = []
+    for batch in range(2):
+        for k in range(count):
+            copy = pltpu.make_async_copy(
+                kept[k].at[batch * half : (batch + 1) * half, :],
+                held.at[batch, k * half : (k + 1) * half, :],
+                sems.at[batch, k],
+            )
+            copy.start()
+            copies.append(copy)
     total = None
     for batch in range(2):
-        for k in range(count):
-            left[k * half : (k + 1) * half, :] = acts[k][batch * half : (batch + 1) * half, :]
-            right[k * half : (k + 1) * half, :] = scaled[k][batch * half : (batch + 1) * half, :]
+        for copy in copies[batch * count : (batch + 1) * count]:
+            copy.wait()
         term = lax.dot_general(
-            left[...], right[...], (((0,), (0,)), ((), ())), preferred_element_type=f32
+            held[batch, :, :hidden],
+            held[batch, :, hidden:],
+            (((0,), (0,)), ((), ())),
+            preferred_element_type=f32,
         )
         term = term.astype(bf16).astype(f32)
         total = term if total is None else total + term
@@ -163,10 +195,18 @@
     def go_z(v):
         return lax.ppermute(v, "expert", [(e, (e + 4) % experts) for e in range(experts)])
 
+    def go_jump(v, by):
+        return lax.ppermute(v, "expert", [(e, e ^ by) for e in range(experts)])
+
     lanes = jnp.arange(LANES, dtype=jnp.int32)
     picks = expert_ids[0][:, :, None] == lanes[None, None, :]
-    gates = jnp.sum(jnp.where(picks, gate_probs[0].astype(f32)[:, :, None], 0.0), axis=1)
-    own = jnp.concatenate([tokens[0], cotangent[0], gates.astype(bf16)], axis=1)
+    own = pl.pallas_call(
+        pack_kernel,
+        out_shape=jax.ShapeDtypeStruct((block, 2 * width + LANES), bf16),
+        in_specs=[whole()] * 4,
+        out_specs=whole(),
+        name="pack",
+    )(tokens[0], cotangent[0], expert_ids[0].T, gate_probs[0].T)
 
     flat_in = w_in[0].reshape(2 * hidden, width)
     flat_down = w_down[0]
@@ -182,23 +222,24 @@
         for core in range(2)
         for y in range(2)
     )
-    params = pltpu.CompilerParams(vmem_limit_bytes=40 << 20)
+    params = pltpu.CompilerParams(vmem_limit_bytes=14 << 20)
 
     def first_half(arrays):
         return pl.pallas_call(
             functools.partial(rows_kernel, segments, width, hidden),
             out_shape=(
                 jax.ShapeDtypeStruct((rows, 2 * hidden), bf16),
-                jax.ShapeDtypeStruct((rows, hidden), bf16),
-                jax.ShapeDtypeStruct((rows, width), bf16),
+                jax.ShapeDtypeStruct((rows, hidden + width), bf16),
                 jax.ShapeDtypeStruct((rows, LANES), bf16),
             ),
             in_specs=[whole()] * 8 + [scalar(), scalar()],
-            out_specs=(whole(),) * 4,
+            out_specs=(whole(), pl.BlockSpec(memory_space=pl.ANY), whole()),
             scratch_shapes=[
                 pltpu.VMEM((rows, width), bf16),
                 pltpu.VMEM((rows, width), bf16),
                 pltpu.VMEM((rows, LANES), f32),
+                pltpu.VMEM((rows, hidden + width), bf16),
+                pltpu.SemaphoreType.DMA((2,)),
             ],
             compiler_params=params,
             name="rows",
@@ -222,91 +263,119 @@
             name="grads",
         )(*arrays, near, far, flat_in, *w_far, tail, alpha, side.reshape(1))
 
-    def settle(d_own, d_other):
-        got = go_core(d_other)
-        send = add16(d_own[:, 1], got[:, 1])
-        keep = d_own[:, 0].astype(f32) + got[:, 0].astype(f32)
-        return keep + go_y(send).astype(f32)
-
     fence = lax.optimization_barrier
     own = jnp.concatenate([own, go_x(own)], axis=0)
-    parts = planes - 1
-    deep = 2 * hidden // parts
-    w_parts = [w_send[k * deep : (k + 1) * deep] for k in range(parts)]
+    most = 3 * half // 8
+    w_parts = [w_send[:, k * most : min((k + 1) * most, half)] for k in range(3)]
     near, far, near_c, far_c, w_far = {0: own}, {}, {}, {}, []
+    state = {"near": near, "far": far, "near_c": near_c, "far_c": far_c, "w": w_far}
+    grads, kept, tails, other = {}, {}, {}, {}
+    state.update(grads=grads, other=other)
+    d_own, d_got, totals, sent, value = {}, {}, {}, {}, {}
+    state.update(d_own=d_own, d_got=d_got, totals=totals, sent=sent, value=value)
     near[0], w_parts = fence((near[0], w_parts))
-    first, other, acts, scaled, totals = {}, {}, {}, {}, []
+
+    def make_down(held):
+        return pl.pallas_call(
+            functools.partial(down_kernel, planes, hidden),
+            out_shape=jax.ShapeDtypeStruct((hidden, width), bf16),
+            in_specs=[pl.BlockSpec(memory_space=pl.ANY)] * planes,
+            out_specs=whole(),
+            scratch_shapes=[
+                pltpu.VMEM((2, planes * rows // 2, hidden + width), bf16),
+                pltpu.SemaphoreType.DMA((2, planes)),
+            ],
+            compiler_params=pltpu.CompilerParams(vmem_limit_bytes=20 << 20),
+            name="down",
+        )(*held)
+
+    def step():
+        new = fence(state)
+        for name, held in state.items():
+            if isinstance(held, dict):
+                held.update(new[name])
+            else:
+                held[:] = new[name]
 
     def rows_of(k):
         arrays = (near[k], far[k], near_c[k], far_c[k])
-        grads, acts[k], scaled[k], tail = first_half(arrays)
-        first[k] = (arrays, grads, tail)
-
-    for k in range(planes):
-        if k < parts:
-            near[k + 1] = go_z(near[k])
+        grads[k], kept[k], tails[k] = first_half(arrays)
+
+    def grads_of(k):
+        arrays = (near[k], far[k], near_c[k], far_c[k])
+        d_own[k], moved, totals[k] = second_half(arrays, grads[k], other[k], w_far, tails[k])
+        d_got[k] = go_core(moved)
+
+    def send_y(k):
+        sent[k] = go_y(add16(d_own[k][:, 1], d_got[k][:, 1]))
+
+    def total_of(k):
+        kept = d_own[k][:, 0].astype(f32) + d_got[k][:, 0].astype(f32)
+        return kept + sent[k].astype(f32)
+
+    def hop(k):
+        carried = total_of(k)
+        if k > 1:
+            carried = carried + value[k].astype(f32)
+        value[(k + 1) % planes] = go_z(carried.astype(bf16))
+
+    for k in range(3):
+        w_far.append(go_x(w_parts[k]))
+        near[k + 1] = go_z(near[k])
         far[k] = go_y(near[k])
-        if k < parts:
-            w_far.append(go_x(w_parts[k]))
         near_c[k] = go_core(near[k])
         if k:
             far_c[k - 1] = go_core(far[k - 1])
             rows_of(k - 1)
-        if k == parts:
-            for j in range(k - 1):
-                other[j] = go_x(first[j][1])
-        near, far, near_c, far_c, w_far, first, other = fence(
-            (near, far, near_c, far_c, w_far, first, other)
-        )
-    last = planes - 1
-    far_c[last] = go_core(far[last])
-    other[last - 1] = go_x(first[last - 1][1])
-    rows_of(last)
-    first, other = fence((first, other))
-    other[last] = go_x(first[last][1])
-
-    carry = None
-    order = list(range(planes))
-    for k in order[1:] + order[:1]:
-        arrays, grads, tail = first[k]
-        d_own, d_other, sums = second_half(arrays, grads, other[k], w_far, tail)
-        totals.append(sums)
-        value = settle(d_own, d_other)
-        if carry is not None:
-            value = value + go_z(carry).astype(f32)
-        carry = value.astype(bf16)
-    acts = [acts[k] for k in order]
-    scaled = [scaled[k] for k in order]
-    crossed = go_x(carry[1]).astype(f32)
-    left = jnp.where(side == 0, value[0, :, :half], crossed[:, :half])
-    right = jnp.where(side == 0, crossed[:, :half], value[0, :, :half])
+        if k == 2:
+            other[0] = go_x(grads[0])
+        step()
+    other[1] = go_x(grads[1])
+    far[3] = go_y(near[3])
+    near_c[3] = go_core(near[3])
+    far_c[2] = go_core(far[2])
+    rows_of(2)
+    grads_of(0)
+    step()
+    other[2] = go_x(grads[2])
+    far_c[3] = go_core(far[3])
+    rows_of(3)
+    grads_of(1)
+    step()
+    other[3] = go_x(grads[3])
+    send_y(1)
+    grads_of(2)
+    send_y(0)
+    step()
+    send_y(2)
+    hop(1)
+    grads_of(3)
+    step()
+    pool = [sum(totals[k] for k in range(1, planes)) + totals[0]]
+    state["pool"] = pool
+    send_y(3)
+    hop(2)
+    pool[0] = pool[0] + go_core(pool[0])
+    step()
+    hop(3)
+    pool[0] = pool[0] + go_y(pool[0])
+    grad_down = make_down([kept[k] for k in range(planes)])
+    state["down"] = [grad_down]
+    step()
+    grad_down = state["down"][0]
+    pool[0] = pool[0] + go_jump(pool[0], 4)
+    sums = pool[0]
+    final = total_of(0) + value[0].astype(f32)
+    crossed = go_x(final[1].astype(bf16)).astype(f32)
+    left = jnp.where(side == 0, final[0, :, :half], crossed[:, :half])
+    right = jnp.where(side == 0, crossed[:, :half], final[0, :, :half])
     grad_normed = jnp.concatenate([left, right], axis=1)
-    row_grads = value[0, :, half:] + crossed[:, half:]
-
-    sums = sum(totals[1:], totals[0])
-    for go in (go_core, go_y):
-        sums = sums + go(sums)
-    hop = 4
-    while hop < experts:
-        sums = sums + lax.ppermute(sums, "expert", [(e, e ^ hop) for e in range(experts)])
-        hop *= 2
+    row_grads = final[0, :, half:] + crossed[:, half:]
+    sums = sums + go_jump(sums, 8)
     crossed = go_x(sums)
     sums = jnp.concatenate(
         [jnp.where(side == 0, sums, crossed), jnp.where(side == 0, crossed, sums)], axis=1
     )
-
-    grad_down = pl.pallas_call(
-        functools.partial(down_kernel, planes),
-        out_shape=jax.ShapeDtypeStruct((hidden, width), bf16),
-        in_specs=[whole()] * (2 * planes),
-        out_specs=whole(),
-        scratch_shapes=[
-            pltpu.VMEM((planes * rows // 2, hidden), bf16),
-            pltpu.VMEM((planes * rows // 2, width), bf16),
-        ],
-        compiler_params=pltpu.CompilerParams(vmem_limit_bytes=40 << 20),
-        name="down",
-    )(*acts, *scaled)
 
     inputs = tokens[0].astype(f32)
     squashed = jnp.tanh(alpha[0] * inputs)
@@ -414,11 +483,9 @@
     top_count = arrays[2].shape[2]
     dense = (
         lax.axis_size("dp") == 2
-        and experts % 4 == 0
-        and (experts & (experts - 1)) == 0
-        and experts <= LANES
+        and experts == 16
         and 2 * top_count >= experts
-        and 2 * arrays[8].shape[1] % (16 * (experts // 4 - 1)) == 0
+        and arrays[0].shape[2] % 2048 == 0
     )
     return (dense_shards if dense else routed_shards)(*arrays)
 

time: 167 us -> 154 us (0.922)
  local copies, waits for them, and re-layouts: 26.9 us -> 10.2 us
  waiting for transfers between devices: 66 us -> 76.4 us
  starting transfers between devices: 35.9 us -> 29.5 us
  Pallas kernels: 27.5 us -> 31.9 us
  other arithmetic: 8.06 us -> 3.67 us
    ppermute x9, waiting for transfers between devices: 3.67 us -> 22.2 us  [go_y(): return lax.ppermute(v, 'expert', [(e, e ^ 2) for e in range(experts)])]
    ppermute x10, waiting for transfers between devices: 48.5 us -> 31.5 us  [go_x(): return lax.ppermute(v, 'dp', [(0, 1), (1, 0)])]
    unnamed x143 -> x35, local copies, waits for them, and re-layouts: 23.3 us -> 6.68 us
    ppermute x2, waiting for transfers between devices: 3.33 us -> 8.67 us  [go_jump(): return lax.ppermute(v, 'expert', [(e, e ^ by) for e in range(experts)])]
    ppermute x10, starting transfers between devices: 14.6 us -> 11.1 us  [go_x(): return lax.ppermute(v, 'dp', [(0, 1), (1, 0)])]
    pallas_call x1 -> x2, Pallas kernels: 3.05 us -> 6.43 us  [the longest x1 4.55 us: make_down(): pl.pallas_call(functools.partial(down_kernel, planes, hidden), out_shape=...]
    pallas_call x4, Pallas kernels: 12.7 us -> 14.9 us  [first_half(): pl.pallas_call(functools.partial(rows_kernel, segments, width, hidden), o...]
    ppermute x6, waiting for transfers between devices: 10.1 us -> 12.1 us  [go_z(): lax.ppermute(v, 'expert', [(e, (e + 4) % experts) for e in range(experts)])]
  transfers between devices with their start and end apart: 40 -> 40, of which waited for: 16 -> 21; matrix products, arithmetic and copies ran while one was open for 4% -> 3% of each run, Pallas kernels for 17% -> 20%
where the time goes in v3:
time: 154 us; the launch traced here: 153 us
  waiting for transfers between devices  76.4 us (50%)
  Pallas kernels  31.9 us (21%)
  starting transfers between devices  29.5 us (19%)
  local copies, waits for them, and re-layouts  10.2 us (7%)
  other arithmetic  3.67 us (2%)
  between operations  1.69 us (1%)
    ppermute x10, waiting for transfers between devices, go_x(): return lax.ppermute(v, 'dp', [(0, 1), (1, 0)])  31.5 us
    ppermute x9, waiting for transfers between devices, go_y(): return lax.ppermute(v, 'expert', [(e, e ^ 2) for e in range(experts)])  22.2 us
    pallas_call x4, Pallas kernels, first_half(): pl.pallas_call(functools.partial(rows_kernel, segments, width, hidden), o...  14.9 us
    ppermute x6, waiting for transfers between devices, go_z(): lax.ppermute(v, 'expert', [(e, (e + 4) % experts) for e in range(experts)])  12.1 us
    ppermute x10, starting transfers between devices, go_x(): return lax.ppermute(v, 'dp', [(0, 1), (1, 0)])  11.1 us
    pallas_call x4, Pallas kernels, second_half(): pl.pallas_call(functools.partial(grad_kernel, segments, half, len(w_far))...  10.6 us
    ppermute x9, starting transfers between devices, go_y(): return lax.ppermute(v, 'expert', [(e, e ^ 2) for e in range(experts)])  10.1 us
    ppermute x2, waiting for transfers between devices, go_jump(): return lax.ppermute(v, 'expert', [(e, e ^ by) for e in range(experts)])  8.67 us
  transfers between devices with their start and end apart: 40, of which 21 were waited for; matrix products, arithmetic and copies ran while one was open for 3% of the time, Pallas kernels for 20%

profile of v3, /device:TPU:0, one launch (start us, length us, event | category | flops | bytes accessed | tf_op | source)
XLA Modules:
  0.0 153.4 jit_solution(6444134611822737938)
XLA Ops:
  2.5 2.9 %collective-permute-start = (bf16[32,4224]{1,0:T(8,128)(2,1)}, bf16[32,4224]{1,0:T(8,128)(2,1)}, u32[]{:S(2)}, u32[]{:S(2)}) collective-permute-start(bf16[32,4224]{1,0:T(8,128)(2,1)} %pack.1), channel_id=1, source_target_pairs={{0,1},{1,0},{2,3},{3,2},{4,5},{5,4},{6,7},{7,6},{8,9},{9,8},{10,11... | collective-permute-start | bytes 811016 | tf_op jit(solution)/shard_map/ppermute | solution.py:187
  8.9 3.3 %collective-permute-done = bf16[32,4224]{1,0:T(8,128)(2,1)} collective-permute-done((bf16[32,4224]{1,0:T(8,128)(2,1)}, bf16[32,4224]{1,0:T(8,128)(2,1)}, u32[]{:S(2)}, u32[]{:S(2)}) %collective-permute-start) | collective-permute-done | bytes 270368 | tf_op jit(solution)/shard_map/ppermute | solution.py:187
  19.5 8.5 %collective-permute-done.1.refs_1_ = bf16[64,4224]{1,0:T(8,128)(2,1)} collective-permute-done((bf16[64,4224]{1,0:T(8,128)(2,1)S(1)}, bf16[64,4224]{1,0:T(8,128)(2,1)}, u32[]{:S(2)}, u32[]{:S(2)}) %collective-permute-start.1) | collective-permute-done | bytes 540704 | tf_op jit(solution)/shard_map/ppermute | solution.py:190
  28.0 3.1 %collective-permute-done.2.refs_0_ = bf16[64,4224]{1,0:T(8,128)(2,1)} collective-permute-done((bf16[64,4224]{1,0:T(8,128)(2,1)S(1)}, bf16[64,4224]{1,0:T(8,128)(2,1)}, u32[]{:S(2)}, u32[]{:S(2)}) %collective-permute-start.2) | collective-permute-done | bytes 540704 | tf_op jit(solution)/shard_map/ppermute | solution.py:196
  38.6 4.1 %rows.4 = (bf16[256,768]{1,0:T(8,128)(2,1)S(1)}, bf16[256,2432]{1,0:T(8,128)(2,1)S(1)}, bf16[256,128]{1,0:T(8,128)(2,1)S(1)}) custom-call(bf16[64,4224]{1,0:T(8,128)(2,1)S(1)} %copy-done.6, bf16[64,4224]{1,0:T(8,128)(2,1)} %collective-permute-done.1.refs_1_, bf16[64,4224]{1,0:T(8,128)(2,1)S(1)} %copy-done.9, ...), custom_call_target="tpu_custom_call" | custom-call | tf_op jit(solution)/shard_map/rows/pallas_call | solution.py:228
  42.7 5.1 %collective-permute-done.5.refs_1_ = bf16[64,4224]{1,0:T(8,128)(2,1)} collective-permute-done((bf16[64,4224]{1,0:T(8,128)(2,1)}, bf16[64,4224]{1,0:T(8,128)(2,1)}, u32[]{:S(2)}, u32[]{:S(2)}) %collective-permute-start.5) | collective-permute-done | bytes 540704 | tf_op jit(solution)/shard_map/ppermute | solution.py:190
  53.7 4.3 %rows.5 = (bf16[256,768]{1,0:T(8,128)(2,1)S(1)}, bf16[256,2432]{1,0:T(8,128)(2,1)S(1)}, bf16[256,128]{1,0:T(8,128)(2,1)S(1)}) custom-call(bf16[64,4224]{1,0:T(8,128)(2,1)} %collective-permute-done.2.refs_0_, bf16[64,4224]{1,0:T(8,128)(2,1)} %collective-permute-done.5.refs_1_, bf16[64,4224]{1,0:T(8,128)(2,1)} %collective-permute-done.8.refs_2_, ...), custom_call_target="tpu_custom_call" | custom-call | tf_op jit(solution)/shard_map/rows/pallas_call | solution.py:228
  58.0 5.6 %collective-permute-done.15.refs_9_ = bf16[768,256]{1,0:T(8,128)(2,1)S(1)} collective-permute-done((bf16[768,256]{1,0:T(8,128)(2,1)S(1)}, bf16[768,256]{1,0:T(8,128)(2,1)S(1)}, u32[]{:S(2)}, u32[]{:S(2)}) %collective-permute-start.15) | collective-permute-done | bytes 393248 | tf_op jit(solution)/shard_map/ppermute | solution.py:187
  63.6 7.9 %collective-permute-done.14.refs_5_ = bf16[256,768]{1,0:T(8,128)(2,1)S(1)} collective-permute-done((bf16[256,768]{1,0:T(8,128)(2,1)S(1)}, bf16[256,768]{1,0:T(8,128)(2,1)S(1)}, u32[]{:S(2)}, u32[]{:S(2)}) %collective-permute-start.14) | collective-permute-done | bytes 393248 | tf_op jit(solution)/shard_map/ppermute | solution.py:187
  72.8 2.7 %grads.4 = (bf16[2,2,32,1152]{3,2,1,0:T(8,128)(2,1)S(1)}, bf16[2,2,32,1152]{3,2,1,0:T(8,128)(2,1)S(1)}, f32[8,1024]{1,0:T(8,128)S(1)}) custom-call(bf16[64,4224]{1,0:T(8,128)(2,1)S(1)} %copy-done.7, bf16[64,4224]{1,0:T(8,128)(2,1)} %collective-permute-done.1.refs_1_, bf16[64,4224]{1,0:T(8,128)(2,1)S(1)} %copy-done.10, ...), custom_call_target="tpu_custom_call" | custom-call | tf_op jit(solution)/shard_map/grads/pallas_call | solution.py:249
  75.7 3.8 %rows.6 = (bf16[256,768]{1,0:T(8,128)(2,1)S(1)}, bf16[256,2432]{1,0:T(8,128)(2,1)S(1)}, bf16[256,128]{1,0:T(8,128)(2,1)S(1)}) custom-call(bf16[64,4224]{1,0:T(8,128)(2,1)} %collective-permute-done.7.refs_0_, bf16[64,4224]{1,0:T(8,128)(2,1)S(1)} %collective-permute-done.10.refs_1_, bf16[64,4224]{1,0:T(8,128)(2,1)S(1)} %collective-permute-done.13.refs_2_, ...), custom_call_target="tpu_custom_call" | custom-call | tf_op jit(solution)/shard_map/rows/pallas_call | solution.py:228
  79.6 4.1 %collective-permute-done.20.refs_5_ = bf16[256,768]{1,0:T(8,128)(2,1)S(1)} collective-permute-done((bf16[256,768]{1,0:T(8,128)(2,1)S(1)}, bf16[256,768]{1,0:T(8,128)(2,1)S(1)}, u32[]{:S(2)}, u32[]{:S(2)}) %collective-permute-start.20) | collective-permute-done | bytes 393248 | tf_op jit(solution)/shard_map/ppermute | solution.py:187
  83.6 2.6 %collective-permute-done.17.refs_1_ = bf16[64,4224]{1,0:T(8,128)(2,1)S(1)} collective-permute-done((bf16[64,4224]{1,0:T(8,128)(2,1)S(1)}, bf16[64,4224]{1,0:T(8,128)(2,1)S(1)}, u32[]{:S(2)}, u32[]{:S(2)}) %collective-permute-start.17) | collective-permute-done | bytes 540704 | tf_op jit(solution)/shard_map/ppermute | solution.py:190
  86.8 2.9 %grads.5 = (bf16[2,2,32,1152]{3,2,1,0:T(8,128)(2,1)S(1)}, bf16[2,2,32,1152]{3,2,1,0:T(8,128)(2,1)S(1)}, f32[8,1024]{1,0:T(8,128)S(1)}) custom-call(bf16[64,4224]{1,0:T(8,128)(2,1)} %collective-permute-done.2.refs_0_, bf16[64,4224]{1,0:T(8,128)(2,1)} %collective-permute-done.5.refs_1_, bf16[64,4224]{1,0:T(8,128)(2,1)} %collective-permute-done.8.refs_2_, ...), custom_call_target="tpu_custom_call" | custom-call | tf_op jit(solution)/shard_map/grads/pallas_call | solution.py:249
  90.0 2.8 %rows.7 = (bf16[256,768]{1,0:T(8,128)(2,1)S(1)}, bf16[256,2432]{1,0:T(8,128)(2,1)S(1)}, bf16[256,128]{1,0:T(8,128)(2,1)S(1)}) custom-call(bf16[64,4224]{1,0:T(8,128)(2,1)S(1)} %collective-permute-done.12.refs_0_, bf16[64,4224]{1,0:T(8,128)(2,1)S(1)} %collective-permute-done.17.refs_1_, bf16[64,4224]{1,0:T(8,128)(2,1)S(1)} %collective-permute-done.19.refs_2_, ...), custom_call_target="tpu_custom_call" | custom-call | tf_op jit(solution)/shard_map/rows/pallas_call | solution.py:228
  92.8 5.0 %collective-permute-done.23.refs_5_ = bf16[256,768]{1,0:T(8,128)(2,1)S(1)} collective-permute-done((bf16[256,768]{1,0:T(8,128)(2,1)S(1)}, bf16[256,768]{1,0:T(8,128)(2,1)S(1)}, u32[]{:S(2)}, u32[]{:S(2)}) %collective-permute-start.23) | collective-permute-done | bytes 393248 | tf_op jit(solution)/shard_map/ppermute | solution.py:187
  103.4 4.3 %collective-permute-done.26 = bf16[2,32,1152]{2,1,0:T(8,128)(2,1)S(1)} collective-permute-done((bf16[2,32,1152]{2,1,0:T(8,128)(2,1)S(1)}, bf16[2,32,1152]{2,1,0:T(8,128)(2,1)S(1)}, u32[]{:S(2)}, u32[]{:S(2)}) %collective-permute-start.26) | collective-permute-done | bytes 147488 | tf_op jit(solution)/shard_map/ppermute | solution.py:190
  107.7 4.9 %collective-permute-done.25.refs_5_ = bf16[256,768]{1,0:T(8,128)(2,1)S(1)} collective-permute-done((bf16[256,768]{1,0:T(8,128)(2,1)S(1)}, bf16[256,768]{1,0:T(8,128)(2,1)S(1)}, u32[]{:S(2)}, u32[]{:S(2)}) %collective-permute-start.25) | collective-permute-done | bytes 393248 | tf_op jit(solution)/shard_map/ppermute | solution.py:187
  117.1 3.4 %collective-permute-done.30 = bf16[2,32,1152]{2,1,0:T(8,128)(2,1)S(1)} collective-permute-done((bf16[2,32,1152]{2,1,0:T(8,128)(2,1)S(1)}, bf16[2,32,1152]{2,1,0:T(8,128)(2,1)S(1)}, u32[]{:S(2)}, u32[]{:S(2)}) %collective-permute-start.30) | collective-permute-done | bytes 147488 | tf_op jit(solution)/shard_map/ppermute | solution.py:196
  125.9 3.6 %collective-permute-done.33 = bf16[2,32,1152]{2,1,0:T(8,128)(2,1)S(1)} collective-permute-done((bf16[2,32,1152]{2,1,0:T(8,128)(2,1)S(1)}, bf16[2,32,1152]{2,1,0:T(8,128)(2,1)S(1)}, u32[]{:S(2)}, u32[]{:S(2)}) %collective-permute-start.33) | collective-permute-done | bytes 147488 | tf_op jit(solution)/shard_map/ppermute | solution.py:196
  129.6 2.7 %collective-permute-start.35 = (bf16[2,32,1152]{2,1,0:T(8,128)(2,1)S(1)}, bf16[2,32,1152]{2,1,0:T(8,128)(2,1)S(1)}, u32[]{:S(2)}, u32[]{:S(2)}) collective-permute-start(bf16[2,32,1152]{2,1,0:T(8,128)(2,1)S(1)} %fusion.2), channel_id=1, source_target_pairs={{0,8},{2,10},{4,12},{6,14},{8,16},{10,18},{12,20},{14,22},{16,24},... | collective-permute-start | bytes 442376 | tf_op jit(solution)/shard_map/ppermute | solution.py:196
  133.8 4.6 %down.1 = bf16[384,2048]{1,0:T(8,128)(2,1)} custom-call(bf16[256,2432]{1,0:T(8,128)(2,1)S(1)} %get-tuple-element.290.refs_0_, bf16[256,2432]{1,0:T(8,128)(2,1)S(1)} %get-tuple-element.291.refs_1_, bf16[256,2432]{1,0:T(8,128)(2,1)S(1)} %get-tuple-element.292.refs_2_, bf16[256,2432]{1,0:T(8,128)(2,1)S(1)} %get-tuple-element.293.refs_3_), custom_call_target="tpu_custom_call" | custom-call | tf_op jit(solution)/shard_map/down/pallas_call | solution.py:279
  139.4 4.0 %collective-permute-done.37 = f32[8,1024]{1,0:T(8,128)S(1)} collective-permute-done((f32[8,1024]{1,0:T(8,128)S(1)}, f32[8,1024]{1,0:T(8,128)S(1)}, u32[]{:S(2)}, u32[]{:S(2)}) %collective-permute-start.37) | collective-permute-done | bytes 32800 | tf_op jit(solution)/shard_map/ppermute | solution.py:199
  143.5 4.7 %collective-permute-done.38 = f32[8,1024]{1,0:T(8,128)S(1)} collective-permute-done((f32[8,1024]{1,0:T(8,128)S(1)}, f32[8,1024]{1,0:T(8,128)S(1)}, u32[]{:S(2)}, u32[]{:S(2)}) %collective-permute-start.38) | collective-permute-done | bytes 32800 | tf_op jit(solution)/shard_map/ppermute | solution.py:199
  (130 shorter events, 50.8 us)
Async XLA Ops:
  2.5 9.7 %collective-permute-start = (bf16[32,4224]{1,0:T(8,128)(2,1)}, bf16[32,4224]{1,0:T(8,128)(2,1)}, u32[]{:S(2)}, u32[]{:S(2)}) collective-permute-start(bf16[32,4224]{1,0:T(8,128)(2,1)} %pack.1), channel_id=1, source_target_pairs={{0,1},{1,0},{2,3},{3,2},{4,5},{5,4},{6,7},{7,6},{8,9},{9,8},{10,11... | collective-permute-start | bytes 811016 | tf_op jit(solution)/shard_map/ppermute | solution.py:187
  13.2 18.7 %collective-permute-start.4 = (bf16[768,384]{1,0:T(8,128)(2,1)S(1)}, bf16[768,384]{1,0:T(8,128)(2,1)S(1)}, u32[]{:S(2)}, u32[]{:S(2)}) collective-permute-start(bf16[768,384]{1,0:T(8,128)(2,1)S(1)} %get-tuple-element.156), channel_id=1, source_target_pairs={{0,1},{1,0},{2,3},{3,2},{4,5},{5,4},{6,7},{7,6},{8,9},{9,8},{10,11... | collective-permute-start | bytes 1769480 | tf_op jit(solution)/shard_map/ppermute | solution.py:187
  15.0 13.0 %collective-permute-start.1 = (bf16[64,4224]{1,0:T(8,128)(2,1)S(1)}, bf16[64,4224]{1,0:T(8,128)(2,1)}, u32[]{:S(2)}, u32[]{:S(2)}) collective-permute-start(bf16[64,4224]{1,0:T(8,128)(2,1)S(1)} %pad_maximum_fusion.refs_0_), channel_id=1, source_target_pairs={{0,4},{2,6},{4,0},{6,2},{8,12},{10,14},{12,8},{14,10},{16,20},{18,... | collective-permute-start | bytes 1622024 | tf_op jit(solution)/shard_map/ppermute | solution.py:190
  16.6 14.5 %collective-permute-start.2 = (bf16[64,4224]{1,0:T(8,128)(2,1)S(1)}, bf16[64,4224]{1,0:T(8,128)(2,1)}, u32[]{:S(2)}, u32[]{:S(2)}) collective-permute-start(bf16[64,4224]{1,0:T(8,128)(2,1)S(1)} %pad_maximum_fusion.refs_0_), channel_id=1, source_target_pairs={{0,8},{2,10},{4,12},{6,14},{8,16},{10,18},{12,20},{14,22},{16,24},... | collective-permute-start | bytes 1622024 | tf_op jit(solution)/shard_map/ppermute | solution.py:196
  18.1 13.0 %collective-permute-start.3 = (bf16[64,4224]{1,0:T(8,128)(2,1)S(1)}, bf16[64,4224]{1,0:T(8,128)(2,1)S(1)}, u32[]{:S(2)}, u32[]{:S(2)}) collective-permute-start(bf16[64,4224]{1,0:T(8,128)(2,1)S(1)} %pad_maximum_fusion.refs_0_), channel_id=1, source_target_pairs={{0,2},{2,0},{4,6},{6,4},{8,10},{10,8},{12,14},{14,12},{16,18},{18,... | collective-permute-start | bytes 1622024 | tf_op jit(solution)/shard_map/ppermute | solution.py:193
  18.9 23.7 %collective-permute-start.9 = (bf16[768,384]{1,0:T(8,128)(2,1)}, bf16[768,384]{1,0:T(8,128)(2,1)}, u32[]{:S(2)}, u32[]{:S(2)}) collective-permute-start(bf16[768,384]{1,0:T(8,128)(2,1)} %get-tuple-element.163), channel_id=1, source_target_pairs={{0,1},{1,0},{2,3},{3,2},{4,5},{5,4},{6,7},{7,6},{8,9},{9,8},{10,11... | collective-permute-start | bytes 1769480 | tf_op jit(solution)/shard_map/ppermute | solution.py:187
  32.8 15.0 %collective-permute-start.5 = (bf16[64,4224]{1,0:T(8,128)(2,1)}, bf16[64,4224]{1,0:T(8,128)(2,1)}, u32[]{:S(2)}, u32[]{:S(2)}) collective-permute-start(bf16[64,4224]{1,0:T(8,128)(2,1)} %collective-permute-done.2.refs_0_), channel_id=1, source_target_pairs={{0,4},{2,6},{4,0},{6,2},{8,12},{10,14},{12,8},{14,10},{16,20},{18,... | collective-permute-start | bytes 1622024 | tf_op jit(solution)/shard_map/ppermute | solution.py:190
  33.3 16.5 %collective-permute-start.7 = (bf16[64,4224]{1,0:T(8,128)(2,1)}, bf16[64,4224]{1,0:T(8,128)(2,1)}, u32[]{:S(2)}, u32[]{:S(2)}) collective-permute-start(bf16[64,4224]{1,0:T(8,128)(2,1)} %collective-permute-done.2.refs_0_), channel_id=1, source_target_pairs={{0,8},{2,10},{4,12},{6,14},{8,16},{10,18},{12,20},{14,22},{16,24},... | collective-permute-start | bytes 1622024 | tf_op jit(solution)/shard_map/ppermute | solution.py:196
  33.7 16.1 %collective-permute-start.8 = (bf16[64,4224]{1,0:T(8,128)(2,1)}, bf16[64,4224]{1,0:T(8,128)(2,1)}, u32[]{:S(2)}, u32[]{:S(2)}) collective-permute-start(bf16[64,4224]{1,0:T(8,128)(2,1)} %collective-permute-done.2.refs_0_), channel_id=1, source_target_pairs={{0,2},{2,0},{4,6},{6,4},{8,10},{10,8},{12,14},{14,12},{16,18},{18,... | collective-permute-start | bytes 1622024 | tf_op jit(solution)/shard_map/ppermute | solution.py:193
  49.9 21.5 %collective-permute-start.10 = (bf16[64,4224]{1,0:T(8,128)(2,1)}, bf16[64,4224]{1,0:T(8,128)(2,1)S(1)}, u32[]{:S(2)}, u32[]{:S(2)}) collective-permute-start(bf16[64,4224]{1,0:T(8,128)(2,1)} %collective-permute-done.7.refs_0_), channel_id=1, source_target_pairs={{0,4},{2,6},{4,0},{6,2},{8,12},{10,14},{12,8},{14,10},{16,20},{18,... | collective-permute-start | bytes 1622024 | tf_op jit(solution)/shard_map/ppermute | solution.py:190
  51.5 20.0 %collective-permute-start.12 = (bf16[64,4224]{1,0:T(8,128)(2,1)}, bf16[64,4224]{1,0:T(8,128)(2,1)S(1)}, u32[]{:S(2)}, u32[]{:S(2)}) collective-permute-start(bf16[64,4224]{1,0:T(8,128)(2,1)} %collective-permute-done.7.refs_0_), channel_id=1, source_target_pairs={{0,8},{2,10},{4,12},{6,14},{8,16},{10,18},{12,20},{14,22},{16,24},... | collective-permute-start | bytes 1622024 | tf_op jit(solution)/shard_map/ppermute | solution.py:196
  51.5 20.0 %collective-permute-start.13 = (bf16[64,4224]{1,0:T(8,128)(2,1)}, bf16[64,4224]{1,0:T(8,128)(2,1)S(1)}, u32[]{:S(2)}, u32[]{:S(2)}) collective-permute-start(bf16[64,4224]{1,0:T(8,128)(2,1)} %collective-permute-done.7.refs_0_), channel_id=1, source_target_pairs={{0,2},{2,0},{4,6},{6,4},{8,10},{10,8},{12,14},{14,12},{16,18},{18,... | collective-permute-start | bytes 1622024 | tf_op jit(solution)/shard_map/ppermute | solution.py:193
  51.7 11.9 %collective-permute-start.15 = (bf16[768,256]{1,0:T(8,128)(2,1)S(1)}, bf16[768,256]{1,0:T(8,128)(2,1)S(1)}, u32[]{:S(2)}, u32[]{:S(2)}) collective-permute-start(bf16[768,256]{1,0:T(8,128)(2,1)S(1)} %constant_dynamic-slice_fusion.2), channel_id=1, source_target_pairs={{0,1},{1,0},{2,3},{3,2},{4,5},{5,4},{6,7},{7,6},{8,9},{9,8},{10,11... | collective-permute-start | bytes 1179656 | tf_op jit(solution)/shard_map/ppermute | solution.py:187
  52.2 19.3 %collective-permute-start.14 = (bf16[256,768]{1,0:T(8,128)(2,1)S(1)}, bf16[256,768]{1,0:T(8,128)(2,1)S(1)}, u32[]{:S(2)}, u32[]{:S(2)}) collective-permute-start(bf16[256,768]{1,0:T(8,128)(2,1)S(1)} %get-tuple-element.181.refs_4_), channel_id=1, source_target_pairs={{0,1},{1,0},{2,3},{3,2},{4,5},{5,4},{6,7},{7,6},{8,9},{9,8},{10,11... | collective-permute-start | bytes 1179656 | tf_op jit(solution)/shard_map/ppermute | solution.py:187
  71.5 14.7 %collective-permute-start.17 = (bf16[64,4224]{1,0:T(8,128)(2,1)S(1)}, bf16[64,4224]{1,0:T(8,128)(2,1)S(1)}, u32[]{:S(2)}, u32[]{:S(2)}) collective-permute-start(bf16[64,4224]{1,0:T(8,128)(2,1)S(1)} %collective-permute-done.12.refs_0_), channel_id=1, source_target_pairs={{0,4},{2,6},{4,0},{6,2},{8,12},{10,14},{12,8},{14,10},{16,20},{18,... | collective-permute-start | bytes 1622024 | tf_op jit(solution)/shard_map/ppermute | solution.py:190
  72.1 14.1 %collective-permute-start.19 = (bf16[64,4224]{1,0:T(8,128)(2,1)S(1)}, bf16[64,4224]{1,0:T(8,128)(2,1)S(1)}, u32[]{:S(2)}, u32[]{:S(2)}) collective-permute-start(bf16[64,4224]{1,0:T(8,128)(2,1)S(1)} %collective-permute-done.12.refs_0_), channel_id=1, source_target_pairs={{0,2},{2,0},{4,6},{6,4},{8,10},{10,8},{12,14},{14,12},{16,18},{18,... | collective-permute-start | bytes 1622024 | tf_op jit(solution)/shard_map/ppermute | solution.py:193
  72.3 11.4 %collective-permute-start.20 = (bf16[256,768]{1,0:T(8,128)(2,1)S(1)}, bf16[256,768]{1,0:T(8,128)(2,1)S(1)}, u32[]{:S(2)}, u32[]{:S(2)}) collective-permute-start(bf16[256,768]{1,0:T(8,128)(2,1)S(1)} %get-tuple-element.205.refs_4_), channel_id=1, source_target_pairs={{0,1},{1,0},{2,3},{3,2},{4,5},{5,4},{6,7},{7,6},{8,9},{9,8},{10,11... | collective-permute-start | bytes 1179656 | tf_op jit(solution)/shard_map/ppermute | solution.py:187
  86.2 11.5 %collective-permute-start.23 = (bf16[256,768]{1,0:T(8,128)(2,1)S(1)}, bf16[256,768]{1,0:T(8,128)(2,1)S(1)}, u32[]{:S(2)}, u32[]{:S(2)}) collective-permute-start(bf16[256,768]{1,0:T(8,128)(2,1)S(1)} %get-tuple-element.231.refs_4_), channel_id=1, source_target_pairs={{0,1},{1,0},{2,3},{3,2},{4,5},{5,4},{6,7},{7,6},{8,9},{9,8},{10,11... | collective-permute-start | bytes 1179656 | tf_op jit(solution)/shard_map/ppermute | solution.py:187
  101.0 6.7 %collective-permute-start.24 = (bf16[2,2,32,1152]{3,2,0,1:T(8,128)(2,1)S(1)}, bf16[2,2,32,1152]{3,2,0,1:T(8,128)(2,1)S(1)}, u32[]{:S(2)}, u32[]{:S(2)}) collective-permute-start(bf16[2,2,32,1152]{3,2,0,1:T(8,128)(2,1)S(1)} %copy.29), channel_id=1, source_target_pairs={{0,2},{2,0},{4,6},{6,4},{8,10},{10,8},{12,14},{14,12},{16,18},{18,... | collective-permute-start | bytes 884744 | tf_op jit(solution)/shard_map/ppermute | solution.py:193
  101.1 11.5 %collective-permute-start.25 = (bf16[256,768]{1,0:T(8,128)(2,1)S(1)}, bf16[256,768]{1,0:T(8,128)(2,1)S(1)}, u32[]{:S(2)}, u32[]{:S(2)}) collective-permute-start(bf16[256,768]{1,0:T(8,128)(2,1)S(1)} %get-tuple-element.256.refs_4_), channel_id=1, source_target_pairs={{0,1},{1,0},{2,3},{3,2},{4,5},{5,4},{6,7},{7,6},{8,9},{9,8},{10,11... | collective-permute-start | bytes 1179656 | tf_op jit(solution)/shard_map/ppermute | solution.py:187
  112.7 7.8 %collective-permute-start.30 = (bf16[2,32,1152]{2,1,0:T(8,128)(2,1)S(1)}, bf16[2,32,1152]{2,1,0:T(8,128)(2,1)S(1)}, u32[]{:S(2)}, u32[]{:S(2)}) collective-permute-start(bf16[2,32,1152]{2,1,0:T(8,128)(2,1)S(1)} %fusion.5), channel_id=1, source_target_pairs={{0,8},{2,10},{4,12},{6,14},{8,16},{10,18},{12,20},{14,22},{16,24},... | collective-permute-start | bytes 442376 | tf_op jit(solution)/shard_map/ppermute | solution.py:196
  122.1 7.4 %collective-permute-start.33 = (bf16[2,32,1152]{2,1,0:T(8,128)(2,1)S(1)}, bf16[2,32,1152]{2,1,0:T(8,128)(2,1)S(1)}, u32[]{:S(2)}, u32[]{:S(2)}) collective-permute-start(bf16[2,32,1152]{2,1,0:T(8,128)(2,1)S(1)} %fusion.4), channel_id=1, source_target_pairs={{0,8},{2,10},{4,12},{6,14},{8,16},{10,18},{12,20},{14,22},{16,24},... | collective-permute-start | bytes 442376 | tf_op jit(solution)/shard_map/ppermute | solution.py:196
  129.6 8.9 %collective-permute-start.35 = (bf16[2,32,1152]{2,1,0:T(8,128)(2,1)S(1)}, bf16[2,32,1152]{2,1,0:T(8,128)(2,1)S(1)}, u32[]{:S(2)}, u32[]{:S(2)}) collective-permute-start(bf16[2,32,1152]{2,1,0:T(8,128)(2,1)S(1)} %fusion.2), channel_id=1, source_target_pairs={{0,8},{2,10},{4,12},{6,14},{8,16},{10,18},{12,20},{14,22},{16,24},... | collective-permute-start | bytes 442376 | tf_op jit(solution)/shard_map/ppermute | solution.py:196
  138.5 11.2 %collective-permute-start.36 = (bf16[32,1152]{1,0:T(8,128)(2,1)S(1)}, bf16[32,1152]{1,0:T(8,128)(2,1)S(1)}, u32[]{:S(2)}, u32[]{:S(2)}) collective-permute-start(bf16[32,1152]{1,0:T(8,128)(2,1)S(1)} %fusion.14), channel_id=1, source_target_pairs={{0,1},{1,0},{2,3},{3,2},{4,5},{5,4},{6,7},{7,6},{8,9},{9,8},{10,11... | collective-permute-start | bytes 221192 | tf_op jit(solution)/shard_map/ppermute | solution.py:187
  (33 other events, 285.0 us)

commit v4 on v3

--- a/solution.py
+++ b/solution.py
@@ -73,11 +73,11 @@
     save_act.wait()
 
 
-def grad_kernel(segments, half, parts, *refs):
+def grad_kernel(segments, half, *refs):
     count = len(segments)
     blocks = refs[:count]
-    (near, far, w_in, *w_far) = refs[count : count + 3 + parts]
-    (tail, alpha, side, d_own, d_other, sums, squash, slope) = refs[count + 3 + parts :]
+    (near, far, w_in, w_far, tail, alpha, side) = refs[count : count + 7]
+    (d_own, d_other, sums, squash, slope) = refs[count + 7 :]
     rows = near.shape[0]
     block = rows // 8
     gain = alpha[0]
@@ -100,16 +100,15 @@
                 d_other[x, y, :, cols] = value[row : row + block]
 
     place(slice(half, half + LANES), tail[...])
-    at = 0
-    for held in w_far:
-        step = held.shape[1]
+    step = 512
+    for at in range(0, half, step):
         cols = slice(at, at + step)
         part = jnp.dot(
             near[...],
-            w_in[:, pl.ds(pl.multiple_of(start + at, LANES), step)],
+            w_in[:, pl.ds(pl.multiple_of(start + at, step), step)],
             preferred_element_type=f32,
         )
-        part = part + jnp.dot(mirrored, held[...], preferred_element_type=f32)
+        part = part + jnp.dot(mirrored, w_far[:, cols], preferred_element_type=f32)
         short = part.astype(bf16)
         place(cols, short)
         part = short.astype(f32)
@@ -117,7 +116,6 @@
         sums[1:2, cols] = jnp.sum(part * squash[:, cols], axis=0, keepdims=True)
         sums[2:3, cols] = jnp.sum(part * slope[:, cols], axis=0, keepdims=True)
         sums[3:8, cols] = jnp.zeros((5, step), f32)
-        at += step
 
 
 def pack_kernel(tokens, cotangent, ids, probs, out):
@@ -198,6 +196,12 @@
     def go_jump(v, by):
         return lax.ppermute(v, "expert", [(e, e ^ by) for e in range(experts)])
 
+    def go_far(v, by):
+        pairs = [
+            (2 * e + x, 2 * (e ^ by) + 1 - x) for e in range(experts) for x in range(2)
+        ]
+        return lax.ppermute(v, ("expert", "dp"), pairs)
+
     lanes = jnp.arange(LANES, dtype=jnp.int32)
     picks = expert_ids[0][:, :, None] == lanes[None, None, :]
     own = pl.pallas_call(
@@ -247,13 +251,13 @@
 
     def second_half(arrays, near, far, w_far, tail):
         return pl.pallas_call(
-            functools.partial(grad_kernel, segments, half, len(w_far)),
+            functools.partial(grad_kernel, segments, half),
             out_shape=(
                 jax.ShapeDtypeStruct((2, 2, block, half + LANES), bf16),
                 jax.ShapeDtypeStruct((2, 2, block, half + LANES), bf16),
                 jax.ShapeDtypeStruct((8, half), f32),
             ),
-            in_specs=[whole()] * (8 + len(w_far)) + [scalar(), scalar()],
+            in_specs=[whole()] * 9 + [scalar(), scalar()],
             out_specs=(whole(),) * 3,
             scratch_shapes=[
                 pltpu.VMEM((rows, half), f32),
@@ -261,19 +265,18 @@
             ],
             compiler_params=params,
             name="grads",
-        )(*arrays, near, far, flat_in, *w_far, tail, alpha, side.reshape(1))
+        )(*arrays, near, far, flat_in, w_far, tail, alpha, side.reshape(1))
 
     fence = lax.optimization_barrier
     own = jnp.concatenate([own, go_x(own)], axis=0)
-    most = 3 * half // 8
-    w_parts = [w_send[:, k * most : min((k + 1) * most, half)] for k in range(3)]
-    near, far, near_c, far_c, w_far = {0: own}, {}, {}, {}, []
+    near, far, near_c, far_c, w_far = {0: own}, {}, {}, {}, {}
     state = {"near": near, "far": far, "near_c": near_c, "far_c": far_c, "w": w_far}
     grads, kept, tails, other = {}, {}, {}, {}
     state.update(grads=grads, other=other)
     d_own, d_got, totals, sent, value = {}, {}, {}, {}, {}
     state.update(d_own=d_own, d_got=d_got, totals=totals, sent=sent, value=value)
-    near[0], w_parts = fence((near[0], w_parts))
+    near[0], w_send = fence((near[0], w_send))
+    w_far[0] = go_x(w_send)
 
     def make_down(held):
         return pl.pallas_call(
@@ -289,13 +292,14 @@
             name="down",
         )(*held)
 
-    def step():
-        new = fence(state)
+    def step(*late):
+        now = {
+            name: {k: v for k, v in held.items() if (name, k) not in late}
+            for name, held in state.items()
+        }
+        new = fence(now)
         for name, held in state.items():
-            if isinstance(held, dict):
-                held.update(new[name])
-            else:
-                held[:] = new[name]
+            held.update(new[name])
 
     def rows_of(k):
         arrays = (near[k], far[k], near_c[k], far_c[k])
@@ -303,7 +307,7 @@
 
     def grads_of(k):
         arrays = (near[k], far[k], near_c[k], far_c[k])
-        d_own[k], moved, totals[k] = second_half(arrays, grads[k], other[k], w_far, tails[k])
+        d_own[k], moved, totals[k] = second_half(arrays, grads[k], other[k], w_far[0], tails[k])
         d_got[k] = go_core(moved)
 
     def send_y(k):
@@ -320,7 +324,6 @@
         value[(k + 1) % planes] = go_z(carried.astype(bf16))
 
     for k in range(3):
-        w_far.append(go_x(w_parts[k]))
         near[k + 1] = go_z(near[k])
         far[k] = go_y(near[k])
         near_c[k] = go_core(near[k])
@@ -329,7 +332,7 @@
             rows_of(k - 1)
         if k == 2:
             other[0] = go_x(grads[0])
-        step()
+        step(*([("w", 0)] if k == 0 else []))
     other[1] = go_x(grads[1])
     far[3] = go_y(near[3])
     near_c[3] = go_core(near[3])
@@ -340,41 +343,43 @@
     other[2] = go_x(grads[2])
     far_c[3] = go_core(far[3])
     rows_of(3)
+    other[1], far_c[3] = fence((other[1], far_c[3]))
     grads_of(1)
-    step()
+    step(("other", 2))
     other[3] = go_x(grads[3])
     send_y(1)
+    send_y(0)
+    other[2], sent[1] = fence((other[2], sent[1]))
     grads_of(2)
-    send_y(0)
-    step()
+    hop(1)
     send_y(2)
-    hop(1)
+    step(("sent", 2), ("value", 2))
     grads_of(3)
-    step()
-    pool = [sum(totals[k] for k in range(1, planes)) + totals[0]]
+    hop(2)
+    pool = {}
+    pool[0] = sum(totals[k] for k in range(1, planes)) + totals[0]
+    pool[0] = pool[0] + go_core(pool[0])
     state["pool"] = pool
+    step(("value", 3), ("sent", 2), ("value", 2))
     send_y(3)
-    hop(2)
-    pool[0] = pool[0] + go_core(pool[0])
+    pool[0] = pool[0] + go_y(pool[0])
     step()
     hop(3)
-    pool[0] = pool[0] + go_y(pool[0])
-    grad_down = make_down([kept[k] for k in range(planes)])
-    state["down"] = [grad_down]
+    pool[0] = pool[0] + go_jump(pool[0], 4)
     step()
-    grad_down = state["down"][0]
-    pool[0] = pool[0] + go_jump(pool[0], 4)
-    sums = pool[0]
     final = total_of(0) + value[0].astype(f32)
     crossed = go_x(final[1].astype(bf16)).astype(f32)
     left = jnp.where(side == 0, final[0, :, :half], crossed[:, :half])
     right = jnp.where(side == 0, crossed[:, :half], final[0, :, :half])
     grad_normed = jnp.concatenate([left, right], axis=1)
     row_grads = final[0, :, half:] + crossed[:, half:]
-    sums = sums + go_jump(sums, 8)
-    crossed = go_x(sums)
+    grad_down = make_down([kept[k] for k in range(planes)])
+    part = pool[0]
+    mine_sums = part + go_jump(part, 8)
+    crossed = go_x(part) + go_far(part, 8)
     sums = jnp.concatenate(
-        [jnp.where(side == 0, sums, crossed), jnp.where(side == 0, crossed, sums)], axis=1
+        [jnp.where(side == 0, mine_sums, crossed), jnp.where(side == 0, crossed, mine_sums)],
+        axis=1,
     )
 
     inputs = tokens[0].astype(f32)

time: 154 us -> 143 us (0.929)
  waiting for transfers between devices: 76.4 us -> 55.8 us
  local copies, waits for them, and re-layouts: 10.2 us -> 16.9 us
  starting transfers between devices: 29.5 us -> 31.1 us
    ppermute x10 -> x8, waiting for transfers between devices: 31.5 us -> 18.8 us  [go_x(): return lax.ppermute(v, 'dp', [(0, 1), (1, 0)])]
    unnamed x35 -> x53, local copies, waits for them, and re-layouts: 6.68 us -> 13.9 us
    ppermute x2, waiting for transfers between devices: 8.67 us -> 1.98 us  [go_jump(): return lax.ppermute(v, 'expert', [(e, e ^ by) for e in range(experts)])]
    ppermute x6, waiting for transfers between devices: 12.1 us -> 8.61 us  [go_z(): lax.ppermute(v, 'expert', [(e, (e + 4) % experts) for e in range(experts)])]
    slice x2 -> x0, local copies, waits for them, and re-layouts: 3.41 us -> none  [dense_shards(): w_parts = [w_send[:, k * most:min((k + 1) * most, half)] for k in range(3)]]
    ppermute x6, starting transfers between devices: 6.87 us -> 3.52 us  [go_z(): lax.ppermute(v, 'expert', [(e, (e + 4) % experts) for e in range(experts)])]
    dynamic_slice x0 -> x1, local copies, waits for them, and re-layouts: none -> 2.82 us  [dense_shards(): w_send = lax.dynamic_slice_in_dim(flat_in, (1 - side) * half, half, axis=1)]
    ppermute x0 -> x1, starting transfers between devices: none -> 2.76 us  [go_far(): return lax.ppermute(v, ('expert', 'dp'), pairs)]
  transfers between devices with their start and end apart: 40 -> 39, of which waited for: 21 -> 22; matrix products, arithmetic and copies ran while one was open for 3% -> 3% of each run, Pallas kernels for 20% -> 20%
where the time goes in v4:
time: 143 us
  waiting for transfers between devices  55.8 us (39%)
  Pallas kernels  33 us (23%)
  starting transfers between devices  31.1 us (22%)
  local copies, waits for them, and re-layouts  16.9 us (12%)
  other arithmetic  4.33 us (3%)
  between operations  1.66 us (1%)
    ppermute x9, waiting for transfers between devices, go_y(): return lax.ppermute(v, 'expert', [(e, e ^ 2) for e in range(experts)])  21.4 us
    ppermute x8, waiting for transfers between devices, go_x(): return lax.ppermute(v, 'dp', [(0, 1), (1, 0)])  18.8 us
    pallas_call x4, Pallas kernels, first_half(): pl.pallas_call(functools.partial(rows_kernel, segments, width, hidden), o...  14.8 us
    unnamed x53, local copies, waits for them, and re-layouts  13.9 us
    ppermute x8, starting transfers between devices, go_x(): return lax.ppermute(v, 'dp', [(0, 1), (1, 0)])  12.9 us
    pallas_call x4, Pallas kernels, second_half(): pl.pallas_call(functools.partial(grad_kernel, segments, half), out_shape=...  11.8 us
    ppermute x9, starting transfers between devices, go_y(): return lax.ppermute(v, 'expert', [(e, e ^ 2) for e in range(experts)])  8.87 us
    ppermute x6, waiting for transfers between devices, go_z(): lax.ppermute(v, 'expert', [(e, (e + 4) % experts) for e in range(experts)])  8.61 us
  transfers between devices with their start and end apart: 39, of which 22 were waited for; matrix products, arithmetic and copies ran while one was open for 3% of the time, Pallas kernels for 20%

profile of v4, /device:TPU:0, one launch (start us, length us, event | category | flops | bytes accessed | tf_op | source)
XLA Modules:
  0.0 142.8 jit_solution(12963958997543633081)
XLA Ops:
  2.5 2.9 %collective-permute-start = (bf16[32,4224]{1,0:T(8,128)(2,1)}, bf16[32,4224]{1,0:T(8,128)(2,1)S(1)}, u32[]{:S(2)}, u32[]{:S(2)}) collective-permute-start(bf16[32,4224]{1,0:T(8,128)(2,1)} %pack.1), channel_id=1, source_target_pairs={{0,1},{1,0},{2,3},{3,2},{4,5},{5,4},{6,7},{7,6},{8,9},{9,8},{10,11... | collective-permute-start | bytes 811016 | tf_op jit(solution)/shard_map/ppermute | solution.py:185
  5.4 2.8 %constant_dynamic-slice_fusion = bf16[768,1024]{1,0:T(8,128)(2,1)} fusion(bf16[768,2048]{1,0:T(8,128)(2,1)} %bitcast.68, s32[]{:T(128)S(6)} %select_n.32), kind=kLoop, calls=%fused_computation.41 | loop fusion | bytes 3145732 | tf_op jit(solution)/shard_map/dynamic_slice | solution.py:222
  8.3 3.9 %collective-permute-done = bf16[32,4224]{1,0:T(8,128)(2,1)S(1)} collective-permute-done((bf16[32,4224]{1,0:T(8,128)(2,1)}, bf16[32,4224]{1,0:T(8,128)(2,1)S(1)}, u32[]{:S(2)}, u32[]{:S(2)}) %collective-permute-start) | collective-permute-done | bytes 270368 | tf_op jit(solution)/shard_map/ppermute | solution.py:185
  18.8 9.1 %collective-permute-done.1.refs_1_ = bf16[64,4224]{1,0:T(8,128)(2,1)} collective-permute-done((bf16[64,4224]{1,0:T(8,128)(2,1)S(1)}, bf16[64,4224]{1,0:T(8,128)(2,1)}, u32[]{:S(2)}, u32[]{:S(2)}) %collective-permute-start.1) | collective-permute-done | bytes 540704 | tf_op jit(solution)/shard_map/ppermute | solution.py:188
  27.9 3.1 %collective-permute-done.2.refs_0_ = bf16[64,4224]{1,0:T(8,128)(2,1)} collective-permute-done((bf16[64,4224]{1,0:T(8,128)(2,1)S(1)}, bf16[64,4224]{1,0:T(8,128)(2,1)}, u32[]{:S(2)}, u32[]{:S(2)}) %collective-permute-start.2) | collective-permute-done | bytes 540704 | tf_op jit(solution)/shard_map/ppermute | solution.py:194
  37.6 4.1 %rows.4 = (bf16[256,768]{1,0:T(8,128)(2,1)S(1)}, bf16[256,2432]{1,0:T(8,128)(2,1)S(1)}, bf16[256,128]{1,0:T(8,128)(2,1)S(1)}) custom-call(bf16[64,4224]{1,0:T(8,128)(2,1)S(1)} %copy-done.4, bf16[64,4224]{1,0:T(8,128)(2,1)} %collective-permute-done.1.refs_1_, bf16[64,4224]{1,0:T(8,128)(2,1)S(1)} %copy-done.7, ...), custom_call_target="tpu_custom_call" | custom-call | tf_op jit(solution)/shard_map/rows/pallas_call | solution.py:232
  42.8 4.1 %collective-permute-done.4.refs_1_ = bf16[64,4224]{1,0:T(8,128)(2,1)} collective-permute-done((bf16[64,4224]{1,0:T(8,128)(2,1)}, bf16[64,4224]{1,0:T(8,128)(2,1)}, u32[]{:S(2)}, u32[]{:S(2)}) %collective-permute-start.4) | collective-permute-done | bytes 540704 | tf_op jit(solution)/shard_map/ppermute | solution.py:188
  46.8 2.0 %collective-permute-done.6.refs_0_ = bf16[64,4224]{1,0:T(8,128)(2,1)} collective-permute-done((bf16[64,4224]{1,0:T(8,128)(2,1)}, bf16[64,4224]{1,0:T(8,128)(2,1)}, u32[]{:S(2)}, u32[]{:S(2)}) %collective-permute-start.6) | collective-permute-done | bytes 540704 | tf_op jit(solution)/shard_map/ppermute | solution.py:194
  53.7 4.1 %rows.5 = (bf16[256,768]{1,0:T(8,128)(2,1)S(1)}, bf16[256,2432]{1,0:T(8,128)(2,1)S(1)}, bf16[256,128]{1,0:T(8,128)(2,1)S(1)}) custom-call(bf16[64,4224]{1,0:T(8,128)(2,1)} %collective-permute-done.2.refs_0_, bf16[64,4224]{1,0:T(8,128)(2,1)} %collective-permute-done.4.refs_1_, bf16[64,4224]{1,0:T(8,128)(2,1)} %collective-permute-done.7.refs_2_, ...), custom_call_target="tpu_custom_call" | custom-call | tf_op jit(solution)/shard_map/rows/pallas_call | solution.py:232
  58.9 4.9 %collective-permute-done.13.refs_5_ = bf16[256,768]{1,0:T(8,128)(2,1)S(1)} collective-permute-done((bf16[256,768]{1,0:T(8,128)(2,1)S(1)}, bf16[256,768]{1,0:T(8,128)(2,1)S(1)}, u32[]{:S(2)}, u32[]{:S(2)}) %collective-permute-start.13) | collective-permute-done | bytes 393248 | tf_op jit(solution)/shard_map/ppermute | solution.py:185
  64.0 3.1 %collective-permute-done.11.refs_0_ = bf16[64,4224]{1,0:T(8,128)(2,1)S(1)} collective-permute-done((bf16[64,4224]{1,0:T(8,128)(2,1)}, bf16[64,4224]{1,0:T(8,128)(2,1)S(1)}, u32[]{:S(2)}, u32[]{:S(2)}) %collective-permute-start.11) | collective-permute-done | bytes 540704 | tf_op jit(solution)/shard_map/ppermute | solution.py:194
  69.3 3.0 %grads.4 = (bf16[2,2,32,1152]{3,2,1,0:T(8,128)(2,1)S(1)}, bf16[2,2,32,1152]{3,2,1,0:T(8,128)(2,1)S(1)}, f32[8,1024]{1,0:T(8,128)S(1)}) custom-call(bf16[64,4224]{1,0:T(8,128)(2,1)S(1)} %copy-done.5, bf16[64,4224]{1,0:T(8,128)(2,1)} %collective-permute-done.1.refs_1_, bf16[64,4224]{1,0:T(8,128)(2,1)S(1)} %copy-done.8, ...), custom_call_target="tpu_custom_call" | custom-call | tf_op jit(solution)/shard_map/grads/pallas_call | solution.py:253
  72.5 3.8 %rows.6 = (bf16[256,768]{1,0:T(8,128)(2,1)S(1)}, bf16[256,2432]{1,0:T(8,128)(2,1)S(1)}, bf16[256,128]{1,0:T(8,128)(2,1)S(1)}) custom-call(bf16[64,4224]{1,0:T(8,128)(2,1)} %collective-permute-done.6.refs_0_, bf16[64,4224]{1,0:T(8,128)(2,1)S(1)} %collective-permute-done.9.refs_1_, bf16[64,4224]{1,0:T(8,128)(2,1)S(1)} %collective-permute-done.12.refs_2_, ...), custom_call_target="tpu_custom_call" | custom-call | tf_op jit(solution)/shard_map/rows/pallas_call | solution.py:232
  79.1 2.6 %collective-permute-done.15.refs_1_ = bf16[64,4224]{1,0:T(8,128)(2,1)S(1)} collective-permute-done((bf16[64,4224]{1,0:T(8,128)(2,1)S(1)}, bf16[64,4224]{1,0:T(8,128)(2,1)S(1)}, u32[]{:S(2)}, u32[]{:S(2)}) %collective-permute-start.15) | collective-permute-done | bytes 540704 | tf_op jit(solution)/shard_map/ppermute | solution.py:188
  83.7 3.2 %grads.5 = (bf16[2,2,32,1152]{3,2,1,0:T(8,128)(2,1)S(1)}, bf16[2,2,32,1152]{3,2,1,0:T(8,128)(2,1)S(1)}, f32[8,1024]{1,0:T(8,128)S(1)}) custom-call(bf16[64,4224]{1,0:T(8,128)(2,1)} %collective-permute-done.2.refs_0_, bf16[64,4224]{1,0:T(8,128)(2,1)} %collective-permute-done.4.refs_1_, bf16[64,4224]{1,0:T(8,128)(2,1)} %collective-permute-done.7.refs_2_, ...), custom_call_target="tpu_custom_call" | custom-call | tf_op jit(solution)/shard_map/grads/pallas_call | solution.py:253
  88.6 2.8 %rows.7 = (bf16[256,768]{1,0:T(8,128)(2,1)S(1)}, bf16[256,2432]{1,0:T(8,128)(2,1)S(1)}, bf16[256,128]{1,0:T(8,128)(2,1)S(1)}) custom-call(bf16[64,4224]{1,0:T(8,128)(2,1)S(1)} %collective-permute-done.11.refs_0_, bf16[64,4224]{1,0:T(8,128)(2,1)S(1)} %collective-permute-done.15.refs_1_, bf16[64,4224]{1,0:T(8,128)(2,1)S(1)} %collective-permute-done.17.refs_2_, ...), custom_call_target="tpu_custom_call" | custom-call | tf_op jit(solution)/shard_map/rows/pallas_call | solution.py:232
  95.3 3.8 %collective-permute-done.21.refs_5_ = bf16[256,768]{1,0:T(8,128)(2,1)S(1)} collective-permute-done((bf16[256,768]{1,0:T(8,128)(2,1)S(1)}, bf16[256,768]{1,0:T(8,128)(2,1)S(1)}, u32[]{:S(2)}, u32[]{:S(2)}) %collective-permute-start.21) | collective-permute-done | bytes 393248 | tf_op jit(solution)/shard_map/ppermute | solution.py:185
  99.3 2.9 %grads.6 = (bf16[2,2,32,1152]{3,2,1,0:T(8,128)(2,1)S(1)}, bf16[2,2,32,1152]{3,2,1,0:T(8,128)(2,1)S(1)}, f32[8,1024]{1,0:T(8,128)S(1)}) custom-call(bf16[64,4224]{1,0:T(8,128)(2,1)} %collective-permute-done.6.refs_0_, bf16[64,4224]{1,0:T(8,128)(2,1)S(1)} %collective-permute-done.9.refs_1_, bf16[64,4224]{1,0:T(8,128)(2,1)S(1)} %collective-permute-done.12.refs_2_, ...), custom_call_target="tpu_custom_call" | custom-call | tf_op jit(solution)/shard_map/grads/pallas_call | solution.py:253
  102.7 4.3 %collective-permute-done.24.refs_5_ = bf16[256,768]{1,0:T(8,128)(2,1)S(1)} collective-permute-done((bf16[256,768]{1,0:T(8,128)(2,1)S(1)}, bf16[256,768]{1,0:T(8,128)(2,1)S(1)}, u32[]{:S(2)}, u32[]{:S(2)}) %collective-permute-start.24) | collective-permute-done | bytes 393248 | tf_op jit(solution)/shard_map/ppermute | solution.py:185
  107.6 2.7 %grads.7 = (bf16[2,2,32,1152]{3,2,1,0:T(8,128)(2,1)S(1)}, bf16[2,2,32,1152]{3,2,1,0:T(8,128)(2,1)S(1)}, f32[8,1024]{1,0:T(8,128)S(1)}) custom-call(bf16[64,4224]{1,0:T(8,128)(2,1)S(1)} %collective-permute-done.11.refs_0_, bf16[64,4224]{1,0:T(8,128)(2,1)S(1)} %collective-permute-done.15.refs_1_, bf16[64,4224]{1,0:T(8,128)(2,1)S(1)} %collective-permute-done.17.refs_2_, ...), custom_call_target="tpu_custom_call" | custom-call | tf_op jit(solution)/shard_map/grads/pallas_call | solution.py:253
  114.7 4.4 %collective-permute-done.28 = f32[8,1024]{1,0:T(8,128)S(1)} collective-permute-done((f32[8,1024]{1,0:T(8,128)S(1)}, f32[8,1024]{1,0:T(8,128)S(1)}, u32[]{:S(2)}, u32[]{:S(2)}) %collective-permute-start.28) | collective-permute-done | bytes 32800 | tf_op jit(solution)/shard_map/ppermute | solution.py:188
  125.8 4.5 %down.1 = bf16[384,2048]{1,0:T(8,128)(2,1)} custom-call(bf16[256,2432]{1,0:T(8,128)(2,1)S(1)} %copy-done.10, bf16[256,2432]{1,0:T(8,128)(2,1)S(1)} %copy-done.12, bf16[256,2432]{1,0:T(8,128)(2,1)S(1)} %copy-done.14, bf16[256,2432]{1,0:T(8,128)(2,1)S(1)} %copy-done.16), custom_call_target="tpu_custom_call" | custom-call | tf_op jit(solution)/shard_map/down/pallas_call | solution.py:282
  131.9 2.8 %collective-permute-start.38 = (f32[8,1024]{1,0:T(8,128)S(1)}, f32[8,1024]{1,0:T(8,128)S(1)}, u32[]{:S(2)}, u32[]{:S(2)}) collective-permute-start(f32[8,1024]{1,0:T(8,128)S(1)} %add.112), channel_id=1, source_target_pairs={{0,17},{1,16},{2,19},{3,18},{4,21},{5,20},{6,23},{7,22},{8,25},{9,... | collective-permute-start | bytes 98312 | tf_op jit(solution)/shard_map/ppermute | solution.py:203
  137.9 2.0 %collective-permute-done.36 = f32[8,1024]{1,0:T(8,128)S(1)} collective-permute-done((f32[8,1024]{1,0:T(8,128)S(1)}, f32[8,1024]{1,0:T(8,128)S(1)}, u32[]{:S(2)}, u32[]{:S(2)}) %collective-permute-start.36) | collective-permute-done | bytes 32800 | tf_op jit(solution)/shard_map/ppermute | solution.py:197
  (144 shorter events, 54.3 us)
Async XLA Ops:
  2.5 9.6 %collective-permute-start = (bf16[32,4224]{1,0:T(8,128)(2,1)}, bf16[32,4224]{1,0:T(8,128)(2,1)S(1)}, u32[]{:S(2)}, u32[]{:S(2)}) collective-permute-start(bf16[32,4224]{1,0:T(8,128)(2,1)} %pack.1), channel_id=1, source_target_pairs={{0,1},{1,0},{2,3},{3,2},{4,5},{5,4},{6,7},{7,6},{8,9},{9,8},{10,11... | collective-permute-start | bytes 811016 | tf_op jit(solution)/shard_map/ppermute | solution.py:185
  13.1 36.0 %collective-permute-start.8 = (bf16[768,1024]{1,0:T(8,128)(2,1)}, bf16[768,1024]{1,0:T(8,128)(2,1)}, u32[]{:S(2)}, u32[]{:S(2)}) collective-permute-start(bf16[768,1024]{1,0:T(8,128)(2,1)} %constant_dynamic-slice_fusion), channel_id=1, source_target_pairs={{0,1},{1,0},{2,3},{3,2},{4,5},{5,4},{6,7},{7,6},{8,9},{9,8},{10,11... | collective-permute-start | bytes 4718600 | tf_op jit(solution)/shard_map/ppermute | solution.py:185
  14.9 13.0 %collective-permute-start.1 = (bf16[64,4224]{1,0:T(8,128)(2,1)S(1)}, bf16[64,4224]{1,0:T(8,128)(2,1)}, u32[]{:S(2)}, u32[]{:S(2)}) collective-permute-start(bf16[64,4224]{1,0:T(8,128)(2,1)S(1)} %pad_maximum_fusion.refs_0_), channel_id=1, source_target_pairs={{0,4},{2,6},{4,0},{6,2},{8,12},{10,14},{12,8},{14,10},{16,20},{18,... | collective-permute-start | bytes 1622024 | tf_op jit(solution)/shard_map/ppermute | solution.py:188
  16.4 14.5 %collective-permute-start.2 = (bf16[64,4224]{1,0:T(8,128)(2,1)S(1)}, bf16[64,4224]{1,0:T(8,128)(2,1)}, u32[]{:S(2)}, u32[]{:S(2)}) collective-permute-start(bf16[64,4224]{1,0:T(8,128)(2,1)S(1)} %pad_maximum_fusion.refs_0_), channel_id=1, source_target_pairs={{0,8},{2,10},{4,12},{6,14},{8,16},{10,18},{12,20},{14,22},{16,24},... | collective-permute-start | bytes 1622024 | tf_op jit(solution)/shard_map/ppermute | solution.py:194
  18.0 13.0 %collective-permute-start.3 = (bf16[64,4224]{1,0:T(8,128)(2,1)S(1)}, bf16[64,4224]{1,0:T(8,128)(2,1)S(1)}, u32[]{:S(2)}, u32[]{:S(2)}) collective-permute-start(bf16[64,4224]{1,0:T(8,128)(2,1)S(1)} %pad_maximum_fusion.refs_0_), channel_id=1, source_target_pairs={{0,2},{2,0},{4,6},{6,4},{8,10},{10,8},{12,14},{14,12},{16,18},{18,... | collective-permute-start | bytes 1622024 | tf_op jit(solution)/shard_map/ppermute | solution.py:191
  31.8 15.0 %collective-permute-start.4 = (bf16[64,4224]{1,0:T(8,128)(2,1)}, bf16[64,4224]{1,0:T(8,128)(2,1)}, u32[]{:S(2)}, u32[]{:S(2)}) collective-permute-start(bf16[64,4224]{1,0:T(8,128)(2,1)} %collective-permute-done.2.refs_0_), channel_id=1, source_target_pairs={{0,4},{2,6},{4,0},{6,2},{8,12},{10,14},{12,8},{14,10},{16,20},{18,... | collective-permute-start | bytes 1622024 | tf_op jit(solution)/shard_map/ppermute | solution.py:188
  32.3 16.5 %collective-permute-start.6 = (bf16[64,4224]{1,0:T(8,128)(2,1)}, bf16[64,4224]{1,0:T(8,128)(2,1)}, u32[]{:S(2)}, u32[]{:S(2)}) collective-permute-start(bf16[64,4224]{1,0:T(8,128)(2,1)} %collective-permute-done.2.refs_0_), channel_id=1, source_target_pairs={{0,8},{2,10},{4,12},{6,14},{8,16},{10,18},{12,20},{14,22},{16,24},... | collective-permute-start | bytes 1622024 | tf_op jit(solution)/shard_map/ppermute | solution.py:194
  32.3 16.5 %collective-permute-start.7 = (bf16[64,4224]{1,0:T(8,128)(2,1)}, bf16[64,4224]{1,0:T(8,128)(2,1)}, u32[]{:S(2)}, u32[]{:S(2)}) collective-permute-start(bf16[64,4224]{1,0:T(8,128)(2,1)} %collective-permute-done.2.refs_0_), channel_id=1, source_target_pairs={{0,2},{2,0},{4,6},{6,4},{8,10},{10,8},{12,14},{14,12},{16,18},{18,... | collective-permute-start | bytes 1622024 | tf_op jit(solution)/shard_map/ppermute | solution.py:191
  49.1 14.9 %collective-permute-start.9 = (bf16[64,4224]{1,0:T(8,128)(2,1)}, bf16[64,4224]{1,0:T(8,128)(2,1)S(1)}, u32[]{:S(2)}, u32[]{:S(2)}) collective-permute-start(bf16[64,4224]{1,0:T(8,128)(2,1)} %collective-permute-done.6.refs_0_), channel_id=1, source_target_pairs={{0,4},{2,6},{4,0},{6,2},{8,12},{10,14},{12,8},{14,10},{16,20},{18,... | collective-permute-start | bytes 1622024 | tf_op jit(solution)/shard_map/ppermute | solution.py:188
  50.6 16.4 %collective-permute-start.11 = (bf16[64,4224]{1,0:T(8,128)(2,1)}, bf16[64,4224]{1,0:T(8,128)(2,1)S(1)}, u32[]{:S(2)}, u32[]{:S(2)}) collective-permute-start(bf16[64,4224]{1,0:T(8,128)(2,1)} %collective-permute-done.6.refs_0_), channel_id=1, source_target_pairs={{0,8},{2,10},{4,12},{6,14},{8,16},{10,18},{12,20},{14,22},{16,24},... | collective-permute-start | bytes 1622024 | tf_op jit(solution)/shard_map/ppermute | solution.py:194
  52.2 14.9 %collective-permute-start.12 = (bf16[64,4224]{1,0:T(8,128)(2,1)}, bf16[64,4224]{1,0:T(8,128)(2,1)S(1)}, u32[]{:S(2)}, u32[]{:S(2)}) collective-permute-start(bf16[64,4224]{1,0:T(8,128)(2,1)} %collective-permute-done.6.refs_0_), channel_id=1, source_target_pairs={{0,2},{2,0},{4,6},{6,4},{8,10},{10,8},{12,14},{14,12},{16,18},{18,... | collective-permute-start | bytes 1622024 | tf_op jit(solution)/shard_map/ppermute | solution.py:191
  52.2 11.5 %collective-permute-start.13 = (bf16[256,768]{1,0:T(8,128)(2,1)S(1)}, bf16[256,768]{1,0:T(8,128)(2,1)S(1)}, u32[]{:S(2)}, u32[]{:S(2)}) collective-permute-start(bf16[256,768]{1,0:T(8,128)(2,1)S(1)} %get-tuple-element.157.refs_4_), channel_id=1, source_target_pairs={{0,1},{1,0},{2,3},{3,2},{4,5},{5,4},{6,7},{7,6},{8,9},{9,8},{10,11... | collective-permute-start | bytes 1179656 | tf_op jit(solution)/shard_map/ppermute | solution.py:185
  67.1 14.7 %collective-permute-start.15 = (bf16[64,4224]{1,0:T(8,128)(2,1)S(1)}, bf16[64,4224]{1,0:T(8,128)(2,1)S(1)}, u32[]{:S(2)}, u32[]{:S(2)}) collective-permute-start(bf16[64,4224]{1,0:T(8,128)(2,1)S(1)} %collective-permute-done.11.refs_0_), channel_id=1, source_target_pairs={{0,4},{2,6},{4,0},{6,2},{8,12},{10,14},{12,8},{14,10},{16,20},{18,... | collective-permute-start | bytes 1622024 | tf_op jit(solution)/shard_map/ppermute | solution.py:188
  67.6 14.2 %collective-permute-start.17 = (bf16[64,4224]{1,0:T(8,128)(2,1)S(1)}, bf16[64,4224]{1,0:T(8,128)(2,1)S(1)}, u32[]{:S(2)}, u32[]{:S(2)}) collective-permute-start(bf16[64,4224]{1,0:T(8,128)(2,1)S(1)} %collective-permute-done.11.refs_0_), channel_id=1, source_target_pairs={{0,2},{2,0},{4,6},{6,4},{8,10},{10,8},{12,14},{14,12},{16,18},{18,... | collective-permute-start | bytes 1622024 | tf_op jit(solution)/shard_map/ppermute | solution.py:191
  67.8 11.3 %collective-permute-start.18 = (bf16[256,768]{1,0:T(8,128)(2,1)S(1)}, bf16[256,768]{1,0:T(8,128)(2,1)S(1)}, u32[]{:S(2)}, u32[]{:S(2)}) collective-permute-start(bf16[256,768]{1,0:T(8,128)(2,1)S(1)} %get-tuple-element.179.refs_4_), channel_id=1, source_target_pairs={{0,1},{1,0},{2,3},{3,2},{4,5},{5,4},{6,7},{7,6},{8,9},{9,8},{10,11... | collective-permute-start | bytes 1179656 | tf_op jit(solution)/shard_map/ppermute | solution.py:185
  87.1 11.9 %collective-permute-start.21 = (bf16[256,768]{1,0:T(8,128)(2,1)S(1)}, bf16[256,768]{1,0:T(8,128)(2,1)S(1)}, u32[]{:S(2)}, u32[]{:S(2)}) collective-permute-start(bf16[256,768]{1,0:T(8,128)(2,1)S(1)} %get-tuple-element.205.refs_4_), channel_id=1, source_target_pairs={{0,1},{1,0},{2,3},{3,2},{4,5},{5,4},{6,7},{7,6},{8,9},{9,8},{10,11... | collective-permute-start | bytes 1179656 | tf_op jit(solution)/shard_map/ppermute | solution.py:185
  92.5 6.8 %collective-permute-start.22 = (bf16[2,32,1152]{2,1,0:T(8,128)(2,1)S(1)}, bf16[2,32,1152]{2,1,0:T(8,128)(2,1)S(1)}, u32[]{:S(2)}, u32[]{:S(2)}) collective-permute-start(bf16[2,32,1152]{2,1,0:T(8,128)(2,1)S(1)} %fusion.10), channel_id=1, source_target_pairs={{0,4},{2,6},{4,0},{6,2},{8,12},{10,14},{12,8},{14,10},{16,20},{18,... | collective-permute-start | bytes 442376 | tf_op jit(solution)/shard_map/ppermute | solution.py:188
  93.1 13.8 %collective-permute-start.24 = (bf16[256,768]{1,0:T(8,128)(2,1)S(1)}, bf16[256,768]{1,0:T(8,128)(2,1)S(1)}, u32[]{:S(2)}, u32[]{:S(2)}) collective-permute-start(bf16[256,768]{1,0:T(8,128)(2,1)S(1)} %get-tuple-element.228.refs_4_), channel_id=1, source_target_pairs={{0,1},{1,0},{2,3},{3,2},{4,5},{5,4},{6,7},{7,6},{8,9},{9,8},{10,11... | collective-permute-start | bytes 1179656 | tf_op jit(solution)/shard_map/ppermute | solution.py:185
  93.7 9.0 %collective-permute-start.25 = (bf16[2,32,1152]{2,1,0:T(8,128)(2,1)S(1)}, bf16[2,32,1152]{2,1,0:T(8,128)(2,1)S(1)}, u32[]{:S(2)}, u32[]{:S(2)}) collective-permute-start(bf16[2,32,1152]{2,1,0:T(8,128)(2,1)S(1)} %fusion.11), channel_id=1, source_target_pairs={{0,4},{2,6},{4,0},{6,2},{8,12},{10,14},{12,8},{14,10},{16,20},{18,... | collective-permute-start | bytes 442376 | tf_op jit(solution)/shard_map/ppermute | solution.py:188
  102.4 9.2 %collective-permute-start.31 = (bf16[2,32,1152]{2,1,0:T(8,128)(2,1)S(1)}, bf16[2,32,1152]{2,1,0:T(8,128)(2,1)S(1)}, u32[]{:S(2)}, u32[]{:S(2)}) collective-permute-start(bf16[2,32,1152]{2,1,0:T(8,128)(2,1)S(1)} %fusion.5), channel_id=1, source_target_pairs={{0,8},{2,10},{4,12},{6,14},{8,16},{10,18},{12,20},{14,22},{16,24},... | collective-permute-start | bytes 442376 | tf_op jit(solution)/shard_map/ppermute | solution.py:194
  112.4 7.0 %collective-permute-start.32 = (bf16[2,32,1152]{2,1,0:T(8,128)(2,1)S(1)}, bf16[2,32,1152]{2,1,0:T(8,128)(2,1)S(1)}, u32[]{:S(2)}, u32[]{:S(2)}) collective-permute-start(bf16[2,32,1152]{2,1,0:T(8,128)(2,1)S(1)} %fusion.4), channel_id=1, source_target_pairs={{0,8},{2,10},{4,12},{6,14},{8,16},{10,18},{12,20},{14,22},{16,24},... | collective-permute-start | bytes 442376 | tf_op jit(solution)/shard_map/ppermute | solution.py:194
  112.6 6.9 %collective-permute-start.30 = (bf16[2,32,1152]{2,1,0:T(8,128)(2,1)S(1)}, bf16[2,32,1152]{2,1,0:T(8,128)(2,1)S(1)}, u32[]{:S(2)}, u32[]{:S(2)}) collective-permute-start(bf16[2,32,1152]{2,1,0:T(8,128)(2,1)S(1)} %fusion.13), channel_id=1, source_target_pairs={{0,4},{2,6},{4,0},{6,2},{8,12},{10,14},{12,8},{14,10},{16,20},{18,... | collective-permute-start | bytes 442376 | tf_op jit(solution)/shard_map/ppermute | solution.py:188
  120.2 10.2 %collective-permute-start.34 = (bf16[2,32,1152]{2,1,0:T(8,128)(2,1)}, bf16[2,32,1152]{2,1,0:T(8,128)(2,1)S(1)}, u32[]{:S(2)}, u32[]{:S(2)}) collective-permute-start(bf16[2,32,1152]{2,1,0:T(8,128)(2,1)} %fusion.2), channel_id=1, source_target_pairs={{0,8},{2,10},{4,12},{6,14},{8,16},{10,18},{12,20},{14,22},{16,24},... | collective-permute-start | bytes 442376 | tf_op jit(solution)/shard_map/ppermute | solution.py:194
  120.2 10.1 %collective-permute-start.33 = (f32[8,1024]{1,0:T(8,128)S(1)}, f32[8,1024]{1,0:T(8,128)S(1)}, u32[]{:S(2)}, u32[]{:S(2)}) collective-permute-start(f32[8,1024]{1,0:T(8,128)S(1)} %add.102), channel_id=1, source_target_pairs={{0,8},{2,10},{4,12},{6,14},{8,0},{10,2},{12,4},{14,6},{16,24},{18,... | collective-permute-start | bytes 98312 | tf_op jit(solution)/shard_map/ppermute | solution.py:197
  (41 other events, 308.5 us)

commit v5 on v4

--- a/solution.py
+++ b/solution.py
@@ -237,7 +237,7 @@
                 jax.ShapeDtypeStruct((rows, LANES), bf16),
             ),
             in_specs=[whole()] * 8 + [scalar(), scalar()],
-            out_specs=(whole(), pl.BlockSpec(memory_space=pl.ANY), whole()),
+            out_specs=(whole(), pl.BlockSpec(memory_space=pltpu.HBM), whole()),
             scratch_shapes=[
                 pltpu.VMEM((rows, width), bf16),
                 pltpu.VMEM((rows, width), bf16),
@@ -270,7 +270,7 @@
     fence = lax.optimization_barrier
     own = jnp.concatenate([own, go_x(own)], axis=0)
     near, far, near_c, far_c, w_far = {0: own}, {}, {}, {}, {}
-    state = {"near": near, "far": far, "near_c": near_c, "far_c": far_c, "w": w_far}
+    state = {"a": near, "b": far, "c": near_c, "d": far_c, "w": w_far}
     grads, kept, tails, other = {}, {}, {}, {}
     state.update(grads=grads, other=other)
     d_own, d_got, totals, sent, value = {}, {}, {}, {}, {}
@@ -282,7 +282,7 @@
         return pl.pallas_call(
             functools.partial(down_kernel, planes, hidden),
             out_shape=jax.ShapeDtypeStruct((hidden, width), bf16),
-            in_specs=[pl.BlockSpec(memory_space=pl.ANY)] * planes,
+            in_specs=[pl.BlockSpec(memory_space=pltpu.HBM)] * planes,
             out_specs=whole(),
             scratch_shapes=[
                 pltpu.VMEM((2, planes * rows // 2, hidden + width), bf16),
@@ -349,10 +349,12 @@
     other[3] = go_x(grads[3])
     send_y(1)
     send_y(0)
-    other[2], sent[1] = fence((other[2], sent[1]))
+    other[2], sent[1], kept[3] = fence((other[2], sent[1], kept[3]))
     grads_of(2)
     hop(1)
     send_y(2)
+    down = {0: make_down([kept[k] for k in range(planes)])}
+    state["down"] = down
     step(("sent", 2), ("value", 2))
     grads_of(3)
     hop(2)
@@ -362,7 +364,10 @@
     state["pool"] = pool
     step(("value", 3), ("sent", 2), ("value", 2))
     send_y(3)
-    pool[0] = pool[0] + go_y(pool[0])
+    part = pool[0]
+    mine_sums = part + go_y(part)
+    cross_sums = go_x(part) + go_far(part, 2)
+    pool[0] = jnp.concatenate([mine_sums, cross_sums], axis=0)
     step()
     hop(3)
     pool[0] = pool[0] + go_jump(pool[0], 4)
@@ -373,12 +378,14 @@
     right = jnp.where(side == 0, crossed[:, :half], final[0, :, :half])
     grad_normed = jnp.concatenate([left, right], axis=1)
     row_grads = final[0, :, half:] + crossed[:, half:]
-    grad_down = make_down([kept[k] for k in range(planes)])
-    part = pool[0]
-    mine_sums = part + go_jump(part, 8)
-    crossed = go_x(part) + go_far(part, 8)
+    grad_down = down[0]
+    sums = pool[0] + go_jump(pool[0], 8)
+    mine_sums, cross_sums = sums[:8], sums[8:]
     sums = jnp.concatenate(
-        [jnp.where(side == 0, mine_sums, crossed), jnp.where(side == 0, crossed, mine_sums)],
+        [
+            jnp.where(side == 0, mine_sums, cross_sums),
+            jnp.where(side == 0, cross_sums, mine_sums),
+        ],
         axis=1,
     )
 

time: 143 us -> 140 us (0.979)
  local copies, waits for them, and re-layouts: 16.9 us -> 8.82 us
  starting transfers between devices: 31.1 us -> 37.4 us
  waiting for transfers between devices: 55.8 us -> 54.3 us
    ppermute x9, waiting for transfers between devices: 21.4 us -> 3.28 us  [go_y(): return lax.ppermute(v, 'expert', [(e, e ^ 2) for e in range(experts)])]
    ppermute x6, waiting for transfers between devices: 8.61 us -> 21.9 us  [go_z(): lax.ppermute(v, 'expert', [(e, (e + 4) % experts) for e in range(experts)])]
    unnamed x53 -> x37, local copies, waits for them, and re-layouts: 13.9 us -> 5.84 us
    ppermute x6, starting transfers between devices: 3.52 us -> 7.59 us  [go_z(): lax.ppermute(v, 'expert', [(e, (e + 4) % experts) for e in range(experts)])]
    ppermute x2, waiting for transfers between devices: 1.98 us -> 5.34 us  [go_jump(): return lax.ppermute(v, 'expert', [(e, e ^ by) for e in range(experts)])]
    ppermute x9, starting transfers between devices: 8.87 us -> 12 us  [go_y(): return lax.ppermute(v, 'expert', [(e, e ^ 2) for e in range(experts)])]
    ppermute x2, starting transfers between devices: 1.72 us -> 3.34 us  [go_jump(): return lax.ppermute(v, 'expert', [(e, e ^ by) for e in range(experts)])]
  transfers between devices with their start and end apart: 39 -> 39, of which waited for: 22 -> 17; matrix products, arithmetic and copies ran while one was open for 3% -> 3% of each run, Pallas kernels for 20% -> 20%
where the time goes in v5:
time: 140 us; the launch traced here: 139 us
  waiting for transfers between devices  54.3 us (39%)
  starting transfers between devices  37.4 us (27%)
  Pallas kernels  33 us (24%)
  local copies, waits for them, and re-layouts  8.82 us (6%)
  other arithmetic  3.69 us (3%)
  between operations  1.7 us (1%)
    ppermute x6, waiting for transfers between devices, go_z(): lax.ppermute(v, 'expert', [(e, (e + 4) % experts) for e in range(experts)])  21.9 us
    ppermute x8, waiting for transfers between devices, go_x(): return lax.ppermute(v, 'dp', [(0, 1), (1, 0)])  19.1 us
    pallas_call x4, Pallas kernels, first_half(): pl.pallas_call(functools.partial(rows_kernel, segments, width, hidden), o...  14.8 us
    ppermute x9, starting transfers between devices, go_y(): return lax.ppermute(v, 'expert', [(e, e ^ 2) for e in range(experts)])  12 us
    ppermute x8, starting transfers between devices, go_x(): return lax.ppermute(v, 'dp', [(0, 1), (1, 0)])  11.8 us
    pallas_call x4, Pallas kernels, second_half(): pl.pallas_call(functools.partial(grad_kernel, segments, half), out_shape=...  11.8 us
    ppermute x6, starting transfers between devices, go_z(): lax.ppermute(v, 'expert', [(e, (e + 4) % experts) for e in range(experts)])  7.59 us
    unnamed x37, local copies, waits for them, and re-layouts  5.84 us
  transfers between devices with their start and end apart: 39, of which 17 were waited for; matrix products, arithmetic and copies ran while one was open for 3% of the time, Pallas kernels for 20%

profile of v5, /device:TPU:0, one launch (start us, length us, event | category | flops | bytes accessed | tf_op | source)
XLA Modules:
  0.0 139.0 jit_solution(74696524448970183)
XLA Ops:
  2.5 2.9 %collective-permute-start = (bf16[32,4224]{1,0:T(8,128)(2,1)}, bf16[32,4224]{1,0:T(8,128)(2,1)S(1)}, u32[]{:S(2)}, u32[]{:S(2)}) collective-permute-start(bf16[32,4224]{1,0:T(8,128)(2,1)} %pack.1), channel_id=1, source_target_pairs={{0,1},{1,0},{2,3},{3,2},{4,5},{5,4},{6,7},{7,6},{8,9},{9,8},{10,11... | collective-permute-start | bytes 811016 | tf_op jit(solution)/shard_map/ppermute | solution.py:185
  5.5 2.8 %constant_dynamic-slice_fusion = bf16[768,1024]{1,0:T(8,128)(2,1)} fusion(bf16[768,2048]{1,0:T(8,128)(2,1)} %bitcast.68, s32[]{:T(128)S(6)} %select_n.32), kind=kLoop, calls=%fused_computation.42 | loop fusion | bytes 3145732 | tf_op jit(solution)/shard_map/dynamic_slice | solution.py:222
  8.3 3.9 %collective-permute-done = bf16[32,4224]{1,0:T(8,128)(2,1)S(1)} collective-permute-done((bf16[32,4224]{1,0:T(8,128)(2,1)}, bf16[32,4224]{1,0:T(8,128)(2,1)S(1)}, u32[]{:S(2)}, u32[]{:S(2)}) %collective-permute-start) | collective-permute-done | bytes 270368 | tf_op jit(solution)/shard_map/ppermute | solution.py:185
  18.8 10.9 %collective-permute-done.1.refs_0_ = bf16[64,4224]{1,0:T(8,128)(2,1)} collective-permute-done((bf16[64,4224]{1,0:T(8,128)(2,1)S(1)}, bf16[64,4224]{1,0:T(8,128)(2,1)}, u32[]{:S(2)}, u32[]{:S(2)}) %collective-permute-start.1) | collective-permute-done | bytes 540704 | tf_op jit(solution)/shard_map/ppermute | solution.py:194
  37.3 4.1 %rows.4 = (bf16[256,768]{1,0:T(8,128)(2,1)S(1)}, bf16[256,2432]{1,0:T(8,128)(2,1)S(1)}, bf16[256,128]{1,0:T(8,128)(2,1)S(1)}) custom-call(bf16[64,4224]{1,0:T(8,128)(2,1)S(1)} %copy-done.4, bf16[64,4224]{1,0:T(8,128)(2,1)} %collective-permute-done.2.refs_1_, bf16[64,4224]{1,0:T(8,128)(2,1)S(1)} %copy-done.7, ...), custom_call_target="tpu_custom_call" | custom-call | tf_op jit(solution)/shard_map/rows/pallas_call | solution.py:232
  41.4 6.0 %collective-permute-done.4.refs_0_ = bf16[64,4224]{1,0:T(8,128)(2,1)} collective-permute-done((bf16[64,4224]{1,0:T(8,128)(2,1)}, bf16[64,4224]{1,0:T(8,128)(2,1)}, u32[]{:S(2)}, u32[]{:S(2)}) %collective-permute-start.4) | collective-permute-done | bytes 540704 | tf_op jit(solution)/shard_map/ppermute | solution.py:194
  53.9 4.1 %rows.5 = (bf16[256,768]{1,0:T(8,128)(2,1)S(1)}, bf16[256,2432]{1,0:T(8,128)(2,1)S(1)}, bf16[256,128]{1,0:T(8,128)(2,1)S(1)}) custom-call(bf16[64,4224]{1,0:T(8,128)(2,1)} %collective-permute-done.1.refs_0_, bf16[64,4224]{1,0:T(8,128)(2,1)} %collective-permute-done.5.refs_1_, bf16[64,4224]{1,0:T(8,128)(2,1)} %collective-permute-done.6.refs_2_, ...), custom_call_target="tpu_custom_call" | custom-call | tf_op jit(solution)/shard_map/rows/pallas_call | solution.py:232
  58.0 5.9 %collective-permute-done.13.refs_5_ = bf16[256,768]{1,0:T(8,128)(2,1)S(1)} collective-permute-done((bf16[256,768]{1,0:T(8,128)(2,1)S(1)}, bf16[256,768]{1,0:T(8,128)(2,1)S(1)}, u32[]{:S(2)}, u32[]{:S(2)}) %collective-permute-start.13) | collective-permute-done | bytes 393248 | tf_op jit(solution)/shard_map/ppermute | solution.py:185
  63.9 1.9 %collective-permute-done.9.refs_0_ = bf16[64,4224]{1,0:T(8,128)(2,1)S(1)} collective-permute-done((bf16[64,4224]{1,0:T(8,128)(2,1)}, bf16[64,4224]{1,0:T(8,128)(2,1)S(1)}, u32[]{:S(2)}, u32[]{:S(2)}) %collective-permute-start.9) | collective-permute-done | bytes 540704 | tf_op jit(solution)/shard_map/ppermute | solution.py:194
  69.0 3.0 %grads.4 = (bf16[2,2,32,1152]{3,2,1,0:T(8,128)(2,1)S(1)}, bf16[2,2,32,1152]{3,2,1,0:T(8,128)(2,1)S(1)}, f32[8,1024]{1,0:T(8,128)S(1)}) custom-call(bf16[64,4224]{1,0:T(8,128)(2,1)S(1)} %copy-done.5, bf16[64,4224]{1,0:T(8,128)(2,1)} %collective-permute-done.2.refs_1_, bf16[64,4224]{1,0:T(8,128)(2,1)S(1)} %copy-done.8, ...), custom_call_target="tpu_custom_call" | custom-call | tf_op jit(solution)/shard_map/grads/pallas_call | solution.py:253
  72.3 3.8 %rows.6 = (bf16[256,768]{1,0:T(8,128)(2,1)S(1)}, bf16[256,2432]{1,0:T(8,128)(2,1)S(1)}, bf16[256,128]{1,0:T(8,128)(2,1)S(1)}) custom-call(bf16[64,4224]{1,0:T(8,128)(2,1)} %collective-permute-done.4.refs_0_, bf16[64,4224]{1,0:T(8,128)(2,1)S(1)} %collective-permute-done.10.refs_1_, bf16[64,4224]{1,0:T(8,128)(2,1)S(1)} %collective-permute-done.11.refs_2_, ...), custom_call_target="tpu_custom_call" | custom-call | tf_op jit(solution)/shard_map/rows/pallas_call | solution.py:232
  76.1 2.8 %collective-permute-done.18.refs_5_ = bf16[256,768]{1,0:T(8,128)(2,1)S(1)} collective-permute-done((bf16[256,768]{1,0:T(8,128)(2,1)S(1)}, bf16[256,768]{1,0:T(8,128)(2,1)S(1)}, u32[]{:S(2)}, u32[]{:S(2)}) %collective-permute-start.18) | collective-permute-done | bytes 393248 | tf_op jit(solution)/shard_map/ppermute | solution.py:185
  80.5 1.9 %collective-permute-done.19.refs_3_ = bf16[64,4224]{1,0:T(8,128)(2,1)S(1)} collective-permute-done((bf16[64,4224]{1,0:T(8,128)(2,1)S(1)}, bf16[64,4224]{1,0:T(8,128)(2,1)S(1)}, u32[]{:S(2)}, u32[]{:S(2)}) %collective-permute-start.19) | collective-permute-done | bytes 540704 | tf_op jit(solution)/shard_map/ppermute | solution.py:191
  82.4 3.2 %grads.5 = (bf16[2,2,32,1152]{3,2,1,0:T(8,128)(2,1)S(1)}, bf16[2,2,32,1152]{3,2,1,0:T(8,128)(2,1)S(1)}, f32[8,1024]{1,0:T(8,128)S(1)}) custom-call(bf16[64,4224]{1,0:T(8,128)(2,1)} %collective-permute-done.1.refs_0_, bf16[64,4224]{1,0:T(8,128)(2,1)} %collective-permute-done.5.refs_1_, bf16[64,4224]{1,0:T(8,128)(2,1)} %collective-permute-done.6.refs_2_, ...), custom_call_target="tpu_custom_call" | custom-call | tf_op jit(solution)/shard_map/grads/pallas_call | solution.py:253
  87.4 2.8 %rows.7 = (bf16[256,768]{1,0:T(8,128)(2,1)S(1)}, bf16[256,2432]{1,0:T(8,128)(2,1)S(1)}, bf16[256,128]{1,0:T(8,128)(2,1)S(1)}) custom-call(bf16[64,4224]{1,0:T(8,128)(2,1)S(1)} %collective-permute-done.9.refs_0_, bf16[64,4224]{1,0:T(8,128)(2,1)S(1)} %collective-permute-done.14.refs_1_, bf16[64,4224]{1,0:T(8,128)(2,1)S(1)} %collective-permute-done.15.refs_2_, ...), custom_call_target="tpu_custom_call" | custom-call | tf_op jit(solution)/shard_map/rows/pallas_call | solution.py:232
  93.0 4.9 %collective-permute-done.21.refs_5_ = bf16[256,768]{1,0:T(8,128)(2,1)S(1)} collective-permute-done((bf16[256,768]{1,0:T(8,128)(2,1)S(1)}, bf16[256,768]{1,0:T(8,128)(2,1)S(1)}, u32[]{:S(2)}, u32[]{:S(2)}) %collective-permute-start.21) | collective-permute-done | bytes 393248 | tf_op jit(solution)/shard_map/ppermute | solution.py:185
  97.8 2.9 %grads.6 = (bf16[2,2,32,1152]{3,2,1,0:T(8,128)(2,1)S(1)}, bf16[2,2,32,1152]{3,2,1,0:T(8,128)(2,1)S(1)}, f32[8,1024]{1,0:T(8,128)S(1)}) custom-call(bf16[64,4224]{1,0:T(8,128)(2,1)} %collective-permute-done.4.refs_0_, bf16[64,4224]{1,0:T(8,128)(2,1)S(1)} %collective-permute-done.10.refs_1_, bf16[64,4224]{1,0:T(8,128)(2,1)S(1)} %collective-permute-done.11.refs_2_, ...), custom_call_target="tpu_custom_call" | custom-call | tf_op jit(solution)/shard_map/grads/pallas_call | solution.py:253
  102.2 4.6 %down.1 = bf16[384,2048]{1,0:T(8,128)(2,1)} custom-call(bf16[256,2432]{1,0:T(8,128)(2,1)S(1)} %get-tuple-element.223.refs_0_, bf16[256,2432]{1,0:T(8,128)(2,1)S(1)} %get-tuple-element.224.refs_1_, bf16[256,2432]{1,0:T(8,128)(2,1)S(1)} %get-tuple-element.225.refs_2_, bf16[256,2432]{1,0:T(8,128)(2,1)S(1)} %get-tuple-element.226.refs_3_), custom_call_target="tpu_custom_call" | custom-call | tf_op jit(solution)/shard_map/down/pallas_call | solution.py:282
  108.4 2.7 %grads.7 = (bf16[2,2,32,1152]{3,2,1,0:T(8,128)(2,1)S(1)}, bf16[2,2,32,1152]{3,2,1,0:T(8,128)(2,1)S(1)}, f32[8,1024]{1,0:T(8,128)S(1)}) custom-call(bf16[64,4224]{1,0:T(8,128)(2,1)S(1)} %collective-permute-done.9.refs_0_, bf16[64,4224]{1,0:T(8,128)(2,1)S(1)} %collective-permute-done.14.refs_1_, bf16[64,4224]{1,0:T(8,128)(2,1)S(1)} %collective-permute-done.15.refs_2_, ...), custom_call_target="tpu_custom_call" | custom-call | tf_op jit(solution)/shard_map/grads/pallas_call | solution.py:253
  121.0 2.0 %collective-permute-done.30 = f32[8,1024]{1,0:T(8,128)S(1)} collective-permute-done((f32[8,1024]{1,0:T(8,128)S(1)}, f32[8,1024]{1,0:T(8,128)S(1)}, u32[]{:S(2)}, u32[]{:S(2)}) %collective-permute-start.30) | collective-permute-done | bytes 32800 | tf_op jit(solution)/shard_map/ppermute | solution.py:203
  123.5 2.1 %collective-permute-start.35 = (f32[16,1024]{1,0:T(8,128)S(1)}, f32[16,1024]{1,0:T(8,128)S(1)}, u32[]{:S(2)}, u32[]{:S(2)}) collective-permute-start(f32[16,1024]{1,0:T(8,128)S(1)} %pad_maximum_fusion.1), channel_id=1, source_target_pairs={{0,8},{2,10},{4,12},{6,14},{8,0},{10,2},{12,4},{14,6},{16,24},{18,... | collective-permute-start | bytes 196616 | tf_op jit(solution)/shard_map/ppermute | solution.py:197
  125.6 2.2 %collective-permute-done.35 = f32[16,1024]{1,0:T(8,128)S(1)} collective-permute-done((f32[16,1024]{1,0:T(8,128)S(1)}, f32[16,1024]{1,0:T(8,128)S(1)}, u32[]{:S(2)}, u32[]{:S(2)}) %collective-permute-start.35) | collective-permute-done | bytes 65568 | tf_op jit(solution)/shard_map/ppermute | solution.py:197
  127.8 3.1 %collective-permute-done.36 = bf16[2,32,1152]{2,1,0:T(8,128)(2,1)S(1)} collective-permute-done((bf16[2,32,1152]{2,1,0:T(8,128)(2,1)S(1)}, bf16[2,32,1152]{2,1,0:T(8,128)(2,1)S(1)}, u32[]{:S(2)}, u32[]{:S(2)}) %collective-permute-start.36) | collective-permute-done | bytes 147488 | tf_op jit(solution)/shard_map/ppermute | solution.py:194
  132.9 3.2 %collective-permute-done.38 = f32[16,1024]{1,0:T(8,128)S(1)} collective-permute-done((f32[16,1024]{1,0:T(8,128)S(1)}, f32[16,1024]{1,0:T(8,128)S(1)}, u32[]{:S(2)}, u32[]{:S(2)}) %collective-permute-start.38) | collective-permute-done | bytes 65568 | tf_op jit(solution)/shard_map/ppermute | solution.py:197
  (131 shorter events, 49.7 us)
Async XLA Ops:
  2.5 9.6 %collective-permute-start = (bf16[32,4224]{1,0:T(8,128)(2,1)}, bf16[32,4224]{1,0:T(8,128)(2,1)S(1)}, u32[]{:S(2)}, u32[]{:S(2)}) collective-permute-start(bf16[32,4224]{1,0:T(8,128)(2,1)} %pack.1), channel_id=1, source_target_pairs={{0,1},{1,0},{2,3},{3,2},{4,5},{5,4},{6,7},{7,6},{8,9},{9,8},{10,11... | collective-permute-start | bytes 811016 | tf_op jit(solution)/shard_map/ppermute | solution.py:185
  13.1 36.0 %collective-permute-start.8 = (bf16[768,1024]{1,0:T(8,128)(2,1)}, bf16[768,1024]{1,0:T(8,128)(2,1)}, u32[]{:S(2)}, u32[]{:S(2)}) collective-permute-start(bf16[768,1024]{1,0:T(8,128)(2,1)} %constant_dynamic-slice_fusion), channel_id=1, source_target_pairs={{0,1},{1,0},{2,3},{3,2},{4,5},{5,4},{6,7},{7,6},{8,9},{9,8},{10,11... | collective-permute-start | bytes 4718600 | tf_op jit(solution)/shard_map/ppermute | solution.py:185
  14.9 14.8 %collective-permute-start.1 = (bf16[64,4224]{1,0:T(8,128)(2,1)S(1)}, bf16[64,4224]{1,0:T(8,128)(2,1)}, u32[]{:S(2)}, u32[]{:S(2)}) collective-permute-start(bf16[64,4224]{1,0:T(8,128)(2,1)S(1)} %pad_maximum_fusion.refs_0_), channel_id=1, source_target_pairs={{0,8},{2,10},{4,12},{6,14},{8,16},{10,18},{12,20},{14,22},{16,24},... | collective-permute-start | bytes 1622024 | tf_op jit(solution)/shard_map/ppermute | solution.py:194
  16.5 13.3 %collective-permute-start.2 = (bf16[64,4224]{1,0:T(8,128)(2,1)S(1)}, bf16[64,4224]{1,0:T(8,128)(2,1)}, u32[]{:S(2)}, u32[]{:S(2)}) collective-permute-start(bf16[64,4224]{1,0:T(8,128)(2,1)S(1)} %pad_maximum_fusion.refs_0_), channel_id=1, source_target_pairs={{0,4},{2,6},{4,0},{6,2},{8,12},{10,14},{12,8},{14,10},{16,20},{18,... | collective-permute-start | bytes 1622024 | tf_op jit(solution)/shard_map/ppermute | solution.py:188
  18.0 11.7 %collective-permute-start.3 = (bf16[64,4224]{1,0:T(8,128)(2,1)S(1)}, bf16[64,4224]{1,0:T(8,128)(2,1)S(1)}, u32[]{:S(2)}, u32[]{:S(2)}) collective-permute-start(bf16[64,4224]{1,0:T(8,128)(2,1)S(1)} %pad_maximum_fusion.refs_0_), channel_id=1, source_target_pairs={{0,2},{2,0},{4,6},{6,4},{8,10},{10,8},{12,14},{14,12},{16,18},{18,... | collective-permute-start | bytes 1622024 | tf_op jit(solution)/shard_map/ppermute | solution.py:191
  30.6 16.8 %collective-permute-start.4 = (bf16[64,4224]{1,0:T(8,128)(2,1)}, bf16[64,4224]{1,0:T(8,128)(2,1)}, u32[]{:S(2)}, u32[]{:S(2)}) collective-permute-start(bf16[64,4224]{1,0:T(8,128)(2,1)} %collective-permute-done.1.refs_0_), channel_id=1, source_target_pairs={{0,8},{2,10},{4,12},{6,14},{8,16},{10,18},{12,20},{14,22},{16,24},... | collective-permute-start | bytes 1622024 | tf_op jit(solution)/shard_map/ppermute | solution.py:194
  31.6 15.8 %collective-permute-start.5 = (bf16[64,4224]{1,0:T(8,128)(2,1)}, bf16[64,4224]{1,0:T(8,128)(2,1)}, u32[]{:S(2)}, u32[]{:S(2)}) collective-permute-start(bf16[64,4224]{1,0:T(8,128)(2,1)} %collective-permute-done.1.refs_0_), channel_id=1, source_target_pairs={{0,4},{2,6},{4,0},{6,2},{8,12},{10,14},{12,8},{14,10},{16,20},{18,... | collective-permute-start | bytes 1622024 | tf_op jit(solution)/shard_map/ppermute | solution.py:188
  33.1 14.3 %collective-permute-start.6 = (bf16[64,4224]{1,0:T(8,128)(2,1)}, bf16[64,4224]{1,0:T(8,128)(2,1)}, u32[]{:S(2)}, u32[]{:S(2)}) collective-permute-start(bf16[64,4224]{1,0:T(8,128)(2,1)} %collective-permute-done.1.refs_0_), channel_id=1, source_target_pairs={{0,2},{2,0},{4,6},{6,4},{8,10},{10,8},{12,14},{14,12},{16,18},{18,... | collective-permute-start | bytes 1622024 | tf_op jit(solution)/shard_map/ppermute | solution.py:191
  49.1 16.7 %collective-permute-start.9 = (bf16[64,4224]{1,0:T(8,128)(2,1)}, bf16[64,4224]{1,0:T(8,128)(2,1)S(1)}, u32[]{:S(2)}, u32[]{:S(2)}) collective-permute-start(bf16[64,4224]{1,0:T(8,128)(2,1)} %collective-permute-done.4.refs_0_), channel_id=1, source_target_pairs={{0,8},{2,10},{4,12},{6,14},{8,16},{10,18},{12,20},{14,22},{16,24},... | collective-permute-start | bytes 1622024 | tf_op jit(solution)/shard_map/ppermute | solution.py:194
  50.8 15.0 %collective-permute-start.10 = (bf16[64,4224]{1,0:T(8,128)(2,1)}, bf16[64,4224]{1,0:T(8,128)(2,1)S(1)}, u32[]{:S(2)}, u32[]{:S(2)}) collective-permute-start(bf16[64,4224]{1,0:T(8,128)(2,1)} %collective-permute-done.4.refs_0_), channel_id=1, source_target_pairs={{0,4},{2,6},{4,0},{6,2},{8,12},{10,14},{12,8},{14,10},{16,20},{18,... | collective-permute-start | bytes 1622024 | tf_op jit(solution)/shard_map/ppermute | solution.py:188
  52.4 13.4 %collective-permute-start.11 = (bf16[64,4224]{1,0:T(8,128)(2,1)}, bf16[64,4224]{1,0:T(8,128)(2,1)S(1)}, u32[]{:S(2)}, u32[]{:S(2)}) collective-permute-start(bf16[64,4224]{1,0:T(8,128)(2,1)} %collective-permute-done.4.refs_0_), channel_id=1, source_target_pairs={{0,2},{2,0},{4,6},{6,4},{8,10},{10,8},{12,14},{14,12},{16,18},{18,... | collective-permute-start | bytes 1622024 | tf_op jit(solution)/shard_map/ppermute | solution.py:191
  52.4 11.5 %collective-permute-start.13 = (bf16[256,768]{1,0:T(8,128)(2,1)S(1)}, bf16[256,768]{1,0:T(8,128)(2,1)S(1)}, u32[]{:S(2)}, u32[]{:S(2)}) collective-permute-start(bf16[256,768]{1,0:T(8,128)(2,1)S(1)} %get-tuple-element.170.refs_4_), channel_id=1, source_target_pairs={{0,1},{1,0},{2,3},{3,2},{4,5},{5,4},{6,7},{7,6},{8,9},{9,8},{10,11... | collective-permute-start | bytes 1179656 | tf_op jit(solution)/shard_map/ppermute | solution.py:185
  65.8 6.5 %collective-permute-start.16 = (bf16[64,4224]{1,0:T(8,128)(2,1)S(1)}, bf16[64,4224]{1,0:T(8,128)(2,1)S(1)}, u32[]{:S(2)}, u32[]{:S(2)}) collective-permute-start(bf16[64,4224]{1,0:T(8,128)(2,1)S(1)} %collective-permute-done.10.refs_1_), channel_id=1, source_target_pairs={{0,2},{2,0},{4,6},{6,4},{8,10},{10,8},{12,14},{14,12},{16,18},{18,... | collective-permute-start | bytes 1622024 | tf_op jit(solution)/shard_map/ppermute | solution.py:191
  65.8 14.7 %collective-permute-start.14 = (bf16[64,4224]{1,0:T(8,128)(2,1)S(1)}, bf16[64,4224]{1,0:T(8,128)(2,1)S(1)}, u32[]{:S(2)}, u32[]{:S(2)}) collective-permute-start(bf16[64,4224]{1,0:T(8,128)(2,1)S(1)} %collective-permute-done.9.refs_0_), channel_id=1, source_target_pairs={{0,4},{2,6},{4,0},{6,2},{8,12},{10,14},{12,8},{14,10},{16,20},{18,... | collective-permute-start | bytes 1622024 | tf_op jit(solution)/shard_map/ppermute | solution.py:188
  67.4 13.1 %collective-permute-start.15 = (bf16[64,4224]{1,0:T(8,128)(2,1)S(1)}, bf16[64,4224]{1,0:T(8,128)(2,1)S(1)}, u32[]{:S(2)}, u32[]{:S(2)}) collective-permute-start(bf16[64,4224]{1,0:T(8,128)(2,1)S(1)} %collective-permute-done.9.refs_0_), channel_id=1, source_target_pairs={{0,2},{2,0},{4,6},{6,4},{8,10},{10,8},{12,14},{14,12},{16,18},{18,... | collective-permute-start | bytes 1622024 | tf_op jit(solution)/shard_map/ppermute | solution.py:191
  67.5 11.4 %collective-permute-start.18 = (bf16[256,768]{1,0:T(8,128)(2,1)S(1)}, bf16[256,768]{1,0:T(8,128)(2,1)S(1)}, u32[]{:S(2)}, u32[]{:S(2)}) collective-permute-start(bf16[256,768]{1,0:T(8,128)(2,1)S(1)} %get-tuple-element.193.refs_4_), channel_id=1, source_target_pairs={{0,1},{1,0},{2,3},{3,2},{4,5},{5,4},{6,7},{7,6},{8,9},{9,8},{10,11... | collective-permute-start | bytes 1179656 | tf_op jit(solution)/shard_map/ppermute | solution.py:185
  85.9 11.9 %collective-permute-start.21 = (bf16[256,768]{1,0:T(8,128)(2,1)S(1)}, bf16[256,768]{1,0:T(8,128)(2,1)S(1)}, u32[]{:S(2)}, u32[]{:S(2)}) collective-permute-start(bf16[256,768]{1,0:T(8,128)(2,1)S(1)} %get-tuple-element.214.refs_4_), channel_id=1, source_target_pairs={{0,1},{1,0},{2,3},{3,2},{4,5},{5,4},{6,7},{7,6},{8,9},{9,8},{10,11... | collective-permute-start | bytes 1179656 | tf_op jit(solution)/shard_map/ppermute | solution.py:185
  90.2 7.6 %collective-permute-start.22 = (bf16[2,32,1152]{2,1,0:T(8,128)(2,1)S(1)}, bf16[2,32,1152]{2,1,0:T(8,128)(2,1)S(1)}, u32[]{:S(2)}, u32[]{:S(2)}) collective-permute-start(bf16[2,32,1152]{2,1,0:T(8,128)(2,1)S(1)} %fusion.10), channel_id=1, source_target_pairs={{0,4},{2,6},{4,0},{6,2},{8,12},{10,14},{12,8},{14,10},{16,20},{18,... | collective-permute-start | bytes 442376 | tf_op jit(solution)/shard_map/ppermute | solution.py:188
  91.8 14.9 %collective-permute-start.24 = (bf16[256,768]{1,0:T(8,128)(2,1)S(1)}, bf16[256,768]{1,0:T(8,128)(2,1)S(1)}, u32[]{:S(2)}, u32[]{:S(2)}) collective-permute-start(bf16[256,768]{1,0:T(8,128)(2,1)S(1)} %get-tuple-element.238.refs_4_), channel_id=1, source_target_pairs={{0,1},{1,0},{2,3},{3,2},{4,5},{5,4},{6,7},{7,6},{8,9},{9,8},{10,11... | collective-permute-start | bytes 1179656 | tf_op jit(solution)/shard_map/ppermute | solution.py:185
  92.4 14.4 %collective-permute-start.25 = (bf16[2,32,1152]{2,1,0:T(8,128)(2,1)S(1)}, bf16[2,32,1152]{2,1,0:T(8,128)(2,1)S(1)}, u32[]{:S(2)}, u32[]{:S(2)}) collective-permute-start(bf16[2,32,1152]{2,1,0:T(8,128)(2,1)S(1)} %fusion.11), channel_id=1, source_target_pairs={{0,4},{2,6},{4,0},{6,2},{8,12},{10,14},{12,8},{14,10},{16,20},{18,... | collective-permute-start | bytes 442376 | tf_op jit(solution)/shard_map/ppermute | solution.py:188
  100.9 11.6 %collective-permute-start.33 = (bf16[2,32,1152]{2,1,0:T(8,128)(2,1)S(1)}, bf16[2,32,1152]{2,1,0:T(8,128)(2,1)S(1)}, u32[]{:S(2)}, u32[]{:S(2)}) collective-permute-start(bf16[2,32,1152]{2,1,0:T(8,128)(2,1)S(1)} %fusion.5), channel_id=1, source_target_pairs={{0,8},{2,10},{4,12},{6,14},{8,16},{10,18},{12,20},{14,22},{16,24},... | collective-permute-start | bytes 442376 | tf_op jit(solution)/shard_map/ppermute | solution.py:194
  112.9 10.1 %collective-permute-start.34 = (bf16[2,32,1152]{2,1,0:T(8,128)(2,1)S(1)}, bf16[2,32,1152]{2,1,0:T(8,128)(2,1)S(1)}, u32[]{:S(2)}, u32[]{:S(2)}) collective-permute-start(bf16[2,32,1152]{2,1,0:T(8,128)(2,1)S(1)} %fusion.4), channel_id=1, source_target_pairs={{0,8},{2,10},{4,12},{6,14},{8,16},{10,18},{12,20},{14,22},{16,24},... | collective-permute-start | bytes 442376 | tf_op jit(solution)/shard_map/ppermute | solution.py:194
  114.6 8.5 %collective-permute-start.32 = (bf16[2,32,1152]{2,1,0:T(8,128)(2,1)S(1)}, bf16[2,32,1152]{2,1,0:T(8,128)(2,1)S(1)}, u32[]{:S(2)}, u32[]{:S(2)}) collective-permute-start(bf16[2,32,1152]{2,1,0:T(8,128)(2,1)S(1)} %fusion.13), channel_id=1, source_target_pairs={{0,4},{2,6},{4,0},{6,2},{8,12},{10,14},{12,8},{14,10},{16,20},{18,... | collective-permute-start | bytes 442376 | tf_op jit(solution)/shard_map/ppermute | solution.py:188
  123.1 7.8 %collective-permute-start.36 = (bf16[2,32,1152]{2,1,0:T(8,128)(2,1)S(1)}, bf16[2,32,1152]{2,1,0:T(8,128)(2,1)S(1)}, u32[]{:S(2)}, u32[]{:S(2)}) collective-permute-start(bf16[2,32,1152]{2,1,0:T(8,128)(2,1)S(1)} %fusion.2), channel_id=1, source_target_pairs={{0,8},{2,10},{4,12},{6,14},{8,16},{10,18},{12,20},{14,22},{16,24},... | collective-permute-start | bytes 442376 | tf_op jit(solution)/shard_map/ppermute | solution.py:194
  (33 other events, 317.7 us)

commit v6 on v5

--- a/solution.py
+++ b/solution.py
@@ -275,8 +275,6 @@
     state.update(grads=grads, other=other)
     d_own, d_got, totals, sent, value = {}, {}, {}, {}, {}
     state.update(d_own=d_own, d_got=d_got, totals=totals, sent=sent, value=value)
-    near[0], w_send = fence((near[0], w_send))
-    w_far[0] = go_x(w_send)
 
     def make_down(held):
         return pl.pallas_call(
@@ -327,12 +325,15 @@
         near[k + 1] = go_z(near[k])
         far[k] = go_y(near[k])
         near_c[k] = go_core(near[k])
-        if k:
+        if k == 0:
+            w_send, near_c[0] = fence((w_send, near_c[0]))
+            w_far[0] = go_x(w_send)
+        else:
             far_c[k - 1] = go_core(far[k - 1])
             rows_of(k - 1)
         if k == 2:
             other[0] = go_x(grads[0])
-        step(*([("w", 0)] if k == 0 else []))
+        step(*([("w", 0)] if k < 2 else []))
     other[1] = go_x(grads[1])
     far[3] = go_y(near[3])
     near_c[3] = go_core(near[3])
@@ -342,19 +343,17 @@
     step()
     other[2] = go_x(grads[2])
     far_c[3] = go_core(far[3])
+    send_y(0)
     rows_of(3)
-    other[1], far_c[3] = fence((other[1], far_c[3]))
+    other[1], grads[3] = fence((other[1], grads[3]))
     grads_of(1)
-    step(("other", 2))
+    step()
     other[3] = go_x(grads[3])
     send_y(1)
-    send_y(0)
-    other[2], sent[1], kept[3] = fence((other[2], sent[1], kept[3]))
+    other[2], sent[1] = fence((other[2], sent[1]))
     grads_of(2)
     hop(1)
     send_y(2)
-    down = {0: make_down([kept[k] for k in range(planes)])}
-    state["down"] = down
     step(("sent", 2), ("value", 2))
     grads_of(3)
     hop(2)
@@ -368,8 +367,11 @@
     mine_sums = part + go_y(part)
     cross_sums = go_x(part) + go_far(part, 2)
     pool[0] = jnp.concatenate([mine_sums, cross_sums], axis=0)
-    step()
+    step(("pool", 0))
     hop(3)
+    kept[3], value[3] = fence((kept[3], value[3]))
+    down = {0: make_down([kept[k] for k in range(planes)])}
+    state["down"] = down
     pool[0] = pool[0] + go_jump(pool[0], 4)
     step()
     final = total_of(0) + value[0].astype(f32)

time: 140 us -> 145 us (1.036)
  local copies, waits for them, and re-layouts: 8.82 us -> 12.5 us
  other arithmetic: 3.69 us -> 6.91 us
  starting transfers between devices: 37.4 us -> 34.6 us
    ppermute x9, waiting for transfers between devices: 3.28 us -> 11.8 us  [go_y(): return lax.ppermute(v, 'expert', [(e, e ^ 2) for e in range(experts)])]
    ppermute x6, waiting for transfers between devices: 21.9 us -> 17.4 us  [go_z(): lax.ppermute(v, 'expert', [(e, (e + 4) % experts) for e in range(experts)])]
    unnamed x37 -> x43, local copies, waits for them, and re-layouts: 5.84 us -> 9.51 us
    ppermute x8, waiting for transfers between devices: 19.1 us -> 16.4 us  [go_x(): return lax.ppermute(v, 'dp', [(0, 1), (1, 0)])]
    convert_element_type x3, other arithmetic: 0.21 us -> 1.86 us  [hop(): value[(k + 1) % planes] = go_z(carried.astype(bf16))]
    ppermute x2, starting transfers between devices: 3.34 us -> 1.84 us  [go_jump(): return lax.ppermute(v, 'expert', [(e, e ^ by) for e in range(experts)])]
    ppermute x13, waiting for transfers between devices: 2.66 us -> 1.16 us  [go_core(): return lax.ppermute(v, 'expert', [(e, e ^ 1) for e in range(experts)])]
  transfers between devices with their start and end apart: 39 -> 39, of which waited for: 17 -> 16; matrix products, arithmetic and copies ran while one was open for 3% -> 5% of each run, Pallas kernels for 20% -> 22%
where the time goes in v6:
time: 145 us; the launch traced here: 144 us
  waiting for transfers between devices  54.6 us (38%)
  starting transfers between devices  34.6 us (24%)
  Pallas kernels  33.7 us (23%)
  local copies, waits for them, and re-layouts  12.5 us (9%)
  other arithmetic  6.91 us (5%)
  between operations  1.68 us (1%)
    ppermute x6, waiting for transfers between devices, go_z(): lax.ppermute(v, 'expert', [(e, (e + 4) % experts) for e in range(experts)])  17.4 us
    ppermute x8, waiting for transfers between devices, go_x(): return lax.ppermute(v, 'dp', [(0, 1), (1, 0)])  16.4 us
    pallas_call x4, Pallas kernels, first_half(): pl.pallas_call(functools.partial(rows_kernel, segments, width, hidden), o...  15.1 us
    ppermute x8, starting transfers between devices, go_x(): return lax.ppermute(v, 'dp', [(0, 1), (1, 0)])  12.5 us
    pallas_call x4, Pallas kernels, second_half(): pl.pallas_call(functools.partial(grad_kernel, segments, half), out_shape=...  12.2 us
    ppermute x9, waiting for transfers between devices, go_y(): return lax.ppermute(v, 'expert', [(e, e ^ 2) for e in range(experts)])  11.8 us
    ppermute x9, starting transfers between devices, go_y(): return lax.ppermute(v, 'expert', [(e, e ^ 2) for e in range(experts)])  10.8 us
    unnamed x43, local copies, waits for them, and re-layouts  9.51 us
  transfers between devices with their start and end apart: 39, of which 16 were waited for; matrix products, arithmetic and copies ran while one was open for 5% of the time, Pallas kernels for 22%

profile of v6, /device:TPU:0, one launch (start us, length us, event | category | flops | bytes accessed | tf_op | source)
XLA Modules:
  0.0 144.0 jit_solution(15709866829730606616)
XLA Ops:
  0.6 1.9 %pack.1 = bf16[32,4224]{1,0:T(8,128)(2,1)} custom-call(bf16[32,2048]{1,0:T(8,128)(2,1)} %bitcast.90, bf16[32,2048]{1,0:T(8,128)(2,1)} %bitcast.91, s32[8,32]{1,0:T(8,128)} %bitcast.94, bf16[8,32]{1,0:T(8,128)(2,1)} %bitcast.98), custom_call_target="tpu_custom_call" | custom-call | tf_op jit(solution)/shard_map/pack/pallas_call | solution.py:207
  2.5 2.9 %collective-permute-start = (bf16[32,4224]{1,0:T(8,128)(2,1)}, bf16[32,4224]{1,0:T(8,128)(2,1)S(1)}, u32[]{:S(2)}, u32[]{:S(2)}) collective-permute-start(bf16[32,4224]{1,0:T(8,128)(2,1)} %pack.1), channel_id=1, source_target_pairs={{0,1},{1,0},{2,3},{3,2},{4,5},{5,4},{6,7},{7,6},{8,9},{9,8},{10,11... | collective-permute-start | bytes 811016 | tf_op jit(solution)/shard_map/ppermute | solution.py:185
  5.4 6.7 %collective-permute-done = bf16[32,4224]{1,0:T(8,128)(2,1)S(1)} collective-permute-done((bf16[32,4224]{1,0:T(8,128)(2,1)}, bf16[32,4224]{1,0:T(8,128)(2,1)S(1)}, u32[]{:S(2)}, u32[]{:S(2)}) %collective-permute-start) | collective-permute-done | bytes 270368 | tf_op jit(solution)/shard_map/ppermute | solution.py:185
  13.9 1.8 %collective-permute-start.1 = (bf16[64,4224]{1,0:T(8,128)(2,1)}, bf16[64,4224]{1,0:T(8,128)(2,1)}, u32[]{:S(2)}, u32[]{:S(2)}) collective-permute-start(bf16[64,4224]{1,0:T(8,128)(2,1)} %pad_maximum_fusion.refs_0_), channel_id=1, source_target_pairs={{0,8},{2,10},{4,12},{6,14},{8,16},{10,18},{12,20},{14,22},{16,24},... | collective-permute-start | bytes 1622024 | tf_op jit(solution)/shard_map/ppermute | solution.py:194
  17.3 2.8 %constant_dynamic-slice_fusion = bf16[768,1024]{1,0:T(8,128)(2,1)} fusion(bf16[768,2048]{1,0:T(8,128)(2,1)} %bitcast.68, s32[]{:T(128)S(6)} %select_n.32), kind=kLoop, calls=%fused_computation.42 | loop fusion | bytes 3145732 | tf_op jit(solution)/shard_map/dynamic_slice | solution.py:222
  21.6 9.4 %collective-permute-done.1.refs_0_ = bf16[64,4224]{1,0:T(8,128)(2,1)} collective-permute-done((bf16[64,4224]{1,0:T(8,128)(2,1)}, bf16[64,4224]{1,0:T(8,128)(2,1)}, u32[]{:S(2)}, u32[]{:S(2)}) %collective-permute-start.1) | collective-permute-done | bytes 540704 | tf_op jit(solution)/shard_map/ppermute | solution.py:194
  35.7 4.4 %rows.4 = (bf16[256,768]{1,0:T(8,128)(2,1)S(1)}, bf16[256,2432]{1,0:T(8,128)(2,1)S(1)}, bf16[256,128]{1,0:T(8,128)(2,1)S(1)}) custom-call(bf16[64,4224]{1,0:T(8,128)(2,1)} %pad_maximum_fusion.refs_0_, bf16[64,4224]{1,0:T(8,128)(2,1)} %collective-permute-done.2.refs_1_, bf16[64,4224]{1,0:T(8,128)(2,1)} %collective-permute-done.3.refs_2_, ...), custom_call_target="tpu_custom_call" | custom-call | tf_op jit(solution)/shard_map/rows/pallas_call | solution.py:232
  41.2 6.7 %collective-permute-done.4.refs_0_ = bf16[64,4224]{1,0:T(8,128)(2,1)} collective-permute-done((bf16[64,4224]{1,0:T(8,128)(2,1)}, bf16[64,4224]{1,0:T(8,128)(2,1)}, u32[]{:S(2)}, u32[]{:S(2)}) %collective-permute-start.4) | collective-permute-done | bytes 540704 | tf_op jit(solution)/shard_map/ppermute | solution.py:194
  51.9 4.1 %rows.5 = (bf16[256,768]{1,0:T(8,128)(2,1)S(1)}, bf16[256,2432]{1,0:T(8,128)(2,1)S(1)}, bf16[256,128]{1,0:T(8,128)(2,1)S(1)}) custom-call(bf16[64,4224]{1,0:T(8,128)(2,1)} %collective-permute-done.1.refs_0_, bf16[64,4224]{1,0:T(8,128)(2,1)} %collective-permute-done.5.refs_1_, bf16[64,4224]{1,0:T(8,128)(2,1)} %collective-permute-done.6.refs_2_, ...), custom_call_target="tpu_custom_call" | custom-call | tf_op jit(solution)/shard_map/rows/pallas_call | solution.py:232
  57.1 7.9 %collective-permute-done.12.refs_5_ = bf16[256,768]{1,0:T(8,128)(2,1)S(1)} collective-permute-done((bf16[256,768]{1,0:T(8,128)(2,1)S(1)}, bf16[256,768]{1,0:T(8,128)(2,1)S(1)}, u32[]{:S(2)}, u32[]{:S(2)}) %collective-permute-start.12) | collective-permute-done | bytes 393248 | tf_op jit(solution)/shard_map/ppermute | solution.py:185
  67.9 3.4 %grads.4 = (bf16[2,2,32,1152]{3,2,1,0:T(8,128)(2,1)S(1)}, bf16[2,2,32,1152]{3,2,1,0:T(8,128)(2,1)S(1)}, f32[8,1024]{1,0:T(8,128)S(1)}) custom-call(bf16[64,4224]{1,0:T(8,128)(2,1)} %pad_maximum_fusion.refs_0_, bf16[64,4224]{1,0:T(8,128)(2,1)} %collective-permute-done.2.refs_1_, bf16[64,4224]{1,0:T(8,128)(2,1)} %collective-permute-done.3.refs_2_, ...), custom_call_target="tpu_custom_call" | custom-call | tf_op jit(solution)/shard_map/grads/pallas_call | solution.py:253
  71.4 3.8 %rows.6 = (bf16[256,768]{1,0:T(8,128)(2,1)S(1)}, bf16[256,2432]{1,0:T(8,128)(2,1)S(1)}, bf16[256,128]{1,0:T(8,128)(2,1)S(1)}) custom-call(bf16[64,4224]{1,0:T(8,128)(2,1)} %collective-permute-done.4.refs_0_, bf16[64,4224]{1,0:T(8,128)(2,1)S(1)} %collective-permute-done.9.refs_1_, bf16[64,4224]{1,0:T(8,128)(2,1)S(1)} %collective-permute-done.10.refs_2_, ...), custom_call_target="tpu_custom_call" | custom-call | tf_op jit(solution)/shard_map/rows/pallas_call | solution.py:232
  77.8 2.0 %collective-permute-done.14.refs_1_ = bf16[64,4224]{1,0:T(8,128)(2,1)S(1)} collective-permute-done((bf16[64,4224]{1,0:T(8,128)(2,1)S(1)}, bf16[64,4224]{1,0:T(8,128)(2,1)S(1)}, u32[]{:S(2)}, u32[]{:S(2)}) %collective-permute-start.14) | collective-permute-done | bytes 540704 | tf_op jit(solution)/shard_map/ppermute | solution.py:188
  81.7 2.8 %rows.7 = (bf16[256,768]{1,0:T(8,128)(2,1)S(1)}, bf16[256,2432]{1,0:T(8,128)(2,1)S(1)}, bf16[256,128]{1,0:T(8,128)(2,1)S(1)}) custom-call(bf16[64,4224]{1,0:T(8,128)(2,1)S(1)} %collective-permute-done.8.refs_0_, bf16[64,4224]{1,0:T(8,128)(2,1)S(1)} %collective-permute-done.14.refs_1_, bf16[64,4224]{1,0:T(8,128)(2,1)S(1)} %collective-permute-done.15.refs_2_, ...), custom_call_target="tpu_custom_call" | custom-call | tf_op jit(solution)/shard_map/rows/pallas_call | solution.py:232
  85.6 3.2 %grads.5 = (bf16[2,2,32,1152]{3,2,1,0:T(8,128)(2,1)S(1)}, bf16[2,2,32,1152]{3,2,1,0:T(8,128)(2,1)S(1)}, f32[8,1024]{1,0:T(8,128)S(1)}) custom-call(bf16[64,4224]{1,0:T(8,128)(2,1)} %collective-permute-done.1.refs_0_, bf16[64,4224]{1,0:T(8,128)(2,1)} %collective-permute-done.5.refs_1_, bf16[64,4224]{1,0:T(8,128)(2,1)} %collective-permute-done.6.refs_2_, ...), custom_call_target="tpu_custom_call" | custom-call | tf_op jit(solution)/shard_map/grads/pallas_call | solution.py:253
  90.2 5.0 %collective-permute-done.22 = bf16[2,32,1152]{2,1,0:T(8,128)(2,1)S(1)} collective-permute-done((bf16[2,32,1152]{2,1,0:T(8,128)(2,1)S(1)}, bf16[2,32,1152]{2,1,0:T(8,128)(2,1)S(1)}, u32[]{:S(2)}, u32[]{:S(2)}) %collective-permute-start.22) | collective-permute-done | bytes 147488 | tf_op jit(solution)/shard_map/ppermute | solution.py:188
  98.5 2.7 %collective-permute-done.23 = bf16[2,32,1152]{2,1,0:T(8,128)(2,1)S(1)} collective-permute-done((bf16[2,32,1152]{2,1,0:T(8,128)(2,1)S(1)}, bf16[2,32,1152]{2,1,0:T(8,128)(2,1)S(1)}, u32[]{:S(2)}, u32[]{:S(2)}) %collective-permute-start.23) | collective-permute-done | bytes 147488 | tf_op jit(solution)/shard_map/ppermute | solution.py:188
  101.2 2.9 %grads.6 = (bf16[2,2,32,1152]{3,2,1,0:T(8,128)(2,1)S(1)}, bf16[2,2,32,1152]{3,2,1,0:T(8,128)(2,1)S(1)}, f32[8,1024]{1,0:T(8,128)S(1)}) custom-call(bf16[64,4224]{1,0:T(8,128)(2,1)} %collective-permute-done.4.refs_0_, bf16[64,4224]{1,0:T(8,128)(2,1)S(1)} %collective-permute-done.9.refs_1_, bf16[64,4224]{1,0:T(8,128)(2,1)S(1)} %collective-permute-done.10.refs_2_, ...), custom_call_target="tpu_custom_call" | custom-call | tf_op jit(solution)/shard_map/grads/pallas_call | solution.py:253
  104.3 1.9 %collective-permute-start.30 = (bf16[2,32,1152]{2,1,0:T(8,128)(2,1)S(1)}, bf16[2,32,1152]{2,1,0:T(8,128)(2,1)S(1)}, u32[]{:S(2)}, u32[]{:S(2)}) collective-permute-start(bf16[2,32,1152]{2,1,0:T(8,128)(2,1)S(1)} %fusion.5), channel_id=1, source_target_pairs={{0,8},{2,10},{4,12},{6,14},{8,16},{10,18},{12,20},{14,22},{16,24},... | collective-permute-start | bytes 442376 | tf_op jit(solution)/shard_map/ppermute | solution.py:194
  107.3 2.7 %grads.7 = (bf16[2,2,32,1152]{3,2,1,0:T(8,128)(2,1)S(1)}, bf16[2,2,32,1152]{3,2,1,0:T(8,128)(2,1)S(1)}, f32[8,1024]{1,0:T(8,128)S(1)}) custom-call(bf16[64,4224]{1,0:T(8,128)(2,1)S(1)} %collective-permute-done.8.refs_0_, bf16[64,4224]{1,0:T(8,128)(2,1)S(1)} %collective-permute-done.14.refs_1_, bf16[64,4224]{1,0:T(8,128)(2,1)S(1)} %collective-permute-done.15.refs_2_, ...), custom_call_target="tpu_custom_call" | custom-call | tf_op jit(solution)/shard_map/grads/pallas_call | solution.py:253
  118.7 1.9 %collective-permute-done.32 = f32[8,1024]{1,0:T(8,128)} collective-permute-done((f32[8,1024]{1,0:T(8,128)S(1)}, f32[8,1024]{1,0:T(8,128)}, u32[]{:S(2)}, u32[]{:S(2)}) %collective-permute-start.32) | collective-permute-done | bytes 32800 | tf_op jit(solution)/shard_map/ppermute | solution.py:188
  126.2 2.4 %collective-permute-done.35 = f32[16,1024]{1,0:T(8,128)S(1)} collective-permute-done((f32[16,1024]{1,0:T(8,128)S(1)}, f32[16,1024]{1,0:T(8,128)S(1)}, u32[]{:S(2)}, u32[]{:S(2)}) %collective-permute-start.35) | collective-permute-done | bytes 65568 | tf_op jit(solution)/shard_map/ppermute | solution.py:197
  131.3 4.6 %down.1 = bf16[384,2048]{1,0:T(8,128)(2,1)} custom-call(bf16[256,2432]{1,0:T(8,128)(2,1)S(1)} %copy-done.4, bf16[256,2432]{1,0:T(8,128)(2,1)S(1)} %copy-done.6, bf16[256,2432]{1,0:T(8,128)(2,1)S(1)} %copy-done.8, bf16[256,2432]{1,0:T(8,128)(2,1)S(1)} %copy-done.10), custom_call_target="tpu_custom_call" | custom-call | tf_op jit(solution)/shard_map/down/pallas_call | solution.py:280
  137.2 3.9 %collective-permute-done.38 = f32[16,1024]{1,0:T(8,128)S(1)} collective-permute-done((f32[16,1024]{1,0:T(8,128)S(1)}, f32[16,1024]{1,0:T(8,128)S(1)}, u32[]{:S(2)}, u32[]{:S(2)}) %collective-permute-start.38) | collective-permute-done | bytes 65568 | tf_op jit(solution)/shard_map/ppermute | solution.py:197
  (137 shorter events, 50.4 us)
Async XLA Ops:
  2.5 9.6 %collective-permute-start = (bf16[32,4224]{1,0:T(8,128)(2,1)}, bf16[32,4224]{1,0:T(8,128)(2,1)S(1)}, u32[]{:S(2)}, u32[]{:S(2)}) collective-permute-start(bf16[32,4224]{1,0:T(8,128)(2,1)} %pack.1), channel_id=1, source_target_pairs={{0,1},{1,0},{2,3},{3,2},{4,5},{5,4},{6,7},{7,6},{8,9},{9,8},{10,11... | collective-permute-start | bytes 811016 | tf_op jit(solution)/shard_map/ppermute | solution.py:185
  13.9 17.1 %collective-permute-start.1 = (bf16[64,4224]{1,0:T(8,128)(2,1)}, bf16[64,4224]{1,0:T(8,128)(2,1)}, u32[]{:S(2)}, u32[]{:S(2)}) collective-permute-start(bf16[64,4224]{1,0:T(8,128)(2,1)} %pad_maximum_fusion.refs_0_), channel_id=1, source_target_pairs={{0,8},{2,10},{4,12},{6,14},{8,16},{10,18},{12,20},{14,22},{16,24},... | collective-permute-start | bytes 1622024 | tf_op jit(solution)/shard_map/ppermute | solution.py:194
  15.8 15.3 %collective-permute-start.2 = (bf16[64,4224]{1,0:T(8,128)(2,1)}, bf16[64,4224]{1,0:T(8,128)(2,1)}, u32[]{:S(2)}, u32[]{:S(2)}) collective-permute-start(bf16[64,4224]{1,0:T(8,128)(2,1)} %pad_maximum_fusion.refs_0_), channel_id=1, source_target_pairs={{0,4},{2,6},{4,0},{6,2},{8,12},{10,14},{12,8},{14,10},{16,20},{18,... | collective-permute-start | bytes 1622024 | tf_op jit(solution)/shard_map/ppermute | solution.py:188
  20.1 44.9 %collective-permute-start.13 = (bf16[768,1024]{1,0:T(8,128)(2,1)}, bf16[768,1024]{1,0:T(8,128)(2,1)}, u32[]{:S(2)}, u32[]{:S(2)}) collective-permute-start(bf16[768,1024]{1,0:T(8,128)(2,1)} %constant_dynamic-slice_fusion), channel_id=1, source_target_pairs={{0,1},{1,0},{2,3},{3,2},{4,5},{5,4},{6,7},{7,6},{8,9},{9,8},{10,11... | collective-permute-start | bytes 4718600 | tf_op jit(solution)/shard_map/ppermute | solution.py:185
  31.1 16.8 %collective-permute-start.4 = (bf16[64,4224]{1,0:T(8,128)(2,1)}, bf16[64,4224]{1,0:T(8,128)(2,1)}, u32[]{:S(2)}, u32[]{:S(2)}) collective-permute-start(bf16[64,4224]{1,0:T(8,128)(2,1)} %collective-permute-done.1.refs_0_), channel_id=1, source_target_pairs={{0,8},{2,10},{4,12},{6,14},{8,16},{10,18},{12,20},{14,22},{16,24},... | collective-permute-start | bytes 1622024 | tf_op jit(solution)/shard_map/ppermute | solution.py:194
  32.1 15.8 %collective-permute-start.5 = (bf16[64,4224]{1,0:T(8,128)(2,1)}, bf16[64,4224]{1,0:T(8,128)(2,1)}, u32[]{:S(2)}, u32[]{:S(2)}) collective-permute-start(bf16[64,4224]{1,0:T(8,128)(2,1)} %collective-permute-done.1.refs_0_), channel_id=1, source_target_pairs={{0,4},{2,6},{4,0},{6,2},{8,12},{10,14},{12,8},{14,10},{16,20},{18,... | collective-permute-start | bytes 1622024 | tf_op jit(solution)/shard_map/ppermute | solution.py:188
  33.6 14.3 %collective-permute-start.6 = (bf16[64,4224]{1,0:T(8,128)(2,1)}, bf16[64,4224]{1,0:T(8,128)(2,1)}, u32[]{:S(2)}, u32[]{:S(2)}) collective-permute-start(bf16[64,4224]{1,0:T(8,128)(2,1)} %collective-permute-done.1.refs_0_), channel_id=1, source_target_pairs={{0,2},{2,0},{4,6},{6,4},{8,10},{10,8},{12,14},{14,12},{16,18},{18,... | collective-permute-start | bytes 1622024 | tf_op jit(solution)/shard_map/ppermute | solution.py:191
  47.9 17.1 %collective-permute-start.10 = (bf16[64,4224]{1,0:T(8,128)(2,1)}, bf16[64,4224]{1,0:T(8,128)(2,1)S(1)}, u32[]{:S(2)}, u32[]{:S(2)}) collective-permute-start(bf16[64,4224]{1,0:T(8,128)(2,1)} %collective-permute-done.4.refs_0_), channel_id=1, source_target_pairs={{0,2},{2,0},{4,6},{6,4},{8,10},{10,8},{12,14},{14,12},{16,18},{18,... | collective-permute-start | bytes 1622024 | tf_op jit(solution)/shard_map/ppermute | solution.py:191
  48.4 16.6 %collective-permute-start.8 = (bf16[64,4224]{1,0:T(8,128)(2,1)}, bf16[64,4224]{1,0:T(8,128)(2,1)S(1)}, u32[]{:S(2)}, u32[]{:S(2)}) collective-permute-start(bf16[64,4224]{1,0:T(8,128)(2,1)} %collective-permute-done.4.refs_0_), channel_id=1, source_target_pairs={{0,8},{2,10},{4,12},{6,14},{8,16},{10,18},{12,20},{14,22},{16,24},... | collective-permute-start | bytes 1622024 | tf_op jit(solution)/shard_map/ppermute | solution.py:194
  48.9 16.1 %collective-permute-start.9 = (bf16[64,4224]{1,0:T(8,128)(2,1)}, bf16[64,4224]{1,0:T(8,128)(2,1)S(1)}, u32[]{:S(2)}, u32[]{:S(2)}) collective-permute-start(bf16[64,4224]{1,0:T(8,128)(2,1)} %collective-permute-done.4.refs_0_), channel_id=1, source_target_pairs={{0,4},{2,6},{4,0},{6,2},{8,12},{10,14},{12,8},{14,10},{16,20},{18,... | collective-permute-start | bytes 1622024 | tf_op jit(solution)/shard_map/ppermute | solution.py:188
  50.4 14.6 %collective-permute-start.12 = (bf16[256,768]{1,0:T(8,128)(2,1)S(1)}, bf16[256,768]{1,0:T(8,128)(2,1)S(1)}, u32[]{:S(2)}, u32[]{:S(2)}) collective-permute-start(bf16[256,768]{1,0:T(8,128)(2,1)S(1)} %get-tuple-element.166.refs_4_), channel_id=1, source_target_pairs={{0,1},{1,0},{2,3},{3,2},{4,5},{5,4},{6,7},{7,6},{8,9},{9,8},{10,11... | collective-permute-start | bytes 1179656 | tf_op jit(solution)/shard_map/ppermute | solution.py:185
  65.0 6.4 %collective-permute-start.16 = (bf16[64,4224]{1,0:T(8,128)(2,1)S(1)}, bf16[64,4224]{1,0:T(8,128)(2,1)S(1)}, u32[]{:S(2)}, u32[]{:S(2)}) collective-permute-start(bf16[64,4224]{1,0:T(8,128)(2,1)S(1)} %collective-permute-done.9.refs_1_), channel_id=1, source_target_pairs={{0,2},{2,0},{4,6},{6,4},{8,10},{10,8},{12,14},{14,12},{16,18},{18,... | collective-permute-start | bytes 1622024 | tf_op jit(solution)/shard_map/ppermute | solution.py:191
  65.1 14.7 %collective-permute-start.14 = (bf16[64,4224]{1,0:T(8,128)(2,1)S(1)}, bf16[64,4224]{1,0:T(8,128)(2,1)S(1)}, u32[]{:S(2)}, u32[]{:S(2)}) collective-permute-start(bf16[64,4224]{1,0:T(8,128)(2,1)S(1)} %collective-permute-done.8.refs_0_), channel_id=1, source_target_pairs={{0,4},{2,6},{4,0},{6,2},{8,12},{10,14},{12,8},{14,10},{16,20},{18,... | collective-permute-start | bytes 1622024 | tf_op jit(solution)/shard_map/ppermute | solution.py:188
  66.2 13.6 %collective-permute-start.15 = (bf16[64,4224]{1,0:T(8,128)(2,1)S(1)}, bf16[64,4224]{1,0:T(8,128)(2,1)S(1)}, u32[]{:S(2)}, u32[]{:S(2)}) collective-permute-start(bf16[64,4224]{1,0:T(8,128)(2,1)S(1)} %collective-permute-done.8.refs_0_), channel_id=1, source_target_pairs={{0,2},{2,0},{4,6},{6,4},{8,10},{10,8},{12,14},{14,12},{16,18},{18,... | collective-permute-start | bytes 1622024 | tf_op jit(solution)/shard_map/ppermute | solution.py:191
  66.4 11.4 %collective-permute-start.18 = (bf16[256,768]{1,0:T(8,128)(2,1)S(1)}, bf16[256,768]{1,0:T(8,128)(2,1)S(1)}, u32[]{:S(2)}, u32[]{:S(2)}) collective-permute-start(bf16[256,768]{1,0:T(8,128)(2,1)S(1)} %get-tuple-element.187.refs_4_), channel_id=1, source_target_pairs={{0,1},{1,0},{2,3},{3,2},{4,5},{5,4},{6,7},{7,6},{8,9},{9,8},{10,11... | collective-permute-start | bytes 1179656 | tf_op jit(solution)/shard_map/ppermute | solution.py:185
  79.8 15.5 %collective-permute-start.21 = (bf16[256,768]{1,0:T(8,128)(2,1)S(1)}, bf16[256,768]{1,0:T(8,128)(2,1)S(1)}, u32[]{:S(2)}, u32[]{:S(2)}) collective-permute-start(bf16[256,768]{1,0:T(8,128)(2,1)S(1)} %get-tuple-element.210.refs_4_), channel_id=1, source_target_pairs={{0,1},{1,0},{2,3},{3,2},{4,5},{5,4},{6,7},{7,6},{8,9},{9,8},{10,11... | collective-permute-start | bytes 1179656 | tf_op jit(solution)/shard_map/ppermute | solution.py:185
  88.8 6.4 %collective-permute-start.20 = (bf16[2,2,32,1152]{3,2,0,1:T(8,128)(2,1)S(1)}, bf16[2,2,32,1152]{3,2,0,1:T(8,128)(2,1)S(1)}, u32[]{:S(2)}, u32[]{:S(2)}) collective-permute-start(bf16[2,2,32,1152]{3,2,0,1:T(8,128)(2,1)S(1)} %copy.28), channel_id=1, source_target_pairs={{0,2},{2,0},{4,6},{6,4},{8,10},{10,8},{12,14},{14,12},{16,18},{18,... | collective-permute-start | bytes 884744 | tf_op jit(solution)/shard_map/ppermute | solution.py:191
  89.1 6.2 %collective-permute-start.22 = (bf16[2,32,1152]{2,1,0:T(8,128)(2,1)S(1)}, bf16[2,32,1152]{2,1,0:T(8,128)(2,1)S(1)}, u32[]{:S(2)}, u32[]{:S(2)}) collective-permute-start(bf16[2,32,1152]{2,1,0:T(8,128)(2,1)S(1)} %fusion.10), channel_id=1, source_target_pairs={{0,4},{2,6},{4,0},{6,2},{8,12},{10,14},{12,8},{14,10},{16,20},{18,... | collective-permute-start | bytes 442376 | tf_op jit(solution)/shard_map/ppermute | solution.py:188
  97.0 10.3 %collective-permute-start.25 = (bf16[256,768]{1,0:T(8,128)(2,1)S(1)}, bf16[256,768]{1,0:T(8,128)(2,1)S(1)}, u32[]{:S(2)}, u32[]{:S(2)}) collective-permute-start(bf16[256,768]{1,0:T(8,128)(2,1)S(1)} %get-tuple-element.231.refs_4_), channel_id=1, source_target_pairs={{0,1},{1,0},{2,3},{3,2},{4,5},{5,4},{6,7},{7,6},{8,9},{9,8},{10,11... | collective-permute-start | bytes 1179656 | tf_op jit(solution)/shard_map/ppermute | solution.py:185
  104.3 8.3 %collective-permute-start.30 = (bf16[2,32,1152]{2,1,0:T(8,128)(2,1)S(1)}, bf16[2,32,1152]{2,1,0:T(8,128)(2,1)S(1)}, u32[]{:S(2)}, u32[]{:S(2)}) collective-permute-start(bf16[2,32,1152]{2,1,0:T(8,128)(2,1)S(1)} %fusion.5), channel_id=1, source_target_pairs={{0,8},{2,10},{4,12},{6,14},{8,16},{10,18},{12,20},{14,22},{16,24},... | collective-permute-start | bytes 442376 | tf_op jit(solution)/shard_map/ppermute | solution.py:194
  106.2 6.4 %collective-permute-start.28 = (bf16[2,32,1152]{2,1,0:T(8,128)(2,1)S(1)}, bf16[2,32,1152]{2,1,0:T(8,128)(2,1)S(1)}, u32[]{:S(2)}, u32[]{:S(2)}) collective-permute-start(bf16[2,32,1152]{2,1,0:T(8,128)(2,1)S(1)} %fusion.12), channel_id=1, source_target_pairs={{0,4},{2,6},{4,0},{6,2},{8,12},{10,14},{12,8},{14,10},{16,20},{18,... | collective-permute-start | bytes 442376 | tf_op jit(solution)/shard_map/ppermute | solution.py:188
  113.3 10.9 %collective-permute-start.31 = (bf16[2,32,1152]{2,1,0:T(8,128)(2,1)}, bf16[2,32,1152]{2,1,0:T(8,128)(2,1)S(1)}, u32[]{:S(2)}, u32[]{:S(2)}) collective-permute-start(bf16[2,32,1152]{2,1,0:T(8,128)(2,1)} %fusion.4), channel_id=1, source_target_pairs={{0,8},{2,10},{4,12},{6,14},{8,16},{10,18},{12,20},{14,22},{16,24},... | collective-permute-start | bytes 442376 | tf_op jit(solution)/shard_map/ppermute | solution.py:194
  114.6 9.6 %collective-permute-start.29 = (bf16[2,32,1152]{2,1,0:T(8,128)(2,1)S(1)}, bf16[2,32,1152]{2,1,0:T(8,128)(2,1)}, u32[]{:S(2)}, u32[]{:S(2)}) collective-permute-start(bf16[2,32,1152]{2,1,0:T(8,128)(2,1)S(1)} %fusion.13), channel_id=1, source_target_pairs={{0,4},{2,6},{4,0},{6,2},{8,12},{10,14},{12,8},{14,10},{16,20},{18,... | collective-permute-start | bytes 442376 | tf_op jit(solution)/shard_map/ppermute | solution.py:188
  125.3 10.6 %collective-permute-start.36 = (bf16[2,32,1152]{2,1,0:T(8,128)(2,1)S(1)}, bf16[2,32,1152]{2,1,0:T(8,128)(2,1)S(1)}, u32[]{:S(2)}, u32[]{:S(2)}) collective-permute-start(bf16[2,32,1152]{2,1,0:T(8,128)(2,1)S(1)} %fusion.2), channel_id=1, source_target_pairs={{0,8},{2,10},{4,12},{6,14},{8,16},{10,18},{12,20},{14,22},{16,24},... | collective-permute-start | bytes 442376 | tf_op jit(solution)/shard_map/ppermute | solution.py:194
  (36 other events, 235.9 us)

commit v7 on v6

--- a/solution.py
+++ b/solution.py
@@ -233,7 +233,7 @@
             functools.partial(rows_kernel, segments, width, hidden),
             out_shape=(
                 jax.ShapeDtypeStruct((rows, 2 * hidden), bf16),
-                jax.ShapeDtypeStruct((rows, hidden + width), bf16),
+                pltpu.HBM((rows, hidden + width), bf16),
                 jax.ShapeDtypeStruct((rows, LANES), bf16),
             ),
             in_specs=[whole()] * 8 + [scalar(), scalar()],
@@ -288,7 +288,7 @@
             ],
             compiler_params=pltpu.CompilerParams(vmem_limit_bytes=20 << 20),
             name="down",
-        )(*held)
+        )(*[pltpu.with_memory_space_constraint(one, pltpu.HBM) for one in held])
 
     def step(*late):
         now = {
@@ -347,7 +347,7 @@
     rows_of(3)
     other[1], grads[3] = fence((other[1], grads[3]))
     grads_of(1)
-    step()
+    step(("sent", 0))
     other[3] = go_x(grads[3])
     send_y(1)
     other[2], sent[1] = fence((other[2], sent[1]))

time: 145 us -> 139 us (0.959)
  local copies, waits for them, and re-layouts: 12.5 us -> 5.1 us
  waiting for transfers between devices: 54.6 us -> 58.7 us
  other arithmetic: 6.91 us -> 5.42 us
    unnamed x43 -> x27, local copies, waits for them, and re-layouts: 9.51 us -> 2.12 us
    ppermute x8, waiting for transfers between devices: 16.4 us -> 22.8 us  [go_x(): return lax.ppermute(v, 'dp', [(0, 1), (1, 0)])]
    ppermute x9, waiting for transfers between devices: 11.8 us -> 7.01 us  [go_y(): return lax.ppermute(v, 'expert', [(e, e ^ 2) for e in range(experts)])]
    pallas_call x4, Pallas kernels: 15.1 us -> 13.4 us  [first_half(): pl.pallas_call(functools.partial(rows_kernel, segments, width, hidden), o...]
    ppermute x6, waiting for transfers between devices: 17.4 us -> 19 us  [go_z(): lax.ppermute(v, 'expert', [(e, (e + 4) % experts) for e in range(experts)])]
  transfers between devices with their start and end apart: 39 -> 39, of which waited for: 16 -> 15; matrix products, arithmetic and copies ran while one was open for 5% -> 4% of each run, Pallas kernels for 22% -> 22%
where the time goes in v7:
time: 139 us; the launch traced here: 138 us
  waiting for transfers between devices  58.7 us (42%)
  starting transfers between devices  35.1 us (25%)
  Pallas kernels  32.4 us (23%)
  other arithmetic  5.42 us (4%)
  local copies, waits for them, and re-layouts  5.1 us (4%)
  between operations  1.65 us (1%)
    ppermute x8, waiting for transfers between devices, go_x(): return lax.ppermute(v, 'dp', [(0, 1), (1, 0)])  22.8 us
    ppermute x6, waiting for transfers between devices, go_z(): lax.ppermute(v, 'expert', [(e, (e + 4) % experts) for e in range(experts)])  19 us
    pallas_call x4, Pallas kernels, first_half(): pl.pallas_call(functools.partial(rows_kernel, segments, width, hidden), o...  13.4 us
    ppermute x8, starting transfers between devices, go_x(): return lax.ppermute(v, 'dp', [(0, 1), (1, 0)])  12.5 us
    pallas_call x4, Pallas kernels, second_half(): pl.pallas_call(functools.partial(grad_kernel, segments, half), out_shape=...  12.2 us
    ppermute x9, starting transfers between devices, go_y(): return lax.ppermute(v, 'expert', [(e, e ^ 2) for e in range(experts)])  10.9 us
    ppermute x6, starting transfers between devices, go_z(): lax.ppermute(v, 'expert', [(e, (e + 4) % experts) for e in range(experts)])  7.14 us
    ppermute x9, waiting for transfers between devices, go_y(): return lax.ppermute(v, 'expert', [(e, e ^ 2) for e in range(experts)])  7.01 us
  transfers between devices with their start and end apart: 39, of which 15 were waited for; matrix products, arithmetic and copies ran while one was open for 4% of the time, Pallas kernels for 22%

profile of v7, /device:TPU:0, one launch (start us, length us, event | category | flops | bytes accessed | tf_op | source)
XLA Modules:
  0.0 138.4 jit_solution(18288349476221724523)
XLA Ops:
  0.6 1.9 %pack.1 = bf16[32,4224]{1,0:T(8,128)(2,1)} custom-call(bf16[32,2048]{1,0:T(8,128)(2,1)} %bitcast.90, bf16[32,2048]{1,0:T(8,128)(2,1)} %bitcast.91, s32[8,32]{1,0:T(8,128)} %bitcast.94, bf16[8,32]{1,0:T(8,128)(2,1)} %bitcast.98), custom_call_target="tpu_custom_call" | custom-call | tf_op jit(solution)/shard_map/pack/pallas_call | solution.py:207
  2.5 2.9 %collective-permute-start = (bf16[32,4224]{1,0:T(8,128)(2,1)}, bf16[32,4224]{1,0:T(8,128)(2,1)S(1)}, u32[]{:S(2)}, u32[]{:S(2)}) collective-permute-start(bf16[32,4224]{1,0:T(8,128)(2,1)} %pack.1), channel_id=1, source_target_pairs={{0,1},{1,0},{2,3},{3,2},{4,5},{5,4},{6,7},{7,6},{8,9},{9,8},{10,11... | collective-permute-start | bytes 811016 | tf_op jit(solution)/shard_map/ppermute | solution.py:185
  5.4 6.7 %collective-permute-done = bf16[32,4224]{1,0:T(8,128)(2,1)S(1)} collective-permute-done((bf16[32,4224]{1,0:T(8,128)(2,1)}, bf16[32,4224]{1,0:T(8,128)(2,1)S(1)}, u32[]{:S(2)}, u32[]{:S(2)}) %collective-permute-start) | collective-permute-done | bytes 270368 | tf_op jit(solution)/shard_map/ppermute | solution.py:185
  17.3 2.8 %constant_dynamic-slice_fusion = bf16[768,1024]{1,0:T(8,128)(2,1)} fusion(bf16[768,2048]{1,0:T(8,128)(2,1)} %bitcast.68, s32[]{:T(128)S(6)} %select_n.32), kind=kLoop, calls=%fused_computation.42 | loop fusion | bytes 3145732 | tf_op jit(solution)/shard_map/dynamic_slice | solution.py:222
  21.6 9.4 %collective-permute-done.1.refs_0_ = bf16[64,4224]{1,0:T(8,128)(2,1)} collective-permute-done((bf16[64,4224]{1,0:T(8,128)(2,1)}, bf16[64,4224]{1,0:T(8,128)(2,1)}, u32[]{:S(2)}, u32[]{:S(2)}) %collective-permute-start.1) | collective-permute-done | bytes 540704 | tf_op jit(solution)/shard_map/ppermute | solution.py:194
  35.7 3.9 %rows.4 = (bf16[256,768]{1,0:T(8,128)(2,1)S(1)}, bf16[256,2432]{1,0:T(8,128)(2,1)}, bf16[256,128]{1,0:T(8,128)(2,1)S(1)}) custom-call(bf16[64,4224]{1,0:T(8,128)(2,1)} %pad_maximum_fusion.refs_0_, bf16[64,4224]{1,0:T(8,128)(2,1)} %collective-permute-done.2.refs_1_, bf16[64,4224]{1,0:T(8,128)(2,1)} %collective-permute-done.3.refs_2_, ...), custom_call_target="tpu_custom_call" | custom-call | tf_op jit(solution)/shard_map/rows/pallas_call | solution.py:232
  39.6 8.2 %collective-permute-done.4.refs_0_ = bf16[64,4224]{1,0:T(8,128)(2,1)} collective-permute-done((bf16[64,4224]{1,0:T(8,128)(2,1)}, bf16[64,4224]{1,0:T(8,128)(2,1)}, u32[]{:S(2)}, u32[]{:S(2)}) %collective-permute-start.4) | collective-permute-done | bytes 540704 | tf_op jit(solution)/shard_map/ppermute | solution.py:194
  51.9 3.7 %rows.5 = (bf16[256,768]{1,0:T(8,128)(2,1)S(1)}, bf16[256,2432]{1,0:T(8,128)(2,1)}, bf16[256,128]{1,0:T(8,128)(2,1)S(1)}) custom-call(bf16[64,4224]{1,0:T(8,128)(2,1)} %collective-permute-done.1.refs_0_, bf16[64,4224]{1,0:T(8,128)(2,1)} %collective-permute-done.5.refs_1_, bf16[64,4224]{1,0:T(8,128)(2,1)} %collective-permute-done.6.refs_2_, ...), custom_call_target="tpu_custom_call" | custom-call | tf_op jit(solution)/shard_map/rows/pallas_call | solution.py:232
  55.6 9.4 %collective-permute-done.12.refs_5_ = bf16[256,768]{1,0:T(8,128)(2,1)S(1)} collective-permute-done((bf16[256,768]{1,0:T(8,128)(2,1)S(1)}, bf16[256,768]{1,0:T(8,128)(2,1)S(1)}, u32[]{:S(2)}, u32[]{:S(2)}) %collective-permute-start.12) | collective-permute-done | bytes 393248 | tf_op jit(solution)/shard_map/ppermute | solution.py:185
  67.9 3.4 %grads.4 = (bf16[2,2,32,1152]{3,2,1,0:T(8,128)(2,1)S(1)}, bf16[2,2,32,1152]{3,2,1,0:T(8,128)(2,1)S(1)}, f32[8,1024]{1,0:T(8,128)S(1)}) custom-call(bf16[64,4224]{1,0:T(8,128)(2,1)} %pad_maximum_fusion.refs_0_, bf16[64,4224]{1,0:T(8,128)(2,1)} %collective-permute-done.2.refs_1_, bf16[64,4224]{1,0:T(8,128)(2,1)} %collective-permute-done.3.refs_2_, ...), custom_call_target="tpu_custom_call" | custom-call | tf_op jit(solution)/shard_map/grads/pallas_call | solution.py:253
  71.4 3.4 %rows.6 = (bf16[256,768]{1,0:T(8,128)(2,1)S(1)}, bf16[256,2432]{1,0:T(8,128)(2,1)}, bf16[256,128]{1,0:T(8,128)(2,1)S(1)}) custom-call(bf16[64,4224]{1,0:T(8,128)(2,1)} %collective-permute-done.4.refs_0_, bf16[64,4224]{1,0:T(8,128)(2,1)S(1)} %collective-permute-done.9.refs_1_, bf16[64,4224]{1,0:T(8,128)(2,1)S(1)} %collective-permute-done.10.refs_2_, ...), custom_call_target="tpu_custom_call" | custom-call | tf_op jit(solution)/shard_map/rows/pallas_call | solution.py:232
  74.8 2.9 %collective-permute-done.18.refs_5_ = bf16[256,768]{1,0:T(8,128)(2,1)S(1)} collective-permute-done((bf16[256,768]{1,0:T(8,128)(2,1)S(1)}, bf16[256,768]{1,0:T(8,128)(2,1)S(1)}, u32[]{:S(2)}, u32[]{:S(2)}) %collective-permute-start.18) | collective-permute-done | bytes 393248 | tf_op jit(solution)/shard_map/ppermute | solution.py:185
  77.8 2.0 %collective-permute-done.14.refs_1_ = bf16[64,4224]{1,0:T(8,128)(2,1)S(1)} collective-permute-done((bf16[64,4224]{1,0:T(8,128)(2,1)S(1)}, bf16[64,4224]{1,0:T(8,128)(2,1)S(1)}, u32[]{:S(2)}, u32[]{:S(2)}) %collective-permute-start.14) | collective-permute-done | bytes 540704 | tf_op jit(solution)/shard_map/ppermute | solution.py:188
  81.7 2.4 %rows.7 = (bf16[256,768]{1,0:T(8,128)(2,1)S(1)}, bf16[256,2432]{1,0:T(8,128)(2,1)}, bf16[256,128]{1,0:T(8,128)(2,1)S(1)}) custom-call(bf16[64,4224]{1,0:T(8,128)(2,1)S(1)} %collective-permute-done.8.refs_0_, bf16[64,4224]{1,0:T(8,128)(2,1)S(1)} %collective-permute-done.14.refs_1_, bf16[64,4224]{1,0:T(8,128)(2,1)S(1)} %collective-permute-done.15.refs_2_, ...), custom_call_target="tpu_custom_call" | custom-call | tf_op jit(solution)/shard_map/rows/pallas_call | solution.py:232
  84.1 3.2 %grads.5 = (bf16[2,2,32,1152]{3,2,1,0:T(8,128)(2,1)S(1)}, bf16[2,2,32,1152]{3,2,1,0:T(8,128)(2,1)S(1)}, f32[8,1024]{1,0:T(8,128)S(1)}) custom-call(bf16[64,4224]{1,0:T(8,128)(2,1)} %collective-permute-done.1.refs_0_, bf16[64,4224]{1,0:T(8,128)(2,1)} %collective-permute-done.5.refs_1_, bf16[64,4224]{1,0:T(8,128)(2,1)} %collective-permute-done.6.refs_2_, ...), custom_call_target="tpu_custom_call" | custom-call | tf_op jit(solution)/shard_map/grads/pallas_call | solution.py:253
  87.6 3.8 %collective-permute-done.21.refs_5_ = bf16[256,768]{1,0:T(8,128)(2,1)S(1)} collective-permute-done((bf16[256,768]{1,0:T(8,128)(2,1)S(1)}, bf16[256,768]{1,0:T(8,128)(2,1)S(1)}, u32[]{:S(2)}, u32[]{:S(2)}) %collective-permute-start.21) | collective-permute-done | bytes 393248 | tf_op jit(solution)/shard_map/ppermute | solution.py:185
  95.1 3.1 %collective-permute-done.22 = bf16[2,32,1152]{2,1,0:T(8,128)(2,1)S(1)} collective-permute-done((bf16[2,32,1152]{2,1,0:T(8,128)(2,1)S(1)}, bf16[2,32,1152]{2,1,0:T(8,128)(2,1)S(1)}, u32[]{:S(2)}, u32[]{:S(2)}) %collective-permute-start.22) | collective-permute-done | bytes 147488 | tf_op jit(solution)/shard_map/ppermute | solution.py:188
  98.2 2.9 %grads.6 = (bf16[2,2,32,1152]{3,2,1,0:T(8,128)(2,1)S(1)}, bf16[2,2,32,1152]{3,2,1,0:T(8,128)(2,1)S(1)}, f32[8,1024]{1,0:T(8,128)S(1)}) custom-call(bf16[64,4224]{1,0:T(8,128)(2,1)} %collective-permute-done.4.refs_0_, bf16[64,4224]{1,0:T(8,128)(2,1)S(1)} %collective-permute-done.9.refs_1_, bf16[64,4224]{1,0:T(8,128)(2,1)S(1)} %collective-permute-done.10.refs_2_, ...), custom_call_target="tpu_custom_call" | custom-call | tf_op jit(solution)/shard_map/grads/pallas_call | solution.py:253
  103.9 2.8 %grads.7 = (bf16[2,2,32,1152]{3,2,1,0:T(8,128)(2,1)S(1)}, bf16[2,2,32,1152]{3,2,1,0:T(8,128)(2,1)S(1)}, f32[8,1024]{1,0:T(8,128)S(1)}) custom-call(bf16[64,4224]{1,0:T(8,128)(2,1)S(1)} %collective-permute-done.8.refs_0_, bf16[64,4224]{1,0:T(8,128)(2,1)S(1)} %collective-permute-done.14.refs_1_, bf16[64,4224]{1,0:T(8,128)(2,1)S(1)} %collective-permute-done.15.refs_2_, ...), custom_call_target="tpu_custom_call" | custom-call | tf_op jit(solution)/shard_map/grads/pallas_call | solution.py:253
  115.1 1.8 %collective-permute-done.32 = f32[8,1024]{1,0:T(8,128)S(1)} collective-permute-done((f32[8,1024]{1,0:T(8,128)S(1)}, f32[8,1024]{1,0:T(8,128)S(1)}, u32[]{:S(2)}, u32[]{:S(2)}) %collective-permute-start.32) | collective-permute-done | bytes 32800 | tf_op jit(solution)/shard_map/ppermute | solution.py:188
  116.9 2.4 %collective-permute-done.34 = f32[8,1024]{1,0:T(8,128)S(1)} collective-permute-done((f32[8,1024]{1,0:T(8,128)S(1)}, f32[8,1024]{1,0:T(8,128)S(1)}, u32[]{:S(2)}, u32[]{:S(2)}) %collective-permute-start.34) | collective-permute-done | bytes 32800 | tf_op jit(solution)/shard_map/ppermute | solution.py:203
  122.5 2.2 %collective-permute-done.35 = f32[16,1024]{1,0:T(8,128)S(1)} collective-permute-done((f32[16,1024]{1,0:T(8,128)S(1)}, f32[16,1024]{1,0:T(8,128)S(1)}, u32[]{:S(2)}, u32[]{:S(2)}) %collective-permute-start.35) | collective-permute-done | bytes 65568 | tf_op jit(solution)/shard_map/ppermute | solution.py:197
  124.8 4.9 %down.1 = bf16[384,2048]{1,0:T(8,128)(2,1)} custom-call(bf16[256,2432]{1,0:T(8,128)(2,1)} %get-tuple-element.251.refs_0_, bf16[256,2432]{1,0:T(8,128)(2,1)} %get-tuple-element.252.refs_1_, bf16[256,2432]{1,0:T(8,128)(2,1)} %get-tuple-element.253.refs_2_, bf16[256,2432]{1,0:T(8,128)(2,1)} %get-tuple-element.256.refs_3_), custom_call_target="tpu_custom_call" | custom-call | tf_op jit(solution)/shard_map/down/pallas_call | solution.py:280
  131.3 4.1 %collective-permute-done.38 = f32[16,1024]{1,0:T(8,128)S(1)} collective-permute-done((f32[16,1024]{1,0:T(8,128)S(1)}, f32[16,1024]{1,0:T(8,128)S(1)}, u32[]{:S(2)}, u32[]{:S(2)}) %collective-permute-start.38) | collective-permute-done | bytes 65568 | tf_op jit(solution)/shard_map/ppermute | solution.py:197
  (121 shorter events, 42.4 us)
Async XLA Ops:
  2.5 9.6 %collective-permute-start = (bf16[32,4224]{1,0:T(8,128)(2,1)}, bf16[32,4224]{1,0:T(8,128)(2,1)S(1)}, u32[]{:S(2)}, u32[]{:S(2)}) collective-permute-start(bf16[32,4224]{1,0:T(8,128)(2,1)} %pack.1), channel_id=1, source_target_pairs={{0,1},{1,0},{2,3},{3,2},{4,5},{5,4},{6,7},{7,6},{8,9},{9,8},{10,11... | collective-permute-start | bytes 811016 | tf_op jit(solution)/shard_map/ppermute | solution.py:185
  13.9 17.1 %collective-permute-start.1 = (bf16[64,4224]{1,0:T(8,128)(2,1)}, bf16[64,4224]{1,0:T(8,128)(2,1)}, u32[]{:S(2)}, u32[]{:S(2)}) collective-permute-start(bf16[64,4224]{1,0:T(8,128)(2,1)} %pad_maximum_fusion.refs_0_), channel_id=1, source_target_pairs={{0,8},{2,10},{4,12},{6,14},{8,16},{10,18},{12,20},{14,22},{16,24},... | collective-permute-start | bytes 1622024 | tf_op jit(solution)/shard_map/ppermute | solution.py:194
  15.8 15.3 %collective-permute-start.2 = (bf16[64,4224]{1,0:T(8,128)(2,1)}, bf16[64,4224]{1,0:T(8,128)(2,1)}, u32[]{:S(2)}, u32[]{:S(2)}) collective-permute-start(bf16[64,4224]{1,0:T(8,128)(2,1)} %pad_maximum_fusion.refs_0_), channel_id=1, source_target_pairs={{0,4},{2,6},{4,0},{6,2},{8,12},{10,14},{12,8},{14,10},{16,20},{18,... | collective-permute-start | bytes 1622024 | tf_op jit(solution)/shard_map/ppermute | solution.py:188
  20.1 44.9 %collective-permute-start.13 = (bf16[768,1024]{1,0:T(8,128)(2,1)}, bf16[768,1024]{1,0:T(8,128)(2,1)}, u32[]{:S(2)}, u32[]{:S(2)}) collective-permute-start(bf16[768,1024]{1,0:T(8,128)(2,1)} %constant_dynamic-slice_fusion), channel_id=1, source_target_pairs={{0,1},{1,0},{2,3},{3,2},{4,5},{5,4},{6,7},{7,6},{8,9},{9,8},{10,11... | collective-permute-start | bytes 4718600 | tf_op jit(solution)/shard_map/ppermute | solution.py:185
  31.1 16.8 %collective-permute-start.4 = (bf16[64,4224]{1,0:T(8,128)(2,1)}, bf16[64,4224]{1,0:T(8,128)(2,1)}, u32[]{:S(2)}, u32[]{:S(2)}) collective-permute-start(bf16[64,4224]{1,0:T(8,128)(2,1)} %collective-permute-done.1.refs_0_), channel_id=1, source_target_pairs={{0,8},{2,10},{4,12},{6,14},{8,16},{10,18},{12,20},{14,22},{16,24},... | collective-permute-start | bytes 1622024 | tf_op jit(solution)/shard_map/ppermute | solution.py:194
  32.1 15.8 %collective-permute-start.5 = (bf16[64,4224]{1,0:T(8,128)(2,1)}, bf16[64,4224]{1,0:T(8,128)(2,1)}, u32[]{:S(2)}, u32[]{:S(2)}) collective-permute-start(bf16[64,4224]{1,0:T(8,128)(2,1)} %collective-permute-done.1.refs_0_), channel_id=1, source_target_pairs={{0,4},{2,6},{4,0},{6,2},{8,12},{10,14},{12,8},{14,10},{16,20},{18,... | collective-permute-start | bytes 1622024 | tf_op jit(solution)/shard_map/ppermute | solution.py:188
  33.6 14.3 %collective-permute-start.6 = (bf16[64,4224]{1,0:T(8,128)(2,1)}, bf16[64,4224]{1,0:T(8,128)(2,1)}, u32[]{:S(2)}, u32[]{:S(2)}) collective-permute-start(bf16[64,4224]{1,0:T(8,128)(2,1)} %collective-permute-done.1.refs_0_), channel_id=1, source_target_pairs={{0,2},{2,0},{4,6},{6,4},{8,10},{10,8},{12,14},{14,12},{16,18},{18,... | collective-permute-start | bytes 1622024 | tf_op jit(solution)/shard_map/ppermute | solution.py:191
  47.9 17.1 %collective-permute-start.10 = (bf16[64,4224]{1,0:T(8,128)(2,1)}, bf16[64,4224]{1,0:T(8,128)(2,1)S(1)}, u32[]{:S(2)}, u32[]{:S(2)}) collective-permute-start(bf16[64,4224]{1,0:T(8,128)(2,1)} %collective-permute-done.4.refs_0_), channel_id=1, source_target_pairs={{0,2},{2,0},{4,6},{6,4},{8,10},{10,8},{12,14},{14,12},{16,18},{18,... | collective-permute-start | bytes 1622024 | tf_op jit(solution)/shard_map/ppermute | solution.py:191
  48.4 16.6 %collective-permute-start.8 = (bf16[64,4224]{1,0:T(8,128)(2,1)}, bf16[64,4224]{1,0:T(8,128)(2,1)S(1)}, u32[]{:S(2)}, u32[]{:S(2)}) collective-permute-start(bf16[64,4224]{1,0:T(8,128)(2,1)} %collective-permute-done.4.refs_0_), channel_id=1, source_target_pairs={{0,8},{2,10},{4,12},{6,14},{8,16},{10,18},{12,20},{14,22},{16,24},... | collective-permute-start | bytes 1622024 | tf_op jit(solution)/shard_map/ppermute | solution.py:194
  48.9 16.1 %collective-permute-start.9 = (bf16[64,4224]{1,0:T(8,128)(2,1)}, bf16[64,4224]{1,0:T(8,128)(2,1)S(1)}, u32[]{:S(2)}, u32[]{:S(2)}) collective-permute-start(bf16[64,4224]{1,0:T(8,128)(2,1)} %collective-permute-done.4.refs_0_), channel_id=1, source_target_pairs={{0,4},{2,6},{4,0},{6,2},{8,12},{10,14},{12,8},{14,10},{16,20},{18,... | collective-permute-start | bytes 1622024 | tf_op jit(solution)/shard_map/ppermute | solution.py:188
  50.4 14.6 %collective-permute-start.12 = (bf16[256,768]{1,0:T(8,128)(2,1)S(1)}, bf16[256,768]{1,0:T(8,128)(2,1)S(1)}, u32[]{:S(2)}, u32[]{:S(2)}) collective-permute-start(bf16[256,768]{1,0:T(8,128)(2,1)S(1)} %get-tuple-element.165.refs_4_), channel_id=1, source_target_pairs={{0,1},{1,0},{2,3},{3,2},{4,5},{5,4},{6,7},{7,6},{8,9},{9,8},{10,11... | collective-permute-start | bytes 1179656 | tf_op jit(solution)/shard_map/ppermute | solution.py:185
  65.0 6.4 %collective-permute-start.16 = (bf16[64,4224]{1,0:T(8,128)(2,1)S(1)}, bf16[64,4224]{1,0:T(8,128)(2,1)S(1)}, u32[]{:S(2)}, u32[]{:S(2)}) collective-permute-start(bf16[64,4224]{1,0:T(8,128)(2,1)S(1)} %collective-permute-done.9.refs_1_), channel_id=1, source_target_pairs={{0,2},{2,0},{4,6},{6,4},{8,10},{10,8},{12,14},{14,12},{16,18},{18,... | collective-permute-start | bytes 1622024 | tf_op jit(solution)/shard_map/ppermute | solution.py:191
  65.1 14.7 %collective-permute-start.14 = (bf16[64,4224]{1,0:T(8,128)(2,1)S(1)}, bf16[64,4224]{1,0:T(8,128)(2,1)S(1)}, u32[]{:S(2)}, u32[]{:S(2)}) collective-permute-start(bf16[64,4224]{1,0:T(8,128)(2,1)S(1)} %collective-permute-done.8.refs_0_), channel_id=1, source_target_pairs={{0,4},{2,6},{4,0},{6,2},{8,12},{10,14},{12,8},{14,10},{16,20},{18,... | collective-permute-start | bytes 1622024 | tf_op jit(solution)/shard_map/ppermute | solution.py:188
  66.2 13.6 %collective-permute-start.15 = (bf16[64,4224]{1,0:T(8,128)(2,1)S(1)}, bf16[64,4224]{1,0:T(8,128)(2,1)S(1)}, u32[]{:S(2)}, u32[]{:S(2)}) collective-permute-start(bf16[64,4224]{1,0:T(8,128)(2,1)S(1)} %collective-permute-done.8.refs_0_), channel_id=1, source_target_pairs={{0,2},{2,0},{4,6},{6,4},{8,10},{10,8},{12,14},{14,12},{16,18},{18,... | collective-permute-start | bytes 1622024 | tf_op jit(solution)/shard_map/ppermute | solution.py:191
  66.4 11.4 %collective-permute-start.18 = (bf16[256,768]{1,0:T(8,128)(2,1)S(1)}, bf16[256,768]{1,0:T(8,128)(2,1)S(1)}, u32[]{:S(2)}, u32[]{:S(2)}) collective-permute-start(bf16[256,768]{1,0:T(8,128)(2,1)S(1)} %get-tuple-element.186.refs_4_), channel_id=1, source_target_pairs={{0,1},{1,0},{2,3},{3,2},{4,5},{5,4},{6,7},{7,6},{8,9},{9,8},{10,11... | collective-permute-start | bytes 1179656 | tf_op jit(solution)/shard_map/ppermute | solution.py:185
  79.8 11.5 %collective-permute-start.21 = (bf16[256,768]{1,0:T(8,128)(2,1)S(1)}, bf16[256,768]{1,0:T(8,128)(2,1)S(1)}, u32[]{:S(2)}, u32[]{:S(2)}) collective-permute-start(bf16[256,768]{1,0:T(8,128)(2,1)S(1)} %get-tuple-element.209.refs_4_), channel_id=1, source_target_pairs={{0,1},{1,0},{2,3},{3,2},{4,5},{5,4},{6,7},{7,6},{8,9},{9,8},{10,11... | collective-permute-start | bytes 1179656 | tf_op jit(solution)/shard_map/ppermute | solution.py:185
  91.4 6.8 %collective-permute-start.22 = (bf16[2,32,1152]{2,1,0:T(8,128)(2,1)S(1)}, bf16[2,32,1152]{2,1,0:T(8,128)(2,1)S(1)}, u32[]{:S(2)}, u32[]{:S(2)}) collective-permute-start(bf16[2,32,1152]{2,1,0:T(8,128)(2,1)S(1)} %fusion.10), channel_id=1, source_target_pairs={{0,4},{2,6},{4,0},{6,2},{8,12},{10,14},{12,8},{14,10},{16,20},{18,... | collective-permute-start | bytes 442376 | tf_op jit(solution)/shard_map/ppermute | solution.py:188
  92.5 11.4 %collective-permute-start.25 = (bf16[2,32,1152]{2,1,0:T(8,128)(2,1)S(1)}, bf16[2,32,1152]{2,1,0:T(8,128)(2,1)S(1)}, u32[]{:S(2)}, u32[]{:S(2)}) collective-permute-start(bf16[2,32,1152]{2,1,0:T(8,128)(2,1)S(1)} %fusion.11), channel_id=1, source_target_pairs={{0,4},{2,6},{4,0},{6,2},{8,12},{10,14},{12,8},{14,10},{16,20},{18,... | collective-permute-start | bytes 442376 | tf_op jit(solution)/shard_map/ppermute | solution.py:188
  93.6 10.4 %collective-permute-start.24 = (bf16[256,768]{1,0:T(8,128)(2,1)S(1)}, bf16[256,768]{1,0:T(8,128)(2,1)S(1)}, u32[]{:S(2)}, u32[]{:S(2)}) collective-permute-start(bf16[256,768]{1,0:T(8,128)(2,1)S(1)} %get-tuple-element.229.refs_4_), channel_id=1, source_target_pairs={{0,1},{1,0},{2,3},{3,2},{4,5},{5,4},{6,7},{7,6},{8,9},{9,8},{10,11... | collective-permute-start | bytes 1179656 | tf_op jit(solution)/shard_map/ppermute | solution.py:185
  101.2 8.1 %collective-permute-start.30 = (bf16[2,32,1152]{2,1,0:T(8,128)(2,1)S(1)}, bf16[2,32,1152]{2,1,0:T(8,128)(2,1)S(1)}, u32[]{:S(2)}, u32[]{:S(2)}) collective-permute-start(bf16[2,32,1152]{2,1,0:T(8,128)(2,1)S(1)} %fusion.5), channel_id=1, source_target_pairs={{0,8},{2,10},{4,12},{6,14},{8,16},{10,18},{12,20},{14,22},{16,24},... | collective-permute-start | bytes 442376 | tf_op jit(solution)/shard_map/ppermute | solution.py:194
  102.9 6.4 %collective-permute-start.28 = (bf16[2,32,1152]{2,1,0:T(8,128)(2,1)S(1)}, bf16[2,32,1152]{2,1,0:T(8,128)(2,1)S(1)}, u32[]{:S(2)}, u32[]{:S(2)}) collective-permute-start(bf16[2,32,1152]{2,1,0:T(8,128)(2,1)S(1)} %fusion.12), channel_id=1, source_target_pairs={{0,4},{2,6},{4,0},{6,2},{8,12},{10,14},{12,8},{14,10},{16,20},{18,... | collective-permute-start | bytes 442376 | tf_op jit(solution)/shard_map/ppermute | solution.py:188
  109.4 11.4 %collective-permute-start.31 = (bf16[2,32,1152]{2,1,0:T(8,128)(2,1)S(1)}, bf16[2,32,1152]{2,1,0:T(8,128)(2,1)S(1)}, u32[]{:S(2)}, u32[]{:S(2)}) collective-permute-start(bf16[2,32,1152]{2,1,0:T(8,128)(2,1)S(1)} %fusion.4), channel_id=1, source_target_pairs={{0,8},{2,10},{4,12},{6,14},{8,16},{10,18},{12,20},{14,22},{16,24},... | collective-permute-start | bytes 442376 | tf_op jit(solution)/shard_map/ppermute | solution.py:194
  110.9 9.9 %collective-permute-start.29 = (bf16[2,32,1152]{2,1,0:T(8,128)(2,1)S(1)}, bf16[2,32,1152]{2,1,0:T(8,128)(2,1)S(1)}, u32[]{:S(2)}, u32[]{:S(2)}) collective-permute-start(bf16[2,32,1152]{2,1,0:T(8,128)(2,1)S(1)} %fusion.13), channel_id=1, source_target_pairs={{0,4},{2,6},{4,0},{6,2},{8,12},{10,14},{12,8},{14,10},{16,20},{18,... | collective-permute-start | bytes 442376 | tf_op jit(solution)/shard_map/ppermute | solution.py:188
  121.8 8.0 %collective-permute-start.36 = (bf16[2,32,1152]{2,1,0:T(8,128)(2,1)S(1)}, bf16[2,32,1152]{2,1,0:T(8,128)(2,1)S(1)}, u32[]{:S(2)}, u32[]{:S(2)}) collective-permute-start(bf16[2,32,1152]{2,1,0:T(8,128)(2,1)S(1)} %fusion.2), channel_id=1, source_target_pairs={{0,8},{2,10},{4,12},{6,14},{8,16},{10,18},{12,20},{14,22},{16,24},... | collective-permute-start | bytes 442376 | tf_op jit(solution)/shard_map/ppermute | solution.py:194
  (28 other events, 196.6 us)

commit v8 on v7

--- a/solution.py
+++ b/solution.py
@@ -22,12 +22,17 @@
     return (left.astype(f32) + right.astype(f32)).astype(bf16)
 
 
+def one_hot(spot, slots):
+    label = lax.broadcasted_iota(jnp.int32, (spot.shape[0], slots), 1).astype(f32)
+    return jnp.where(label == spot[:, 0:1], 1.0, 0.0).astype(bf16)
+
+
 def rows_kernel(segments, width, hidden, *refs):
     count = len(segments)
     blocks = refs[:count]
     (w_in, w_down, gamma, beta, alpha, expert) = refs[count : count + 6]
-    (grads_out, kept_out, tail_out) = refs[count + 6 : count + 9]
-    (normed, cot, weight, kept, sems) = refs[count + 9 :]
+    (grads_out, packed_out, spot_out, kept_out, tail_out) = refs[count + 6 : count + 11]
+    (normed, cot, weight, kept, sems) = refs[count + 11 :]
     rows = normed.shape[0]
     gain = alpha[0]
     mine = expert[0]
@@ -67,6 +72,25 @@
     d_gate = d_act * up_value * sigma * (1.0 + gate_pre * (1.0 - sigma))
     grads_out[:, :hidden] = d_gate.astype(bf16)
     grads_out[:, hidden:] = (d_act * gate_pre * sigma).astype(bf16)
+    routed = weight[...] > 0.0
+    block = rows // 8
+    row = lax.broadcasted_iota(jnp.int32, (rows, rows), 0)
+    column = lax.broadcasted_iota(jnp.int32, (rows, rows), 1)
+    earlier = (column < row) & (column >= row - lax.rem(row, block))
+    count_before = jnp.dot(
+        jnp.where(earlier, 1.0, 0.0).astype(bf16),
+        jnp.where(routed, 1.0, 0.0).astype(bf16),
+        preferred_element_type=f32,
+    )
+    slots = packed_out.shape[0] // 8
+    row = lax.broadcasted_iota(jnp.int32, (rows, LANES), 0)
+    base = (lax.div(row, block) * slots).astype(f32)
+    spot = jnp.where(routed, base + count_before, -1.0)
+    spot_out[...] = spot
+    packed_out[...] = lax.dot_general(
+        one_hot(spot, 8 * slots), grads_out[...], (((0,), (0,)), ((), ())),
+        preferred_element_type=f32,
+    ).astype(bf16)
     lane = lax.broadcasted_iota(jnp.int32, (rows, LANES), 1)
     tail_out[...] = jnp.where(lane == mine, row_grad, 0.0).astype(bf16)
     save_cot.wait()
@@ -76,8 +100,8 @@
 def grad_kernel(segments, half, *refs):
     count = len(segments)
     blocks = refs[:count]
-    (near, far, w_in, w_far, tail, alpha, side) = refs[count : count + 7]
-    (d_own, d_other, sums, squash, slope) = refs[count + 7 :]
+    (near, far, spot, w_in, w_far, tail, alpha, side) = refs[count : count + 8]
+    (d_own, d_other, sums, squash, slope) = refs[count + 8 :]
     rows = near.shape[0]
     block = rows // 8
     gain = alpha[0]
@@ -89,7 +113,11 @@
             squashed = jnp.tanh(gain * inputs)
             squash[to : to + size, :] = squashed
             slope[to : to + size, :] = (1.0 - squashed * squashed) * inputs
-    mirrored = jnp.concatenate([far[rows // 2 :, :], far[: rows // 2, :]], axis=0)
+    slots = far.shape[0]
+    mirrored = jnp.concatenate([far[slots // 2 :, :], far[: slots // 2, :]], axis=0)
+    mirrored = jnp.dot(
+        one_hot(spot[...], slots), mirrored, preferred_element_type=f32
+    ).astype(bf16)
 
     def place(cols, value):
         for x in range(2):
@@ -133,6 +161,12 @@
     out[:, 2 * width :] = contract_width(unit, table.astype(bf16)).astype(bf16)
     out[:, :width] = tokens[...]
     out[:, width : 2 * width] = cotangent[...]
+
+
+def join_kernel(first, second, out):
+    size = first.shape[0]
+    out[:size, :] = first[...]
+    out[size:, :] = second[...]
 
 
 def down_kernel(count, hidden, *refs):
@@ -179,6 +213,7 @@
     width = tokens.shape[2]
     hidden = w_down.shape[1]
     rows = 8 * block
+    slots = 3 * block * expert_ids.shape[2] // (2 * experts)
     me = lax.axis_index("expert")
 
     def go_x(v):
@@ -233,11 +268,13 @@
             functools.partial(rows_kernel, segments, width, hidden),
             out_shape=(
                 jax.ShapeDtypeStruct((rows, 2 * hidden), bf16),
+                jax.ShapeDtypeStruct((8 * slots, 2 * hidden), bf16),
+                jax.ShapeDtypeStruct((rows, LANES), f32),
                 pltpu.HBM((rows, hidden + width), bf16),
                 jax.ShapeDtypeStruct((rows, LANES), bf16),
             ),
             in_specs=[whole()] * 8 + [scalar(), scalar()],
-            out_specs=(whole(), pl.BlockSpec(memory_space=pltpu.HBM), whole()),
+            out_specs=(whole(),) * 3 + (pl.BlockSpec(memory_space=pltpu.HBM), whole()),
             scratch_shapes=[
                 pltpu.VMEM((rows, width), bf16),
                 pltpu.VMEM((rows, width), bf16),
@@ -249,7 +286,7 @@
             name="rows",
         )(*arrays, flat_in, flat_down, gamma_row, beta_row, alpha, mine)
 
-    def second_half(arrays, near, far, w_far, tail):
+    def second_half(arrays, near, far, spot, w_far, tail):
         return pl.pallas_call(
             functools.partial(grad_kernel, segments, half),
             out_shape=(
@@ -257,7 +294,7 @@
                 jax.ShapeDtypeStruct((2, 2, block, half + LANES), bf16),
                 jax.ShapeDtypeStruct((8, half), f32),
             ),
-            in_specs=[whole()] * 9 + [scalar(), scalar()],
+            in_specs=[whole()] * 10 + [scalar(), scalar()],
             out_specs=(whole(),) * 3,
             scratch_shapes=[
                 pltpu.VMEM((rows, half), f32),
@@ -265,14 +302,20 @@
             ],
             compiler_params=params,
             name="grads",
-        )(*arrays, near, far, flat_in, w_far, tail, alpha, side.reshape(1))
+        )(*arrays, near, far, spot, flat_in, w_far, tail, alpha, side.reshape(1))
 
     fence = lax.optimization_barrier
-    own = jnp.concatenate([own, go_x(own)], axis=0)
+    own = pl.pallas_call(
+        join_kernel,
+        out_shape=jax.ShapeDtypeStruct((2 * block, 2 * width + LANES), bf16),
+        in_specs=[whole()] * 2,
+        out_specs=whole(),
+        name="join",
+    )(own, go_x(own))
     near, far, near_c, far_c, w_far = {0: own}, {}, {}, {}, {}
     state = {"a": near, "b": far, "c": near_c, "d": far_c, "w": w_far}
-    grads, kept, tails, other = {}, {}, {}, {}
-    state.update(grads=grads, other=other)
+    grads, kept, tails, other, packed, spots = {}, {}, {}, {}, {}, {}
+    state.update(grads=grads, other=other, packed=packed)
     d_own, d_got, totals, sent, value = {}, {}, {}, {}, {}
     state.update(d_own=d_own, d_got=d_got, totals=totals, sent=sent, value=value)
 
@@ -301,11 +344,13 @@
 
     def rows_of(k):
         arrays = (near[k], far[k], near_c[k], far_c[k])
-        grads[k], kept[k], tails[k] = first_half(arrays)
+        grads[k], packed[k], spots[k], kept[k], tails[k] = first_half(arrays)
 
     def grads_of(k):
         arrays = (near[k], far[k], near_c[k], far_c[k])
-        d_own[k], moved, totals[k] = second_half(arrays, grads[k], other[k], w_far[0], tails[k])
+        d_own[k], moved, totals[k] = second_half(
+            arrays, grads[k], other[k], spots[k], w_far[0], tails[k]
+        )
         d_got[k] = go_core(moved)
 
     def send_y(k):
@@ -332,23 +377,22 @@
             far_c[k - 1] = go_core(far[k - 1])
             rows_of(k - 1)
         if k == 2:
-            other[0] = go_x(grads[0])
+            other[0] = go_x(packed[0])
         step(*([("w", 0)] if k < 2 else []))
-    other[1] = go_x(grads[1])
+    other[1] = go_x(packed[1])
     far[3] = go_y(near[3])
     near_c[3] = go_core(near[3])
     far_c[2] = go_core(far[2])
     rows_of(2)
     grads_of(0)
     step()
-    other[2] = go_x(grads[2])
+    other[2] = go_x(packed[2])
     far_c[3] = go_core(far[3])
-    send_y(0)
     rows_of(3)
-    other[1], grads[3] = fence((other[1], grads[3]))
+    other[1], packed[3] = fence((other[1], packed[3]))
     grads_of(1)
-    step(("sent", 0))
-    other[3] = go_x(grads[3])
+    step()
+    other[3] = go_x(packed[3])
     send_y(1)
     other[2], sent[1] = fence((other[2], sent[1]))
     grads_of(2)
@@ -369,18 +413,17 @@
     pool[0] = jnp.concatenate([mine_sums, cross_sums], axis=0)
     step(("pool", 0))
     hop(3)
-    kept[3], value[3] = fence((kept[3], value[3]))
-    down = {0: make_down([kept[k] for k in range(planes)])}
-    state["down"] = down
+    send_y(0)
     pool[0] = pool[0] + go_jump(pool[0], 4)
     step()
+    kept[3], pool[0] = fence((kept[3], pool[0]))
     final = total_of(0) + value[0].astype(f32)
     crossed = go_x(final[1].astype(bf16)).astype(f32)
     left = jnp.where(side == 0, final[0, :, :half], crossed[:, :half])
     right = jnp.where(side == 0, crossed[:, :half], final[0, :, :half])
     grad_normed = jnp.concatenate([left, right], axis=1)
     row_grads = final[0, :, half:] + crossed[:, half:]
-    grad_down = down[0]
+    grad_down = make_down([kept[k] for k in range(planes)])
     sums = pool[0] + go_jump(pool[0], 8)
     mine_sums, cross_sums = sums[:8], sums[8:]
     sums = jnp.concatenate(
@@ -498,6 +541,8 @@
     dense = (
         lax.axis_size("dp") == 2
         and experts == 16
+        and arrays[0].shape[1] == 32
+        and top_count == 8
         and 2 * top_count >= experts
         and arrays[0].shape[2] % 2048 == 0
     )

time: 139 us -> 137 us (0.986)
  waiting for transfers between devices: 58.7 us -> 51.8 us
  starting transfers between devices: 35.1 us -> 37.9 us
  Pallas kernels: 32.4 us -> 34.4 us
  other arithmetic: 5.42 us -> 3.63 us
  local copies, waits for them, and re-layouts: 5.1 us -> 6.84 us
    ppermute x2, waiting for transfers between devices: 6.35 us -> 1.14 us  [go_jump(): return lax.ppermute(v, 'expert', [(e, e ^ by) for e in range(experts)])]
    ppermute x6, waiting for transfers between devices: 19 us -> 22.6 us  [go_z(): lax.ppermute(v, 'expert', [(e, (e + 4) % experts) for e in range(experts)])]
    ppermute x8, waiting for transfers between devices: 22.8 us -> 19.7 us  [go_x(): return lax.ppermute(v, 'dp', [(0, 1), (1, 0)])]
    ppermute x9, waiting for transfers between devices: 7.01 us -> 4.31 us  [go_y(): return lax.ppermute(v, 'expert', [(e, e ^ 2) for e in range(experts)])]
    ppermute x6, starting transfers between devices: 7.14 us -> 4.83 us  [go_z(): lax.ppermute(v, 'expert', [(e, (e + 4) % experts) for e in range(experts)])]
    ppermute x9, starting transfers between devices: 10.9 us -> 13 us  [go_y(): return lax.ppermute(v, 'expert', [(e, e ^ 2) for e in range(experts)])]
    pallas_call x0 -> x1, Pallas kernels: none -> 1.89 us  [dense_shards(): pl.pallas_call(join_kernel, out_shape=jax.ShapeDtypeStruct((2 * block, 2...]
    concatenate x1 -> x0, other arithmetic: 1.81 us -> none  [dense_shards(): own = jnp.concatenate([own, go_x(own)], axis=0)]
  transfers between devices with their start and end apart: 39 -> 39, of which waited for: 15 -> 17; matrix products, arithmetic and copies ran while one was open for 4% -> 4% of each run, Pallas kernels for 22% -> 23%
where the time goes in v8:
time: 137 us; the launch traced here: 136 us
  waiting for transfers between devices  51.8 us (38%)
  starting transfers between devices  37.9 us (28%)
  Pallas kernels  34.4 us (25%)
  local copies, waits for them, and re-layouts  6.84 us (5%)
  other arithmetic  3.63 us (3%)
  between operations  1.67 us (1%)
    ppermute x6, waiting for transfers between devices, go_z(): lax.ppermute(v, 'expert', [(e, (e + 4) % experts) for e in range(experts)])  22.6 us
    ppermute x8, waiting for transfers between devices, go_x(): return lax.ppermute(v, 'dp', [(0, 1), (1, 0)])  19.7 us
    pallas_call x4, Pallas kernels, first_half(): pl.pallas_call(functools.partial(rows_kernel, segments, width, hidden), o...  13.3 us
    ppermute x9, starting transfers between devices, go_y(): return lax.ppermute(v, 'expert', [(e, e ^ 2) for e in range(experts)])  13 us
    ppermute x8, starting transfers between devices, go_x(): return lax.ppermute(v, 'dp', [(0, 1), (1, 0)])  12.6 us
    pallas_call x4, Pallas kernels, second_half(): pl.pallas_call(functools.partial(grad_kernel, segments, half), out_shape=...  12.5 us
    pallas_call x1, Pallas kernels, make_down(): pl.pallas_call(functools.partial(down_kernel, planes, hidden), out_shape=...  4.93 us
    ppermute x6, starting transfers between devices, go_z(): lax.ppermute(v, 'expert', [(e, (e + 4) % experts) for e in range(experts)])  4.83 us
  transfers between devices with their start and end apart: 39, of which 17 were waited for; matrix products, arithmetic and copies ran while one was open for 4% of the time, Pallas kernels for 23%

profile of v8, /device:TPU:0, one launch (start us, length us, event | category | flops | bytes accessed | tf_op | source)
XLA Modules:
  0.0 136.3 jit_solution(3187710490330193019)
XLA Ops:
  0.6 1.9 %pack.1.first = bf16[32,4224]{1,0:T(8,128)(2,1)} custom-call(bf16[32,2048]{1,0:T(8,128)(2,1)} %bitcast.90, bf16[32,2048]{1,0:T(8,128)(2,1)} %bitcast.91, s32[8,32]{1,0:T(8,128)} %bitcast.94, bf16[8,32]{1,0:T(8,128)(2,1)} %bitcast.98), custom_call_target="tpu_custom_call" | custom-call | tf_op jit(solution)/shard_map/pack/pallas_call | solution.py:242
  2.5 2.9 %collective-permute-start = (bf16[32,4224]{1,0:T(8,128)(2,1)}, bf16[32,4224]{1,0:T(8,128)(2,1)S(1)}, u32[]{:S(2)}, u32[]{:S(2)}) collective-permute-start(bf16[32,4224]{1,0:T(8,128)(2,1)} %pack.1.first), channel_id=1, source_target_pairs={{0,1},{1,0},{2,3},{3,2},{4,5},{5,4},{6,7},{7,6},{8,9},{9,8},{10,11... | collective-permute-start | bytes 811016 | tf_op jit(solution)/shard_map/ppermute | solution.py:220
  5.4 6.7 %collective-permute-done.second = bf16[32,4224]{1,0:T(8,128)(2,1)S(1)} collective-permute-done((bf16[32,4224]{1,0:T(8,128)(2,1)}, bf16[32,4224]{1,0:T(8,128)(2,1)S(1)}, u32[]{:S(2)}, u32[]{:S(2)}) %collective-permute-start) | collective-permute-done | bytes 270368 | tf_op jit(solution)/shard_map/ppermute | solution.py:220
  12.8 1.9 %join.1.refs_0_ = bf16[64,4224]{1,0:T(8,128)(2,1)} custom-call(bf16[32,4224]{1,0:T(8,128)(2,1)} %pack.1.first, bf16[32,4224]{1,0:T(8,128)(2,1)} %copy-done.12), custom_call_target="tpu_custom_call" | custom-call | tf_op jit(solution)/shard_map/join/pallas_call | solution.py:308
  14.7 1.8 %collective-permute-start.1 = (bf16[64,4224]{1,0:T(8,128)(2,1)}, bf16[64,4224]{1,0:T(8,128)(2,1)}, u32[]{:S(2)}, u32[]{:S(2)}) collective-permute-start(bf16[64,4224]{1,0:T(8,128)(2,1)} %join.1.refs_0_), channel_id=1, source_target_pairs={{0,8},{2,10},{4,12},{6,14},{8,16},{10,18},{12,20},{14,22},{16,24},... | collective-permute-start | bytes 1622024 | tf_op jit(solution)/shard_map/ppermute | solution.py:229
  18.1 2.8 %constant_dynamic-slice_fusion = bf16[768,1024]{1,0:T(8,128)(2,1)} fusion(bf16[768,2048]{1,0:T(8,128)(2,1)} %bitcast.68, s32[]{:T(128)S(6)} %select_n.32), kind=kLoop, calls=%fused_computation.41 | loop fusion | bytes 3145732 | tf_op jit(solution)/shard_map/dynamic_slice | solution.py:257
  22.4 9.4 %collective-permute-done.1.refs_0_ = bf16[64,4224]{1,0:T(8,128)(2,1)} collective-permute-done((bf16[64,4224]{1,0:T(8,128)(2,1)}, bf16[64,4224]{1,0:T(8,128)(2,1)}, u32[]{:S(2)}, u32[]{:S(2)}) %collective-permute-start.1) | collective-permute-done | bytes 540704 | tf_op jit(solution)/shard_map/ppermute | solution.py:229
  37.5 3.8 %rows.4 = (bf16[256,768]{1,0:T(8,128)(2,1)S(1)}, bf16[192,768]{1,0:T(8,128)(2,1)S(1)}, f32[256,128]{1,0:T(8,128)S(1)}, bf16[256,2432]{1,0:T(8,128)(2,1)}, bf16[256,128]{1,0:T(8,128)(2,1)S(1)}) custom-call(bf16[64,4224]{1,0:T(8,128)(2,1)S(1)} %copy-done.3, bf16[64,4224]{1,0:T(8,128)(2,1)} %collective-permute-done.2.refs_1_, ...), custom_call_target="tpu_custom_call" | custom-call | tf_op jit(solution)/shard_map/rows/pallas_call | solution.py:267
  41.3 7.3 %collective-permute-done.4.refs_0_ = bf16[64,4224]{1,0:T(8,128)(2,1)} collective-permute-done((bf16[64,4224]{1,0:T(8,128)(2,1)}, bf16[64,4224]{1,0:T(8,128)(2,1)}, u32[]{:S(2)}, u32[]{:S(2)}) %collective-permute-start.4) | collective-permute-done | bytes 540704 | tf_op jit(solution)/shard_map/ppermute | solution.py:229
  52.7 3.7 %rows.5 = (bf16[256,768]{1,0:T(8,128)(2,1)S(1)}, bf16[192,768]{1,0:T(8,128)(2,1)S(1)}, f32[256,128]{1,0:T(8,128)S(1)}, bf16[256,2432]{1,0:T(8,128)(2,1)}, bf16[256,128]{1,0:T(8,128)(2,1)S(1)}) custom-call(bf16[64,4224]{1,0:T(8,128)(2,1)} %collective-permute-done.1.refs_0_, bf16[64,4224]{1,0:T(8,128)(2,1)} %collective-permute-done.5.refs_1_, ...), custom_call_target="tpu_custom_call" | custom-call | tf_op jit(solution)/shard_map/rows/pallas_call | solution.py:267
  56.4 7.3 %collective-permute-done.12.refs_5_ = bf16[192,768]{1,0:T(8,128)(2,1)S(1)} collective-permute-done((bf16[192,768]{1,0:T(8,128)(2,1)S(1)}, bf16[192,768]{1,0:T(8,128)(2,1)S(1)}, u32[]{:S(2)}, u32[]{:S(2)}) %collective-permute-start.12) | collective-permute-done | bytes 294944 | tf_op jit(solution)/shard_map/ppermute | solution.py:220
  63.7 1.8 %collective-permute-done.8.refs_0_ = bf16[64,4224]{1,0:T(8,128)(2,1)S(1)} collective-permute-done((bf16[64,4224]{1,0:T(8,128)(2,1)}, bf16[64,4224]{1,0:T(8,128)(2,1)S(1)}, u32[]{:S(2)}, u32[]{:S(2)}) %collective-permute-start.8) | collective-permute-done | bytes 540704 | tf_op jit(solution)/shard_map/ppermute | solution.py:229
  67.3 3.3 %grads.4 = (bf16[2,2,32,1152]{3,2,1,0:T(8,128)(2,1)S(1)}, bf16[2,2,32,1152]{3,2,1,0:T(8,128)(2,1)S(1)}, f32[8,1024]{1,0:T(8,128)S(1)}) custom-call(bf16[64,4224]{1,0:T(8,128)(2,1)S(1)} %copy-done.4, bf16[64,4224]{1,0:T(8,128)(2,1)} %collective-permute-done.2.refs_1_, bf16[64,4224]{1,0:T(8,128)(2,1)} %collective-permute-done.3.refs_2_, ...), custom_call_target="tpu_custom_call" | custom-call | tf_op jit(solution)/shard_map/grads/pallas_call | solution.py:290
  72.5 3.4 %rows.6 = (bf16[256,768]{1,0:T(8,128)(2,1)S(1)}, bf16[192,768]{1,0:T(8,128)(2,1)S(1)}, f32[256,128]{1,0:T(8,128)S(1)}, bf16[256,2432]{1,0:T(8,128)(2,1)}, bf16[256,128]{1,0:T(8,128)(2,1)S(1)}) custom-call(bf16[64,4224]{1,0:T(8,128)(2,1)} %collective-permute-done.4.refs_0_, bf16[64,4224]{1,0:T(8,128)(2,1)S(1)} %collective-permute-done.9.refs_1_, ...), custom_call_target="tpu_custom_call" | custom-call | tf_op jit(solution)/shard_map/rows/pallas_call | solution.py:267
  76.0 4.1 %collective-permute-done.18.refs_5_ = bf16[192,768]{1,0:T(8,128)(2,1)S(1)} collective-permute-done((bf16[192,768]{1,0:T(8,128)(2,1)S(1)}, bf16[192,768]{1,0:T(8,128)(2,1)S(1)}, u32[]{:S(2)}, u32[]{:S(2)}) %collective-permute-start.18) | collective-permute-done | bytes 294944 | tf_op jit(solution)/shard_map/ppermute | solution.py:220
  82.1 2.4 %rows.7 = (bf16[256,768]{1,0:T(8,128)(2,1)S(1)}, bf16[192,768]{1,0:T(8,128)(2,1)S(1)}, f32[256,128]{1,0:T(8,128)S(1)}, bf16[256,2432]{1,0:T(8,128)(2,1)}, bf16[256,128]{1,0:T(8,128)(2,1)S(1)}) custom-call(bf16[64,4224]{1,0:T(8,128)(2,1)S(1)} %collective-permute-done.8.refs_0_, bf16[64,4224]{1,0:T(8,128)(2,1)S(1)} %collective-permute-done.14.refs_1_, ...), custom_call_target="tpu_custom_call" | custom-call | tf_op jit(solution)/shard_map/rows/pallas_call | solution.py:267
  84.5 3.3 %grads.5 = (bf16[2,2,32,1152]{3,2,1,0:T(8,128)(2,1)S(1)}, bf16[2,2,32,1152]{3,2,1,0:T(8,128)(2,1)S(1)}, f32[8,1024]{1,0:T(8,128)S(1)}) custom-call(bf16[64,4224]{1,0:T(8,128)(2,1)} %collective-permute-done.1.refs_0_, bf16[64,4224]{1,0:T(8,128)(2,1)} %collective-permute-done.5.refs_1_, bf16[64,4224]{1,0:T(8,128)(2,1)} %collective-permute-done.6.refs_2_, ...), custom_call_target="tpu_custom_call" | custom-call | tf_op jit(solution)/shard_map/grads/pallas_call | solution.py:290
  92.7 2.8 %collective-permute-done.22 = bf16[2,32,1152]{2,1,0:T(8,128)(2,1)S(1)} collective-permute-done((bf16[2,32,1152]{2,1,0:T(8,128)(2,1)S(1)}, bf16[2,32,1152]{2,1,0:T(8,128)(2,1)S(1)}, u32[]{:S(2)}, u32[]{:S(2)}) %collective-permute-start.22) | collective-permute-done | bytes 147488 | tf_op jit(solution)/shard_map/ppermute | solution.py:223
  95.5 3.0 %grads.6 = (bf16[2,2,32,1152]{3,2,1,0:T(8,128)(2,1)S(1)}, bf16[2,2,32,1152]{3,2,1,0:T(8,128)(2,1)S(1)}, f32[8,1024]{1,0:T(8,128)S(1)}) custom-call(bf16[64,4224]{1,0:T(8,128)(2,1)} %collective-permute-done.4.refs_0_, bf16[64,4224]{1,0:T(8,128)(2,1)S(1)} %collective-permute-done.9.refs_1_, bf16[64,4224]{1,0:T(8,128)(2,1)S(1)} %collective-permute-done.10.refs_2_, ...), custom_call_target="tpu_custom_call" | custom-call | tf_op jit(solution)/shard_map/grads/pallas_call | solution.py:290
  101.8 2.8 %grads.7 = (bf16[2,2,32,1152]{3,2,1,0:T(8,128)(2,1)S(1)}, bf16[2,2,32,1152]{3,2,1,0:T(8,128)(2,1)S(1)}, f32[8,1024]{1,0:T(8,128)S(1)}) custom-call(bf16[64,4224]{1,0:T(8,128)(2,1)S(1)} %collective-permute-done.8.refs_0_, bf16[64,4224]{1,0:T(8,128)(2,1)S(1)} %collective-permute-done.14.refs_1_, bf16[64,4224]{1,0:T(8,128)(2,1)S(1)} %collective-permute-done.15.refs_2_, ...), custom_call_target="tpu_custom_call" | custom-call | tf_op jit(solution)/shard_map/grads/pallas_call | solution.py:290
  113.8 1.8 %collective-permute-done.33 = f32[8,1024]{1,0:T(8,128)S(1)} collective-permute-done((f32[8,1024]{1,0:T(8,128)S(1)}, f32[8,1024]{1,0:T(8,128)S(1)}, u32[]{:S(2)}, u32[]{:S(2)}) %collective-permute-start.33) | collective-permute-done | bytes 32800 | tf_op jit(solution)/shard_map/ppermute | solution.py:238
  121.6 3.0 %collective-permute-done.36 = bf16[2,32,1152]{2,1,0:T(8,128)(2,1)S(1)} collective-permute-done((bf16[2,32,1152]{2,1,0:T(8,128)(2,1)S(1)}, bf16[2,32,1152]{2,1,0:T(8,128)(2,1)S(1)}, u32[]{:S(2)}, u32[]{:S(2)}) %collective-permute-start.36) | collective-permute-done | bytes 147488 | tf_op jit(solution)/shard_map/ppermute | solution.py:229
  124.6 3.1 %collective-permute-start.38 = (f32[16,1024]{1,0:T(8,128)S(1)}, f32[16,1024]{1,0:T(8,128)S(1)}, u32[]{:S(2)}, u32[]{:S(2)}) collective-permute-start(f32[16,1024]{1,0:T(8,128)S(1)} %fusion.15), channel_id=1, source_target_pairs={{0,16},{2,18},{4,20},{6,22},{8,24},{10,26},{12,28},{14,30},{16,0},... | collective-permute-start | bytes 196616 | tf_op jit(solution)/shard_map/ppermute | solution.py:232
  128.4 4.9 %down.1 = bf16[384,2048]{1,0:T(8,128)(2,1)} custom-call(bf16[256,2432]{1,0:T(8,128)(2,1)} %get-tuple-element.277.refs_0_, bf16[256,2432]{1,0:T(8,128)(2,1)} %get-tuple-element.278.refs_1_, bf16[256,2432]{1,0:T(8,128)(2,1)} %get-tuple-element.279.refs_2_, bf16[256,2432]{1,0:T(8,128)(2,1)} %get-tuple-element.282.refs_3_), custom_call_target="tpu_custom_call" | custom-call | tf_op jit(solution)/shard_map/down/pallas_call | solution.py:323
  (123 shorter events, 45.2 us)
Async XLA Ops:
  2.5 9.6 %collective-permute-start = (bf16[32,4224]{1,0:T(8,128)(2,1)}, bf16[32,4224]{1,0:T(8,128)(2,1)S(1)}, u32[]{:S(2)}, u32[]{:S(2)}) collective-permute-start(bf16[32,4224]{1,0:T(8,128)(2,1)} %pack.1.first), channel_id=1, source_target_pairs={{0,1},{1,0},{2,3},{3,2},{4,5},{5,4},{6,7},{7,6},{8,9},{9,8},{10,11... | collective-permute-start | bytes 811016 | tf_op jit(solution)/shard_map/ppermute | solution.py:220
  14.7 17.1 %collective-permute-start.1 = (bf16[64,4224]{1,0:T(8,128)(2,1)}, bf16[64,4224]{1,0:T(8,128)(2,1)}, u32[]{:S(2)}, u32[]{:S(2)}) collective-permute-start(bf16[64,4224]{1,0:T(8,128)(2,1)} %join.1.refs_0_), channel_id=1, source_target_pairs={{0,8},{2,10},{4,12},{6,14},{8,16},{10,18},{12,20},{14,22},{16,24},... | collective-permute-start | bytes 1622024 | tf_op jit(solution)/shard_map/ppermute | solution.py:229
  16.5 15.3 %collective-permute-start.2 = (bf16[64,4224]{1,0:T(8,128)(2,1)}, bf16[64,4224]{1,0:T(8,128)(2,1)}, u32[]{:S(2)}, u32[]{:S(2)}) collective-permute-start(bf16[64,4224]{1,0:T(8,128)(2,1)} %join.1.refs_0_), channel_id=1, source_target_pairs={{0,4},{2,6},{4,0},{6,2},{8,12},{10,14},{12,8},{14,10},{16,20},{18,... | collective-permute-start | bytes 1622024 | tf_op jit(solution)/shard_map/ppermute | solution.py:223
  20.9 44.6 %collective-permute-start.13 = (bf16[768,1024]{1,0:T(8,128)(2,1)}, bf16[768,1024]{1,0:T(8,128)(2,1)}, u32[]{:S(2)}, u32[]{:S(2)}) collective-permute-start(bf16[768,1024]{1,0:T(8,128)(2,1)} %constant_dynamic-slice_fusion), channel_id=1, source_target_pairs={{0,1},{1,0},{2,3},{3,2},{4,5},{5,4},{6,7},{7,6},{8,9},{9,8},{10,11... | collective-permute-start | bytes 4718600 | tf_op jit(solution)/shard_map/ppermute | solution.py:220
  31.8 16.8 %collective-permute-start.4 = (bf16[64,4224]{1,0:T(8,128)(2,1)}, bf16[64,4224]{1,0:T(8,128)(2,1)}, u32[]{:S(2)}, u32[]{:S(2)}) collective-permute-start(bf16[64,4224]{1,0:T(8,128)(2,1)} %collective-permute-done.1.refs_0_), channel_id=1, source_target_pairs={{0,8},{2,10},{4,12},{6,14},{8,16},{10,18},{12,20},{14,22},{16,24},... | collective-permute-start | bytes 1622024 | tf_op jit(solution)/shard_map/ppermute | solution.py:229
  32.9 15.8 %collective-permute-start.5 = (bf16[64,4224]{1,0:T(8,128)(2,1)}, bf16[64,4224]{1,0:T(8,128)(2,1)}, u32[]{:S(2)}, u32[]{:S(2)}) collective-permute-start(bf16[64,4224]{1,0:T(8,128)(2,1)} %collective-permute-done.1.refs_0_), channel_id=1, source_target_pairs={{0,4},{2,6},{4,0},{6,2},{8,12},{10,14},{12,8},{14,10},{16,20},{18,... | collective-permute-start | bytes 1622024 | tf_op jit(solution)/shard_map/ppermute | solution.py:223
  34.4 14.3 %collective-permute-start.6 = (bf16[64,4224]{1,0:T(8,128)(2,1)}, bf16[64,4224]{1,0:T(8,128)(2,1)}, u32[]{:S(2)}, u32[]{:S(2)}) collective-permute-start(bf16[64,4224]{1,0:T(8,128)(2,1)} %collective-permute-done.1.refs_0_), channel_id=1, source_target_pairs={{0,2},{2,0},{4,6},{6,4},{8,10},{10,8},{12,14},{14,12},{16,18},{18,... | collective-permute-start | bytes 1622024 | tf_op jit(solution)/shard_map/ppermute | solution.py:226
  48.7 14.9 %collective-permute-start.10 = (bf16[64,4224]{1,0:T(8,128)(2,1)}, bf16[64,4224]{1,0:T(8,128)(2,1)S(1)}, u32[]{:S(2)}, u32[]{:S(2)}) collective-permute-start(bf16[64,4224]{1,0:T(8,128)(2,1)} %collective-permute-done.4.refs_0_), channel_id=1, source_target_pairs={{0,2},{2,0},{4,6},{6,4},{8,10},{10,8},{12,14},{14,12},{16,18},{18,... | collective-permute-start | bytes 1622024 | tf_op jit(solution)/shard_map/ppermute | solution.py:226
  49.2 16.3 %collective-permute-start.8 = (bf16[64,4224]{1,0:T(8,128)(2,1)}, bf16[64,4224]{1,0:T(8,128)(2,1)S(1)}, u32[]{:S(2)}, u32[]{:S(2)}) collective-permute-start(bf16[64,4224]{1,0:T(8,128)(2,1)} %collective-permute-done.4.refs_0_), channel_id=1, source_target_pairs={{0,8},{2,10},{4,12},{6,14},{8,16},{10,18},{12,20},{14,22},{16,24},... | collective-permute-start | bytes 1622024 | tf_op jit(solution)/shard_map/ppermute | solution.py:229
  49.7 15.8 %collective-permute-start.9 = (bf16[64,4224]{1,0:T(8,128)(2,1)}, bf16[64,4224]{1,0:T(8,128)(2,1)S(1)}, u32[]{:S(2)}, u32[]{:S(2)}) collective-permute-start(bf16[64,4224]{1,0:T(8,128)(2,1)} %collective-permute-done.4.refs_0_), channel_id=1, source_target_pairs={{0,4},{2,6},{4,0},{6,2},{8,12},{10,14},{12,8},{14,10},{16,20},{18,... | collective-permute-start | bytes 1622024 | tf_op jit(solution)/shard_map/ppermute | solution.py:223
  51.2 12.5 %collective-permute-start.12 = (bf16[192,768]{1,0:T(8,128)(2,1)S(1)}, bf16[192,768]{1,0:T(8,128)(2,1)S(1)}, u32[]{:S(2)}, u32[]{:S(2)}) collective-permute-start(bf16[192,768]{1,0:T(8,128)(2,1)S(1)} %get-tuple-element.162), channel_id=1, source_target_pairs={{0,1},{1,0},{2,3},{3,2},{4,5},{5,4},{6,7},{7,6},{8,9},{9,8},{10,11... | collective-permute-start | bytes 884744 | tf_op jit(solution)/shard_map/ppermute | solution.py:220
  65.5 7.0 %collective-permute-start.16 = (bf16[64,4224]{1,0:T(8,128)(2,1)S(1)}, bf16[64,4224]{1,0:T(8,128)(2,1)S(1)}, u32[]{:S(2)}, u32[]{:S(2)}) collective-permute-start(bf16[64,4224]{1,0:T(8,128)(2,1)S(1)} %collective-permute-done.9.refs_1_), channel_id=1, source_target_pairs={{0,2},{2,0},{4,6},{6,4},{8,10},{10,8},{12,14},{14,12},{16,18},{18,... | collective-permute-start | bytes 1622024 | tf_op jit(solution)/shard_map/ppermute | solution.py:226
  65.5 14.7 %collective-permute-start.14 = (bf16[64,4224]{1,0:T(8,128)(2,1)S(1)}, bf16[64,4224]{1,0:T(8,128)(2,1)S(1)}, u32[]{:S(2)}, u32[]{:S(2)}) collective-permute-start(bf16[64,4224]{1,0:T(8,128)(2,1)S(1)} %collective-permute-done.8.refs_0_), channel_id=1, source_target_pairs={{0,4},{2,6},{4,0},{6,2},{8,12},{10,14},{12,8},{14,10},{16,20},{18,... | collective-permute-start | bytes 1622024 | tf_op jit(solution)/shard_map/ppermute | solution.py:223
  67.1 13.1 %collective-permute-start.15 = (bf16[64,4224]{1,0:T(8,128)(2,1)S(1)}, bf16[64,4224]{1,0:T(8,128)(2,1)S(1)}, u32[]{:S(2)}, u32[]{:S(2)}) collective-permute-start(bf16[64,4224]{1,0:T(8,128)(2,1)S(1)} %collective-permute-done.8.refs_0_), channel_id=1, source_target_pairs={{0,2},{2,0},{4,6},{6,4},{8,10},{10,8},{12,14},{14,12},{16,18},{18,... | collective-permute-start | bytes 1622024 | tf_op jit(solution)/shard_map/ppermute | solution.py:226
  71.0 9.1 %collective-permute-start.18 = (bf16[192,768]{1,0:T(8,128)(2,1)S(1)}, bf16[192,768]{1,0:T(8,128)(2,1)S(1)}, u32[]{:S(2)}, u32[]{:S(2)}) collective-permute-start(bf16[192,768]{1,0:T(8,128)(2,1)S(1)} %get-tuple-element.186), channel_id=1, source_target_pairs={{0,1},{1,0},{2,3},{3,2},{4,5},{5,4},{6,7},{7,6},{8,9},{9,8},{10,11... | collective-permute-start | bytes 884744 | tf_op jit(solution)/shard_map/ppermute | solution.py:220
  80.2 9.4 %collective-permute-start.21 = (bf16[192,768]{1,0:T(8,128)(2,1)S(1)}, bf16[192,768]{1,0:T(8,128)(2,1)S(1)}, u32[]{:S(2)}, u32[]{:S(2)}) collective-permute-start(bf16[192,768]{1,0:T(8,128)(2,1)S(1)} %get-tuple-element.213), channel_id=1, source_target_pairs={{0,1},{1,0},{2,3},{3,2},{4,5},{5,4},{6,7},{7,6},{8,9},{9,8},{10,11... | collective-permute-start | bytes 884744 | tf_op jit(solution)/shard_map/ppermute | solution.py:220
  91.3 10.6 %collective-permute-start.24 = (bf16[192,768]{1,0:T(8,128)(2,1)S(1)}, bf16[192,768]{1,0:T(8,128)(2,1)S(1)}, u32[]{:S(2)}, u32[]{:S(2)}) collective-permute-start(bf16[192,768]{1,0:T(8,128)(2,1)S(1)} %get-tuple-element.238), channel_id=1, source_target_pairs={{0,1},{1,0},{2,3},{3,2},{4,5},{5,4},{6,7},{7,6},{8,9},{9,8},{10,11... | collective-permute-start | bytes 884744 | tf_op jit(solution)/shard_map/ppermute | solution.py:220
  98.7 8.3 %collective-permute-start.29 = (bf16[2,32,1152]{2,1,0:T(8,128)(2,1)S(1)}, bf16[2,32,1152]{2,1,0:T(8,128)(2,1)S(1)}, u32[]{:S(2)}, u32[]{:S(2)}) collective-permute-start(bf16[2,32,1152]{2,1,0:T(8,128)(2,1)S(1)} %fusion.5), channel_id=1, source_target_pairs={{0,8},{2,10},{4,12},{6,14},{8,16},{10,18},{12,20},{14,22},{16,24},... | collective-permute-start | bytes 442376 | tf_op jit(solution)/shard_map/ppermute | solution.py:229
  100.3 6.8 %collective-permute-start.27 = (bf16[2,32,1152]{2,1,0:T(8,128)(2,1)S(1)}, bf16[2,32,1152]{2,1,0:T(8,128)(2,1)S(1)}, u32[]{:S(2)}, u32[]{:S(2)}) collective-permute-start(bf16[2,32,1152]{2,1,0:T(8,128)(2,1)S(1)} %fusion.11), channel_id=1, source_target_pairs={{0,4},{2,6},{4,0},{6,2},{8,12},{10,14},{12,8},{14,10},{16,20},{18,... | collective-permute-start | bytes 442376 | tf_op jit(solution)/shard_map/ppermute | solution.py:223
  107.1 9.5 %collective-permute-start.30 = (bf16[2,32,1152]{2,1,0:T(8,128)(2,1)S(1)}, bf16[2,32,1152]{2,1,0:T(8,128)(2,1)S(1)}, u32[]{:S(2)}, u32[]{:S(2)}) collective-permute-start(bf16[2,32,1152]{2,1,0:T(8,128)(2,1)S(1)} %fusion.4), channel_id=1, source_target_pairs={{0,8},{2,10},{4,12},{6,14},{8,16},{10,18},{12,20},{14,22},{16,24},... | collective-permute-start | bytes 442376 | tf_op jit(solution)/shard_map/ppermute | solution.py:229
  107.2 9.4 %collective-permute-start.28 = (bf16[2,32,1152]{2,1,0:T(8,128)(2,1)S(1)}, bf16[2,32,1152]{2,1,0:T(8,128)(2,1)S(1)}, u32[]{:S(2)}, u32[]{:S(2)}) collective-permute-start(bf16[2,32,1152]{2,1,0:T(8,128)(2,1)S(1)} %fusion.12), channel_id=1, source_target_pairs={{0,4},{2,6},{4,0},{6,2},{8,12},{10,14},{12,8},{14,10},{16,20},{18,... | collective-permute-start | bytes 442376 | tf_op jit(solution)/shard_map/ppermute | solution.py:223
  117.6 7.0 %collective-permute-start.36 = (bf16[2,32,1152]{2,1,0:T(8,128)(2,1)S(1)}, bf16[2,32,1152]{2,1,0:T(8,128)(2,1)S(1)}, u32[]{:S(2)}, u32[]{:S(2)}) collective-permute-start(bf16[2,32,1152]{2,1,0:T(8,128)(2,1)S(1)} %fusion.2), channel_id=1, source_target_pairs={{0,8},{2,10},{4,12},{6,14},{8,16},{10,18},{12,20},{14,22},{16,24},... | collective-permute-start | bytes 442376 | tf_op jit(solution)/shard_map/ppermute | solution.py:229
  124.6 8.7 %collective-permute-start.38 = (f32[16,1024]{1,0:T(8,128)S(1)}, f32[16,1024]{1,0:T(8,128)S(1)}, u32[]{:S(2)}, u32[]{:S(2)}) collective-permute-start(f32[16,1024]{1,0:T(8,128)S(1)} %fusion.15), channel_id=1, source_target_pairs={{0,16},{2,18},{4,20},{6,22},{8,24},{10,26},{12,28},{14,30},{16,0},... | collective-permute-start | bytes 196616 | tf_op jit(solution)/shard_map/ppermute | solution.py:232
  127.8 6.8 %collective-permute-start.37 = (bf16[32,1152]{1,0:T(8,128)(2,1)S(1)}, bf16[32,1152]{1,0:T(8,128)(2,1)S(1)}, u32[]{:S(2)}, u32[]{:S(2)}) collective-permute-start(bf16[32,1152]{1,0:T(8,128)(2,1)S(1)} %fusion.14), channel_id=1, source_target_pairs={{0,1},{1,0},{2,3},{3,2},{4,5},{5,4},{6,7},{7,6},{8,9},{9,8},{10,11... | collective-permute-start | bytes 221192 | tf_op jit(solution)/shard_map/ppermute | solution.py:220
  (29 other events, 196.7 us)

commit v9 on v8

--- a/solution.py
+++ b/solution.py
@@ -256,16 +256,21 @@
     side = lax.axis_index("dp").astype(jnp.int32)
     w_send = lax.dynamic_slice_in_dim(flat_in, (1 - side) * half, half, axis=1)
 
-    segments = tuple(
-        tuple((x * 4 + core * 2 + y) * block for x in range(2))
-        for core in range(2)
-        for y in range(2)
-    )
+    def segments_of(arrays):
+        places = [
+            (x * 4 + core * 2 + y) * block
+            for core in range(2)
+            for y in range(2)
+            for x in range(2)
+        ]
+        size = 8 // len(arrays)
+        return tuple(tuple(places[k : k + size]) for k in range(0, 8, size))
+
     params = pltpu.CompilerParams(vmem_limit_bytes=14 << 20)
 
     def first_half(arrays):
         return pl.pallas_call(
-            functools.partial(rows_kernel, segments, width, hidden),
+            functools.partial(rows_kernel, segments_of(arrays), width, hidden),
             out_shape=(
                 jax.ShapeDtypeStruct((rows, 2 * hidden), bf16),
                 jax.ShapeDtypeStruct((8 * slots, 2 * hidden), bf16),
@@ -273,7 +278,7 @@
                 pltpu.HBM((rows, hidden + width), bf16),
                 jax.ShapeDtypeStruct((rows, LANES), bf16),
             ),
-            in_specs=[whole()] * 8 + [scalar(), scalar()],
+            in_specs=[whole()] * (len(arrays) + 4) + [scalar(), scalar()],
             out_specs=(whole(),) * 3 + (pl.BlockSpec(memory_space=pltpu.HBM), whole()),
             scratch_shapes=[
                 pltpu.VMEM((rows, width), bf16),
@@ -288,13 +293,13 @@
 
     def second_half(arrays, near, far, spot, w_far, tail):
         return pl.pallas_call(
-            functools.partial(grad_kernel, segments, half),
+            functools.partial(grad_kernel, segments_of(arrays), half),
             out_shape=(
                 jax.ShapeDtypeStruct((2, 2, block, half + LANES), bf16),
                 jax.ShapeDtypeStruct((2, 2, block, half + LANES), bf16),
                 jax.ShapeDtypeStruct((8, half), f32),
             ),
-            in_specs=[whole()] * 10 + [scalar(), scalar()],
+            in_specs=[whole()] * (len(arrays) + 6) + [scalar(), scalar()],
             out_specs=(whole(),) * 3,
             scratch_shapes=[
                 pltpu.VMEM((rows, half), f32),
@@ -305,14 +310,16 @@
         )(*arrays, near, far, spot, flat_in, w_far, tail, alpha, side.reshape(1))
 
     fence = lax.optimization_barrier
-    own = pl.pallas_call(
-        join_kernel,
-        out_shape=jax.ShapeDtypeStruct((2 * block, 2 * width + LANES), bf16),
-        in_specs=[whole()] * 2,
-        out_specs=whole(),
-        name="join",
-    )(own, go_x(own))
-    near, far, near_c, far_c, w_far = {0: own}, {}, {}, {}, {}
+    def join(first, second):
+        return pl.pallas_call(
+            join_kernel,
+            out_shape=jax.ShapeDtypeStruct((2 * block, 2 * width + LANES), bf16),
+            in_specs=[whole()] * 2,
+            out_specs=whole(),
+            name="join",
+        )(first, second)
+
+    near, far, near_c, far_c, w_far = {0: [own]}, {}, {}, {}, {}
     state = {"a": near, "b": far, "c": near_c, "d": far_c, "w": w_far}
     grads, kept, tails, other, packed, spots = {}, {}, {}, {}, {}, {}
     state.update(grads=grads, other=other, packed=packed)
@@ -343,11 +350,11 @@
             held.update(new[name])
 
     def rows_of(k):
-        arrays = (near[k], far[k], near_c[k], far_c[k])
+        arrays = near[k] + far[k] + near_c[k] + far_c[k]
         grads[k], packed[k], spots[k], kept[k], tails[k] = first_half(arrays)
 
     def grads_of(k):
-        arrays = (near[k], far[k], near_c[k], far_c[k])
+        arrays = near[k] + far[k] + near_c[k] + far_c[k]
         d_own[k], moved, totals[k] = second_half(
             arrays, grads[k], other[k], spots[k], w_far[0], tails[k]
         )
@@ -366,46 +373,59 @@
             carried = carried + value[k].astype(f32)
         value[(k + 1) % planes] = go_z(carried.astype(bf16))
 
-    for k in range(3):
-        near[k + 1] = go_z(near[k])
-        far[k] = go_y(near[k])
-        near_c[k] = go_core(near[k])
-        if k == 0:
-            w_send, near_c[0] = fence((w_send, near_c[0]))
-            w_far[0] = go_x(w_send)
+    near[0].append(go_x(own))
+    near[1] = [go_z(own)]
+    far[0] = [go_y(own)]
+    near_c[0] = [go_core(own)]
+    step()
+    near[1].append(go_z(near[0][1]))
+    far[0].append(go_y(near[0][1]))
+    near_c[0].append(go_core(near[0][1]))
+    far_c[0] = [go_core(far[0][0])]
+    w_send, near_c[0] = fence((w_send, near_c[0]))
+    w_far[0] = go_x(w_send)
+    step(("w", 0))
+    near[1] = [join(*near[1])]
+    for k in range(1, 3):
+        near[k + 1] = [go_z(near[k][0])]
+        far[k] = [go_y(near[k][0])]
+        near_c[k] = [go_core(near[k][0])]
+        if k == 1:
+            far_c[0].append(go_core(far[0][1]))
         else:
-            far_c[k - 1] = go_core(far[k - 1])
-            rows_of(k - 1)
+            far_c[1] = [go_core(far[1][0])]
+        rows_of(k - 1)
         if k == 2:
             other[0] = go_x(packed[0])
-        step(*([("w", 0)] if k < 2 else []))
+        step(*([("w", 0)] if k == 1 else []))
     other[1] = go_x(packed[1])
-    far[3] = go_y(near[3])
-    near_c[3] = go_core(near[3])
-    far_c[2] = go_core(far[2])
+    far[3] = [go_y(near[3][0])]
+    near_c[3] = [go_core(near[3][0])]
+    far_c[2] = [go_core(far[2][0])]
     rows_of(2)
     grads_of(0)
     step()
     other[2] = go_x(packed[2])
-    far_c[3] = go_core(far[3])
+    far_c[3] = [go_core(far[3][0])]
     rows_of(3)
     other[1], packed[3] = fence((other[1], packed[3]))
     grads_of(1)
     step()
     other[3] = go_x(packed[3])
     send_y(1)
-    other[2], sent[1] = fence((other[2], sent[1]))
+    other[2], sent[1], d_got[0] = fence((other[2], sent[1], d_got[0]))
     grads_of(2)
     hop(1)
     send_y(2)
-    step(("sent", 2), ("value", 2))
+    send_y(0)
+    step(("sent", 0), ("sent", 2), ("value", 2))
     grads_of(3)
     hop(2)
     pool = {}
     pool[0] = sum(totals[k] for k in range(1, planes)) + totals[0]
     pool[0] = pool[0] + go_core(pool[0])
     state["pool"] = pool
-    step(("value", 3), ("sent", 2), ("value", 2))
+    step(("value", 3), ("sent", 2), ("value", 2), ("sent", 0))
     send_y(3)
     part = pool[0]
     mine_sums = part + go_y(part)
@@ -413,7 +433,6 @@
     pool[0] = jnp.concatenate([mine_sums, cross_sums], axis=0)
     step(("pool", 0))
     hop(3)
-    send_y(0)
     pool[0] = pool[0] + go_jump(pool[0], 4)
     step()
     kept[3], pool[0] = fence((kept[3], pool[0]))

time: 137 us -> 136 us (level)
  starting transfers between devices: 37.9 us -> 30.2 us
  waiting for transfers between devices: 51.8 us -> 56.6 us
  local copies, waits for them, and re-layouts: 6.84 us -> 9.87 us
    ppermute x8, starting transfers between devices: 12.6 us -> 6.74 us  [go_x(): return lax.ppermute(v, 'dp', [(0, 1), (1, 0)])]
    ppermute x6 -> x7, waiting for transfers between devices: 22.6 us -> 19.5 us  [go_z(): lax.ppermute(v, 'expert', [(e, (e + 4) % experts) for e in range(experts)])]
    unnamed x29 -> x45, local copies, waits for them, and re-layouts: 3.86 us -> 6.88 us
    ppermute x8, waiting for transfers between devices: 19.7 us -> 21.9 us  [go_x(): return lax.ppermute(v, 'dp', [(0, 1), (1, 0)])]
    ppermute x2, waiting for transfers between devices: 1.14 us -> 3.3 us  [go_jump(): return lax.ppermute(v, 'expert', [(e, e ^ by) for e in range(experts)])]
    ppermute x9 -> x10, waiting for transfers between devices: 4.31 us -> 6.04 us  [go_y(): return lax.ppermute(v, 'expert', [(e, e ^ 2) for e in range(experts)])]
    ppermute x6 -> x7, starting transfers between devices: 4.83 us -> 5.11 us  [go_z(): lax.ppermute(v, 'expert', [(e, (e + 4) % experts) for e in range(experts)])]
    ppermute x9 -> x10, starting transfers between devices: 13 us -> 12.9 us  [go_y(): return lax.ppermute(v, 'expert', [(e, e ^ 2) for e in range(experts)])]
  transfers between devices with their start and end apart: 39 -> 43, of which waited for: 17 -> 18; matrix products, arithmetic and copies ran while one was open for 4% -> 3% of each run, Pallas kernels for 23% -> 24%
where the time goes in v9:
time: 136 us; the launch traced here: 135 us
  waiting for transfers between devices  56.6 us (42%)
  Pallas kernels  34.4 us (25%)
  starting transfers between devices  30.2 us (22%)
  local copies, waits for them, and re-layouts  9.87 us (7%)
  other arithmetic  2.74 us (2%)
  between operations  1.7 us (1%)
    ppermute x8, waiting for transfers between devices, go_x(): return lax.ppermute(v, 'dp', [(0, 1), (1, 0)])  21.9 us
    ppermute x7, waiting for transfers between devices, go_z(): lax.ppermute(v, 'expert', [(e, (e + 4) % experts) for e in range(experts)])  19.5 us
    pallas_call x4, Pallas kernels, first_half(): pl.pallas_call(functools.partial(rows_kernel, segments_of(arrays), width,...  13.4 us
    ppermute x10, starting transfers between devices, go_y(): return lax.ppermute(v, 'expert', [(e, e ^ 2) for e in range(experts)])  12.9 us
    pallas_call x4, Pallas kernels, second_half(): pl.pallas_call(functools.partial(grad_kernel, segments_of(arrays), half),...  12.3 us
    unnamed x45, local copies, waits for them, and re-layouts  6.88 us
    ppermute x8, starting transfers between devices, go_x(): return lax.ppermute(v, 'dp', [(0, 1), (1, 0)])  6.74 us
    ppermute x10, waiting for transfers between devices, go_y(): return lax.ppermute(v, 'expert', [(e, e ^ 2) for e in range(experts)])  6.04 us
  transfers between devices with their start and end apart: 43, of which 18 were waited for; matrix products, arithmetic and copies ran while one was open for 3% of the time, Pallas kernels for 24%

profile of v9, /device:TPU:0, one launch (start us, length us, event | category | flops | bytes accessed | tf_op | source)
XLA Modules:
  0.0 135.4 jit_solution(10500048685443216692)
XLA Ops:
  0.6 1.9 %pack.1.refs_0_ = bf16[32,4224]{1,0:T(8,128)(2,1)} custom-call(bf16[32,2048]{1,0:T(8,128)(2,1)} %bitcast.90, bf16[32,2048]{1,0:T(8,128)(2,1)} %bitcast.91, s32[8,32]{1,0:T(8,128)} %bitcast.94, bf16[8,32]{1,0:T(8,128)(2,1)} %bitcast.98), custom_call_target="tpu_custom_call" | custom-call | tf_op jit(solution)/shard_map/pack/pallas_call | solution.py:242
  2.5 2.9 %collective-permute-start = (bf16[32,4224]{1,0:T(8,128)(2,1)}, bf16[32,4224]{1,0:T(8,128)(2,1)}, u32[]{:S(2)}, u32[]{:S(2)}) collective-permute-start(bf16[32,4224]{1,0:T(8,128)(2,1)} %pack.1.refs_0_), channel_id=1, source_target_pairs={{0,1},{1,0},{2,3},{3,2},{4,5},{5,4},{6,7},{7,6},{8,9},{9,8},{10,11... | collective-permute-start | bytes 811016 | tf_op jit(solution)/shard_map/ppermute | solution.py:220
  8.6 3.7 %collective-permute-done.refs_1_ = bf16[32,4224]{1,0:T(8,128)(2,1)} collective-permute-done((bf16[32,4224]{1,0:T(8,128)(2,1)}, bf16[32,4224]{1,0:T(8,128)(2,1)}, u32[]{:S(2)}, u32[]{:S(2)}) %collective-permute-start) | collective-permute-done | bytes 270368 | tf_op jit(solution)/shard_map/ppermute | solution.py:220
  12.2 3.2 %collective-permute-done.1.first = bf16[32,4224]{1,0:T(8,128)(2,1)S(1)} collective-permute-done((bf16[32,4224]{1,0:T(8,128)(2,1)}, bf16[32,4224]{1,0:T(8,128)(2,1)S(1)}, u32[]{:S(2)}, u32[]{:S(2)}) %collective-permute-start.1) | collective-permute-done | bytes 270368 | tf_op jit(solution)/shard_map/ppermute | solution.py:229
  18.9 2.8 %constant_dynamic-slice_fusion = bf16[768,1024]{1,0:T(8,128)(2,1)} fusion(bf16[768,2048]{1,0:T(8,128)(2,1)} %bitcast.68, s32[]{:T(128)S(6)} %select_n.32), kind=kLoop, calls=%fused_computation.41 | loop fusion | bytes 3145732 | tf_op jit(solution)/shard_map/dynamic_slice | solution.py:257
  22.2 5.6 %collective-permute-done.4.second = bf16[32,4224]{1,0:T(8,128)(2,1)S(1)} collective-permute-done((bf16[32,4224]{1,0:T(8,128)(2,1)}, bf16[32,4224]{1,0:T(8,128)(2,1)S(1)}, u32[]{:S(2)}, u32[]{:S(2)}) %collective-permute-start.4) | collective-permute-done | bytes 270368 | tf_op jit(solution)/shard_map/ppermute | solution.py:229
  29.3 1.9 %join.1.refs_0_ = bf16[64,4224]{1,0:T(8,128)(2,1)} custom-call(bf16[32,4224]{1,0:T(8,128)(2,1)} %copy-done.19, bf16[32,4224]{1,0:T(8,128)(2,1)} %copy-done.20), custom_call_target="tpu_custom_call" | custom-call | tf_op jit(solution)/shard_map/join/pallas_call | solution.py:314
  37.9 4.0 %rows.4 = (bf16[256,768]{1,0:T(8,128)(2,1)S(1)}, bf16[192,768]{1,0:T(8,128)(2,1)S(1)}, f32[256,128]{1,0:T(8,128)S(1)}, bf16[256,2432]{1,0:T(8,128)(2,1)}, bf16[256,128]{1,0:T(8,128)(2,1)S(1)}) custom-call(bf16[32,4224]{1,0:T(8,128)(2,1)S(1)} %copy-done.4, bf16[32,4224]{1,0:T(8,128)(2,1)} %collective-permute-done.refs_1_, ...), custom_call_target="tpu_custom_call" | custom-call | tf_op jit(solution)/shard_map/rows/pallas_call | solution.py:272
  41.9 6.0 %collective-permute-done.8.refs_0_ = bf16[64,4224]{1,0:T(8,128)(2,1)} collective-permute-done((bf16[64,4224]{1,0:T(8,128)(2,1)}, bf16[64,4224]{1,0:T(8,128)(2,1)}, u32[]{:S(2)}, u32[]{:S(2)}) %collective-permute-start.8) | collective-permute-done | bytes 540704 | tf_op jit(solution)/shard_map/ppermute | solution.py:229
  50.7 3.6 %rows.5 = (bf16[256,768]{1,0:T(8,128)(2,1)S(1)}, bf16[192,768]{1,0:T(8,128)(2,1)S(1)}, f32[256,128]{1,0:T(8,128)S(1)}, bf16[256,2432]{1,0:T(8,128)(2,1)}, bf16[256,128]{1,0:T(8,128)(2,1)S(1)}) custom-call(bf16[64,4224]{1,0:T(8,128)(2,1)S(1)} %copy-done.3, bf16[64,4224]{1,0:T(8,128)(2,1)} %collective-permute-done.9.refs_1_, ...), custom_call_target="tpu_custom_call" | custom-call | tf_op jit(solution)/shard_map/rows/pallas_call | solution.py:272
  54.3 10.7 %collective-permute-done.16.refs_9_ = bf16[192,768]{1,0:T(8,128)(2,1)S(1)} collective-permute-done((bf16[192,768]{1,0:T(8,128)(2,1)S(1)}, bf16[192,768]{1,0:T(8,128)(2,1)S(1)}, u32[]{:S(2)}, u32[]{:S(2)}) %collective-permute-start.16) | collective-permute-done | bytes 294944 | tf_op jit(solution)/shard_map/ppermute | solution.py:220
  66.6 3.3 %grads.4 = (bf16[2,2,32,1152]{3,2,1,0:T(8,128)(2,1)S(1)}, bf16[2,2,32,1152]{3,2,1,0:T(8,128)(2,1)S(1)}, f32[8,1024]{1,0:T(8,128)S(1)}) custom-call(bf16[32,4224]{1,0:T(8,128)(2,1)S(1)} %copy-done.4, bf16[32,4224]{1,0:T(8,128)(2,1)} %collective-permute-done.refs_1_, bf16[32,4224]{1,0:T(8,128)(2,1)} %collective-permute-done.2.refs_2_, ...), custom_call_target="tpu_custom_call" | custom-call | tf_op jit(solution)/shard_map/grads/pallas_call | solution.py:295
  70.8 3.5 %rows.6 = (bf16[256,768]{1,0:T(8,128)(2,1)S(1)}, bf16[192,768]{1,0:T(8,128)(2,1)S(1)}, f32[256,128]{1,0:T(8,128)S(1)}, bf16[256,2432]{1,0:T(8,128)(2,1)}, bf16[256,128]{1,0:T(8,128)(2,1)S(1)}) custom-call(bf16[64,4224]{1,0:T(8,128)(2,1)} %collective-permute-done.8.refs_0_, bf16[64,4224]{1,0:T(8,128)(2,1)S(1)} %collective-permute-done.13.refs_1_, ...), custom_call_target="tpu_custom_call" | custom-call | tf_op jit(solution)/shard_map/rows/pallas_call | solution.py:272
  74.3 5.1 %collective-permute-done.22.refs_5_ = bf16[192,768]{1,0:T(8,128)(2,1)S(1)} collective-permute-done((bf16[192,768]{1,0:T(8,128)(2,1)S(1)}, bf16[192,768]{1,0:T(8,128)(2,1)S(1)}, u32[]{:S(2)}, u32[]{:S(2)}) %collective-permute-start.22) | collective-permute-done | bytes 294944 | tf_op jit(solution)/shard_map/ppermute | solution.py:220
  81.7 2.4 %rows.7 = (bf16[256,768]{1,0:T(8,128)(2,1)S(1)}, bf16[192,768]{1,0:T(8,128)(2,1)S(1)}, f32[256,128]{1,0:T(8,128)S(1)}, bf16[256,2432]{1,0:T(8,128)(2,1)}, bf16[256,128]{1,0:T(8,128)(2,1)S(1)}) custom-call(bf16[64,4224]{1,0:T(8,128)(2,1)S(1)} %collective-permute-done.12.refs_0_, bf16[64,4224]{1,0:T(8,128)(2,1)S(1)} %collective-permute-done.18.refs_1_, ...), custom_call_target="tpu_custom_call" | custom-call | tf_op jit(solution)/shard_map/rows/pallas_call | solution.py:272
  84.1 3.2 %grads.5 = (bf16[2,2,32,1152]{3,2,1,0:T(8,128)(2,1)S(1)}, bf16[2,2,32,1152]{3,2,1,0:T(8,128)(2,1)S(1)}, f32[8,1024]{1,0:T(8,128)S(1)}) custom-call(bf16[64,4224]{1,0:T(8,128)(2,1)S(1)} %copy-done.3, bf16[64,4224]{1,0:T(8,128)(2,1)} %collective-permute-done.9.refs_1_, bf16[64,4224]{1,0:T(8,128)(2,1)} %collective-permute-done.10.refs_2_, ...), custom_call_target="tpu_custom_call" | custom-call | tf_op jit(solution)/shard_map/grads/pallas_call | solution.py:295
  91.1 3.9 %collective-permute-done.26 = bf16[2,32,1152]{2,1,0:T(8,128)(2,1)S(1)} collective-permute-done((bf16[2,32,1152]{2,1,0:T(8,128)(2,1)S(1)}, bf16[2,32,1152]{2,1,0:T(8,128)(2,1)S(1)}, u32[]{:S(2)}, u32[]{:S(2)}) %collective-permute-start.26) | collective-permute-done | bytes 147488 | tf_op jit(solution)/shard_map/ppermute | solution.py:223
  95.0 3.0 %grads.6 = (bf16[2,2,32,1152]{3,2,1,0:T(8,128)(2,1)S(1)}, bf16[2,2,32,1152]{3,2,1,0:T(8,128)(2,1)S(1)}, f32[8,1024]{1,0:T(8,128)S(1)}) custom-call(bf16[64,4224]{1,0:T(8,128)(2,1)} %collective-permute-done.8.refs_0_, bf16[64,4224]{1,0:T(8,128)(2,1)S(1)} %collective-permute-done.13.refs_1_, bf16[64,4224]{1,0:T(8,128)(2,1)S(1)} %collective-permute-done.14.refs_2_, ...), custom_call_target="tpu_custom_call" | custom-call | tf_op jit(solution)/shard_map/grads/pallas_call | solution.py:295
  101.0 2.8 %grads.7 = (bf16[2,2,32,1152]{3,2,1,0:T(8,128)(2,1)S(1)}, bf16[2,2,32,1152]{3,2,1,0:T(8,128)(2,1)S(1)}, f32[8,1024]{1,0:T(8,128)S(1)}) custom-call(bf16[64,4224]{1,0:T(8,128)(2,1)S(1)} %collective-permute-done.12.refs_0_, bf16[64,4224]{1,0:T(8,128)(2,1)S(1)} %collective-permute-done.18.refs_1_, bf16[64,4224]{1,0:T(8,128)(2,1)S(1)} %collective-permute-done.19.refs_2_, ...), custom_call_target="tpu_custom_call" | custom-call | tf_op jit(solution)/shard_map/grads/pallas_call | solution.py:295
  113.5 3.1 %collective-permute-done.38 = f32[8,1024]{1,0:T(8,128)S(1)} collective-permute-done((f32[8,1024]{1,0:T(8,128)S(1)}, f32[8,1024]{1,0:T(8,128)S(1)}, u32[]{:S(2)}, u32[]{:S(2)}) %collective-permute-start.38) | collective-permute-done | bytes 32800 | tf_op jit(solution)/shard_map/ppermute | solution.py:238
  116.6 1.9 %collective-permute-start.39 = (f32[16,1024]{1,0:T(8,128)S(1)}, f32[16,1024]{1,0:T(8,128)S(1)}, u32[]{:S(2)}, u32[]{:S(2)}) collective-permute-start(f32[16,1024]{1,0:T(8,128)S(1)} %pad_maximum_fusion), channel_id=1, source_target_pairs={{0,8},{2,10},{4,12},{6,14},{8,0},{10,2},{12,4},{14,6},{16,24},{18,... | collective-permute-start | bytes 196616 | tf_op jit(solution)/shard_map/ppermute | solution.py:232
  118.8 3.3 %collective-permute-done.39 = f32[16,1024]{1,0:T(8,128)S(1)} collective-permute-done((f32[16,1024]{1,0:T(8,128)S(1)}, f32[16,1024]{1,0:T(8,128)S(1)}, u32[]{:S(2)}, u32[]{:S(2)}) %collective-permute-start.39) | collective-permute-done | bytes 65568 | tf_op jit(solution)/shard_map/ppermute | solution.py:232
  122.1 3.5 %collective-permute-done.40 = bf16[2,32,1152]{2,1,0:T(8,128)(2,1)S(1)} collective-permute-done((bf16[2,32,1152]{2,1,0:T(8,128)(2,1)S(1)}, bf16[2,32,1152]{2,1,0:T(8,128)(2,1)S(1)}, u32[]{:S(2)}, u32[]{:S(2)}) %collective-permute-start.40) | collective-permute-done | bytes 147488 | tf_op jit(solution)/shard_map/ppermute | solution.py:229
  127.5 4.9 %down.1 = bf16[384,2048]{1,0:T(8,128)(2,1)} custom-call(bf16[256,2432]{1,0:T(8,128)(2,1)} %get-tuple-element.319.refs_0_, bf16[256,2432]{1,0:T(8,128)(2,1)} %get-tuple-element.320.refs_1_, bf16[256,2432]{1,0:T(8,128)(2,1)} %get-tuple-element.321.refs_2_, bf16[256,2432]{1,0:T(8,128)(2,1)} %get-tuple-element.324.refs_3_), custom_call_target="tpu_custom_call" | custom-call | tf_op jit(solution)/shard_map/down/pallas_call | solution.py:330
  (147 shorter events, 43.5 us)
Async XLA Ops:
  2.5 9.7 %collective-permute-start = (bf16[32,4224]{1,0:T(8,128)(2,1)}, bf16[32,4224]{1,0:T(8,128)(2,1)}, u32[]{:S(2)}, u32[]{:S(2)}) collective-permute-start(bf16[32,4224]{1,0:T(8,128)(2,1)} %pack.1.refs_0_), channel_id=1, source_target_pairs={{0,1},{1,0},{2,3},{3,2},{4,5},{5,4},{6,7},{7,6},{8,9},{9,8},{10,11... | collective-permute-start | bytes 811016 | tf_op jit(solution)/shard_map/ppermute | solution.py:220
  5.5 10.0 %collective-permute-start.1 = (bf16[32,4224]{1,0:T(8,128)(2,1)}, bf16[32,4224]{1,0:T(8,128)(2,1)S(1)}, u32[]{:S(2)}, u32[]{:S(2)}) collective-permute-start(bf16[32,4224]{1,0:T(8,128)(2,1)} %pack.1.refs_0_), channel_id=1, source_target_pairs={{0,8},{2,10},{4,12},{6,14},{8,16},{10,18},{12,20},{14,22},{16,24},... | collective-permute-start | bytes 811016 | tf_op jit(solution)/shard_map/ppermute | solution.py:229
  7.0 8.5 %collective-permute-start.2 = (bf16[32,4224]{1,0:T(8,128)(2,1)}, bf16[32,4224]{1,0:T(8,128)(2,1)}, u32[]{:S(2)}, u32[]{:S(2)}) collective-permute-start(bf16[32,4224]{1,0:T(8,128)(2,1)} %pack.1.refs_0_), channel_id=1, source_target_pairs={{0,4},{2,6},{4,0},{6,2},{8,12},{10,14},{12,8},{14,10},{16,20},{18,... | collective-permute-start | bytes 811016 | tf_op jit(solution)/shard_map/ppermute | solution.py:223
  16.9 10.9 %collective-permute-start.4 = (bf16[32,4224]{1,0:T(8,128)(2,1)}, bf16[32,4224]{1,0:T(8,128)(2,1)S(1)}, u32[]{:S(2)}, u32[]{:S(2)}) collective-permute-start(bf16[32,4224]{1,0:T(8,128)(2,1)} %collective-permute-done.refs_1_), channel_id=1, source_target_pairs={{0,8},{2,10},{4,12},{6,14},{8,16},{10,18},{12,20},{14,22},{16,24},... | collective-permute-start | bytes 811016 | tf_op jit(solution)/shard_map/ppermute | solution.py:229
  17.3 11.2 %collective-permute-start.5 = (bf16[32,4224]{1,0:T(8,128)(2,1)}, bf16[32,4224]{1,0:T(8,128)(2,1)}, u32[]{:S(2)}, u32[]{:S(2)}) collective-permute-start(bf16[32,4224]{1,0:T(8,128)(2,1)} %collective-permute-done.refs_1_), channel_id=1, source_target_pairs={{0,4},{2,6},{4,0},{6,2},{8,12},{10,14},{12,8},{14,10},{16,20},{18,... | collective-permute-start | bytes 811016 | tf_op jit(solution)/shard_map/ppermute | solution.py:223
  18.8 9.7 %collective-permute-start.7 = (bf16[32,4224]{1,0:T(8,128)(2,1)}, bf16[32,4224]{1,0:T(8,128)(2,1)S(1)}, u32[]{:S(2)}, u32[]{:S(2)}) collective-permute-start(bf16[32,4224]{1,0:T(8,128)(2,1)} %collective-permute-done.2.refs_2_), channel_id=1, source_target_pairs={{0,2},{2,0},{4,6},{6,4},{8,10},{10,8},{12,14},{14,12},{16,18},{18,... | collective-permute-start | bytes 811016 | tf_op jit(solution)/shard_map/ppermute | solution.py:226
  21.7 43.3 %collective-permute-start.17 = (bf16[768,1024]{1,0:T(8,128)(2,1)}, bf16[768,1024]{1,0:T(8,128)(2,1)}, u32[]{:S(2)}, u32[]{:S(2)}) collective-permute-start(bf16[768,1024]{1,0:T(8,128)(2,1)} %constant_dynamic-slice_fusion), channel_id=1, source_target_pairs={{0,1},{1,0},{2,3},{3,2},{4,5},{5,4},{6,7},{7,6},{8,9},{9,8},{10,11... | collective-permute-start | bytes 4718600 | tf_op jit(solution)/shard_map/ppermute | solution.py:220
  31.1 10.8 %collective-permute-start.10 = (bf16[64,4224]{1,0:T(8,128)(2,1)}, bf16[64,4224]{1,0:T(8,128)(2,1)}, u32[]{:S(2)}, u32[]{:S(2)}) collective-permute-start(bf16[64,4224]{1,0:T(8,128)(2,1)} %join.1.refs_0_), channel_id=1, source_target_pairs={{0,2},{2,0},{4,6},{6,4},{8,10},{10,8},{12,14},{14,12},{16,18},{18,... | collective-permute-start | bytes 1622024 | tf_op jit(solution)/shard_map/ppermute | solution.py:226
  31.1 16.8 %collective-permute-start.8 = (bf16[64,4224]{1,0:T(8,128)(2,1)}, bf16[64,4224]{1,0:T(8,128)(2,1)}, u32[]{:S(2)}, u32[]{:S(2)}) collective-permute-start(bf16[64,4224]{1,0:T(8,128)(2,1)} %join.1.refs_0_), channel_id=1, source_target_pairs={{0,8},{2,10},{4,12},{6,14},{8,16},{10,18},{12,20},{14,22},{16,24},... | collective-permute-start | bytes 1622024 | tf_op jit(solution)/shard_map/ppermute | solution.py:229
  31.1 16.8 %collective-permute-start.9 = (bf16[64,4224]{1,0:T(8,128)(2,1)}, bf16[64,4224]{1,0:T(8,128)(2,1)}, u32[]{:S(2)}, u32[]{:S(2)}) collective-permute-start(bf16[64,4224]{1,0:T(8,128)(2,1)} %join.1.refs_0_), channel_id=1, source_target_pairs={{0,4},{2,6},{4,0},{6,2},{8,12},{10,14},{12,8},{14,10},{16,20},{18,... | collective-permute-start | bytes 1622024 | tf_op jit(solution)/shard_map/ppermute | solution.py:223
  48.0 17.0 %collective-permute-start.12 = (bf16[64,4224]{1,0:T(8,128)(2,1)}, bf16[64,4224]{1,0:T(8,128)(2,1)S(1)}, u32[]{:S(2)}, u32[]{:S(2)}) collective-permute-start(bf16[64,4224]{1,0:T(8,128)(2,1)} %collective-permute-done.8.refs_0_), channel_id=1, source_target_pairs={{0,8},{2,10},{4,12},{6,14},{8,16},{10,18},{12,20},{14,22},{16,24},... | collective-permute-start | bytes 1622024 | tf_op jit(solution)/shard_map/ppermute | solution.py:229
  48.3 16.8 %collective-permute-start.13 = (bf16[64,4224]{1,0:T(8,128)(2,1)}, bf16[64,4224]{1,0:T(8,128)(2,1)S(1)}, u32[]{:S(2)}, u32[]{:S(2)}) collective-permute-start(bf16[64,4224]{1,0:T(8,128)(2,1)} %collective-permute-done.8.refs_0_), channel_id=1, source_target_pairs={{0,4},{2,6},{4,0},{6,2},{8,12},{10,14},{12,8},{14,10},{16,20},{18,... | collective-permute-start | bytes 1622024 | tf_op jit(solution)/shard_map/ppermute | solution.py:223
  49.9 15.2 %collective-permute-start.14 = (bf16[64,4224]{1,0:T(8,128)(2,1)}, bf16[64,4224]{1,0:T(8,128)(2,1)S(1)}, u32[]{:S(2)}, u32[]{:S(2)}) collective-permute-start(bf16[64,4224]{1,0:T(8,128)(2,1)} %collective-permute-done.8.refs_0_), channel_id=1, source_target_pairs={{0,2},{2,0},{4,6},{6,4},{8,10},{10,8},{12,14},{14,12},{16,18},{18,... | collective-permute-start | bytes 1622024 | tf_op jit(solution)/shard_map/ppermute | solution.py:226
  50.2 14.9 %collective-permute-start.16 = (bf16[192,768]{1,0:T(8,128)(2,1)S(1)}, bf16[192,768]{1,0:T(8,128)(2,1)S(1)}, u32[]{:S(2)}, u32[]{:S(2)}) collective-permute-start(bf16[192,768]{1,0:T(8,128)(2,1)S(1)} %get-tuple-element.198), channel_id=1, source_target_pairs={{0,1},{1,0},{2,3},{3,2},{4,5},{5,4},{6,7},{7,6},{8,9},{9,8},{10,11... | collective-permute-start | bytes 884744 | tf_op jit(solution)/shard_map/ppermute | solution.py:220
  65.1 14.7 %collective-permute-start.18 = (bf16[64,4224]{1,0:T(8,128)(2,1)S(1)}, bf16[64,4224]{1,0:T(8,128)(2,1)S(1)}, u32[]{:S(2)}, u32[]{:S(2)}) collective-permute-start(bf16[64,4224]{1,0:T(8,128)(2,1)S(1)} %collective-permute-done.12.refs_0_), channel_id=1, source_target_pairs={{0,4},{2,6},{4,0},{6,2},{8,12},{10,14},{12,8},{14,10},{16,20},{18,... | collective-permute-start | bytes 1622024 | tf_op jit(solution)/shard_map/ppermute | solution.py:223
  66.4 13.4 %collective-permute-start.19 = (bf16[64,4224]{1,0:T(8,128)(2,1)S(1)}, bf16[64,4224]{1,0:T(8,128)(2,1)S(1)}, u32[]{:S(2)}, u32[]{:S(2)}) collective-permute-start(bf16[64,4224]{1,0:T(8,128)(2,1)S(1)} %collective-permute-done.12.refs_0_), channel_id=1, source_target_pairs={{0,2},{2,0},{4,6},{6,4},{8,10},{10,8},{12,14},{14,12},{16,18},{18,... | collective-permute-start | bytes 1622024 | tf_op jit(solution)/shard_map/ppermute | solution.py:226
  70.3 9.1 %collective-permute-start.22 = (bf16[192,768]{1,0:T(8,128)(2,1)S(1)}, bf16[192,768]{1,0:T(8,128)(2,1)S(1)}, u32[]{:S(2)}, u32[]{:S(2)}) collective-permute-start(bf16[192,768]{1,0:T(8,128)(2,1)S(1)} %get-tuple-element.226), channel_id=1, source_target_pairs={{0,1},{1,0},{2,3},{3,2},{4,5},{5,4},{6,7},{7,6},{8,9},{9,8},{10,11... | collective-permute-start | bytes 884744 | tf_op jit(solution)/shard_map/ppermute | solution.py:220
  79.8 9.4 %collective-permute-start.25 = (bf16[192,768]{1,0:T(8,128)(2,1)S(1)}, bf16[192,768]{1,0:T(8,128)(2,1)S(1)}, u32[]{:S(2)}, u32[]{:S(2)}) collective-permute-start(bf16[192,768]{1,0:T(8,128)(2,1)S(1)} %get-tuple-element.253), channel_id=1, source_target_pairs={{0,1},{1,0},{2,3},{3,2},{4,5},{5,4},{6,7},{7,6},{8,9},{9,8},{10,11... | collective-permute-start | bytes 884744 | tf_op jit(solution)/shard_map/ppermute | solution.py:220
  90.6 10.5 %collective-permute-start.28 = (bf16[192,768]{1,0:T(8,128)(2,1)S(1)}, bf16[192,768]{1,0:T(8,128)(2,1)S(1)}, u32[]{:S(2)}, u32[]{:S(2)}) collective-permute-start(bf16[192,768]{1,0:T(8,128)(2,1)S(1)} %get-tuple-element.279), channel_id=1, source_target_pairs={{0,1},{1,0},{2,3},{3,2},{4,5},{5,4},{6,7},{7,6},{8,9},{9,8},{10,11... | collective-permute-start | bytes 884744 | tf_op jit(solution)/shard_map/ppermute | solution.py:220
  98.2 8.3 %collective-permute-start.34 = (bf16[2,32,1152]{2,1,0:T(8,128)(2,1)S(1)}, bf16[2,32,1152]{2,1,0:T(8,128)(2,1)S(1)}, u32[]{:S(2)}, u32[]{:S(2)}) collective-permute-start(bf16[2,32,1152]{2,1,0:T(8,128)(2,1)S(1)} %fusion.5), channel_id=1, source_target_pairs={{0,8},{2,10},{4,12},{6,14},{8,16},{10,18},{12,20},{14,22},{16,24},... | collective-permute-start | bytes 442376 | tf_op jit(solution)/shard_map/ppermute | solution.py:229
  104.1 14.4 %collective-permute-start.31 = (bf16[2,32,1152]{2,1,0:T(8,128)(2,1)S(1)}, bf16[2,32,1152]{2,1,0:T(8,128)(2,1)S(1)}, u32[]{:S(2)}, u32[]{:S(2)}) collective-permute-start(bf16[2,32,1152]{2,1,0:T(8,128)(2,1)S(1)} %fusion.11), channel_id=1, source_target_pairs={{0,4},{2,6},{4,0},{6,2},{8,12},{10,14},{12,8},{14,10},{16,20},{18,... | collective-permute-start | bytes 442376 | tf_op jit(solution)/shard_map/ppermute | solution.py:223
  106.6 11.8 %collective-permute-start.35 = (bf16[2,32,1152]{2,1,0:T(8,128)(2,1)S(1)}, bf16[2,32,1152]{2,1,0:T(8,128)(2,1)S(1)}, u32[]{:S(2)}, u32[]{:S(2)}) collective-permute-start(bf16[2,32,1152]{2,1,0:T(8,128)(2,1)S(1)} %fusion.4), channel_id=1, source_target_pairs={{0,8},{2,10},{4,12},{6,14},{8,16},{10,18},{12,20},{14,22},{16,24},... | collective-permute-start | bytes 442376 | tf_op jit(solution)/shard_map/ppermute | solution.py:229
  108.0 10.4 %collective-permute-start.33 = (bf16[2,32,1152]{2,1,0:T(8,128)(2,1)S(1)}, bf16[2,32,1152]{2,1,0:T(8,128)(2,1)S(1)}, u32[]{:S(2)}, u32[]{:S(2)}) collective-permute-start(bf16[2,32,1152]{2,1,0:T(8,128)(2,1)S(1)} %fusion.13), channel_id=1, source_target_pairs={{0,4},{2,6},{4,0},{6,2},{8,12},{10,14},{12,8},{14,10},{16,20},{18,... | collective-permute-start | bytes 442376 | tf_op jit(solution)/shard_map/ppermute | solution.py:223
  118.5 7.1 %collective-permute-start.40 = (bf16[2,32,1152]{2,1,0:T(8,128)(2,1)S(1)}, bf16[2,32,1152]{2,1,0:T(8,128)(2,1)S(1)}, u32[]{:S(2)}, u32[]{:S(2)}) collective-permute-start(bf16[2,32,1152]{2,1,0:T(8,128)(2,1)S(1)} %fusion.2), channel_id=1, source_target_pairs={{0,8},{2,10},{4,12},{6,14},{8,16},{10,18},{12,20},{14,22},{16,24},... | collective-permute-start | bytes 442376 | tf_op jit(solution)/shard_map/ppermute | solution.py:229
  (41 other events, 344.3 us)

commit v10 on v9

--- a/solution.py
+++ b/solution.py
@@ -377,12 +377,13 @@
     near[1] = [go_z(own)]
     far[0] = [go_y(own)]
     near_c[0] = [go_core(own)]
+    state["s"] = {0: w_send}
     step()
+    w_send = state.pop("s")[0]
     near[1].append(go_z(near[0][1]))
     far[0].append(go_y(near[0][1]))
     near_c[0].append(go_core(near[0][1]))
     far_c[0] = [go_core(far[0][0])]
-    w_send, near_c[0] = fence((w_send, near_c[0]))
     w_far[0] = go_x(w_send)
     step(("w", 0))
     near[1] = [join(*near[1])]
@@ -397,7 +398,7 @@
         rows_of(k - 1)
         if k == 2:
             other[0] = go_x(packed[0])
-        step(*([("w", 0)] if k == 1 else []))
+        step(("w", 0) if k == 1 else ("other", 0))
     other[1] = go_x(packed[1])
     far[3] = [go_y(near[3][0])]
     near_c[3] = [go_core(near[3][0])]
@@ -413,7 +414,9 @@
     step()
     other[3] = go_x(packed[3])
     send_y(1)
-    other[2], sent[1], d_got[0] = fence((other[2], sent[1], d_got[0]))
+    sent[1], d_got[0] = fence((sent[1], d_got[0]))
+    early = totals[1] + go_core(totals[1])
+    other[2], early = fence((other[2], early))
     grads_of(2)
     hop(1)
     send_y(2)
@@ -422,8 +425,8 @@
     grads_of(3)
     hop(2)
     pool = {}
-    pool[0] = sum(totals[k] for k in range(1, planes)) + totals[0]
-    pool[0] = pool[0] + go_core(pool[0])
+    late = totals[2] + totals[3] + totals[0]
+    pool[0] = early + (late + go_core(late))
     state["pool"] = pool
     step(("value", 3), ("sent", 2), ("value", 2), ("sent", 0))
     send_y(3)

time: 136 us -> 139 us (1.022)
  starting transfers between devices: 30.2 us -> 35.8 us
  waiting for transfers between devices: 56.6 us -> 52.7 us
  other arithmetic: 2.74 us -> 4.29 us
    ppermute x8, waiting for transfers between devices: 21.9 us -> 9.67 us  [go_x(): return lax.ppermute(v, 'dp', [(0, 1), (1, 0)])]
    ppermute x7, waiting for transfers between devices: 19.5 us -> 28.9 us  [go_z(): lax.ppermute(v, 'expert', [(e, (e + 4) % experts) for e in range(experts)])]
    ppermute x8, starting transfers between devices: 6.74 us -> 12.1 us  [go_x(): return lax.ppermute(v, 'dp', [(0, 1), (1, 0)])]
    unnamed x45 -> x43, local copies, waits for them, and re-layouts: 6.88 us -> 6.16 us
  transfers between devices with their start and end apart: 43 -> 44, of which waited for: 18 -> 19; matrix products, arithmetic and copies ran while one was open for 3% -> 5% of each run, Pallas kernels for 24% -> 24%
where the time goes in v10:
time: 139 us; the launch traced here: 138 us
  waiting for transfers between devices  52.7 us (38%)
  starting transfers between devices  35.8 us (26%)
  Pallas kernels  34.4 us (25%)
  local copies, waits for them, and re-layouts  9.15 us (7%)
  other arithmetic  4.29 us (3%)
  between operations  1.71 us (1%)
    ppermute x7, waiting for transfers between devices, go_z(): lax.ppermute(v, 'expert', [(e, (e + 4) % experts) for e in range(experts)])  28.9 us
    pallas_call x4, Pallas kernels, first_half(): pl.pallas_call(functools.partial(rows_kernel, segments_of(arrays), width,...  13.4 us
    pallas_call x4, Pallas kernels, second_half(): pl.pallas_call(functools.partial(grad_kernel, segments_of(arrays), half),...  12.3 us
    ppermute x10, starting transfers between devices, go_y(): return lax.ppermute(v, 'expert', [(e, e ^ 2) for e in range(experts)])  12.2 us
    ppermute x8, starting transfers between devices, go_x(): return lax.ppermute(v, 'dp', [(0, 1), (1, 0)])  12.1 us
    ppermute x8, waiting for transfers between devices, go_x(): return lax.ppermute(v, 'dp', [(0, 1), (1, 0)])  9.67 us
    unnamed x43, local copies, waits for them, and re-layouts  6.16 us
    ppermute x10, waiting for transfers between devices, go_y(): return lax.ppermute(v, 'expert', [(e, e ^ 2) for e in range(experts)])  6.09 us
  transfers between devices with their start and end apart: 44, of which 19 were waited for; matrix products, arithmetic and copies ran while one was open for 5% of the time, Pallas kernels for 24%

profile of v10, /device:TPU:0, one launch (start us, length us, event | category | flops | bytes accessed | tf_op | source)
XLA Modules:
  0.0 138.1 jit_solution(7468941392152870494)
XLA Ops:
  0.6 1.9 %pack.1.refs_0_ = bf16[32,4224]{1,0:T(8,128)(2,1)} custom-call(bf16[32,2048]{1,0:T(8,128)(2,1)} %bitcast.90, bf16[32,2048]{1,0:T(8,128)(2,1)} %bitcast.91, s32[8,32]{1,0:T(8,128)} %bitcast.94, bf16[8,32]{1,0:T(8,128)(2,1)} %bitcast.98), custom_call_target="tpu_custom_call" | custom-call | tf_op jit(solution)/shard_map/pack/pallas_call | solution.py:242
  2.5 2.9 %collective-permute-start = (bf16[32,4224]{1,0:T(8,128)(2,1)}, bf16[32,4224]{1,0:T(8,128)(2,1)}, u32[]{:S(2)}, u32[]{:S(2)}) collective-permute-start(bf16[32,4224]{1,0:T(8,128)(2,1)} %pack.1.refs_0_), channel_id=1, source_target_pairs={{0,1},{1,0},{2,3},{3,2},{4,5},{5,4},{6,7},{7,6},{8,9},{9,8},{10,11... | collective-permute-start | bytes 811016 | tf_op jit(solution)/shard_map/ppermute | solution.py:220
  8.6 2.8 %constant_dynamic-slice_fusion = bf16[768,1024]{1,0:T(8,128)(2,1)} fusion(bf16[768,2048]{1,0:T(8,128)(2,1)} %bitcast.68, s32[]{:T(128)S(6)} %select_n.32), kind=kLoop, calls=%fused_computation.42 | loop fusion | bytes 3145732 | tf_op jit(solution)/shard_map/dynamic_slice | solution.py:257
  12.2 3.4 %collective-permute-done.1.first = bf16[32,4224]{1,0:T(8,128)(2,1)} collective-permute-done((bf16[32,4224]{1,0:T(8,128)(2,1)}, bf16[32,4224]{1,0:T(8,128)(2,1)}, u32[]{:S(2)}, u32[]{:S(2)}) %collective-permute-start.1) | collective-permute-done | bytes 270368 | tf_op jit(solution)/shard_map/ppermute | solution.py:229
  19.2 6.1 %collective-permute-done.4.second = bf16[32,4224]{1,0:T(8,128)(2,1)S(1)} collective-permute-done((bf16[32,4224]{1,0:T(8,128)(2,1)}, bf16[32,4224]{1,0:T(8,128)(2,1)S(1)}, u32[]{:S(2)}, u32[]{:S(2)}) %collective-permute-start.4) | collective-permute-done | bytes 270368 | tf_op jit(solution)/shard_map/ppermute | solution.py:229
  27.4 1.9 %join.1.refs_0_ = bf16[64,4224]{1,0:T(8,128)(2,1)} custom-call(bf16[32,4224]{1,0:T(8,128)(2,1)} %collective-permute-done.1.first, bf16[32,4224]{1,0:T(8,128)(2,1)} %copy-done.19), custom_call_target="tpu_custom_call" | custom-call | tf_op jit(solution)/shard_map/join/pallas_call | solution.py:314
  35.8 4.0 %rows.4 = (bf16[256,768]{1,0:T(8,128)(2,1)S(1)}, bf16[192,768]{1,0:T(8,128)(2,1)S(1)}, f32[256,128]{1,0:T(8,128)S(1)}, bf16[256,2432]{1,0:T(8,128)(2,1)}, bf16[256,128]{1,0:T(8,128)(2,1)S(1)}) custom-call(bf16[32,4224]{1,0:T(8,128)(2,1)S(1)} %copy-done.4, bf16[32,4224]{1,0:T(8,128)(2,1)} %collective-permute-done.refs_1_, ...), custom_call_target="tpu_custom_call" | custom-call | tf_op jit(solution)/shard_map/rows/pallas_call | solution.py:272
  39.8 6.2 %collective-permute-done.8.refs_0_ = bf16[64,4224]{1,0:T(8,128)(2,1)} collective-permute-done((bf16[64,4224]{1,0:T(8,128)(2,1)}, bf16[64,4224]{1,0:T(8,128)(2,1)}, u32[]{:S(2)}, u32[]{:S(2)}) %collective-permute-start.8) | collective-permute-done | bytes 540704 | tf_op jit(solution)/shard_map/ppermute | solution.py:229
  49.5 3.6 %rows.5 = (bf16[256,768]{1,0:T(8,128)(2,1)S(1)}, bf16[192,768]{1,0:T(8,128)(2,1)S(1)}, f32[256,128]{1,0:T(8,128)S(1)}, bf16[256,2432]{1,0:T(8,128)(2,1)}, bf16[256,128]{1,0:T(8,128)(2,1)S(1)}) custom-call(bf16[64,4224]{1,0:T(8,128)(2,1)S(1)} %copy-done.3, bf16[64,4224]{1,0:T(8,128)(2,1)} %collective-permute-done.9.refs_1_, ...), custom_call_target="tpu_custom_call" | custom-call | tf_op jit(solution)/shard_map/rows/pallas_call | solution.py:272
  53.1 9.7 %collective-permute-done.12.refs_0_ = bf16[64,4224]{1,0:T(8,128)(2,1)S(1)} collective-permute-done((bf16[64,4224]{1,0:T(8,128)(2,1)}, bf16[64,4224]{1,0:T(8,128)(2,1)S(1)}, u32[]{:S(2)}, u32[]{:S(2)}) %collective-permute-start.12) | collective-permute-done | bytes 540704 | tf_op jit(solution)/shard_map/ppermute | solution.py:229
  64.4 3.3 %grads.4 = (bf16[2,2,32,1152]{3,2,1,0:T(8,128)(2,1)S(1)}, bf16[2,2,32,1152]{3,2,1,0:T(8,128)(2,1)S(1)}, f32[8,1024]{1,0:T(8,128)S(1)}) custom-call(bf16[32,4224]{1,0:T(8,128)(2,1)S(1)} %copy-done.4, bf16[32,4224]{1,0:T(8,128)(2,1)} %collective-permute-done.refs_1_, bf16[32,4224]{1,0:T(8,128)(2,1)} %collective-permute-done.2.refs_2_, ...), custom_call_target="tpu_custom_call" | custom-call | tf_op jit(solution)/shard_map/grads/pallas_call | solution.py:295
  69.7 3.5 %rows.6 = (bf16[256,768]{1,0:T(8,128)(2,1)S(1)}, bf16[192,768]{1,0:T(8,128)(2,1)S(1)}, f32[256,128]{1,0:T(8,128)S(1)}, bf16[256,2432]{1,0:T(8,128)(2,1)}, bf16[256,128]{1,0:T(8,128)(2,1)S(1)}) custom-call(bf16[64,4224]{1,0:T(8,128)(2,1)} %collective-permute-done.8.refs_0_, bf16[64,4224]{1,0:T(8,128)(2,1)S(1)} %collective-permute-done.13.refs_1_, ...), custom_call_target="tpu_custom_call" | custom-call | tf_op jit(solution)/shard_map/rows/pallas_call | solution.py:272
  73.2 4.1 %collective-permute-done.22.refs_5_ = bf16[192,768]{1,0:T(8,128)(2,1)S(1)} collective-permute-done((bf16[192,768]{1,0:T(8,128)(2,1)S(1)}, bf16[192,768]{1,0:T(8,128)(2,1)S(1)}, u32[]{:S(2)}, u32[]{:S(2)}) %collective-permute-start.22) | collective-permute-done | bytes 294944 | tf_op jit(solution)/shard_map/ppermute | solution.py:220
  79.5 2.4 %rows.7 = (bf16[256,768]{1,0:T(8,128)(2,1)S(1)}, bf16[192,768]{1,0:T(8,128)(2,1)S(1)}, f32[256,128]{1,0:T(8,128)S(1)}, bf16[256,2432]{1,0:T(8,128)(2,1)}, bf16[256,128]{1,0:T(8,128)(2,1)S(1)}) custom-call(bf16[64,4224]{1,0:T(8,128)(2,1)S(1)} %collective-permute-done.12.refs_0_, bf16[64,4224]{1,0:T(8,128)(2,1)S(1)} %collective-permute-done.17.refs_1_, ...), custom_call_target="tpu_custom_call" | custom-call | tf_op jit(solution)/shard_map/rows/pallas_call | solution.py:272
  81.9 3.2 %grads.5 = (bf16[2,2,32,1152]{3,2,1,0:T(8,128)(2,1)S(1)}, bf16[2,2,32,1152]{3,2,1,0:T(8,128)(2,1)S(1)}, f32[8,1024]{1,0:T(8,128)S(1)}) custom-call(bf16[64,4224]{1,0:T(8,128)(2,1)S(1)} %copy-done.3, bf16[64,4224]{1,0:T(8,128)(2,1)} %collective-permute-done.9.refs_1_, bf16[64,4224]{1,0:T(8,128)(2,1)} %collective-permute-done.10.refs_2_, ...), custom_call_target="tpu_custom_call" | custom-call | tf_op jit(solution)/shard_map/grads/pallas_call | solution.py:295
  89.9 3.0 %grads.6 = (bf16[2,2,32,1152]{3,2,1,0:T(8,128)(2,1)S(1)}, bf16[2,2,32,1152]{3,2,1,0:T(8,128)(2,1)S(1)}, f32[8,1024]{1,0:T(8,128)S(1)}) custom-call(bf16[64,4224]{1,0:T(8,128)(2,1)} %collective-permute-done.8.refs_0_, bf16[64,4224]{1,0:T(8,128)(2,1)S(1)} %collective-permute-done.13.refs_1_, bf16[64,4224]{1,0:T(8,128)(2,1)S(1)} %collective-permute-done.14.refs_2_, ...), custom_call_target="tpu_custom_call" | custom-call | tf_op jit(solution)/shard_map/grads/pallas_call | solution.py:295
  95.2 2.7 %collective-permute-done.29.refs_5_ = bf16[192,768]{1,0:T(8,128)(2,1)S(1)} collective-permute-done((bf16[192,768]{1,0:T(8,128)(2,1)S(1)}, bf16[192,768]{1,0:T(8,128)(2,1)S(1)}, u32[]{:S(2)}, u32[]{:S(2)}) %collective-permute-start.29) | collective-permute-done | bytes 294944 | tf_op jit(solution)/shard_map/ppermute | solution.py:220
  97.9 2.8 %grads.7 = (bf16[2,2,32,1152]{3,2,1,0:T(8,128)(2,1)S(1)}, bf16[2,2,32,1152]{3,2,1,0:T(8,128)(2,1)S(1)}, f32[8,1024]{1,0:T(8,128)S(1)}) custom-call(bf16[64,4224]{1,0:T(8,128)(2,1)S(1)} %collective-permute-done.12.refs_0_, bf16[64,4224]{1,0:T(8,128)(2,1)S(1)} %collective-permute-done.17.refs_1_, bf16[64,4224]{1,0:T(8,128)(2,1)S(1)} %collective-permute-done.18.refs_2_, ...), custom_call_target="tpu_custom_call" | custom-call | tf_op jit(solution)/shard_map/grads/pallas_call | solution.py:295
  102.0 5.1 %collective-permute-done.33 = bf16[2,32,1152]{2,1,0:T(8,128)(2,1)S(1)} collective-permute-done((bf16[2,32,1152]{2,1,0:T(8,128)(2,1)S(1)}, bf16[2,32,1152]{2,1,0:T(8,128)(2,1)S(1)}, u32[]{:S(2)}, u32[]{:S(2)}) %collective-permute-start.33) | collective-permute-done | bytes 147488 | tf_op jit(solution)/shard_map/ppermute | solution.py:223
  113.5 3.0 %collective-permute-done.39 = f32[8,1024]{1,0:T(8,128)S(1)} collective-permute-done((f32[8,1024]{1,0:T(8,128)S(1)}, f32[8,1024]{1,0:T(8,128)S(1)}, u32[]{:S(2)}, u32[]{:S(2)}) %collective-permute-start.39) | collective-permute-done | bytes 32800 | tf_op jit(solution)/shard_map/ppermute | solution.py:238
  118.7 2.7 %collective-permute-done.40 = f32[16,1024]{1,0:T(8,128)S(1)} collective-permute-done((f32[16,1024]{1,0:T(8,128)S(1)}, f32[16,1024]{1,0:T(8,128)S(1)}, u32[]{:S(2)}, u32[]{:S(2)}) %collective-permute-start.40) | collective-permute-done | bytes 65568 | tf_op jit(solution)/shard_map/ppermute | solution.py:232
  121.5 3.5 %collective-permute-done.41 = bf16[2,32,1152]{2,1,0:T(8,128)(2,1)S(1)} collective-permute-done((bf16[2,32,1152]{2,1,0:T(8,128)(2,1)S(1)}, bf16[2,32,1152]{2,1,0:T(8,128)(2,1)S(1)}, u32[]{:S(2)}, u32[]{:S(2)}) %collective-permute-start.41) | collective-permute-done | bytes 147488 | tf_op jit(solution)/shard_map/ppermute | solution.py:229
  125.0 2.6 %collective-permute-start.43 = (f32[16,1024]{1,0:T(8,128)S(1)}, f32[16,1024]{1,0:T(8,128)S(1)}, u32[]{:S(2)}, u32[]{:S(2)}) collective-permute-start(f32[16,1024]{1,0:T(8,128)S(1)} %fusion.15), channel_id=1, source_target_pairs={{0,16},{2,18},{4,20},{6,22},{8,24},{10,26},{12,28},{14,30},{16,0},... | collective-permute-start | bytes 196616 | tf_op jit(solution)/shard_map/ppermute | solution.py:232
  130.2 4.9 %down.1 = bf16[384,2048]{1,0:T(8,128)(2,1)} custom-call(bf16[256,2432]{1,0:T(8,128)(2,1)} %get-tuple-element.313.refs_0_, bf16[256,2432]{1,0:T(8,128)(2,1)} %get-tuple-element.314.refs_1_, bf16[256,2432]{1,0:T(8,128)(2,1)} %get-tuple-element.315.refs_2_, bf16[256,2432]{1,0:T(8,128)(2,1)} %get-tuple-element.318.refs_3_), custom_call_target="tpu_custom_call" | custom-call | tf_op jit(solution)/shard_map/down/pallas_call | solution.py:330
  (148 shorter events, 47.1 us)
Async XLA Ops:
  2.5 9.7 %collective-permute-start = (bf16[32,4224]{1,0:T(8,128)(2,1)}, bf16[32,4224]{1,0:T(8,128)(2,1)}, u32[]{:S(2)}, u32[]{:S(2)}) collective-permute-start(bf16[32,4224]{1,0:T(8,128)(2,1)} %pack.1.refs_0_), channel_id=1, source_target_pairs={{0,1},{1,0},{2,3},{3,2},{4,5},{5,4},{6,7},{7,6},{8,9},{9,8},{10,11... | collective-permute-start | bytes 811016 | tf_op jit(solution)/shard_map/ppermute | solution.py:220
  5.5 10.1 %collective-permute-start.1 = (bf16[32,4224]{1,0:T(8,128)(2,1)}, bf16[32,4224]{1,0:T(8,128)(2,1)}, u32[]{:S(2)}, u32[]{:S(2)}) collective-permute-start(bf16[32,4224]{1,0:T(8,128)(2,1)} %pack.1.refs_0_), channel_id=1, source_target_pairs={{0,8},{2,10},{4,12},{6,14},{8,16},{10,18},{12,20},{14,22},{16,24},... | collective-permute-start | bytes 811016 | tf_op jit(solution)/shard_map/ppermute | solution.py:229
  7.0 8.6 %collective-permute-start.2 = (bf16[32,4224]{1,0:T(8,128)(2,1)}, bf16[32,4224]{1,0:T(8,128)(2,1)}, u32[]{:S(2)}, u32[]{:S(2)}) collective-permute-start(bf16[32,4224]{1,0:T(8,128)(2,1)} %pack.1.refs_0_), channel_id=1, source_target_pairs={{0,4},{2,6},{4,0},{6,2},{8,12},{10,14},{12,8},{14,10},{16,20},{18,... | collective-permute-start | bytes 811016 | tf_op jit(solution)/shard_map/ppermute | solution.py:223
  15.6 47.2 %collective-permute-start.16 = (bf16[768,1024]{1,0:T(8,128)(2,1)}, bf16[768,1024]{1,0:T(8,128)(2,1)}, u32[]{:S(2)}, u32[]{:S(2)}) collective-permute-start(bf16[768,1024]{1,0:T(8,128)(2,1)} %constant_dynamic-slice_fusion), channel_id=1, source_target_pairs={{0,1},{1,0},{2,3},{3,2},{4,5},{5,4},{6,7},{7,6},{8,9},{9,8},{10,11... | collective-permute-start | bytes 4718600 | tf_op jit(solution)/shard_map/ppermute | solution.py:220
  16.1 9.1 %collective-permute-start.4 = (bf16[32,4224]{1,0:T(8,128)(2,1)}, bf16[32,4224]{1,0:T(8,128)(2,1)S(1)}, u32[]{:S(2)}, u32[]{:S(2)}) collective-permute-start(bf16[32,4224]{1,0:T(8,128)(2,1)} %collective-permute-done.refs_1_), channel_id=1, source_target_pairs={{0,8},{2,10},{4,12},{6,14},{8,16},{10,18},{12,20},{14,22},{16,24},... | collective-permute-start | bytes 811016 | tf_op jit(solution)/shard_map/ppermute | solution.py:229
  17.1 8.1 %collective-permute-start.5 = (bf16[32,4224]{1,0:T(8,128)(2,1)}, bf16[32,4224]{1,0:T(8,128)(2,1)}, u32[]{:S(2)}, u32[]{:S(2)}) collective-permute-start(bf16[32,4224]{1,0:T(8,128)(2,1)} %collective-permute-done.refs_1_), channel_id=1, source_target_pairs={{0,4},{2,6},{4,0},{6,2},{8,12},{10,14},{12,8},{14,10},{16,20},{18,... | collective-permute-start | bytes 811016 | tf_op jit(solution)/shard_map/ppermute | solution.py:223
  18.6 8.0 %collective-permute-start.7 = (bf16[32,4224]{1,0:T(8,128)(2,1)}, bf16[32,4224]{1,0:T(8,128)(2,1)S(1)}, u32[]{:S(2)}, u32[]{:S(2)}) collective-permute-start(bf16[32,4224]{1,0:T(8,128)(2,1)} %collective-permute-done.2.refs_2_), channel_id=1, source_target_pairs={{0,2},{2,0},{4,6},{6,4},{8,10},{10,8},{12,14},{14,12},{16,18},{18,... | collective-permute-start | bytes 811016 | tf_op jit(solution)/shard_map/ppermute | solution.py:226
  29.2 10.6 %collective-permute-start.10 = (bf16[64,4224]{1,0:T(8,128)(2,1)}, bf16[64,4224]{1,0:T(8,128)(2,1)}, u32[]{:S(2)}, u32[]{:S(2)}) collective-permute-start(bf16[64,4224]{1,0:T(8,128)(2,1)} %join.1.refs_0_), channel_id=1, source_target_pairs={{0,2},{2,0},{4,6},{6,4},{8,10},{10,8},{12,14},{14,12},{16,18},{18,... | collective-permute-start | bytes 1622024 | tf_op jit(solution)/shard_map/ppermute | solution.py:226
  29.2 16.8 %collective-permute-start.8 = (bf16[64,4224]{1,0:T(8,128)(2,1)}, bf16[64,4224]{1,0:T(8,128)(2,1)}, u32[]{:S(2)}, u32[]{:S(2)}) collective-permute-start(bf16[64,4224]{1,0:T(8,128)(2,1)} %join.1.refs_0_), channel_id=1, source_target_pairs={{0,8},{2,10},{4,12},{6,14},{8,16},{10,18},{12,20},{14,22},{16,24},... | collective-permute-start | bytes 1622024 | tf_op jit(solution)/shard_map/ppermute | solution.py:229
  29.2 16.8 %collective-permute-start.9 = (bf16[64,4224]{1,0:T(8,128)(2,1)}, bf16[64,4224]{1,0:T(8,128)(2,1)}, u32[]{:S(2)}, u32[]{:S(2)}) collective-permute-start(bf16[64,4224]{1,0:T(8,128)(2,1)} %join.1.refs_0_), channel_id=1, source_target_pairs={{0,4},{2,6},{4,0},{6,2},{8,12},{10,14},{12,8},{14,10},{16,20},{18,... | collective-permute-start | bytes 1622024 | tf_op jit(solution)/shard_map/ppermute | solution.py:223
  46.1 16.7 %collective-permute-start.12 = (bf16[64,4224]{1,0:T(8,128)(2,1)}, bf16[64,4224]{1,0:T(8,128)(2,1)S(1)}, u32[]{:S(2)}, u32[]{:S(2)}) collective-permute-start(bf16[64,4224]{1,0:T(8,128)(2,1)} %collective-permute-done.8.refs_0_), channel_id=1, source_target_pairs={{0,8},{2,10},{4,12},{6,14},{8,16},{10,18},{12,20},{14,22},{16,24},... | collective-permute-start | bytes 1622024 | tf_op jit(solution)/shard_map/ppermute | solution.py:229
  46.4 16.4 %collective-permute-start.13 = (bf16[64,4224]{1,0:T(8,128)(2,1)}, bf16[64,4224]{1,0:T(8,128)(2,1)S(1)}, u32[]{:S(2)}, u32[]{:S(2)}) collective-permute-start(bf16[64,4224]{1,0:T(8,128)(2,1)} %collective-permute-done.8.refs_0_), channel_id=1, source_target_pairs={{0,4},{2,6},{4,0},{6,2},{8,12},{10,14},{12,8},{14,10},{16,20},{18,... | collective-permute-start | bytes 1622024 | tf_op jit(solution)/shard_map/ppermute | solution.py:223
  47.7 15.1 %collective-permute-start.14 = (bf16[64,4224]{1,0:T(8,128)(2,1)}, bf16[64,4224]{1,0:T(8,128)(2,1)S(1)}, u32[]{:S(2)}, u32[]{:S(2)}) collective-permute-start(bf16[64,4224]{1,0:T(8,128)(2,1)} %collective-permute-done.8.refs_0_), channel_id=1, source_target_pairs={{0,2},{2,0},{4,6},{6,4},{8,10},{10,8},{12,14},{14,12},{16,18},{18,... | collective-permute-start | bytes 1622024 | tf_op jit(solution)/shard_map/ppermute | solution.py:226
  48.3 16.2 %collective-permute-start.20 = (bf16[192,768]{1,0:T(8,128)(2,1)S(1)}, bf16[192,768]{1,0:T(8,128)(2,1)S(1)}, u32[]{:S(2)}, u32[]{:S(2)}) collective-permute-start(bf16[192,768]{1,0:T(8,128)(2,1)S(1)} %get-tuple-element.193), channel_id=1, source_target_pairs={{0,1},{1,0},{2,3},{3,2},{4,5},{5,4},{6,7},{7,6},{8,9},{9,8},{10,11... | collective-permute-start | bytes 884744 | tf_op jit(solution)/shard_map/ppermute | solution.py:220
  62.9 14.7 %collective-permute-start.17 = (bf16[64,4224]{1,0:T(8,128)(2,1)S(1)}, bf16[64,4224]{1,0:T(8,128)(2,1)S(1)}, u32[]{:S(2)}, u32[]{:S(2)}) collective-permute-start(bf16[64,4224]{1,0:T(8,128)(2,1)S(1)} %collective-permute-done.12.refs_0_), channel_id=1, source_target_pairs={{0,4},{2,6},{4,0},{6,2},{8,12},{10,14},{12,8},{14,10},{16,20},{18,... | collective-permute-start | bytes 1622024 | tf_op jit(solution)/shard_map/ppermute | solution.py:223
  64.3 13.3 %collective-permute-start.18 = (bf16[64,4224]{1,0:T(8,128)(2,1)S(1)}, bf16[64,4224]{1,0:T(8,128)(2,1)S(1)}, u32[]{:S(2)}, u32[]{:S(2)}) collective-permute-start(bf16[64,4224]{1,0:T(8,128)(2,1)S(1)} %collective-permute-done.12.refs_0_), channel_id=1, source_target_pairs={{0,2},{2,0},{4,6},{6,4},{8,10},{10,8},{12,14},{14,12},{16,18},{18,... | collective-permute-start | bytes 1622024 | tf_op jit(solution)/shard_map/ppermute | solution.py:226
  68.2 9.1 %collective-permute-start.22 = (bf16[192,768]{1,0:T(8,128)(2,1)S(1)}, bf16[192,768]{1,0:T(8,128)(2,1)S(1)}, u32[]{:S(2)}, u32[]{:S(2)}) collective-permute-start(bf16[192,768]{1,0:T(8,128)(2,1)S(1)} %get-tuple-element.220), channel_id=1, source_target_pairs={{0,1},{1,0},{2,3},{3,2},{4,5},{5,4},{6,7},{7,6},{8,9},{9,8},{10,11... | collective-permute-start | bytes 884744 | tf_op jit(solution)/shard_map/ppermute | solution.py:220
  77.6 9.4 %collective-permute-start.25 = (bf16[192,768]{1,0:T(8,128)(2,1)S(1)}, bf16[192,768]{1,0:T(8,128)(2,1)S(1)}, u32[]{:S(2)}, u32[]{:S(2)}) collective-permute-start(bf16[192,768]{1,0:T(8,128)(2,1)S(1)} %get-tuple-element.247), channel_id=1, source_target_pairs={{0,1},{1,0},{2,3},{3,2},{4,5},{5,4},{6,7},{7,6},{8,9},{9,8},{10,11... | collective-permute-start | bytes 884744 | tf_op jit(solution)/shard_map/ppermute | solution.py:220
  88.4 9.4 %collective-permute-start.29 = (bf16[192,768]{1,0:T(8,128)(2,1)S(1)}, bf16[192,768]{1,0:T(8,128)(2,1)S(1)}, u32[]{:S(2)}, u32[]{:S(2)}) collective-permute-start(bf16[192,768]{1,0:T(8,128)(2,1)S(1)} %get-tuple-element.274), channel_id=1, source_target_pairs={{0,1},{1,0},{2,3},{3,2},{4,5},{5,4},{6,7},{7,6},{8,9},{9,8},{10,11... | collective-permute-start | bytes 884744 | tf_op jit(solution)/shard_map/ppermute | solution.py:220
  93.4 8.7 %collective-permute-start.35 = (bf16[2,32,1152]{2,1,0:T(8,128)(2,1)S(1)}, bf16[2,32,1152]{2,1,0:T(8,128)(2,1)S(1)}, u32[]{:S(2)}, u32[]{:S(2)}) collective-permute-start(bf16[2,32,1152]{2,1,0:T(8,128)(2,1)S(1)} %fusion.5), channel_id=1, source_target_pairs={{0,8},{2,10},{4,12},{6,14},{8,16},{10,18},{12,20},{14,22},{16,24},... | collective-permute-start | bytes 442376 | tf_op jit(solution)/shard_map/ppermute | solution.py:229
  94.4 22.8 %collective-permute-start.32 = (bf16[2,32,1152]{2,1,0:T(8,128)(2,1)}, bf16[2,32,1152]{2,1,0:T(8,128)(2,1)}, u32[]{:S(2)}, u32[]{:S(2)}) collective-permute-start(bf16[2,32,1152]{2,1,0:T(8,128)(2,1)} %fusion.11), channel_id=1, source_target_pairs={{0,4},{2,6},{4,0},{6,2},{8,12},{10,14},{12,8},{14,10},{16,20},{18,... | collective-permute-start | bytes 442376 | tf_op jit(solution)/shard_map/ppermute | solution.py:223
  107.3 9.9 %collective-permute-start.36 = (bf16[2,32,1152]{2,1,0:T(8,128)(2,1)S(1)}, bf16[2,32,1152]{2,1,0:T(8,128)(2,1)S(1)}, u32[]{:S(2)}, u32[]{:S(2)}) collective-permute-start(bf16[2,32,1152]{2,1,0:T(8,128)(2,1)S(1)} %fusion.4), channel_id=1, source_target_pairs={{0,8},{2,10},{4,12},{6,14},{8,16},{10,18},{12,20},{14,22},{16,24},... | collective-permute-start | bytes 442376 | tf_op jit(solution)/shard_map/ppermute | solution.py:229
  108.2 9.0 %collective-permute-start.34 = (bf16[2,32,1152]{2,1,0:T(8,128)(2,1)S(1)}, bf16[2,32,1152]{2,1,0:T(8,128)(2,1)S(1)}, u32[]{:S(2)}, u32[]{:S(2)}) collective-permute-start(bf16[2,32,1152]{2,1,0:T(8,128)(2,1)S(1)} %fusion.13), channel_id=1, source_target_pairs={{0,4},{2,6},{4,0},{6,2},{8,12},{10,14},{12,8},{14,10},{16,20},{18,... | collective-permute-start | bytes 442376 | tf_op jit(solution)/shard_map/ppermute | solution.py:223
  125.0 10.1 %collective-permute-start.43 = (f32[16,1024]{1,0:T(8,128)S(1)}, f32[16,1024]{1,0:T(8,128)S(1)}, u32[]{:S(2)}, u32[]{:S(2)}) collective-permute-start(f32[16,1024]{1,0:T(8,128)S(1)} %fusion.15), channel_id=1, source_target_pairs={{0,16},{2,18},{4,20},{6,22},{8,24},{10,26},{12,28},{14,30},{16,0},... | collective-permute-start | bytes 196616 | tf_op jit(solution)/shard_map/ppermute | solution.py:232
  (41 other events, 385.2 us)

commit v11 on v10

--- a/solution.py
+++ b/solution.py
@@ -414,14 +414,14 @@
     step()
     other[3] = go_x(packed[3])
     send_y(1)
-    sent[1], d_got[0] = fence((sent[1], d_got[0]))
     early = totals[1] + go_core(totals[1])
     other[2], early = fence((other[2], early))
     grads_of(2)
     hop(1)
     send_y(2)
+    d_got[0], d_got[2] = fence((d_got[0], d_got[2]))
     send_y(0)
-    step(("sent", 0), ("sent", 2), ("value", 2))
+    step(("sent", 0), ("value", 2))
     grads_of(3)
     hop(2)
     pool = {}

time: 139 us -> 136 us (0.978)
  starting transfers between devices: 35.8 us -> 34.1 us
    ppermute x16, waiting for transfers between devices: 2.34 us -> 4.24 us  [go_core(): return lax.ppermute(v, 'expert', [(e, e ^ 1) for e in range(experts)])]
    ppermute x8, waiting for transfers between devices: 9.67 us -> 8.23 us  [go_x(): return lax.ppermute(v, 'dp', [(0, 1), (1, 0)])]
  transfers between devices with their start and end apart: 44 -> 44, of which waited for: 19 -> 21; matrix products, arithmetic and copies ran while one was open for 5% -> 5% of each run, Pallas kernels for 24% -> 24%
where the time goes in v11:
time: 136 us; the launch traced here: 135 us
  waiting for transfers between devices  51.8 us (38%)
  Pallas kernels  34.4 us (25%)
  starting transfers between devices  34.1 us (25%)
  local copies, waits for them, and re-layouts  9.15 us (7%)
  other arithmetic  4.29 us (3%)
  between operations  1.67 us (1%)
    ppermute x7, waiting for transfers between devices, go_z(): lax.ppermute(v, 'expert', [(e, (e + 4) % experts) for e in range(experts)])  29.1 us
    pallas_call x4, Pallas kernels, first_half(): pl.pallas_call(functools.partial(rows_kernel, segments_of(arrays), width,...  13.4 us
    ppermute x10, starting transfers between devices, go_y(): return lax.ppermute(v, 'expert', [(e, e ^ 2) for e in range(experts)])  12.7 us
    pallas_call x4, Pallas kernels, second_half(): pl.pallas_call(functools.partial(grad_kernel, segments_of(arrays), half),...  12.3 us
    ppermute x8, starting transfers between devices, go_x(): return lax.ppermute(v, 'dp', [(0, 1), (1, 0)])  11.5 us
    ppermute x8, waiting for transfers between devices, go_x(): return lax.ppermute(v, 'dp', [(0, 1), (1, 0)])  8.23 us
    unnamed x43, local copies, waits for them, and re-layouts  6.16 us
    pallas_call x1, Pallas kernels, make_down(): pl.pallas_call(functools.partial(down_kernel, planes, hidden), out_shape=...  4.93 us
  transfers between devices with their start and end apart: 44, of which 21 were waited for; matrix products, arithmetic and copies ran while one was open for 5% of the time, Pallas kernels for 24%

profile of v11, /device:TPU:0, one launch (start us, length us, event | category | flops | bytes accessed | tf_op | source)
XLA Modules:
  0.0 135.4 jit_solution(2716516519326792134)
XLA Ops:
  0.6 1.9 %pack.1.refs_0_ = bf16[32,4224]{1,0:T(8,128)(2,1)} custom-call(bf16[32,2048]{1,0:T(8,128)(2,1)} %bitcast.90, bf16[32,2048]{1,0:T(8,128)(2,1)} %bitcast.91, s32[8,32]{1,0:T(8,128)} %bitcast.94, bf16[8,32]{1,0:T(8,128)(2,1)} %bitcast.98), custom_call_target="tpu_custom_call" | custom-call | tf_op jit(solution)/shard_map/pack/pallas_call | solution.py:242
  2.5 2.9 %collective-permute-start = (bf16[32,4224]{1,0:T(8,128)(2,1)}, bf16[32,4224]{1,0:T(8,128)(2,1)}, u32[]{:S(2)}, u32[]{:S(2)}) collective-permute-start(bf16[32,4224]{1,0:T(8,128)(2,1)} %pack.1.refs_0_), channel_id=1, source_target_pairs={{0,1},{1,0},{2,3},{3,2},{4,5},{5,4},{6,7},{7,6},{8,9},{9,8},{10,11... | collective-permute-start | bytes 811016 | tf_op jit(solution)/shard_map/ppermute | solution.py:220
  8.6 2.8 %constant_dynamic-slice_fusion = bf16[768,1024]{1,0:T(8,128)(2,1)} fusion(bf16[768,2048]{1,0:T(8,128)(2,1)} %bitcast.68, s32[]{:T(128)S(6)} %select_n.32), kind=kLoop, calls=%fused_computation.42 | loop fusion | bytes 3145732 | tf_op jit(solution)/shard_map/dynamic_slice | solution.py:257
  12.2 3.4 %collective-permute-done.1.first = bf16[32,4224]{1,0:T(8,128)(2,1)} collective-permute-done((bf16[32,4224]{1,0:T(8,128)(2,1)}, bf16[32,4224]{1,0:T(8,128)(2,1)}, u32[]{:S(2)}, u32[]{:S(2)}) %collective-permute-start.1) | collective-permute-done | bytes 270368 | tf_op jit(solution)/shard_map/ppermute | solution.py:229
  19.2 6.1 %collective-permute-done.4.second = bf16[32,4224]{1,0:T(8,128)(2,1)S(1)} collective-permute-done((bf16[32,4224]{1,0:T(8,128)(2,1)}, bf16[32,4224]{1,0:T(8,128)(2,1)S(1)}, u32[]{:S(2)}, u32[]{:S(2)}) %collective-permute-start.4) | collective-permute-done | bytes 270368 | tf_op jit(solution)/shard_map/ppermute | solution.py:229
  27.4 1.9 %join.1.refs_0_ = bf16[64,4224]{1,0:T(8,128)(2,1)} custom-call(bf16[32,4224]{1,0:T(8,128)(2,1)} %collective-permute-done.1.first, bf16[32,4224]{1,0:T(8,128)(2,1)} %copy-done.19), custom_call_target="tpu_custom_call" | custom-call | tf_op jit(solution)/shard_map/join/pallas_call | solution.py:314
  35.8 4.0 %rows.4 = (bf16[256,768]{1,0:T(8,128)(2,1)S(1)}, bf16[192,768]{1,0:T(8,128)(2,1)S(1)}, f32[256,128]{1,0:T(8,128)S(1)}, bf16[256,2432]{1,0:T(8,128)(2,1)}, bf16[256,128]{1,0:T(8,128)(2,1)S(1)}) custom-call(bf16[32,4224]{1,0:T(8,128)(2,1)S(1)} %copy-done.4, bf16[32,4224]{1,0:T(8,128)(2,1)} %collective-permute-done.refs_1_, ...), custom_call_target="tpu_custom_call" | custom-call | tf_op jit(solution)/shard_map/rows/pallas_call | solution.py:272
  39.8 6.2 %collective-permute-done.8.refs_0_ = bf16[64,4224]{1,0:T(8,128)(2,1)} collective-permute-done((bf16[64,4224]{1,0:T(8,128)(2,1)}, bf16[64,4224]{1,0:T(8,128)(2,1)}, u32[]{:S(2)}, u32[]{:S(2)}) %collective-permute-start.8) | collective-permute-done | bytes 540704 | tf_op jit(solution)/shard_map/ppermute | solution.py:229
  49.5 3.6 %rows.5 = (bf16[256,768]{1,0:T(8,128)(2,1)S(1)}, bf16[192,768]{1,0:T(8,128)(2,1)S(1)}, f32[256,128]{1,0:T(8,128)S(1)}, bf16[256,2432]{1,0:T(8,128)(2,1)}, bf16[256,128]{1,0:T(8,128)(2,1)S(1)}) custom-call(bf16[64,4224]{1,0:T(8,128)(2,1)S(1)} %copy-done.3, bf16[64,4224]{1,0:T(8,128)(2,1)} %collective-permute-done.9.refs_1_, ...), custom_call_target="tpu_custom_call" | custom-call | tf_op jit(solution)/shard_map/rows/pallas_call | solution.py:272
  53.1 9.7 %collective-permute-done.12.refs_0_ = bf16[64,4224]{1,0:T(8,128)(2,1)S(1)} collective-permute-done((bf16[64,4224]{1,0:T(8,128)(2,1)}, bf16[64,4224]{1,0:T(8,128)(2,1)S(1)}, u32[]{:S(2)}, u32[]{:S(2)}) %collective-permute-start.12) | collective-permute-done | bytes 540704 | tf_op jit(solution)/shard_map/ppermute | solution.py:229
  64.4 3.3 %grads.4 = (bf16[2,2,32,1152]{3,2,1,0:T(8,128)(2,1)S(1)}, bf16[2,2,32,1152]{3,2,1,0:T(8,128)(2,1)S(1)}, f32[8,1024]{1,0:T(8,128)S(1)}) custom-call(bf16[32,4224]{1,0:T(8,128)(2,1)S(1)} %copy-done.4, bf16[32,4224]{1,0:T(8,128)(2,1)} %collective-permute-done.refs_1_, bf16[32,4224]{1,0:T(8,128)(2,1)} %collective-permute-done.2.refs_2_, ...), custom_call_target="tpu_custom_call" | custom-call | tf_op jit(solution)/shard_map/grads/pallas_call | solution.py:295
  69.7 3.5 %rows.6 = (bf16[256,768]{1,0:T(8,128)(2,1)S(1)}, bf16[192,768]{1,0:T(8,128)(2,1)S(1)}, f32[256,128]{1,0:T(8,128)S(1)}, bf16[256,2432]{1,0:T(8,128)(2,1)}, bf16[256,128]{1,0:T(8,128)(2,1)S(1)}) custom-call(bf16[64,4224]{1,0:T(8,128)(2,1)} %collective-permute-done.8.refs_0_, bf16[64,4224]{1,0:T(8,128)(2,1)S(1)} %collective-permute-done.13.refs_1_, ...), custom_call_target="tpu_custom_call" | custom-call | tf_op jit(solution)/shard_map/rows/pallas_call | solution.py:272
  73.2 4.1 %collective-permute-done.22.refs_5_ = bf16[192,768]{1,0:T(8,128)(2,1)S(1)} collective-permute-done((bf16[192,768]{1,0:T(8,128)(2,1)S(1)}, bf16[192,768]{1,0:T(8,128)(2,1)S(1)}, u32[]{:S(2)}, u32[]{:S(2)}) %collective-permute-start.22) | collective-permute-done | bytes 294944 | tf_op jit(solution)/shard_map/ppermute | solution.py:220
  79.5 2.4 %rows.7 = (bf16[256,768]{1,0:T(8,128)(2,1)S(1)}, bf16[192,768]{1,0:T(8,128)(2,1)S(1)}, f32[256,128]{1,0:T(8,128)S(1)}, bf16[256,2432]{1,0:T(8,128)(2,1)}, bf16[256,128]{1,0:T(8,128)(2,1)S(1)}) custom-call(bf16[64,4224]{1,0:T(8,128)(2,1)S(1)} %collective-permute-done.12.refs_0_, bf16[64,4224]{1,0:T(8,128)(2,1)S(1)} %collective-permute-done.17.refs_1_, ...), custom_call_target="tpu_custom_call" | custom-call | tf_op jit(solution)/shard_map/rows/pallas_call | solution.py:272
  81.9 3.2 %grads.5 = (bf16[2,2,32,1152]{3,2,1,0:T(8,128)(2,1)S(1)}, bf16[2,2,32,1152]{3,2,1,0:T(8,128)(2,1)S(1)}, f32[8,1024]{1,0:T(8,128)S(1)}) custom-call(bf16[64,4224]{1,0:T(8,128)(2,1)S(1)} %copy-done.3, bf16[64,4224]{1,0:T(8,128)(2,1)} %collective-permute-done.9.refs_1_, bf16[64,4224]{1,0:T(8,128)(2,1)} %collective-permute-done.10.refs_2_, ...), custom_call_target="tpu_custom_call" | custom-call | tf_op jit(solution)/shard_map/grads/pallas_call | solution.py:295
  85.3 1.7 %collective-permute-done.25.refs_5_ = bf16[192,768]{1,0:T(8,128)(2,1)S(1)} collective-permute-done((bf16[192,768]{1,0:T(8,128)(2,1)S(1)}, bf16[192,768]{1,0:T(8,128)(2,1)S(1)}, u32[]{:S(2)}, u32[]{:S(2)}) %collective-permute-start.25) | collective-permute-done | bytes 294944 | tf_op jit(solution)/shard_map/ppermute | solution.py:220
  89.9 3.0 %grads.6 = (bf16[2,2,32,1152]{3,2,1,0:T(8,128)(2,1)S(1)}, bf16[2,2,32,1152]{3,2,1,0:T(8,128)(2,1)S(1)}, f32[8,1024]{1,0:T(8,128)S(1)}) custom-call(bf16[64,4224]{1,0:T(8,128)(2,1)} %collective-permute-done.8.refs_0_, bf16[64,4224]{1,0:T(8,128)(2,1)S(1)} %collective-permute-done.13.refs_1_, bf16[64,4224]{1,0:T(8,128)(2,1)S(1)} %collective-permute-done.14.refs_2_, ...), custom_call_target="tpu_custom_call" | custom-call | tf_op jit(solution)/shard_map/grads/pallas_call | solution.py:295
  97.9 3.6 %collective-permute-done.30 = bf16[2,32,1152]{2,1,0:T(8,128)(2,1)S(1)} collective-permute-done((bf16[2,32,1152]{2,1,0:T(8,128)(2,1)S(1)}, bf16[2,32,1152]{2,1,0:T(8,128)(2,1)S(1)}, u32[]{:S(2)}, u32[]{:S(2)}) %collective-permute-start.30) | collective-permute-done | bytes 147488 | tf_op jit(solution)/shard_map/ppermute | solution.py:223
  101.4 2.8 %grads.7 = (bf16[2,2,32,1152]{3,2,1,0:T(8,128)(2,1)S(1)}, bf16[2,2,32,1152]{3,2,1,0:T(8,128)(2,1)S(1)}, f32[8,1024]{1,0:T(8,128)S(1)}) custom-call(bf16[64,4224]{1,0:T(8,128)(2,1)S(1)} %collective-permute-done.12.refs_0_, bf16[64,4224]{1,0:T(8,128)(2,1)S(1)} %collective-permute-done.17.refs_1_, bf16[64,4224]{1,0:T(8,128)(2,1)S(1)} %collective-permute-done.18.refs_2_, ...), custom_call_target="tpu_custom_call" | custom-call | tf_op jit(solution)/shard_map/grads/pallas_call | solution.py:295
  106.7 1.6 %collective-permute-start.34 = (bf16[2,32,1152]{2,1,0:T(8,128)(2,1)S(1)}, bf16[2,32,1152]{2,1,0:T(8,128)(2,1)S(1)}, u32[]{:S(2)}, u32[]{:S(2)}) collective-permute-start(bf16[2,32,1152]{2,1,0:T(8,128)(2,1)S(1)} %fusion.13), channel_id=1, source_target_pairs={{0,4},{2,6},{4,0},{6,2},{8,12},{10,14},{12,8},{14,10},{16,20},{18,... | collective-permute-start | bytes 442376 | tf_op jit(solution)/shard_map/ppermute | solution.py:223
  112.5 2.7 %collective-permute-done.39 = f32[8,1024]{1,0:T(8,128)S(1)} collective-permute-done((f32[8,1024]{1,0:T(8,128)S(1)}, f32[8,1024]{1,0:T(8,128)S(1)}, u32[]{:S(2)}, u32[]{:S(2)}) %collective-permute-start.39) | collective-permute-done | bytes 32800 | tf_op jit(solution)/shard_map/ppermute | solution.py:238
  117.4 2.8 %collective-permute-done.40 = f32[16,1024]{1,0:T(8,128)S(1)} collective-permute-done((f32[16,1024]{1,0:T(8,128)S(1)}, f32[16,1024]{1,0:T(8,128)S(1)}, u32[]{:S(2)}, u32[]{:S(2)}) %collective-permute-start.40) | collective-permute-done | bytes 65568 | tf_op jit(solution)/shard_map/ppermute | solution.py:232
  120.2 3.8 %collective-permute-done.41 = bf16[2,32,1152]{2,1,0:T(8,128)(2,1)S(1)} collective-permute-done((bf16[2,32,1152]{2,1,0:T(8,128)(2,1)S(1)}, bf16[2,32,1152]{2,1,0:T(8,128)(2,1)S(1)}, u32[]{:S(2)}, u32[]{:S(2)}) %collective-permute-start.41) | collective-permute-done | bytes 147488 | tf_op jit(solution)/shard_map/ppermute | solution.py:229
  127.5 4.9 %down.1 = bf16[384,2048]{1,0:T(8,128)(2,1)} custom-call(bf16[256,2432]{1,0:T(8,128)(2,1)} %get-tuple-element.315.refs_0_, bf16[256,2432]{1,0:T(8,128)(2,1)} %get-tuple-element.316.refs_1_, bf16[256,2432]{1,0:T(8,128)(2,1)} %get-tuple-element.317.refs_2_, bf16[256,2432]{1,0:T(8,128)(2,1)} %get-tuple-element.320.refs_3_), custom_call_target="tpu_custom_call" | custom-call | tf_op jit(solution)/shard_map/down/pallas_call | solution.py:330
  (148 shorter events, 48.1 us)
Async XLA Ops:
  2.5 9.7 %collective-permute-start = (bf16[32,4224]{1,0:T(8,128)(2,1)}, bf16[32,4224]{1,0:T(8,128)(2,1)}, u32[]{:S(2)}, u32[]{:S(2)}) collective-permute-start(bf16[32,4224]{1,0:T(8,128)(2,1)} %pack.1.refs_0_), channel_id=1, source_target_pairs={{0,1},{1,0},{2,3},{3,2},{4,5},{5,4},{6,7},{7,6},{8,9},{9,8},{10,11... | collective-permute-start | bytes 811016 | tf_op jit(solution)/shard_map/ppermute | solution.py:220
  5.5 10.1 %collective-permute-start.1 = (bf16[32,4224]{1,0:T(8,128)(2,1)}, bf16[32,4224]{1,0:T(8,128)(2,1)}, u32[]{:S(2)}, u32[]{:S(2)}) collective-permute-start(bf16[32,4224]{1,0:T(8,128)(2,1)} %pack.1.refs_0_), channel_id=1, source_target_pairs={{0,8},{2,10},{4,12},{6,14},{8,16},{10,18},{12,20},{14,22},{16,24},... | collective-permute-start | bytes 811016 | tf_op jit(solution)/shard_map/ppermute | solution.py:229
  7.0 8.6 %collective-permute-start.2 = (bf16[32,4224]{1,0:T(8,128)(2,1)}, bf16[32,4224]{1,0:T(8,128)(2,1)}, u32[]{:S(2)}, u32[]{:S(2)}) collective-permute-start(bf16[32,4224]{1,0:T(8,128)(2,1)} %pack.1.refs_0_), channel_id=1, source_target_pairs={{0,4},{2,6},{4,0},{6,2},{8,12},{10,14},{12,8},{14,10},{16,20},{18,... | collective-permute-start | bytes 811016 | tf_op jit(solution)/shard_map/ppermute | solution.py:223
  15.6 47.2 %collective-permute-start.16 = (bf16[768,1024]{1,0:T(8,128)(2,1)}, bf16[768,1024]{1,0:T(8,128)(2,1)}, u32[]{:S(2)}, u32[]{:S(2)}) collective-permute-start(bf16[768,1024]{1,0:T(8,128)(2,1)} %constant_dynamic-slice_fusion), channel_id=1, source_target_pairs={{0,1},{1,0},{2,3},{3,2},{4,5},{5,4},{6,7},{7,6},{8,9},{9,8},{10,11... | collective-permute-start | bytes 4718600 | tf_op jit(solution)/shard_map/ppermute | solution.py:220
  16.1 9.1 %collective-permute-start.4 = (bf16[32,4224]{1,0:T(8,128)(2,1)}, bf16[32,4224]{1,0:T(8,128)(2,1)S(1)}, u32[]{:S(2)}, u32[]{:S(2)}) collective-permute-start(bf16[32,4224]{1,0:T(8,128)(2,1)} %collective-permute-done.refs_1_), channel_id=1, source_target_pairs={{0,8},{2,10},{4,12},{6,14},{8,16},{10,18},{12,20},{14,22},{16,24},... | collective-permute-start | bytes 811016 | tf_op jit(solution)/shard_map/ppermute | solution.py:229
  17.1 8.1 %collective-permute-start.5 = (bf16[32,4224]{1,0:T(8,128)(2,1)}, bf16[32,4224]{1,0:T(8,128)(2,1)}, u32[]{:S(2)}, u32[]{:S(2)}) collective-permute-start(bf16[32,4224]{1,0:T(8,128)(2,1)} %collective-permute-done.refs_1_), channel_id=1, source_target_pairs={{0,4},{2,6},{4,0},{6,2},{8,12},{10,14},{12,8},{14,10},{16,20},{18,... | collective-permute-start | bytes 811016 | tf_op jit(solution)/shard_map/ppermute | solution.py:223
  18.6 8.0 %collective-permute-start.7 = (bf16[32,4224]{1,0:T(8,128)(2,1)}, bf16[32,4224]{1,0:T(8,128)(2,1)S(1)}, u32[]{:S(2)}, u32[]{:S(2)}) collective-permute-start(bf16[32,4224]{1,0:T(8,128)(2,1)} %collective-permute-done.2.refs_2_), channel_id=1, source_target_pairs={{0,2},{2,0},{4,6},{6,4},{8,10},{10,8},{12,14},{14,12},{16,18},{18,... | collective-permute-start | bytes 811016 | tf_op jit(solution)/shard_map/ppermute | solution.py:226
  29.2 10.6 %collective-permute-start.10 = (bf16[64,4224]{1,0:T(8,128)(2,1)}, bf16[64,4224]{1,0:T(8,128)(2,1)}, u32[]{:S(2)}, u32[]{:S(2)}) collective-permute-start(bf16[64,4224]{1,0:T(8,128)(2,1)} %join.1.refs_0_), channel_id=1, source_target_pairs={{0,2},{2,0},{4,6},{6,4},{8,10},{10,8},{12,14},{14,12},{16,18},{18,... | collective-permute-start | bytes 1622024 | tf_op jit(solution)/shard_map/ppermute | solution.py:226
  29.2 16.8 %collective-permute-start.8 = (bf16[64,4224]{1,0:T(8,128)(2,1)}, bf16[64,4224]{1,0:T(8,128)(2,1)}, u32[]{:S(2)}, u32[]{:S(2)}) collective-permute-start(bf16[64,4224]{1,0:T(8,128)(2,1)} %join.1.refs_0_), channel_id=1, source_target_pairs={{0,8},{2,10},{4,12},{6,14},{8,16},{10,18},{12,20},{14,22},{16,24},... | collective-permute-start | bytes 1622024 | tf_op jit(solution)/shard_map/ppermute | solution.py:229
  29.2 16.8 %collective-permute-start.9 = (bf16[64,4224]{1,0:T(8,128)(2,1)}, bf16[64,4224]{1,0:T(8,128)(2,1)}, u32[]{:S(2)}, u32[]{:S(2)}) collective-permute-start(bf16[64,4224]{1,0:T(8,128)(2,1)} %join.1.refs_0_), channel_id=1, source_target_pairs={{0,4},{2,6},{4,0},{6,2},{8,12},{10,14},{12,8},{14,10},{16,20},{18,... | collective-permute-start | bytes 1622024 | tf_op jit(solution)/shard_map/ppermute | solution.py:223
  46.1 16.7 %collective-permute-start.12 = (bf16[64,4224]{1,0:T(8,128)(2,1)}, bf16[64,4224]{1,0:T(8,128)(2,1)S(1)}, u32[]{:S(2)}, u32[]{:S(2)}) collective-permute-start(bf16[64,4224]{1,0:T(8,128)(2,1)} %collective-permute-done.8.refs_0_), channel_id=1, source_target_pairs={{0,8},{2,10},{4,12},{6,14},{8,16},{10,18},{12,20},{14,22},{16,24},... | collective-permute-start | bytes 1622024 | tf_op jit(solution)/shard_map/ppermute | solution.py:229
  46.4 16.4 %collective-permute-start.13 = (bf16[64,4224]{1,0:T(8,128)(2,1)}, bf16[64,4224]{1,0:T(8,128)(2,1)S(1)}, u32[]{:S(2)}, u32[]{:S(2)}) collective-permute-start(bf16[64,4224]{1,0:T(8,128)(2,1)} %collective-permute-done.8.refs_0_), channel_id=1, source_target_pairs={{0,4},{2,6},{4,0},{6,2},{8,12},{10,14},{12,8},{14,10},{16,20},{18,... | collective-permute-start | bytes 1622024 | tf_op jit(solution)/shard_map/ppermute | solution.py:223
  47.7 15.1 %collective-permute-start.14 = (bf16[64,4224]{1,0:T(8,128)(2,1)}, bf16[64,4224]{1,0:T(8,128)(2,1)S(1)}, u32[]{:S(2)}, u32[]{:S(2)}) collective-permute-start(bf16[64,4224]{1,0:T(8,128)(2,1)} %collective-permute-done.8.refs_0_), channel_id=1, source_target_pairs={{0,2},{2,0},{4,6},{6,4},{8,10},{10,8},{12,14},{14,12},{16,18},{18,... | collective-permute-start | bytes 1622024 | tf_op jit(solution)/shard_map/ppermute | solution.py:226
  48.3 16.2 %collective-permute-start.20 = (bf16[192,768]{1,0:T(8,128)(2,1)S(1)}, bf16[192,768]{1,0:T(8,128)(2,1)S(1)}, u32[]{:S(2)}, u32[]{:S(2)}) collective-permute-start(bf16[192,768]{1,0:T(8,128)(2,1)S(1)} %get-tuple-element.194), channel_id=1, source_target_pairs={{0,1},{1,0},{2,3},{3,2},{4,5},{5,4},{6,7},{7,6},{8,9},{9,8},{10,11... | collective-permute-start | bytes 884744 | tf_op jit(solution)/shard_map/ppermute | solution.py:220
  62.9 14.7 %collective-permute-start.17 = (bf16[64,4224]{1,0:T(8,128)(2,1)S(1)}, bf16[64,4224]{1,0:T(8,128)(2,1)S(1)}, u32[]{:S(2)}, u32[]{:S(2)}) collective-permute-start(bf16[64,4224]{1,0:T(8,128)(2,1)S(1)} %collective-permute-done.12.refs_0_), channel_id=1, source_target_pairs={{0,4},{2,6},{4,0},{6,2},{8,12},{10,14},{12,8},{14,10},{16,20},{18,... | collective-permute-start | bytes 1622024 | tf_op jit(solution)/shard_map/ppermute | solution.py:223
  64.3 13.3 %collective-permute-start.18 = (bf16[64,4224]{1,0:T(8,128)(2,1)S(1)}, bf16[64,4224]{1,0:T(8,128)(2,1)S(1)}, u32[]{:S(2)}, u32[]{:S(2)}) collective-permute-start(bf16[64,4224]{1,0:T(8,128)(2,1)S(1)} %collective-permute-done.12.refs_0_), channel_id=1, source_target_pairs={{0,2},{2,0},{4,6},{6,4},{8,10},{10,8},{12,14},{14,12},{16,18},{18,... | collective-permute-start | bytes 1622024 | tf_op jit(solution)/shard_map/ppermute | solution.py:226
  68.2 9.1 %collective-permute-start.22 = (bf16[192,768]{1,0:T(8,128)(2,1)S(1)}, bf16[192,768]{1,0:T(8,128)(2,1)S(1)}, u32[]{:S(2)}, u32[]{:S(2)}) collective-permute-start(bf16[192,768]{1,0:T(8,128)(2,1)S(1)} %get-tuple-element.221), channel_id=1, source_target_pairs={{0,1},{1,0},{2,3},{3,2},{4,5},{5,4},{6,7},{7,6},{8,9},{9,8},{10,11... | collective-permute-start | bytes 884744 | tf_op jit(solution)/shard_map/ppermute | solution.py:220
  77.6 9.4 %collective-permute-start.25 = (bf16[192,768]{1,0:T(8,128)(2,1)S(1)}, bf16[192,768]{1,0:T(8,128)(2,1)S(1)}, u32[]{:S(2)}, u32[]{:S(2)}) collective-permute-start(bf16[192,768]{1,0:T(8,128)(2,1)S(1)} %get-tuple-element.248), channel_id=1, source_target_pairs={{0,1},{1,0},{2,3},{3,2},{4,5},{5,4},{6,7},{7,6},{8,9},{9,8},{10,11... | collective-permute-start | bytes 884744 | tf_op jit(solution)/shard_map/ppermute | solution.py:220
  88.4 9.4 %collective-permute-start.28 = (bf16[192,768]{1,0:T(8,128)(2,1)S(1)}, bf16[192,768]{1,0:T(8,128)(2,1)S(1)}, u32[]{:S(2)}, u32[]{:S(2)}) collective-permute-start(bf16[192,768]{1,0:T(8,128)(2,1)S(1)} %get-tuple-element.276), channel_id=1, source_target_pairs={{0,1},{1,0},{2,3},{3,2},{4,5},{5,4},{6,7},{7,6},{8,9},{9,8},{10,11... | collective-permute-start | bytes 884744 | tf_op jit(solution)/shard_map/ppermute | solution.py:220
  93.3 11.6 %collective-permute-start.35 = (bf16[2,32,1152]{2,1,0:T(8,128)(2,1)S(1)}, bf16[2,32,1152]{2,1,0:T(8,128)(2,1)S(1)}, u32[]{:S(2)}, u32[]{:S(2)}) collective-permute-start(bf16[2,32,1152]{2,1,0:T(8,128)(2,1)S(1)} %fusion.5), channel_id=1, source_target_pairs={{0,8},{2,10},{4,12},{6,14},{8,16},{10,18},{12,20},{14,22},{16,24},... | collective-permute-start | bytes 442376 | tf_op jit(solution)/shard_map/ppermute | solution.py:229
  95.9 20.1 %collective-permute-start.33 = (bf16[2,32,1152]{2,1,0:T(8,128)(2,1)}, bf16[2,32,1152]{2,1,0:T(8,128)(2,1)}, u32[]{:S(2)}, u32[]{:S(2)}) collective-permute-start(bf16[2,32,1152]{2,1,0:T(8,128)(2,1)} %fusion.12), channel_id=1, source_target_pairs={{0,4},{2,6},{4,0},{6,2},{8,12},{10,14},{12,8},{14,10},{16,20},{18,... | collective-permute-start | bytes 442376 | tf_op jit(solution)/shard_map/ppermute | solution.py:223
  105.0 11.1 %collective-permute-start.36 = (bf16[2,32,1152]{2,1,0:T(8,128)(2,1)S(1)}, bf16[2,32,1152]{2,1,0:T(8,128)(2,1)S(1)}, u32[]{:S(2)}, u32[]{:S(2)}) collective-permute-start(bf16[2,32,1152]{2,1,0:T(8,128)(2,1)S(1)} %fusion.4), channel_id=1, source_target_pairs={{0,8},{2,10},{4,12},{6,14},{8,16},{10,18},{12,20},{14,22},{16,24},... | collective-permute-start | bytes 442376 | tf_op jit(solution)/shard_map/ppermute | solution.py:229
  106.7 9.4 %collective-permute-start.34 = (bf16[2,32,1152]{2,1,0:T(8,128)(2,1)S(1)}, bf16[2,32,1152]{2,1,0:T(8,128)(2,1)S(1)}, u32[]{:S(2)}, u32[]{:S(2)}) collective-permute-start(bf16[2,32,1152]{2,1,0:T(8,128)(2,1)S(1)} %fusion.13), channel_id=1, source_target_pairs={{0,4},{2,6},{4,0},{6,2},{8,12},{10,14},{12,8},{14,10},{16,20},{18,... | collective-permute-start | bytes 442376 | tf_op jit(solution)/shard_map/ppermute | solution.py:223
  123.9 8.5 %collective-permute-start.43 = (f32[16,1024]{1,0:T(8,128)S(1)}, f32[16,1024]{1,0:T(8,128)S(1)}, u32[]{:S(2)}, u32[]{:S(2)}) collective-permute-start(f32[16,1024]{1,0:T(8,128)S(1)} %fusion.15), channel_id=1, source_target_pairs={{0,16},{2,18},{4,20},{6,22},{8,24},{10,26},{12,28},{14,30},{16,0},... | collective-permute-start | bytes 196616 | tf_op jit(solution)/shard_map/ppermute | solution.py:232
  (41 other events, 367.3 us)
